TPU v7x, 32 devices: a whole 2x2x4 slice. The times are simulated.
32 devices in a mesh: group: 1, blk: 32 (over z, y, x, core).
Axes of the slice: x: 2, y: 2, z: 4, core: 2. Of those that a mesh axis runs over, the one named last changes fastest.
Arguments:
- depth_logits: float32 [32, 112, 32, 128], P(('group', 'blk')), may hold values from -18 to 300
- context: bfloat16 [32, 80, 32, 128], P(('group', 'blk')), may hold values from -6 to 6
- lidar_bins: int32 [32, 32, 128], P(('group', 'blk')), may hold values from -1 to 111, as said below
- az_map: int32 [8, 128], replicated, may hold values from 0 to 255, as said below
- rng_map: int32 [8, 112], replicated, may hold values from 0 to 511, as said below
- conv1_weight: bfloat16 [3, 3, 80, 256], replicated, may hold values from -0.21875 to 0.21875
- conv2_weight: bfloat16 [3, 3, 256, 256], replicated, may hold values from -0.125 to 0.125
- out_grad: bfloat16 [256, 512, 256], P(('group', 'blk')), may hold values from -6 to 6
Outputs:
- logit_grad: float32 [32, 112, 32, 128], P(('group', 'blk'))
- context_grad: bfloat16 [32, 80, 32, 128], P(('group', 'blk'))
- conv1_grad: float32 [3, 3, 80, 256], P('group')
- conv2_grad: float32 [3, 3, 256, 256], P('group')
Inputs may be any that keep to these rules, and one draw needn't show every extreme that they name: `lidar_bins`: -1 marks a pixel without a LiDAR return. `az_map`: with S = 32, the columns of camera c, in order and never going back, run through the azimuth cells (c * S - S // 4 + t) mod 256 for t = 0 to 3 * S // 2 - 1, each such cell taking two or three columns. `rng_map`: for each camera the range cell rises strictly with the depth bin.
All inputs are finite; a program needn't handle non-finite values.
Results may differ from a plain program's by a relative error of at most 0.024.
Values may be sent and summed in bfloat16 or wider, within the bound.
No kernel may reach another device: no remote copies, remote signals or barrier semaphores. Data moves between devices by JAX's collectives and lax.ppermute only.
A program may use at most 128 MiB of HBM per device.

v0:
```python
import functools

import jax
import jax.numpy as jnp
from jax import lax
from jax.experimental import pallas as pl
from jax.experimental.pallas import tpu as pltpu
from jax.sharding import PartitionSpec as P

DEPTH_WEIGHT = 3.0
TAPS = 3
LANES = 128
LIMIT = 60 * 1024 * 1024
F32 = jnp.float32
BF16 = jnp.bfloat16


def product(left, right, left_dim, right_dim):
    return lax.dot_general(
        left, right, (((left_dim,), (right_dim,)), ((), ())), preferred_element_type=F32
    )


def padded_rows(value, rows):
    missing = rows - value.shape[0]
    if missing == 0:
        return value
    return jnp.concatenate([value, jnp.zeros((missing, value.shape[1]), value.dtype)], axis=0)


def pool_kernel(
    rows, table, logits, context, probs, probs_t, context_t, kept, sent, wide_p, wide_c, plain_c
):
    columns = logits.shape[1]
    bins = logits.shape[0] // rows
    channels = context.shape[0] // rows
    half = kept.shape[0]
    scores = logits[...].reshape(bins, rows, columns)
    powers = jnp.exp(scores - jnp.max(scores, axis=0, keepdims=True))
    shares = powers / jnp.sum(powers, axis=0, keepdims=True)
    probs[...] = shares.reshape(bins * rows, columns)
    plain_c[...] = context[...].astype(F32)

    def turn(row, _):
        block = padded_rows(probs[pl.ds(row, bins, stride=rows), :], LANES)
        wide_p[pl.ds(row, columns, stride=rows), :] = jnp.transpose(block)
        block = padded_rows(plain_c[pl.ds(row, channels, stride=rows), :], LANES)
        wide_c[pl.ds(row, columns, stride=rows), :] = jnp.transpose(block)
        return 0

    lax.fori_loop(0, rows, turn, 0, unroll=4)
    for wide, narrow in ((wide_p, probs_t), (wide_c, context_t)):
        narrow[0 : columns * rows, :] = wide[...].astype(BF16)
        narrow[columns * rows :, :] = jnp.zeros((rows, LANES), BF16)
    line = lax.broadcasted_iota(jnp.int32, (TAPS * rows, LANES), 0)

    def cell_sum(slot):
        span = pl.ds(pl.multiple_of(table[0, slot] * rows, rows), TAPS * rows)
        features = context_t[span, :]
        features = jnp.where(line < table[1, slot] * rows, features, jnp.zeros_like(features))
        return product(features, probs_t[span, :], 0, 0)[:channels].astype(BF16)

    def one_cell(slot, _):
        sent[slot] = cell_sum(half + slot)
        kept[slot] = cell_sum(slot)
        return 0

    lax.fori_loop(0, half, one_cell, 0, unroll=2)


def act_grad_kernel(first, *refs):
    *sources, weight, out, grid = refs
    base = 0
    for source, low, high in zip(sources, first[0], first[1]):
        grid[base : base + high - low] = source[low:high]
        base += high - low
    hidden = weight.shape[3]
    taps = jnp.concatenate(
        [weight[TAPS - 1 - i].reshape(TAPS * hidden, hidden) for i in range(TAPS)], axis=1
    )
    length = grid.shape[1]
    place = lax.broadcasted_iota(jnp.int32, (hidden, length), 1)

    def one_row(row, start):
        stacked = jnp.concatenate([grid[start + i] for i in range(TAPS)], axis=1)
        sums = product(taps, stacked, 1, 1)
        ahead = pltpu.roll(sums[:hidden], length - 1, 1)
        behind = pltpu.roll(sums[2 * hidden :], 1, 1)
        total = sums[hidden : 2 * hidden]
        total = total + jnp.where(place < length - 1, ahead, 0.0)
        total = total + jnp.where(place > 0, behind, 0.0)
        out[row] = total.astype(BF16)

    starts = first[2]
    if len(starts) > 4:

        def step(row, _):
            one_row(row, row)
            return 0

        lax.fori_loop(0, len(starts), step, 0)
    else:
        for row, start in enumerate(starts):
            one_row(row, start)


def grid_kernel(
    band,
    own,
    edge,
    low_halo,
    high_halo,
    ten,
    two,
    ranges,
    weight_t,
    weight,
    inner_grad,
    outer_grad,
    upstream,
    grads,
    own_reply,
    other_reply,
    cells,
    grid_low,
    grid_taps,
    act_taps,
    slope_rows,
    slope_lanes,
    grid_grad,
):
    sector, channels, lanes = own.shape
    hidden, length = inner_grad.shape[1:]
    bands = band[1]
    mine = band[0]
    wide = sector + 4
    cells[2 : 2 + sector, :, :lanes] = own[...]
    cells[0:2, :, :lanes] = jnp.where(mine == 0, edge[sector - 2 : sector], low_halo[...])
    cells[2 + sector :, :, :lanes] = jnp.where(mine == bands - 1, edge[0:2], high_halo[...])
    cells[:, :, lanes:] = jnp.zeros((wide, channels, lanes), BF16)

    @pl.when(mine == 0)
    def _():
        cells[0 : sector + 2, :, lanes:] = ten[...]

    @pl.when(mine == bands - 1)
    def _():
        cells[2:, :, lanes:] = ten[...]

    @pl.when(mine == 1)
    def _():
        cells[0:2, :, lanes:] = two[...]

    @pl.when(mine == bands - 2)
    def _():
        cells[2 + sector :, :, lanes:] = two[...]

    spots = lax.broadcasted_iota(jnp.int32, (2 * lanes, length), 1)
    range_hot = (spots == ranges[...]).astype(F32).astype(BF16)

    def behind(value):
        place = lax.broadcasted_iota(jnp.int32, value.shape, 1)
        return jnp.where(place > 0, pltpu.roll(value, 1, 1), 0.0)

    def ahead(value):
        place = lax.broadcasted_iota(jnp.int32, value.shape, 1)
        return jnp.where(place < length - 1, pltpu.roll(value, length - 1, 1), 0.0)

    for chunk in range(0, wide, 4):
        block = cells[chunk : chunk + 4].reshape(4 * channels, 2 * lanes)
        summed = product(block, range_hot, 1, 0)
        for row in range(chunk, chunk + 4):
            value = summed[(row - chunk) * channels : (row - chunk + 1) * channels]
            grid_low[row * channels : (row + 1) * channels, :] = value.astype(BF16)
            if 0 < row < wide - 1:
                spread = pl.ds((row - 1) * length, length)
                grid_taps[0:channels, spread] = behind(value).astype(BF16)
                grid_taps[channels : 2 * channels, spread] = value.astype(BF16)
                grid_taps[2 * channels :, spread] = ahead(value).astype(BF16)

    def one_row(row, act_grad):
        source = pl.ds(pl.multiple_of(row * channels, channels), TAPS * channels)
        sums = product(weight_t[...], grid_low[source, :], 1, 0)
        value = behind(sums[:hidden]) + sums[hidden : 2 * hidden] + ahead(sums[2 * hidden :])
        logistic = 1.0 / (1.0 + jnp.exp(-value))
        active = value * logistic
        spread = pl.ds(pl.multiple_of(row * length, length), length)
        act_taps[0:hidden, spread] = behind(active).astype(BF16)
        act_taps[hidden : 2 * hidden, spread] = active.astype(BF16)
        act_taps[2 * hidden :, spread] = ahead(active).astype(BF16)
        slope = logistic * (1.0 + value * (1.0 - logistic))
        result = (act_grad.astype(F32) * slope).astype(BF16)
        slope_rows[pl.ds(pl.multiple_of(row * hidden, hidden), hidden), :] = result
        slope_lanes[:, spread] = result

    for row, index in ((0, 0), (1, 1), (sector, 2), (sector + 1, 3)):
        one_row(row, outer_grad[index])

    def inner(index, _):
        one_row(index + 2, inner_grad[index])
        return 0

    lax.fori_loop(0, sector - 2, inner, 0)
    count = sector * length
    tall = TAPS * hidden
    short = TAPS * channels

    def second(tap, _):
        window = pl.ds(pl.multiple_of(tap * length, length), count)
        result = product(act_taps[:, window], upstream[...], 1, 0)
        grads[pl.ds(pl.multiple_of(tap * tall, tall), tall), :] = result.astype(BF16)
        return 0

    lax.fori_loop(0, TAPS, second, 0)
    for tap in range(TAPS):
        result = product(
            grid_taps[:, tap * length : tap * length + count],
            slope_lanes[:, length : length + count],
            1,
            1,
        )
        base = TAPS * tall + tap * short
        grads[base : base + short, :] = result.astype(BF16)
    base = TAPS * (tall + short)
    grads[base:, :] = jnp.zeros((grads.shape[0] - base, hidden), BF16)
    flipped = jnp.concatenate([weight[TAPS - 1 - i] for i in range(TAPS)], axis=1)

    def back(row, _):
        source = pl.ds(pl.multiple_of(row * hidden, hidden), TAPS * hidden)
        sums = product(flipped, slope_rows[source, :], 1, 0)
        value = ahead(sums[:channels]) + sums[channels : 2 * channels]
        value = value + behind(sums[2 * channels :])
        grid_grad[pl.ds(pl.multiple_of(row * channels, channels), channels), :] = value.astype(BF16)
        return 0

    lax.fori_loop(0, sector, back, 0)
    picked = product(grid_grad[...], range_hot, 1, 1).astype(BF16)
    own_reply[...] = picked[:, :lanes].reshape(sector, channels, lanes)
    other_reply[...] = picked[:, lanes:].reshape(sector, channels, lanes)


def pixel_kernel(
    rows,
    table,
    own,
    partner,
    edge,
    theirs,
    probs,
    probs_t,
    context_t,
    lidar,
    logit_grad,
    context_grad,
    wedges,
    wide_p,
    wide_c,
    plain_c,
):
    columns = probs.shape[1]
    bins = probs.shape[0] // rows
    channels = context_grad.shape[0] // rows
    sector = own.shape[0]
    wedges[0:sector] = own[...]
    wedges[sector : 2 * sector] = partner[...]
    wedges[2 * sector : 3 * sector] = edge[...]
    wedges[3 * sector :] = theirs[...]
    wide_c[...] = jnp.zeros_like(wide_c)

    def one_cell(cell, _):
        span = pl.ds(pl.multiple_of(table[0, cell] * rows, rows), TAPS * rows)
        slope = wedges[table[1, cell]]
        wide_p[span, :] = product(context_t[span, :][:, :channels], slope, 1, 0)
        wide_c[span, 0:channels] = product(probs_t[span, :], slope, 1, 1)
        return 0

    lax.fori_loop(0, wedges.shape[0], one_cell, 0, unroll=4)

    def turn(row, _):
        block = jnp.transpose(wide_p[pl.ds(row, columns, stride=rows), :])
        logit_grad[pl.ds(row, bins, stride=rows), :] = block[:bins]
        block = jnp.transpose(wide_c[pl.ds(row, columns, stride=rows), :])
        plain_c[pl.ds(row, channels, stride=rows), :] = block[:channels]
        return 0

    lax.fori_loop(0, rows, turn, 0, unroll=4)
    context_grad[...] = plain_c[...].astype(BF16)
    share = probs[...].reshape(bins, rows, columns)
    slope = logit_grad[...].reshape(bins, rows, columns)
    expected = jnp.sum(share * slope, axis=0, keepdims=True)
    target = lidar[...][None]
    seen = jnp.where(target >= 0, DEPTH_WEIGHT, 0.0)
    level = lax.broadcasted_iota(jnp.int32, share.shape, 0)
    hit = jnp.where(level == target, DEPTH_WEIGHT, 0.0)
    result = share * (slope - expected) + (seen * share - hit)
    logit_grad[...] = result.reshape(bins * rows, columns)


def vmem():
    return pl.BlockSpec(memory_space=pltpu.VMEM)


def smem():
    return pl.BlockSpec(memory_space=pltpu.SMEM)


def call(kernel, out_shape, scratch, spaces, flops, moved, name):
    many = isinstance(out_shape, (list, tuple))
    return pl.pallas_call(
        kernel,
        out_shape=out_shape,
        in_specs=spaces,
        out_specs=[vmem() for _ in out_shape] if many else vmem(),
        scratch_shapes=scratch,
        compiler_params=pltpu.CompilerParams(vmem_limit_bytes=LIMIT),
        cost_estimate=pl.CostEstimate(flops=flops, bytes_accessed=moved, transcendentals=0),
        name=name,
    )


def halves(part, upper):
    size = part.shape[0] // 2
    keep = lax.dynamic_slice_in_dim(part, upper * size, size, 0)
    send = lax.dynamic_slice_in_dim(part, (1 - upper) * size, size, 0)
    return keep, send


def rounded_sum(left, right):
    return (left.astype(F32) + right.astype(F32)).astype(BF16)


def swapped(value, blocks, mask):
    return lax.ppermute(value, "blk", [(i, i ^ mask) for i in range(blocks)])


def joined(value, other, upper):
    return jnp.where(
        upper == 1,
        jnp.concatenate([other, value], axis=0),
        jnp.concatenate([value, other], axis=0),
    )


def total_over_blocks(value, position, blocks):
    count = blocks.bit_length() - 1
    bit = [(position >> k) & 1 for k in range(count)]
    keep, send = halves(value, bit[0])
    value = rounded_sum(keep, swapped(send, blocks, 1))
    later = list(range(1, count))
    parts = jnp.split(value, TAPS, axis=0)
    orders = [later[k % len(later) :] + later[: k % len(later)] for k in range(TAPS)]
    for step in range(len(later)):
        for k in range(TAPS):
            axis = orders[k][step]
            keep, send = halves(parts[k], bit[axis])
            parts[k] = rounded_sum(keep, swapped(send, blocks, 1 << axis))
    for step in reversed(range(len(later))):
        for k in range(TAPS):
            axis = orders[k][step]
            parts[k] = joined(parts[k], swapped(parts[k], blocks, 1 << axis), bit[axis])
    value = jnp.concatenate(parts, axis=0)
    return joined(value, swapped(value, blocks, 1), bit[0])


def shards(
    depth_logits, context, lidar_bins, az_map, rng_map, conv1_weight, conv2_weight, out_grad
):
    blocks = lax.axis_size("blk")
    position = lax.axis_index("blk")
    cameras, columns = az_map.shape
    bands = blocks // cameras
    sector, length, hidden = out_grad.shape
    bins, rows = depth_logits.shape[1:3]
    channels = context.shape[1]
    if bands != 4 or blocks & (blocks - 1) or bins > LANES or channels > LANES or sector < 6:
        raise ValueError("unsupported sizes")
    camera = position // bands
    band = position % bands
    sight = bands * sector
    seen = sight + sight // 2

    forward = [(i, (i + 1) % blocks) for i in range(blocks)]
    backward = [((i + 1) % blocks, i) for i in range(blocks)]
    low_grad = lax.ppermute(out_grad[sector - 2 :], "blk", forward)
    high_grad = lax.ppermute(out_grad[:2], "blk", backward)

    az_row = lax.dynamic_slice_in_dim(az_map, camera, 1, 0)[0]
    local = (az_row - (camera * sight - sight // 4)) % (blocks * sector)
    marks = jnp.arange(seen + 1, dtype=jnp.int32)
    begins = jnp.sum((local[None, :] < marks[:, None]).astype(jnp.int32), axis=1)
    near = band ^ 1
    order = jnp.stack(
        [1 + band, 1 + (band ^ 2), 5 * (band % 2), 1 + near, 1 + (near ^ 2), 5 * (near % 2)]
    )
    sixth = jnp.arange(6, dtype=jnp.int32)
    inverse = jnp.sum(jnp.where(order[None, :] == sixth[:, None], sixth[None, :], 0), axis=1)
    steps = jnp.arange(sector, dtype=jnp.int32)
    cells = (order[:, None] * sector + steps[None, :]).reshape(-1)
    slots = (inverse[:, None] * sector + steps[None, :]).reshape(-1)
    hot = (cells[:, None] == marks[None, :seen]).astype(jnp.int32)
    widths = begins[1:] - begins[:-1]
    pool_table = jnp.stack(
        [jnp.sum(hot * begins[None, :seen], axis=1), jnp.sum(hot * widths[None, :], axis=1)]
    )
    pixel_table = jnp.stack([begins[:seen], slots])

    turned = (columns + 1) * rows
    half = 3 * sector
    probs, probs_t, context_t, kept, sent = call(
        functools.partial(pool_kernel, rows),
        [
            jax.ShapeDtypeStruct((bins * rows, columns), F32),
            jax.ShapeDtypeStruct((turned, LANES), BF16),
            jax.ShapeDtypeStruct((turned, LANES), BF16),
            jax.ShapeDtypeStruct((half, channels, LANES), BF16),
            jax.ShapeDtypeStruct((half, channels, LANES), BF16),
        ],
        [
            pltpu.VMEM((columns * rows, LANES), F32),
            pltpu.VMEM((columns * rows, LANES), F32),
            pltpu.VMEM((channels * rows, columns), F32),
        ],
        [smem(), vmem(), vmem()],
        2 * seen * 3 * rows * LANES * LANES,
        20 * bins * rows * columns,
        "pool",
    )(
        pool_table,
        depth_logits[0].reshape(bins * rows, columns),
        context[0].reshape(channels * rows, columns),
    )

    row_flops = 2 * TAPS * TAPS * hidden * hidden * length

    def act_grad(sources, lows, highs, starts):
        total = sum(h - l for l, h in zip(lows, highs))
        return call(
            functools.partial(act_grad_kernel, (lows, highs, starts)),
            jax.ShapeDtypeStruct((len(starts), hidden, length), BF16),
            [pltpu.VMEM((total, length, hidden), BF16)],
            [vmem() for _ in sources] + [vmem()],
            row_flops * len(starts),
            2 * (total + len(starts)) * length * hidden,
            "act_grad",
        )(*sources, conv2_weight)

    inner_grad = act_grad([out_grad], (0,), (sector,), tuple(range(sector - 2)))
    outer_grad = act_grad(
        [low_grad, out_grad, out_grad, high_grad],
        (0, 0, sector - 2, 0),
        (2, 2, sector, 2),
        (0, 1, 4, 5),
    )

    summed = rounded_sum(kept, swapped(sent, blocks, 1))
    own = rounded_sum(summed[:sector], swapped(summed[sector : 2 * sector], blocks, 2))
    inward = [(i, i ^ 2) for i in range(blocks) if i % bands in (1, 2)]
    outward = [(i ^ 2, i) for i in range(blocks) if i % bands in (1, 2)]
    edge = rounded_sum(
        summed[2 * sector :], lax.ppermute(summed[2 * sector :], "blk", inward)
    )
    first = band == 0
    firsts = [i for i in range(blocks) if i % bands == 0]
    lasts = [i for i in range(blocks) if i % bands == bands - 1]
    ten = jnp.where(
        first,
        jnp.concatenate([edge, own[:2]], axis=0),
        jnp.concatenate([own[sector - 2 :], edge], axis=0),
    )
    two = jnp.where(first, edge[:2], edge[sector - 2 :])

    def to_next(value, more):
        pairs = [(i, (i - 1 - more) % blocks) for i in firsts]
        pairs = pairs + [(i, (i + 1 + more) % blocks) for i in lasts]
        return lax.ppermute(value, "blk", pairs)

    ten = to_next(ten, 0)
    two = to_next(two, 1)
    low_halo = lax.ppermute(
        own[sector - 2 :], "blk", [(i, i + 1) for i in range(blocks) if i not in lasts]
    )
    high_halo = lax.ppermute(
        own[:2], "blk", [(i, i - 1) for i in range(blocks) if i not in firsts]
    )
    other = jnp.where(band < bands // 2, camera - 1, camera + 1) % cameras
    ranges = jnp.concatenate(
        [lax.dynamic_slice_in_dim(rng_map, k, 1, 0) for k in (camera, other)], axis=0
    )
    ranges = jnp.pad(ranges, ((0, 0), (0, LANES - bins)), constant_values=-1).reshape(-1, 1)
    weight_t = conv1_weight.transpose(1, 3, 0, 2).reshape(TAPS * hidden, TAPS * channels)
    weight = conv1_weight.reshape(TAPS, TAPS * channels, hidden)
    grad_rows = TAPS * TAPS * (hidden + channels)
    unit = TAPS * blocks * 16
    grad_rows = -(-grad_rows // unit) * unit
    wide = sector + 2
    grads, own_reply, other_reply = call(
        grid_kernel,
        [
            jax.ShapeDtypeStruct((grad_rows, hidden), BF16),
            jax.ShapeDtypeStruct((sector, channels, LANES), BF16),
            jax.ShapeDtypeStruct((sector, channels, LANES), BF16),
        ],
        [
            pltpu.VMEM((sector + 4, channels, 2 * LANES), BF16),
            pltpu.VMEM(((sector + 4) * channels, length), BF16),
            pltpu.VMEM((TAPS * channels, wide * length), BF16),
            pltpu.VMEM((TAPS * hidden, wide * length), BF16),
            pltpu.VMEM((wide * hidden, length), BF16),
            pltpu.VMEM((hidden, wide * length), BF16),
            pltpu.VMEM((sector * channels, length), BF16),
        ],
        [smem()] + [vmem()] * 12,
        row_flops * (sector + 3 * sector // 2),
        20 * sector * length * hidden,
        "grid",
    )(
        jnp.stack([band, jnp.full_like(band, bands)]),
        own,
        edge,
        low_halo,
        high_halo,
        ten,
        two,
        ranges,
        weight_t,
        weight,
        inner_grad,
        outer_grad,
        out_grad.reshape(sector * length, hidden),
    )

    partner = swapped(own_reply, blocks, 2)
    edge_reply = to_next(other_reply, 0)
    passed = lax.ppermute(edge_reply, "blk", outward)
    outer = jnp.logical_or(first, band == bands - 1)
    edge_reply = jnp.where(outer, edge_reply, passed)
    theirs = swapped(
        jnp.concatenate([own_reply, partner, edge_reply], axis=0), blocks, 1
    )
    total = total_over_blocks(grads, position, blocks)

    logit_grad, context_grad = call(
        functools.partial(pixel_kernel, rows),
        [
            jax.ShapeDtypeStruct((bins * rows, columns), F32),
            jax.ShapeDtypeStruct((channels * rows, columns), BF16),
        ],
        [
            pltpu.VMEM((seen, channels, LANES), BF16),
            pltpu.VMEM((turned, LANES), F32),
            pltpu.VMEM((turned, LANES), F32),
            pltpu.VMEM((channels * rows, columns), F32),
        ],
        [smem()] + [vmem()] * 8,
        4 * seen * 3 * rows * LANES * LANES,
        20 * bins * rows * columns,
        "pixel",
    )(pixel_table, own_reply, partner, edge_reply, theirs, probs, probs_t, context_t, lidar_bins[0])

    second = TAPS * TAPS * hidden
    both = second + TAPS * TAPS * channels
    return (
        logit_grad.reshape(1, bins, rows, columns),
        context_grad.reshape(1, channels, rows, columns),
        total[second:both].astype(F32).reshape(TAPS, TAPS, channels, hidden),
        total[:second].astype(F32).reshape(TAPS, TAPS, hidden, hidden),
    )


def solution(mesh):
    return jax.shard_map(
        shards,
        mesh=mesh,
        in_specs=(
            P(("group", "blk"), None, None, None),
            P(("group", "blk"), None, None, None),
            P(("group", "blk"), None, None),
            P(),
            P(),
            P(),
            P(),
            P(("group", "blk"), None, None),
        ),
        out_specs=(
            P(("group", "blk"), None, None, None),
            P(("group", "blk"), None, None, None),
            P("group", None, None, None),
            P("group", None, None, None),
        ),
        check_vma=False,
    )
```

profile of v0, /device:TPU:0, one launch (start us, length us, event | category | flops | bytes accessed | tf_op | source)
XLA Modules:
  0.0 160.3 jit_solution(14178504819004383194)
XLA Ops:
  0.7 0.8 fusion.2
  2.8 13.1 %pool.1 = (f32[3584,128]{1,0:T(8,128)}, bf16[4128,128]{1,0:T(8,128)(2,1)}, bf16[4128,128]{1,0:T(8,128)(2,1)}, bf16[24,80,128]{2,1,0:T(8,128)(2,1)}, bf16[24,80,128]{2,1,0:T(8,128)(2,1)}) custom-call(s32[2,48]{1,0:T(2,128)} %pad_add_fusion.1.table, f32[3584,128]{1,0:T(8,128)} %bitcast.28, bf16[2560,128]{1,0:T(8,128)(2,1)} %bitcast.30), custom_call_target="tpu_custom_call" | custom-call | flops 150994944 | bytes 9175040 | tf_op jit(solution)/shard_map/pool/pallas_call | solution.py:409
  16.4 1.0 fusion.5
  17.4 6.6 %collective-permute-start.8 = (bf16[2,512,256]{2,1,0:T(8,128)(2,1)}, bf16[2,512,256]{2,1,0:T(8,128)(2,1)S(1)}, u32[]{:S(2)}, u32[]{:S(2)}) collective-permute-start(bf16[2,512,256]{2,1,0:T(8,128)(2,1)} %get-tuple-element.26), channel_id=1, source_target_pairs={{1,0},{2,1},{3,2},{4,3},{5,4},{6,5},{7,6},{8,7},{9,8},{10,9},{11,1... | collective-permute-start | bytes 1572872 | tf_op jit(solution)/shard_map/ppermute | solution.py:385
  24.0 0.8 constant_dynamic-slice_fusion.14
  24.8 9.0 %act_grad.2.inner_grad = bf16[6,256,512]{2,1,0:T(8,128)(2,1)} custom-call(bf16[8,512,256]{2,1,0:T(8,128)(2,1)} %refs_2_.1, bf16[3,3,256,256]{3,2,1,0:T(8,128)(2,1)} %refs_4_.1), custom_call_target="tpu_custom_call" | custom-call | flops 3623878656 | bytes 3670016 | tf_op jit(solution)/shard_map/act_grad/pallas_call | solution.py:437
  34.0 1.3 collective-permute-start.2
  35.3 2.7 %collective-permute-start.1 = (bf16[8,80,128]{2,1,0:T(8,128)(2,1)S(1)}, bf16[8,80,128]{2,1,0:T(8,128)(2,1)S(1)}, u32[]{:S(2)}, u32[]{:S(2)}) collective-permute-start(bf16[8,80,128]{2,1,0:T(8,128)(2,1)S(1)} %get-tuple-element.34), channel_id=1, source_target_pairs={{0,2},{1,3},{2,0},{3,1},{4,6},{5,7},{6,4},{7,5},{8,10},{9,11},{10,... | collective-permute-start | bytes 491528 | tf_op jit(solution)/shard_map/ppermute | solution.py:333
  38.0 0.8 copy.17.ranges
  39.4 1.1 reshape.146.weight_t
  40.5 0.7 pad_add_fusion.3.band
  41.2 1.8 %collective-permute-done.1 = bf16[8,80,128]{2,1,0:T(8,128)(2,1)S(1)} collective-permute-done((bf16[8,80,128]{2,1,0:T(8,128)(2,1)S(1)}, bf16[8,80,128]{2,1,0:T(8,128)(2,1)S(1)}, u32[]{:S(2)}, u32[]{:S(2)}) %collective-permute-start.1) | collective-permute-done | bytes 163872 | tf_op jit(solution)/shard_map/ppermute | solution.py:333
  43.1 1.3 collective-permute-start.3
  44.4 1.3 collective-permute-start.4
  45.7 5.0 %collective-permute-start.5 = (bf16[10,80,128]{2,1,0:T(8,128)(2,1)S(1)}, bf16[10,80,128]{2,1,0:T(8,128)(2,1)S(1)}, u32[]{:S(2)}, u32[]{:S(2)}) collective-permute-start(bf16[10,80,128]{2,1,0:T(8,128)(2,1)S(1)} %maximum_select_fusion.4), channel_id=1, source_target_pairs={{0,31},{4,3},{8,7},{12,11},{16,15},{20,19},{24,23},{28,27},{3,4},{... | collective-permute-start | bytes 614408 | tf_op jit(solution)/shard_map/ppermute | solution.py:475
  50.7 2.3 %collective-permute-start.6 = (bf16[2,80,128]{2,1,0:T(8,128)(2,1)S(1)}, bf16[2,80,128]{2,1,0:T(8,128)(2,1)S(1)}, u32[]{:S(2)}, u32[]{:S(2)}) collective-permute-start(bf16[2,80,128]{2,1,0:T(8,128)(2,1)S(1)} %slice_select_fusion), channel_id=1, source_target_pairs={{0,30},{4,2},{8,6},{12,10},{16,14},{20,18},{24,22},{28,26},{3,5},{... | collective-permute-start | bytes 122888 | tf_op jit(solution)/shard_map/ppermute | solution.py:475
  53.0 0.8 copy-done.10
  53.8 6.6 %act_grad.3.outer_grad = bf16[4,256,512]{2,1,0:T(8,128)(2,1)} custom-call(bf16[2,512,256]{2,1,0:T(8,128)(2,1)} %copy-done.9, bf16[8,512,256]{2,1,0:T(8,128)(2,1)} %refs_2_.1, bf16[8,512,256]{2,1,0:T(8,128)(2,1)} %refs_2_.1, bf16[2,512,256]{2,1,0:T(8,128)(2,1)} %copy-done.10, bf16[3,3,256,256]{3,2,1,0:T(8,128)(2,1)} %refs_4_.1), custom_call_target="tpu_custom_call" | custom-call | flops 2415919104 | bytes 3145728 | tf_op jit(solution)/shard_map/act_grad/pallas_call | solution.py:437
  61.2 23.4 %grid.1 = (bf16[3072,256]{1,0:T(8,128)(2,1)}, bf16[8,80,128]{2,1,0:T(8,128)(2,1)}, bf16[8,80,128]{2,1,0:T(8,128)(2,1)}) custom-call(s32[2]{0:T(128)} %pad_add_fusion.3.band, bf16[8,80,128]{2,1,0:T(8,128)(2,1)} %copy-done.8, bf16[8,80,128]{2,1,0:T(8,128)(2,1)} %copy-done.2, bf16[2,80,128]{2,1,0:T(8,128)(2,1)} %copy-done.12, bf16[2,80,128]{2,1,0:T(8,128)(2,1)} %copy-done.13, ...), custom_call_target="tpu_custom_call" | custom-call | flops 12079595520 | bytes 20971520 | tf_op jit(solution)/shard_map/grid/pallas_call | solution.py:496
  84.5 1.3 constant_dynamic-slice_fusion.12
  85.9 3.9 %collective-permute-start.10 = (bf16[8,80,128]{2,1,0:T(8,128)(2,1)}, bf16[8,80,128]{2,1,0:T(8,128)(2,1)}, u32[]{:S(2)}, u32[]{:S(2)}) collective-permute-start(bf16[8,80,128]{2,1,0:T(8,128)(2,1)} %get-tuple-element.17), channel_id=1, source_target_pairs={{0,31},{4,3},{8,7},{12,11},{16,15},{20,19},{24,23},{28,27},{3,4},{... | collective-permute-start | bytes 491528 | tf_op jit(solution)/shard_map/ppermute | solution.py:475
  90.1 7.6 %collective-permute-done.10 = bf16[8,80,128]{2,1,0:T(8,128)(2,1)} collective-permute-done((bf16[8,80,128]{2,1,0:T(8,128)(2,1)}, bf16[8,80,128]{2,1,0:T(8,128)(2,1)}, u32[]{:S(2)}, u32[]{:S(2)}) %collective-permute-start.10) | collective-permute-done | bytes 163872 | tf_op jit(solution)/shard_map/ppermute | solution.py:475
  97.7 1.5 collective-permute-start.11
  99.8 5.4 %collective-permute-done.30 = bf16[256,256]{1,0:T(8,128)(2,1)S(1)} collective-permute-done((bf16[256,256]{1,0:T(8,128)(2,1)S(1)}, bf16[256,256]{1,0:T(8,128)(2,1)S(1)}, u32[]{:S(2)}, u32[]{:S(2)}) %collective-permute-start.30) | collective-permute-done | bytes 131104 | tf_op jit(solution)/shard_map/ppermute | solution.py:333
  105.5 1.3 collective-permute-start.23
  106.9 4.3 %collective-permute-done.31 = bf16[128,256]{1,0:T(8,128)(2,1)S(1)} collective-permute-done((bf16[128,256]{1,0:T(8,128)(2,1)S(1)}, bf16[128,256]{1,0:T(8,128)(2,1)S(1)}, u32[]{:S(2)}, u32[]{:S(2)}) %collective-permute-start.31) | collective-permute-done | bytes 65568 | tf_op jit(solution)/shard_map/ppermute | solution.py:333
  111.4 1.8 %collective-permute-start.24 = (bf16[64,256]{1,0:T(8,128)(2,1)S(1)}, bf16[64,256]{1,0:T(8,128)(2,1)S(1)}, u32[]{:S(2)}, u32[]{:S(2)}) collective-permute-start(bf16[64,256]{1,0:T(8,128)(2,1)S(1)} %constant_dynamic-slice_fusion.5), channel_id=1, source_target_pairs={{0,16},{1,17},{2,18},{3,19},{4,20},{5,21},{6,22},{7,23},{8,24},{9,... | collective-permute-start | bytes 98312 | tf_op jit(solution)/shard_map/ppermute | solution.py:333
  113.5 1.8 %collective-permute-done.32 = bf16[64,256]{1,0:T(8,128)(2,1)S(1)} collective-permute-done((bf16[64,256]{1,0:T(8,128)(2,1)S(1)}, bf16[64,256]{1,0:T(8,128)(2,1)S(1)}, u32[]{:S(2)}, u32[]{:S(2)}) %collective-permute-start.32) | collective-permute-done | bytes 32800 | tf_op jit(solution)/shard_map/ppermute | solution.py:333
  115.4 1.1 collective-permute-done.24
  116.5 1.9 %collective-permute-start.25 = (bf16[32,256]{1,0:T(8,128)(2,1)S(1)}, bf16[32,256]{1,0:T(8,128)(2,1)S(1)}, u32[]{:S(2)}, u32[]{:S(2)}) collective-permute-start(bf16[32,256]{1,0:T(8,128)(2,1)S(1)} %constant_dynamic-slice_fusion.4), channel_id=1, source_target_pairs={{0,2},{1,3},{2,0},{3,1},{4,6},{5,7},{6,4},{7,5},{8,10},{9,11},{10,... | collective-permute-start | bytes 49160 | tf_op jit(solution)/shard_map/ppermute | solution.py:333
  119.2 1.1 collective-permute-done.25
  120.3 1.9 %collective-permute-start.26 = (bf16[32,256]{1,0:T(8,128)(2,1)S(1)}, bf16[32,256]{1,0:T(8,128)(2,1)S(1)}, u32[]{:S(2)}, u32[]{:S(2)}) collective-permute-start(bf16[32,256]{1,0:T(8,128)(2,1)S(1)} %add_convert_fusion.14), channel_id=1, source_target_pairs={{0,2},{1,3},{2,0},{3,1},{4,6},{5,7},{6,4},{7,5},{8,10},{9,11},{10,... | collective-permute-start | bytes 49160 | tf_op jit(solution)/shard_map/ppermute | solution.py:333
  122.2 0.9 collective-permute-done.17
  123.3 2.0 %collective-permute-start.35 = (bf16[64,256]{1,0:T(8,128)(2,1)S(1)}, bf16[64,256]{1,0:T(8,128)(2,1)S(1)}, u32[]{:S(2)}, u32[]{:S(2)}) collective-permute-start(bf16[64,256]{1,0:T(8,128)(2,1)S(1)} %maximum_select_fusion.13), channel_id=1, source_target_pairs={{0,2},{1,3},{2,0},{3,1},{4,6},{5,7},{6,4},{7,5},{8,10},{9,11},{10,... | collective-permute-start | bytes 98312 | tf_op jit(solution)/shard_map/ppermute | solution.py:333
  125.3 1.1 collective-permute-start.27
  126.5 1.4 collective-permute-done.18
  128.0 2.2 %collective-permute-start.36 = (bf16[128,256]{1,0:T(8,128)(2,1)S(1)}, bf16[128,256]{1,0:T(8,128)(2,1)S(1)}, u32[]{:S(2)}, u32[]{:S(2)}) collective-permute-start(bf16[128,256]{1,0:T(8,128)(2,1)S(1)} %maximum_select_fusion.10), channel_id=1, source_target_pairs={{0,16},{1,17},{2,18},{3,19},{4,20},{5,21},{6,22},{7,23},{8,24},{9,... | collective-permute-start | bytes 196616 | tf_op jit(solution)/shard_map/ppermute | solution.py:333
  130.7 1.2 collective-permute-done.19
  132.1 1.1 collective-permute-done.36
  133.2 2.1 %collective-permute-start.37 = (bf16[256,256]{1,0:T(8,128)(2,1)S(1)}, bf16[256,256]{1,0:T(8,128)(2,1)S(1)}, u32[]{:S(2)}, u32[]{:S(2)}) collective-permute-start(bf16[256,256]{1,0:T(8,128)(2,1)S(1)} %maximum_select_fusion.7), channel_id=1, source_target_pairs={{0,8},{1,9},{2,10},{3,11},{4,12},{5,13},{6,14},{7,15},{8,0},{9,1},... | collective-permute-start | bytes 393224 | tf_op jit(solution)/shard_map/ppermute | solution.py:333
  136.8 1.5 collective-permute-done.37
  138.4 2.0 %collective-permute-done.29 = bf16[256,256]{1,0:T(8,128)(2,1)S(1)} collective-permute-done((bf16[256,256]{1,0:T(8,128)(2,1)S(1)}, bf16[256,256]{1,0:T(8,128)(2,1)S(1)}, u32[]{:S(2)}, u32[]{:S(2)}) %collective-permute-start.29) | collective-permute-done | bytes 131104 | tf_op jit(solution)/shard_map/ppermute | solution.py:333
  140.5 0.8 collective-permute-done.21
  141.5 0.9 broadcast_select_fusion.edge
  143.4 1.2 collective-permute-done.12.theirs
  144.6 12.6 %pixel.1 = (f32[3584,128]{1,0:T(8,128)}, bf16[2560,128]{1,0:T(8,128)(2,1)}) custom-call(s32[2,48]{1,0:T(2,128)} %pad_add_fusion.table, bf16[8,80,128]{2,1,0:T(8,128)(2,1)} %get-tuple-element.16.own, bf16[8,80,128]{2,1,0:T(8,128)(2,1)} %copy-done.4, bf16[8,80,128]{2,1,0:T(8,128)(2,1)} %copy-done.1, bf16[24,80,128]{2,1,0:T(8,128)(2,1)} %collective-permute-done.12.theirs, ...), custom_call_target="tpu_custom_call" | custom-call | flops 301989888 | bytes 9175040 | tf_op jit(solution)/shard_map/pixel/pallas_call | solution.py:542
  157.8 0.9 convert.2
  158.7 1.6 %convert.3 = f32[3,3,256,256]{3,2,1,0:T(8,128)} convert(bf16[3,3,256,256]{3,2,1,0:T(8,128)(2,1)S(1)} %bitcast.27) | non-fusion elementwise | flops 589824 | bytes 3538944 | tf_op jit(solution)/shard_map/reshape | solution.py:566
  (141 shorter events, 10.1 us)
Async XLA Ops:
  0.6 15.7 %copy-start.5 = (bf16[8,512,256]{2,1,0:T(8,128)(2,1)S(1)}, bf16[8,512,256]{2,1,0:T(8,128)(2,1)}, u32[]{:S(2)}) copy-start(bf16[8,512,256]{2,1,0:T(8,128)(2,1)} %refs_2_.1) | copy-start | bytes 6291460
  15.9 17.9 %collective-permute-start = (bf16[24,80,128]{2,1,0:T(8,128)(2,1)}, bf16[24,80,128]{2,1,0:T(8,128)(2,1)S(1)}, u32[]{:S(2)}, u32[]{:S(2)}) collective-permute-start(bf16[24,80,128]{2,1,0:T(8,128)(2,1)} %get-tuple-element.15), channel_id=1, source_target_pairs={{0,1},{1,0},{2,3},{3,2},{4,5},{5,4},{6,7},{7,6},{8,9},{9,8},{10,11... | collective-permute-start | bytes 1474568 | tf_op jit(solution)/shard_map/ppermute | solution.py:333
  17.4 33.3 %collective-permute-start.7 = (bf16[2,512,256]{2,1,0:T(8,128)(2,1)}, bf16[2,512,256]{2,1,0:T(8,128)(2,1)S(1)}, u32[]{:S(2)}, u32[]{:S(2)}) collective-permute-start(bf16[2,512,256]{2,1,0:T(8,128)(2,1)} %get-tuple-element.27), channel_id=1, source_target_pairs={{0,1},{1,2},{2,3},{3,4},{4,5},{5,6},{6,7},{7,8},{8,9},{9,10},{10,1... | collective-permute-start | bytes 1572872 | tf_op jit(solution)/shard_map/ppermute | solution.py:384
  17.4 35.6 %collective-permute-start.8 = (bf16[2,512,256]{2,1,0:T(8,128)(2,1)}, bf16[2,512,256]{2,1,0:T(8,128)(2,1)S(1)}, u32[]{:S(2)}, u32[]{:S(2)}) collective-permute-start(bf16[2,512,256]{2,1,0:T(8,128)(2,1)} %get-tuple-element.26), channel_id=1, source_target_pairs={{1,0},{2,1},{3,2},{4,3},{5,4},{6,5},{7,6},{8,7},{9,8},{10,9},{11,1... | collective-permute-start | bytes 1572872 | tf_op jit(solution)/shard_map/ppermute | solution.py:385
  24.8 9.0 %copy-start.6 = (bf16[24,80,128]{2,1,0:T(8,128)(2,1)S(1)}, bf16[24,80,128]{2,1,0:T(8,128)(2,1)}, u32[]{:S(2)}) copy-start(bf16[24,80,128]{2,1,0:T(8,128)(2,1)} %get-tuple-element.14) | copy-start | bytes 1474564
  33.8 5.0 %copy-start.7 = (bf16[3,3,80,256]{3,2,1,0:T(8,128)(2,1)S(1)}, bf16[3,3,80,256]{3,2,1,0:T(8,128)(2,1)}, u32[]{:S(2)}) copy-start(bf16[3,3,80,256]{3,2,1,0:T(8,128)(2,1)} %param.13) | copy-start | bytes 1105924
  34.0 7.2 %collective-permute-start.2 = (bf16[8,80,128]{2,1,0:T(8,128)(2,1)S(1)}, bf16[8,80,128]{2,1,0:T(8,128)(2,1)S(1)}, u32[]{:S(2)}, u32[]{:S(2)}) collective-permute-start(bf16[8,80,128]{2,1,0:T(8,128)(2,1)S(1)} %get-tuple-element.33), channel_id=1, source_target_pairs={{1,3},{2,0},{5,7},{6,4},{9,11},{10,8},{13,15},{14,12},{17,19},{18,... | collective-permute-start | bytes 491528 | tf_op jit(solution)/shard_map/ppermute | solution.py:460
  35.3 7.7 %collective-permute-start.1 = (bf16[8,80,128]{2,1,0:T(8,128)(2,1)S(1)}, bf16[8,80,128]{2,1,0:T(8,128)(2,1)S(1)}, u32[]{:S(2)}, u32[]{:S(2)}) collective-permute-start(bf16[8,80,128]{2,1,0:T(8,128)(2,1)S(1)} %get-tuple-element.34), channel_id=1, source_target_pairs={{0,2},{1,3},{2,0},{3,1},{4,6},{5,7},{6,4},{7,5},{8,10},{9,11},{10,... | collective-permute-start | bytes 491528 | tf_op jit(solution)/shard_map/ppermute | solution.py:333
  43.0 17.4 %copy-start.2 = (bf16[8,80,128]{2,1,0:T(8,128)(2,1)}, bf16[8,80,128]{2,1,0:T(8,128)(2,1)S(1)}, u32[]{:S(2)}) copy-start(bf16[8,80,128]{2,1,0:T(8,128)(2,1)S(1)} %get-tuple-element.31.edge) | copy-start | bytes 491524
  43.0 17.4 %copy-start.8 = (bf16[8,80,128]{2,1,0:T(8,128)(2,1)}, bf16[8,80,128]{2,1,0:T(8,128)(2,1)S(1)}, u32[]{:S(2)}) copy-start(bf16[8,80,128]{2,1,0:T(8,128)(2,1)S(1)} %get-tuple-element.32.own) | copy-start | bytes 491524
  43.1 17.4 %collective-permute-start.3 = (bf16[2,80,128]{2,1,0:T(8,128)(2,1)S(1)}, bf16[2,80,128]{2,1,0:T(8,128)(2,1)S(1)}, u32[]{:S(2)}, u32[]{:S(2)}) collective-permute-start(bf16[2,80,128]{2,1,0:T(8,128)(2,1)S(1)} %get-tuple-element.36), channel_id=1, source_target_pairs={{0,1},{1,2},{2,3},{4,5},{5,6},{6,7},{8,9},{9,10},{10,11},{12,13},{... | collective-permute-start | bytes 122888 | tf_op jit(solution)/shard_map/ppermute | solution.py:479
  44.4 16.1 %collective-permute-start.4 = (bf16[2,80,128]{2,1,0:T(8,128)(2,1)S(1)}, bf16[2,80,128]{2,1,0:T(8,128)(2,1)S(1)}, u32[]{:S(2)}, u32[]{:S(2)}) collective-permute-start(bf16[2,80,128]{2,1,0:T(8,128)(2,1)S(1)} %get-tuple-element.35), channel_id=1, source_target_pairs={{1,0},{2,1},{3,2},{5,4},{6,5},{7,6},{9,8},{10,9},{11,10},{13,12},{... | collective-permute-start | bytes 122888 | tf_op jit(solution)/shard_map/ppermute | solution.py:482
  45.7 14.8 %collective-permute-start.5 = (bf16[10,80,128]{2,1,0:T(8,128)(2,1)S(1)}, bf16[10,80,128]{2,1,0:T(8,128)(2,1)S(1)}, u32[]{:S(2)}, u32[]{:S(2)}) collective-permute-start(bf16[10,80,128]{2,1,0:T(8,128)(2,1)S(1)} %maximum_select_fusion.4), channel_id=1, source_target_pairs={{0,31},{4,3},{8,7},{12,11},{16,15},{20,19},{24,23},{28,27},{3,4},{... | collective-permute-start | bytes 614408 | tf_op jit(solution)/shard_map/ppermute | solution.py:475
  50.7 2.3 %copy-start.9 = (bf16[2,512,256]{2,1,0:T(8,128)(2,1)}, bf16[2,512,256]{2,1,0:T(8,128)(2,1)S(1)}, u32[]{:S(2)}) copy-start(bf16[2,512,256]{2,1,0:T(8,128)(2,1)S(1)} %collective-permute-done.7.refs_0_) | copy-start | bytes 1572868
  50.7 9.8 %collective-permute-start.6 = (bf16[2,80,128]{2,1,0:T(8,128)(2,1)S(1)}, bf16[2,80,128]{2,1,0:T(8,128)(2,1)S(1)}, u32[]{:S(2)}, u32[]{:S(2)}) collective-permute-start(bf16[2,80,128]{2,1,0:T(8,128)(2,1)S(1)} %slice_select_fusion), channel_id=1, source_target_pairs={{0,30},{4,2},{8,6},{12,10},{16,14},{20,18},{24,22},{28,26},{3,5},{... | collective-permute-start | bytes 122888 | tf_op jit(solution)/shard_map/ppermute | solution.py:475
  84.5 5.5 %copy-start.3 = (bf16[8,80,128]{2,1,0:T(8,128)(2,1)S(1)}, bf16[8,80,128]{2,1,0:T(8,128)(2,1)}, u32[]{:S(2)}) copy-start(bf16[8,80,128]{2,1,0:T(8,128)(2,1)} %get-tuple-element.16.own) | copy-start | bytes 491524
  84.5 14.7 %copy-start = (bf16[3072,256]{1,0:T(8,128)(2,1)S(1)}, bf16[3072,256]{1,0:T(8,128)(2,1)}, u32[]{:S(2)}) copy-start(bf16[3072,256]{1,0:T(8,128)(2,1)} %get-tuple-element.23) | copy-start | bytes 4718596
  85.9 13.3 %collective-permute-start.13 = (bf16[1536,256]{1,0:T(8,128)(2,1)S(1)}, bf16[1536,256]{1,0:T(8,128)(2,1)S(1)}, u32[]{:S(2)}, u32[]{:S(2)}) collective-permute-start(bf16[1536,256]{1,0:T(8,128)(2,1)S(1)} %constant_dynamic-slice_fusion.12), channel_id=1, source_target_pairs={{0,1},{1,0},{2,3},{3,2},{4,5},{5,4},{6,7},{7,6},{8,9},{9,8},{10,11... | collective-permute-start | bytes 2359304 | tf_op jit(solution)/shard_map/ppermute | solution.py:333
  85.9 11.7 %collective-permute-start.10 = (bf16[8,80,128]{2,1,0:T(8,128)(2,1)}, bf16[8,80,128]{2,1,0:T(8,128)(2,1)}, u32[]{:S(2)}, u32[]{:S(2)}) collective-permute-start(bf16[8,80,128]{2,1,0:T(8,128)(2,1)} %get-tuple-element.17), channel_id=1, source_target_pairs={{0,31},{4,3},{8,7},{12,11},{16,15},{20,19},{24,23},{28,27},{3,4},{... | collective-permute-start | bytes 491528 | tf_op jit(solution)/shard_map/ppermute | solution.py:475
  90.0 52.5 %collective-permute-start.9 = (bf16[8,80,128]{2,1,0:T(8,128)(2,1)S(1)}, bf16[8,80,128]{2,1,0:T(8,128)(2,1)S(1)}, u32[]{:S(2)}, u32[]{:S(2)}) collective-permute-start(bf16[8,80,128]{2,1,0:T(8,128)(2,1)S(1)} %copy-done.3), channel_id=1, source_target_pairs={{0,2},{1,3},{2,0},{3,1},{4,6},{5,7},{6,4},{7,5},{8,10},{9,11},{10,... | collective-permute-start | bytes 491528 | tf_op jit(solution)/shard_map/ppermute | solution.py:333
  97.7 43.8 %collective-permute-start.11 = (bf16[8,80,128]{2,1,0:T(8,128)(2,1)}, bf16[8,80,128]{2,1,0:T(8,128)(2,1)S(1)}, u32[]{:S(2)}, u32[]{:S(2)}) collective-permute-start(bf16[8,80,128]{2,1,0:T(8,128)(2,1)} %collective-permute-done.10), channel_id=1, source_target_pairs={{3,1},{0,2},{7,5},{4,6},{11,9},{8,10},{15,13},{12,14},{19,17},{16,... | collective-permute-start | bytes 491528 | tf_op jit(solution)/shard_map/ppermute | solution.py:534
  99.5 5.7 %collective-permute-start.30 = (bf16[256,256]{1,0:T(8,128)(2,1)S(1)}, bf16[256,256]{1,0:T(8,128)(2,1)S(1)}, u32[]{:S(2)}, u32[]{:S(2)}) collective-permute-start(bf16[256,256]{1,0:T(8,128)(2,1)S(1)} %constant_dynamic-slice_fusion.3), channel_id=1, source_target_pairs={{0,8},{1,9},{2,10},{3,11},{4,12},{5,13},{6,14},{7,15},{8,0},{9,1},... | collective-permute-start | bytes 393224 | tf_op jit(solution)/shard_map/ppermute | solution.py:333
  99.6 5.8 %collective-permute-start.22 = (bf16[256,256]{1,0:T(8,128)(2,1)S(1)}, bf16[256,256]{1,0:T(8,128)(2,1)S(1)}, u32[]{:S(2)}, u32[]{:S(2)}) collective-permute-start(bf16[256,256]{1,0:T(8,128)(2,1)S(1)} %constant_dynamic-slice_fusion.7), channel_id=1, source_target_pairs={{0,4},{1,5},{2,6},{3,7},{4,0},{5,1},{6,2},{7,3},{8,12},{9,13},{10,... | collective-permute-start | bytes 393224 | tf_op jit(solution)/shard_map/ppermute | solution.py:333
  99.7 7.1 %collective-permute-start.14 = (bf16[256,256]{1,0:T(8,128)(2,1)S(1)}, bf16[256,256]{1,0:T(8,128)(2,1)S(1)}, u32[]{:S(2)}, u32[]{:S(2)}) collective-permute-start(bf16[256,256]{1,0:T(8,128)(2,1)S(1)} %constant_dynamic-slice_fusion.11), channel_id=1, source_target_pairs={{0,2},{1,3},{2,0},{3,1},{4,6},{5,7},{6,4},{7,5},{8,10},{9,11},{10,... | collective-permute-start | bytes 393224 | tf_op jit(solution)/shard_map/ppermute | solution.py:333
  105.3 5.9 %collective-permute-start.31 = (bf16[128,256]{1,0:T(8,128)(2,1)S(1)}, bf16[128,256]{1,0:T(8,128)(2,1)S(1)}, u32[]{:S(2)}, u32[]{:S(2)}) collective-permute-start(bf16[128,256]{1,0:T(8,128)(2,1)S(1)} %constant_dynamic-slice_fusion.2), channel_id=1, source_target_pairs={{0,16},{1,17},{2,18},{3,19},{4,20},{5,21},{6,22},{7,23},{8,24},{9,... | collective-permute-start | bytes 196616 | tf_op jit(solution)/shard_map/ppermute | solution.py:333
  105.5 5.9 %collective-permute-start.23 = (bf16[128,256]{1,0:T(8,128)(2,1)S(1)}, bf16[128,256]{1,0:T(8,128)(2,1)S(1)}, u32[]{:S(2)}, u32[]{:S(2)}) collective-permute-start(bf16[128,256]{1,0:T(8,128)(2,1)S(1)} %constant_dynamic-slice_fusion.6), channel_id=1, source_target_pairs={{0,8},{1,9},{2,10},{3,11},{4,12},{5,13},{6,14},{7,15},{8,0},{9,1},... | collective-permute-start | bytes 196616 | tf_op jit(solution)/shard_map/ppermute | solution.py:333
  106.9 6.3 %collective-permute-start.15 = (bf16[128,256]{1,0:T(8,128)(2,1)S(1)}, bf16[128,256]{1,0:T(8,128)(2,1)S(1)}, u32[]{:S(2)}, u32[]{:S(2)}) collective-permute-start(bf16[128,256]{1,0:T(8,128)(2,1)S(1)} %constant_dynamic-slice_fusion.10), channel_id=1, source_target_pairs={{0,4},{1,5},{2,6},{3,7},{4,0},{5,1},{6,2},{7,3},{8,12},{9,13},{10,... | collective-permute-start | bytes 196616 | tf_op jit(solution)/shard_map/ppermute | solution.py:333
  111.3 4.0 %collective-permute-start.32 = (bf16[64,256]{1,0:T(8,128)(2,1)S(1)}, bf16[64,256]{1,0:T(8,128)(2,1)S(1)}, u32[]{:S(2)}, u32[]{:S(2)}) collective-permute-start(bf16[64,256]{1,0:T(8,128)(2,1)S(1)} %constant_dynamic-slice_fusion.1), channel_id=1, source_target_pairs={{0,2},{1,3},{2,0},{3,1},{4,6},{5,7},{6,4},{7,5},{8,10},{9,11},{10,... | collective-permute-start | bytes 98312 | tf_op jit(solution)/shard_map/ppermute | solution.py:333
  111.4 5.0 %collective-permute-start.24 = (bf16[64,256]{1,0:T(8,128)(2,1)S(1)}, bf16[64,256]{1,0:T(8,128)(2,1)S(1)}, u32[]{:S(2)}, u32[]{:S(2)}) collective-permute-start(bf16[64,256]{1,0:T(8,128)(2,1)S(1)} %constant_dynamic-slice_fusion.5), channel_id=1, source_target_pairs={{0,16},{1,17},{2,18},{3,19},{4,20},{5,21},{6,22},{7,23},{8,24},{9,... | collective-permute-start | bytes 98312 | tf_op jit(solution)/shard_map/ppermute | solution.py:333
  113.2 5.2 %collective-permute-start.16 = (bf16[64,256]{1,0:T(8,128)(2,1)S(1)}, bf16[64,256]{1,0:T(8,128)(2,1)S(1)}, u32[]{:S(2)}, u32[]{:S(2)}) collective-permute-start(bf16[64,256]{1,0:T(8,128)(2,1)S(1)} %constant_dynamic-slice_fusion.9), channel_id=1, source_target_pairs={{0,8},{1,9},{2,10},{3,11},{4,12},{5,13},{6,14},{7,15},{8,0},{9,1},... | collective-permute-start | bytes 98312 | tf_op jit(solution)/shard_map/ppermute | solution.py:333
  115.3 3.8 %collective-permute-start.33 = (bf16[32,256]{1,0:T(8,128)(2,1)S(1)}, bf16[32,256]{1,0:T(8,128)(2,1)S(1)}, u32[]{:S(2)}, u32[]{:S(2)}) collective-permute-start(bf16[32,256]{1,0:T(8,128)(2,1)S(1)} %constant_dynamic-slice_fusion), channel_id=1, source_target_pairs={{0,4},{1,5},{2,6},{3,7},{4,0},{5,1},{6,2},{7,3},{8,12},{9,13},{10,... | collective-permute-start | bytes 49160 | tf_op jit(solution)/shard_map/ppermute | solution.py:333
  116.5 3.8 %collective-permute-start.25 = (bf16[32,256]{1,0:T(8,128)(2,1)S(1)}, bf16[32,256]{1,0:T(8,128)(2,1)S(1)}, u32[]{:S(2)}, u32[]{:S(2)}) collective-permute-start(bf16[32,256]{1,0:T(8,128)(2,1)S(1)} %constant_dynamic-slice_fusion.4), channel_id=1, source_target_pairs={{0,2},{1,3},{2,0},{3,1},{4,6},{5,7},{6,4},{7,5},{8,10},{9,11},{10,... | collective-permute-start | bytes 49160 | tf_op jit(solution)/shard_map/ppermute | solution.py:333
  118.4 4.7 %collective-permute-start.17 = (bf16[32,256]{1,0:T(8,128)(2,1)S(1)}, bf16[32,256]{1,0:T(8,128)(2,1)S(1)}, u32[]{:S(2)}, u32[]{:S(2)}) collective-permute-start(bf16[32,256]{1,0:T(8,128)(2,1)S(1)} %constant_dynamic-slice_fusion.8), channel_id=1, source_target_pairs={{0,16},{1,17},{2,18},{3,19},{4,20},{5,21},{6,22},{7,23},{8,24},{9,... | collective-permute-start | bytes 49160 | tf_op jit(solution)/shard_map/ppermute | solution.py:333
  119.1 4.2 %collective-permute-start.34 = (bf16[32,256]{1,0:T(8,128)(2,1)S(1)}, bf16[32,256]{1,0:T(8,128)(2,1)S(1)}, u32[]{:S(2)}, u32[]{:S(2)}) collective-permute-start(bf16[32,256]{1,0:T(8,128)(2,1)S(1)} %add_convert_fusion.13), channel_id=1, source_target_pairs={{0,4},{1,5},{2,6},{3,7},{4,0},{5,1},{6,2},{7,3},{8,12},{9,13},{10,... | collective-permute-start | bytes 49160 | tf_op jit(solution)/shard_map/ppermute | solution.py:333
  120.3 5.0 %collective-permute-start.26 = (bf16[32,256]{1,0:T(8,128)(2,1)S(1)}, bf16[32,256]{1,0:T(8,128)(2,1)S(1)}, u32[]{:S(2)}, u32[]{:S(2)}) collective-permute-start(bf16[32,256]{1,0:T(8,128)(2,1)S(1)} %add_convert_fusion.14), channel_id=1, source_target_pairs={{0,2},{1,3},{2,0},{3,1},{4,6},{5,7},{6,4},{7,5},{8,10},{9,11},{10,... | collective-permute-start | bytes 49160 | tf_op jit(solution)/shard_map/ppermute | solution.py:333
  123.1 4.7 %collective-permute-start.18 = (bf16[32,256]{1,0:T(8,128)(2,1)S(1)}, bf16[32,256]{1,0:T(8,128)(2,1)S(1)}, u32[]{:S(2)}, u32[]{:S(2)}) collective-permute-start(bf16[32,256]{1,0:T(8,128)(2,1)S(1)} %add_convert_fusion.15), channel_id=1, source_target_pairs={{0,16},{1,17},{2,18},{3,19},{4,20},{5,21},{6,22},{7,23},{8,24},{9,... | collective-permute-start | bytes 49160 | tf_op jit(solution)/shard_map/ppermute | solution.py:333
  123.3 4.7 %collective-permute-start.35 = (bf16[64,256]{1,0:T(8,128)(2,1)S(1)}, bf16[64,256]{1,0:T(8,128)(2,1)S(1)}, u32[]{:S(2)}, u32[]{:S(2)}) collective-permute-start(bf16[64,256]{1,0:T(8,128)(2,1)S(1)} %maximum_select_fusion.13), channel_id=1, source_target_pairs={{0,2},{1,3},{2,0},{3,1},{4,6},{5,7},{6,4},{7,5},{8,10},{9,11},{10,... | collective-permute-start | bytes 98312 | tf_op jit(solution)/shard_map/ppermute | solution.py:333
  125.3 5.0 %collective-permute-start.27 = (bf16[64,256]{1,0:T(8,128)(2,1)S(1)}, bf16[64,256]{1,0:T(8,128)(2,1)S(1)}, u32[]{:S(2)}, u32[]{:S(2)}) collective-permute-start(bf16[64,256]{1,0:T(8,128)(2,1)S(1)} %maximum_select_fusion.12), channel_id=1, source_target_pairs={{0,16},{1,17},{2,18},{3,19},{4,20},{5,21},{6,22},{7,23},{8,24},{9,... | collective-permute-start | bytes 98312 | tf_op jit(solution)/shard_map/ppermute | solution.py:333
  127.9 4.0 %collective-permute-start.19 = (bf16[64,256]{1,0:T(8,128)(2,1)S(1)}, bf16[64,256]{1,0:T(8,128)(2,1)S(1)}, u32[]{:S(2)}, u32[]{:S(2)}) collective-permute-start(bf16[64,256]{1,0:T(8,128)(2,1)S(1)} %maximum_select_fusion.11), channel_id=1, source_target_pairs={{0,8},{1,9},{2,10},{3,11},{4,12},{5,13},{6,14},{7,15},{8,0},{9,1},... | collective-permute-start | bytes 98312 | tf_op jit(solution)/shard_map/ppermute | solution.py:333
  128.0 5.2 %collective-permute-start.36 = (bf16[128,256]{1,0:T(8,128)(2,1)S(1)}, bf16[128,256]{1,0:T(8,128)(2,1)S(1)}, u32[]{:S(2)}, u32[]{:S(2)}) collective-permute-start(bf16[128,256]{1,0:T(8,128)(2,1)S(1)} %maximum_select_fusion.10), channel_id=1, source_target_pairs={{0,16},{1,17},{2,18},{3,19},{4,20},{5,21},{6,22},{7,23},{8,24},{9,... | collective-permute-start | bytes 196616 | tf_op jit(solution)/shard_map/ppermute | solution.py:333
  130.3 5.0 %collective-permute-start.28 = (bf16[128,256]{1,0:T(8,128)(2,1)S(1)}, bf16[128,256]{1,0:T(8,128)(2,1)S(1)}, u32[]{:S(2)}, u32[]{:S(2)}) collective-permute-start(bf16[128,256]{1,0:T(8,128)(2,1)S(1)} %maximum_select_fusion.9), channel_id=1, source_target_pairs={{0,8},{1,9},{2,10},{3,11},{4,12},{5,13},{6,14},{7,15},{8,0},{9,1},... | collective-permute-start | bytes 196616 | tf_op jit(solution)/shard_map/ppermute | solution.py:333
  131.9 4.3 %collective-permute-start.20 = (bf16[128,256]{1,0:T(8,128)(2,1)S(1)}, bf16[128,256]{1,0:T(8,128)(2,1)S(1)}, u32[]{:S(2)}, u32[]{:S(2)}) collective-permute-start(bf16[128,256]{1,0:T(8,128)(2,1)S(1)} %maximum_select_fusion.8), channel_id=1, source_target_pairs={{0,4},{1,5},{2,6},{3,7},{4,0},{5,1},{6,2},{7,3},{8,12},{9,13},{10,... | collective-permute-start | bytes 196616 | tf_op jit(solution)/shard_map/ppermute | solution.py:333
  133.2 5.0 %collective-permute-start.37 = (bf16[256,256]{1,0:T(8,128)(2,1)S(1)}, bf16[256,256]{1,0:T(8,128)(2,1)S(1)}, u32[]{:S(2)}, u32[]{:S(2)}) collective-permute-start(bf16[256,256]{1,0:T(8,128)(2,1)S(1)} %maximum_select_fusion.7), channel_id=1, source_target_pairs={{0,8},{1,9},{2,10},{3,11},{4,12},{5,13},{6,14},{7,15},{8,0},{9,1},... | collective-permute-start | bytes 393224 | tf_op jit(solution)/shard_map/ppermute | solution.py:333
  135.3 5.0 %collective-permute-start.29 = (bf16[256,256]{1,0:T(8,128)(2,1)S(1)}, bf16[256,256]{1,0:T(8,128)(2,1)S(1)}, u32[]{:S(2)}, u32[]{:S(2)}) collective-permute-start(bf16[256,256]{1,0:T(8,128)(2,1)S(1)} %maximum_select_fusion.6), channel_id=1, source_target_pairs={{0,4},{1,5},{2,6},{3,7},{4,0},{5,1},{6,2},{7,3},{8,12},{9,13},{10,... | collective-permute-start | bytes 393224 | tf_op jit(solution)/shard_map/ppermute | solution.py:333
  136.2 5.0 %collective-permute-start.21 = (bf16[256,256]{1,0:T(8,128)(2,1)S(1)}, bf16[256,256]{1,0:T(8,128)(2,1)S(1)}, u32[]{:S(2)}, u32[]{:S(2)}) collective-permute-start(bf16[256,256]{1,0:T(8,128)(2,1)S(1)} %maximum_select_fusion.5), channel_id=1, source_target_pairs={{0,2},{1,3},{2,0},{3,1},{4,6},{5,7},{6,4},{7,5},{8,10},{9,11},{10,... | collective-permute-start | bytes 393224 | tf_op jit(solution)/shard_map/ppermute | solution.py:333
  141.4 15.8 %collective-permute-start.38 = (bf16[1536,256]{1,0:T(8,128)(2,1)S(1)}, bf16[1536,256]{1,0:T(8,128)(2,1)S(1)}, u32[]{:S(2)}, u32[]{:S(2)}) collective-permute-start(bf16[1536,256]{1,0:T(8,128)(2,1)S(1)} %pad_maximum_fusion), channel_id=1, source_target_pairs={{0,1},{1,0},{2,3},{3,2},{4,5},{5,4},{6,7},{7,6},{8,9},{9,8},{10,11... | collective-permute-start | bytes 2359304 | tf_op jit(solution)/shard_map/ppermute | solution.py:333
  142.5 2.2 %copy-start.1 = (bf16[8,80,128]{2,1,0:T(8,128)(2,1)}, bf16[8,80,128]{2,1,0:T(8,128)(2,1)S(1)}, u32[]{:S(2)}) copy-start(bf16[8,80,128]{2,1,0:T(8,128)(2,1)S(1)} %broadcast_select_fusion.edge) | copy-start | bytes 491524
  142.6 2.1 %collective-permute-start.12 = (bf16[24,80,128]{2,1,0:T(8,128)(2,1)S(1)}, bf16[24,80,128]{2,1,0:T(8,128)(2,1)}, u32[]{:S(2)}, u32[]{:S(2)}) collective-permute-start(bf16[24,80,128]{2,1,0:T(8,128)(2,1)S(1)} %pad_maximum_fusion.1), channel_id=1, source_target_pairs={{0,1},{1,0},{2,3},{3,2},{4,5},{5,4},{6,7},{7,6},{8,9},{9,8},{10,11... | collective-permute-start | bytes 1474568 | tf_op jit(solution)/shard_map/ppermute | solution.py:333
  (6 other events, 5.5 us)
where the time goes:
time: 161 us; the launch traced here: 160 us
  Pallas kernels  64.7 us (40%)
  starting transfers between devices  43.5 us (27%)
  waiting for transfers between devices  34.4 us (21%)
  other arithmetic  8.57 us (5%)
  local copies, waits for them, and re-layouts  7.75 us (5%)
    ppermute x30, waiting for transfers between devices, swapped(): return lax.ppermute(value, 'blk', [(i, i ^ mask) for i in range(blocks)])  26.8 us
    pallas_call x1, Pallas kernels, shards(): call(grid_kernel, [jax.ShapeDtypeStruct((grad_rows, hidden), BF16), jax.S...  23.4 us
    ppermute x30, starting transfers between devices, swapped(): return lax.ppermute(value, 'blk', [(i, i ^ mask) for i in range(blocks)])  20.3 us
    pallas_call x2, Pallas kernels, act_grad(): call(functools.partial(act_grad_kernel, (lows, highs, starts)), jax.Shape...  15.6 us
    pallas_call x1, Pallas kernels, shards(): call(functools.partial(pool_kernel, rows), [jax.ShapeDtypeStruct((bins *...  13.1 us
    pallas_call x1, Pallas kernels, shards(): call(functools.partial(pixel_kernel, rows), [jax.ShapeDtypeStruct((bins *...  12.6 us
    ppermute x3, starting transfers between devices, to_next(): return lax.ppermute(value, 'blk', pairs)  11.1 us
    ppermute x3, waiting for transfers between devices, to_next(): return lax.ppermute(value, 'blk', pairs)  7.6 us
  transfers between devices with their start and end apart: 39, of which 18 were waited for; matrix products, arithmetic and copies ran while one was open for 5% of the time, Pallas kernels for 18%

commit v1 on v0

--- a/solution.py
+++ b/solution.py
@@ -29,7 +29,22 @@
 
 
 def pool_kernel(
-    rows, table, logits, context, probs, probs_t, context_t, kept, sent, wide_p, wide_c, plain_c
+    rows,
+    table,
+    logits,
+    context,
+    probs_out,
+    probs_t_out,
+    context_t_out,
+    kept,
+    sent,
+    probs,
+    probs_t,
+    context_t,
+    wide_p,
+    wide_c,
+    plain_c,
+    done,
 ):
     columns = logits.shape[1]
     bins = logits.shape[0] // rows
@@ -39,6 +54,8 @@
     powers = jnp.exp(scores - jnp.max(scores, axis=0, keepdims=True))
     shares = powers / jnp.sum(powers, axis=0, keepdims=True)
     probs[...] = shares.reshape(bins * rows, columns)
+    copies = [pltpu.make_async_copy(probs, probs_out, done.at[0])]
+    copies[0].start()
     plain_c[...] = context[...].astype(F32)
 
     def turn(row, _):
@@ -49,9 +66,14 @@
         return 0
 
     lax.fori_loop(0, rows, turn, 0, unroll=4)
-    for wide, narrow in ((wide_p, probs_t), (wide_c, context_t)):
+    for wide, narrow, out in (
+        (wide_p, probs_t, probs_t_out),
+        (wide_c, context_t, context_t_out),
+    ):
         narrow[0 : columns * rows, :] = wide[...].astype(BF16)
         narrow[columns * rows :, :] = jnp.zeros((rows, LANES), BF16)
+        copies.append(pltpu.make_async_copy(narrow, out, done.at[len(copies)]))
+        copies[-1].start()
     line = lax.broadcasted_iota(jnp.int32, (TAPS * rows, LANES), 0)
 
     def cell_sum(slot):
@@ -65,7 +87,9 @@
         kept[slot] = cell_sum(slot)
         return 0
 
-    lax.fori_loop(0, half, one_cell, 0, unroll=2)
+    lax.fori_loop(0, half, one_cell, 0, unroll=4)
+    for copy in copies:
+        copy.wait()
 
 
 def act_grad_kernel(first, *refs):
@@ -92,7 +116,7 @@
         out[row] = total.astype(BF16)
 
     starts = first[2]
-    if len(starts) > 4:
+    if len(starts) > 4 or tuple(starts) == tuple(range(len(starts))):
 
         def step(row, _):
             one_row(row, row)
@@ -105,20 +129,20 @@
 
 
 def grid_kernel(
-    band,
+    place,
     own,
     edge,
-    low_halo,
-    high_halo,
-    ten,
+    near_halo,
+    far_halo,
     two,
     ranges,
     weight_t,
     weight,
     inner_grad,
     outer_grad,
-    upstream,
-    grads,
+    upstream_in,
+    keep,
+    send,
     own_reply,
     other_reply,
     cells,
@@ -128,43 +152,70 @@
     slope_rows,
     slope_lanes,
     grid_grad,
+    act_grads,
+    upstream,
+    grads,
+    done,
 ):
     sector, channels, lanes = own.shape
-    hidden, length = inner_grad.shape[1:]
-    bands = band[1]
-    mine = band[0]
+    hidden, length = outer_grad.shape[1:]
+    mine, bands, core = place[0], place[1], place[2]
     wide = sector + 4
+    rows = sector + 2
+    copies = [
+        pltpu.make_async_copy(source, target, done.at[k])
+        for k, (source, target) in enumerate(
+            (
+                (inner_grad, act_grads.at[2:sector]),
+                (outer_grad.at[0:2], act_grads.at[0:2]),
+                (outer_grad.at[2:4], act_grads.at[sector:]),
+                (upstream_in, upstream),
+            )
+        )
+    ]
+    for copy in copies:
+        copy.start()
     cells[2 : 2 + sector, :, :lanes] = own[...]
-    cells[0:2, :, :lanes] = jnp.where(mine == 0, edge[sector - 2 : sector], low_halo[...])
-    cells[2 + sector :, :, :lanes] = jnp.where(mine == bands - 1, edge[0:2], high_halo[...])
     cells[:, :, lanes:] = jnp.zeros((wide, channels, lanes), BF16)
 
     @pl.when(mine == 0)
     def _():
-        cells[0 : sector + 2, :, lanes:] = ten[...]
+        cells[0:2, :, :lanes] = edge[sector - 2 : sector]
+        cells[2 + sector :, :, :lanes] = near_halo[...]
+        cells[0 : sector + 2, :, lanes:] = far_halo[...]
+
+    @pl.when(mine == 1)
+    def _():
+        cells[0:2, :, :lanes] = near_halo[...]
+        cells[2 + sector :, :, :lanes] = far_halo[0:2]
+        cells[0:2, :, lanes:] = two[...]
+
+    @pl.when(mine == bands - 2)
+    def _():
+        cells[0:2, :, :lanes] = far_halo[0:2]
+        cells[2 + sector :, :, :lanes] = near_halo[...]
+        cells[2 + sector :, :, lanes:] = two[...]
 
     @pl.when(mine == bands - 1)
     def _():
-        cells[2:, :, lanes:] = ten[...]
-
-    @pl.when(mine == 1)
-    def _():
-        cells[0:2, :, lanes:] = two[...]
-
-    @pl.when(mine == bands - 2)
-    def _():
-        cells[2 + sector :, :, lanes:] = two[...]
+        cells[0:2, :, :lanes] = near_halo[...]
+        cells[2 + sector :, :, :lanes] = edge[0:2]
+        cells[2:, :, lanes:] = far_halo[...]
 
     spots = lax.broadcasted_iota(jnp.int32, (2 * lanes, length), 1)
     range_hot = (spots == ranges[...]).astype(F32).astype(BF16)
 
     def behind(value):
-        place = lax.broadcasted_iota(jnp.int32, value.shape, 1)
-        return jnp.where(place > 0, pltpu.roll(value, 1, 1), 0.0)
+        turned = pltpu.roll(value, 1, 1)
+        lane = lax.broadcasted_iota(jnp.int32, (value.shape[0], LANES), 1)
+        first = jnp.where(lane > 0, turned[:, :LANES], 0.0)
+        return jnp.concatenate([first, turned[:, LANES:]], axis=1)
 
     def ahead(value):
-        place = lax.broadcasted_iota(jnp.int32, value.shape, 1)
-        return jnp.where(place < length - 1, pltpu.roll(value, length - 1, 1), 0.0)
+        turned = pltpu.roll(value, length - 1, 1)
+        lane = lax.broadcasted_iota(jnp.int32, (value.shape[0], LANES), 1)
+        last = jnp.where(lane < LANES - 1, turned[:, length - LANES :], 0.0)
+        return jnp.concatenate([turned[:, : length - LANES], last], axis=1)
 
     for chunk in range(0, wide, 4):
         block = cells[chunk : chunk + 4].reshape(4 * channels, 2 * lanes)
@@ -177,30 +228,27 @@
                 grid_taps[0:channels, spread] = behind(value).astype(BF16)
                 grid_taps[channels : 2 * channels, spread] = value.astype(BF16)
                 grid_taps[2 * channels :, spread] = ahead(value).astype(BF16)
-
-    def one_row(row, act_grad):
+    for copy in copies[:3]:
+        copy.wait()
+
+    def one_row(row, _):
         source = pl.ds(pl.multiple_of(row * channels, channels), TAPS * channels)
         sums = product(weight_t[...], grid_low[source, :], 1, 0)
         value = behind(sums[:hidden]) + sums[hidden : 2 * hidden] + ahead(sums[2 * hidden :])
-        logistic = 1.0 / (1.0 + jnp.exp(-value))
+        logistic = 0.5 + 0.5 * jnp.tanh(0.5 * value)
         active = value * logistic
         spread = pl.ds(pl.multiple_of(row * length, length), length)
         act_taps[0:hidden, spread] = behind(active).astype(BF16)
         act_taps[hidden : 2 * hidden, spread] = active.astype(BF16)
         act_taps[2 * hidden :, spread] = ahead(active).astype(BF16)
         slope = logistic * (1.0 + value * (1.0 - logistic))
-        result = (act_grad.astype(F32) * slope).astype(BF16)
+        result = (act_grads[row].astype(F32) * slope).astype(BF16)
         slope_rows[pl.ds(pl.multiple_of(row * hidden, hidden), hidden), :] = result
         slope_lanes[:, spread] = result
-
-    for row, index in ((0, 0), (1, 1), (sector, 2), (sector + 1, 3)):
-        one_row(row, outer_grad[index])
-
-    def inner(index, _):
-        one_row(index + 2, inner_grad[index])
-        return 0
-
-    lax.fori_loop(0, sector - 2, inner, 0)
+        return 0
+
+    lax.fori_loop(0, rows, one_row, 0, unroll=2)
+    copies[3].wait()
     count = sector * length
     tall = TAPS * hidden
     short = TAPS * channels
@@ -223,6 +271,9 @@
         grads[base : base + short, :] = result.astype(BF16)
     base = TAPS * (tall + short)
     grads[base:, :] = jnp.zeros((grads.shape[0] - base, hidden), BF16)
+    half = keep.shape[0]
+    keep[...] = grads[pl.ds(pl.multiple_of(core * half, half), half), :]
+    send[...] = grads[pl.ds(pl.multiple_of((1 - core) * half, half), half), :]
     flipped = jnp.concatenate([weight[TAPS - 1 - i] for i in range(TAPS)], axis=1)
 
     def back(row, _):
@@ -233,58 +284,55 @@
         grid_grad[pl.ds(pl.multiple_of(row * channels, channels), channels), :] = value.astype(BF16)
         return 0
 
-    lax.fori_loop(0, sector, back, 0)
+    lax.fori_loop(0, sector, back, 0, unroll=2)
     picked = product(grid_grad[...], range_hot, 1, 1).astype(BF16)
     own_reply[...] = picked[:, :lanes].reshape(sector, channels, lanes)
     other_reply[...] = picked[:, lanes:].reshape(sector, channels, lanes)
 
 
-def pixel_kernel(
-    rows,
-    table,
-    own,
-    partner,
-    edge,
-    theirs,
-    probs,
-    probs_t,
-    context_t,
-    lidar,
-    logit_grad,
-    context_grad,
-    wedges,
-    wide_p,
-    wide_c,
-    plain_c,
+def finish_kernel(place, value, other, second, first):
+    half = value.shape[0]
+    cut = second.shape[0] - half
+
+    def write(low, high):
+        second[0:half, :] = low[...].astype(F32)
+        second[half:, :] = high[0:cut, :].astype(F32)
+        first[...] = high[cut : cut + first.shape[0], :].astype(F32)
+
+    @pl.when(place[2] == 0)
+    def _():
+        write(value, other)
+
+    @pl.when(place[2] == 1)
+    def _():
+        write(other, value)
+
+
+def logit_kernel(
+    rows, table, own, partner, edge, theirs, probs, context_t, lidar, logit_grad, wedges, wide
 ):
     columns = probs.shape[1]
     bins = probs.shape[0] // rows
-    channels = context_grad.shape[0] // rows
-    sector = own.shape[0]
+    sector, channels, _ = own.shape
     wedges[0:sector] = own[...]
     wedges[sector : 2 * sector] = partner[...]
     wedges[2 * sector : 3 * sector] = edge[...]
     wedges[3 * sector :] = theirs[...]
-    wide_c[...] = jnp.zeros_like(wide_c)
 
     def one_cell(cell, _):
         span = pl.ds(pl.multiple_of(table[0, cell] * rows, rows), TAPS * rows)
         slope = wedges[table[1, cell]]
-        wide_p[span, :] = product(context_t[span, :][:, :channels], slope, 1, 0)
-        wide_c[span, 0:channels] = product(probs_t[span, :], slope, 1, 1)
-        return 0
-
-    lax.fori_loop(0, wedges.shape[0], one_cell, 0, unroll=4)
+        wide[span, :] = product(context_t[span, :][:, :channels], slope, 1, 0)
+        return 0
+
+    lax.fori_loop(0, wedges.shape[0], one_cell, 0, unroll=8)
 
     def turn(row, _):
-        block = jnp.transpose(wide_p[pl.ds(row, columns, stride=rows), :])
+        block = jnp.transpose(wide[pl.ds(row, columns, stride=rows), :])
         logit_grad[pl.ds(row, bins, stride=rows), :] = block[:bins]
-        block = jnp.transpose(wide_c[pl.ds(row, columns, stride=rows), :])
-        plain_c[pl.ds(row, channels, stride=rows), :] = block[:channels]
         return 0
 
     lax.fori_loop(0, rows, turn, 0, unroll=4)
-    context_grad[...] = plain_c[...].astype(BF16)
     share = probs[...].reshape(bins, rows, columns)
     slope = logit_grad[...].reshape(bins, rows, columns)
     expected = jnp.sum(share * slope, axis=0, keepdims=True)
@@ -296,6 +344,33 @@
     logit_grad[...] = result.reshape(bins * rows, columns)
 
 
+def context_kernel(
+    rows, table, own, partner, edge, theirs, probs_t, context_grad, wedges, wide, plain
+):
+    columns = context_grad.shape[1]
+    sector, channels, _ = own.shape
+    wedges[0:sector] = own[...]
+    wedges[sector : 2 * sector] = partner[...]
+    wedges[2 * sector : 3 * sector] = edge[...]
+    wedges[3 * sector :] = theirs[...]
+    wide[...] = jnp.zeros_like(wide)
+
+    def one_cell(cell, _):
+        span = pl.ds(pl.multiple_of(table[0, cell] * rows, rows), TAPS * rows)
+        wide[span, 0:channels] = product(probs_t[span, :], wedges[table[1, cell]], 1, 1)
+        return 0
+
+    lax.fori_loop(0, wedges.shape[0], one_cell, 0, unroll=8)
+
+    def turn(row, _):
+        block = jnp.transpose(wide[pl.ds(row, columns, stride=rows), :])
+        plain[pl.ds(row, channels, stride=rows), :] = block[:channels]
+        return 0
+
+    lax.fori_loop(0, rows, turn, 0, unroll=4)
+    context_grad[...] = plain[...].astype(BF16)
+
+
 def vmem():
     return pl.BlockSpec(memory_space=pltpu.VMEM)
 
@@ -304,25 +379,21 @@
     return pl.BlockSpec(memory_space=pltpu.SMEM)
 
 
-def call(kernel, out_shape, scratch, spaces, flops, moved, name):
+def anywhere():
+    return pl.BlockSpec(memory_space=pl.ANY)
+
+
+def call(kernel, out_shape, scratch, spaces, flops, moved, outs=None):
     many = isinstance(out_shape, (list, tuple))
     return pl.pallas_call(
         kernel,
         out_shape=out_shape,
         in_specs=spaces,
-        out_specs=[vmem() for _ in out_shape] if many else vmem(),
+        out_specs=outs or ([vmem() for _ in out_shape] if many else vmem()),
         scratch_shapes=scratch,
         compiler_params=pltpu.CompilerParams(vmem_limit_bytes=LIMIT),
         cost_estimate=pl.CostEstimate(flops=flops, bytes_accessed=moved, transcendentals=0),
-        name=name,
-    )
-
-
-def halves(part, upper):
-    size = part.shape[0] // 2
-    keep = lax.dynamic_slice_in_dim(part, upper * size, size, 0)
-    send = lax.dynamic_slice_in_dim(part, (1 - upper) * size, size, 0)
-    return keep, send
+    )
 
 
 def rounded_sum(left, right):
@@ -333,33 +404,42 @@
     return lax.ppermute(value, "blk", [(i, i ^ mask) for i in range(blocks)])
 
 
-def joined(value, other, upper):
-    return jnp.where(
-        upper == 1,
-        jnp.concatenate([other, value], axis=0),
-        jnp.concatenate([value, other], axis=0),
-    )
-
-
-def total_over_blocks(value, position, blocks):
+def piece(value, index, count):
+    size = value.shape[0] // count
+    return lax.dynamic_slice_in_dim(value, index * size, size, 0)
+
+
+def total_over_blocks(keep, send, position, blocks):
     count = blocks.bit_length() - 1
-    bit = [(position >> k) & 1 for k in range(count)]
-    keep, send = halves(value, bit[0])
+    pairs = list(range(1, count, 2))
+    orders = (pairs, pairs[1:] + pairs[:1])
+    core = position & 1
+    digits = [
+        jnp.where(core == 0, position >> one, position >> two) & 3 for one, two in zip(*orders)
+    ]
+
+    def sent(part, step, mask):
+        to = [(i, i ^ (mask << orders[i & 1][step])) for i in range(blocks)]
+        return lax.ppermute(part, "blk", to)
+
     value = rounded_sum(keep, swapped(send, blocks, 1))
-    later = list(range(1, count))
-    parts = jnp.split(value, TAPS, axis=0)
-    orders = [later[k % len(later) :] + later[: k % len(later)] for k in range(TAPS)]
-    for step in range(len(later)):
-        for k in range(TAPS):
-            axis = orders[k][step]
-            keep, send = halves(parts[k], bit[axis])
-            parts[k] = rounded_sum(keep, swapped(send, blocks, 1 << axis))
-    for step in reversed(range(len(later))):
-        for k in range(TAPS):
-            axis = orders[k][step]
-            parts[k] = joined(parts[k], swapped(parts[k], blocks, 1 << axis), bit[axis])
-    value = jnp.concatenate(parts, axis=0)
-    return joined(value, swapped(value, blocks, 1), bit[0])
+    for step, digit in enumerate(digits):
+        arrived = [sent(piece(value, digit ^ mask, 4), step, mask) for mask in (3, 1, 2)]
+        total = piece(value, digit, 4).astype(F32)
+        for part in arrived:
+            total = total + part.astype(F32)
+        value = total.astype(BF16)
+    for step, digit in reversed(list(enumerate(digits))):
+        held = [value] + [sent(value, step, mask) for mask in (1, 2, 3)]
+        high, low = digit >> 1 == 1, digit & 1 == 1
+
+        def at(k):
+            one = jnp.where(low, held[k ^ 1], held[k])
+            two = jnp.where(low, held[k ^ 3], held[k ^ 2])
+            return jnp.where(high, two, one)
+
+        value = jnp.concatenate([at(k) for k in range(4)], axis=0)
+    return value, swapped(value, blocks, 1)
 
 
 def shards(
@@ -372,17 +452,27 @@
     sector, length, hidden = out_grad.shape
     bins, rows = depth_logits.shape[1:3]
     channels = context.shape[1]
-    if bands != 4 or blocks & (blocks - 1) or bins > LANES or channels > LANES or sector < 6:
+    if bands != 4 or blocks != 1 << (blocks.bit_length() - 1) or blocks.bit_length() % 2 or bins > LANES or channels > LANES or sector < 6:
         raise ValueError("unsupported sizes")
     camera = position // bands
     band = position % bands
     sight = bands * sector
     seen = sight + sight // 2
 
-    forward = [(i, (i + 1) % blocks) for i in range(blocks)]
-    backward = [((i + 1) % blocks, i) for i in range(blocks)]
-    low_grad = lax.ppermute(out_grad[sector - 2 :], "blk", forward)
-    high_grad = lax.ppermute(out_grad[:2], "blk", backward)
+    core = position & 1
+    place = jnp.stack([band, jnp.full_like(band, bands), core])
+    on_chip = [(i, i ^ 1) for i in range(blocks)]
+    off_chip = [(i, (i + 1 if i & 1 else i - 1) % blocks) for i in range(blocks)]
+
+    def ends(value, near):
+        count = value.shape[0]
+        start = jnp.where((core == 0) == near, count - 2, 0)
+        return lax.dynamic_slice_in_dim(value, start, 2, 0)
+
+    near_grad = lax.ppermute(ends(out_grad, True), "blk", on_chip)
+    far_grad = lax.ppermute(ends(out_grad, False), "blk", off_chip)
+    low_grad = jnp.where(core == 0, far_grad, near_grad)
+    high_grad = jnp.where(core == 0, near_grad, far_grad)
 
     az_row = lax.dynamic_slice_in_dim(az_map, camera, 1, 0)[0]
     local = (az_row - (camera * sight - sight // 4)) % (blocks * sector)
@@ -416,14 +506,18 @@
             jax.ShapeDtypeStruct((half, channels, LANES), BF16),
         ],
         [
+            pltpu.VMEM((bins * rows, columns), F32),
+            pltpu.VMEM((turned, LANES), BF16),
+            pltpu.VMEM((turned, LANES), BF16),
             pltpu.VMEM((columns * rows, LANES), F32),
             pltpu.VMEM((columns * rows, LANES), F32),
             pltpu.VMEM((channels * rows, columns), F32),
+            pltpu.SemaphoreType.DMA((3,)),
         ],
         [smem(), vmem(), vmem()],
         2 * seen * 3 * rows * LANES * LANES,
         20 * bins * rows * columns,
-        "pool",
+        [anywhere()] * 3 + [vmem()] * 2,
     )(
         pool_table,
         depth_logits[0].reshape(bins * rows, columns),
@@ -441,7 +535,6 @@
             [vmem() for _ in sources] + [vmem()],
             row_flops * len(starts),
             2 * (total + len(starts)) * length * hidden,
-            "act_grad",
         )(*sources, conv2_weight)
 
     inner_grad = act_grad([out_grad], (0,), (sector,), tuple(range(sector - 2)))
@@ -462,10 +555,17 @@
     first = band == 0
     firsts = [i for i in range(blocks) if i % bands == 0]
     lasts = [i for i in range(blocks) if i % bands == bands - 1]
-    ten = jnp.where(
+    last = band == bands - 1
+    outer = jnp.logical_or(first, last)
+    more = ((0, sector), (0, 0), (0, 0))
+    far = jnp.where(
         first,
         jnp.concatenate([edge, own[:2]], axis=0),
-        jnp.concatenate([own[sector - 2 :], edge], axis=0),
+        jnp.where(
+            last,
+            jnp.concatenate([own[sector - 2 :], edge], axis=0),
+            jnp.pad(ends(own, False), more),
+        ),
     )
     two = jnp.where(first, edge[:2], edge[sector - 2 :])
 
@@ -474,14 +574,9 @@
         pairs = pairs + [(i, (i + 1 + more) % blocks) for i in lasts]
         return lax.ppermute(value, "blk", pairs)
 
-    ten = to_next(ten, 0)
+    far_halo = lax.ppermute(far, "blk", off_chip)
     two = to_next(two, 1)
-    low_halo = lax.ppermute(
-        own[sector - 2 :], "blk", [(i, i + 1) for i in range(blocks) if i not in lasts]
-    )
-    high_halo = lax.ppermute(
-        own[:2], "blk", [(i, i - 1) for i in range(blocks) if i not in firsts]
-    )
+    near_halo = lax.ppermute(ends(own, True), "blk", on_chip)
     other = jnp.where(band < bands // 2, camera - 1, camera + 1) % cameras
     ranges = jnp.concatenate(
         [lax.dynamic_slice_in_dim(rng_map, k, 1, 0) for k in (camera, other)], axis=0
@@ -490,13 +585,14 @@
     weight_t = conv1_weight.transpose(1, 3, 0, 2).reshape(TAPS * hidden, TAPS * channels)
     weight = conv1_weight.reshape(TAPS, TAPS * channels, hidden)
     grad_rows = TAPS * TAPS * (hidden + channels)
-    unit = TAPS * blocks * 16
+    unit = blocks * 16
     grad_rows = -(-grad_rows // unit) * unit
     wide = sector + 2
-    grads, own_reply, other_reply = call(
+    keep, send, own_reply, other_reply = call(
         grid_kernel,
         [
-            jax.ShapeDtypeStruct((grad_rows, hidden), BF16),
+            jax.ShapeDtypeStruct((grad_rows // 2, hidden), BF16),
+            jax.ShapeDtypeStruct((grad_rows // 2, hidden), BF16),
             jax.ShapeDtypeStruct((sector, channels, LANES), BF16),
             jax.ShapeDtypeStruct((sector, channels, LANES), BF16),
         ],
@@ -508,18 +604,20 @@
             pltpu.VMEM((wide * hidden, length), BF16),
             pltpu.VMEM((hidden, wide * length), BF16),
             pltpu.VMEM((sector * channels, length), BF16),
+            pltpu.VMEM((wide, hidden, length), BF16),
+            pltpu.VMEM((sector * length, hidden), BF16),
+            pltpu.VMEM((grad_rows, hidden), BF16),
+            pltpu.SemaphoreType.DMA((4,)),
         ],
-        [smem()] + [vmem()] * 12,
+        [smem()] + [vmem()] * 8 + [anywhere()] * 3,
         row_flops * (sector + 3 * sector // 2),
         20 * sector * length * hidden,
-        "grid",
     )(
-        jnp.stack([band, jnp.full_like(band, bands)]),
+        place,
         own,
         edge,
-        low_halo,
-        high_halo,
-        ten,
+        near_halo,
+        far_halo,
         two,
         ranges,
         weight_t,
@@ -532,38 +630,50 @@
     partner = swapped(own_reply, blocks, 2)
     edge_reply = to_next(other_reply, 0)
     passed = lax.ppermute(edge_reply, "blk", outward)
-    outer = jnp.logical_or(first, band == bands - 1)
     edge_reply = jnp.where(outer, edge_reply, passed)
     theirs = swapped(
         jnp.concatenate([own_reply, partner, edge_reply], axis=0), blocks, 1
     )
-    total = total_over_blocks(grads, position, blocks)
-
-    logit_grad, context_grad = call(
-        functools.partial(pixel_kernel, rows),
+    value, other_value = total_over_blocks(keep, send, position, blocks)
+
+    replies = (own_reply, partner, edge_reply, theirs)
+    scratch = [pltpu.VMEM((seen, channels, LANES), BF16), pltpu.VMEM((turned, LANES), F32)]
+    cell_flops = 2 * seen * 3 * rows * LANES * LANES
+    context_grad = call(
+        functools.partial(context_kernel, rows),
+        jax.ShapeDtypeStruct((channels * rows, columns), BF16),
+        scratch + [pltpu.VMEM((channels * rows, columns), F32)],
+        [smem()] + [vmem()] * 5,
+        cell_flops,
+        10 * bins * rows * columns,
+    )(pixel_table, *replies, probs_t)
+    logit_grad = call(
+        functools.partial(logit_kernel, rows),
+        jax.ShapeDtypeStruct((bins * rows, columns), F32),
+        scratch,
+        [smem()] + [vmem()] * 7,
+        cell_flops,
+        20 * bins * rows * columns,
+    )(pixel_table, *replies, probs, context_t, lidar_bins[0])
+
+    second = TAPS * TAPS * hidden
+    first_rows = TAPS * TAPS * channels
+    second_grad, first_grad = call(
+        finish_kernel,
         [
-            jax.ShapeDtypeStruct((bins * rows, columns), F32),
-            jax.ShapeDtypeStruct((channels * rows, columns), BF16),
+            jax.ShapeDtypeStruct((second, hidden), F32),
+            jax.ShapeDtypeStruct((first_rows, hidden), F32),
         ],
-        [
-            pltpu.VMEM((seen, channels, LANES), BF16),
-            pltpu.VMEM((turned, LANES), F32),
-            pltpu.VMEM((turned, LANES), F32),
-            pltpu.VMEM((channels * rows, columns), F32),
-        ],
-        [smem()] + [vmem()] * 8,
-        4 * seen * 3 * rows * LANES * LANES,
-        20 * bins * rows * columns,
-        "pixel",
-    )(pixel_table, own_reply, partner, edge_reply, theirs, probs, probs_t, context_t, lidar_bins[0])
-
-    second = TAPS * TAPS * hidden
-    both = second + TAPS * TAPS * channels
+        [],
+        [smem(), vmem(), vmem()],
+        1,
+        6 * grad_rows * hidden,
+    )(place, value, other_value)
     return (
         logit_grad.reshape(1, bins, rows, columns),
         context_grad.reshape(1, channels, rows, columns),
-        total[second:both].astype(F32).reshape(TAPS, TAPS, channels, hidden),
-        total[:second].astype(F32).reshape(TAPS, TAPS, hidden, hidden),
+        first_grad.reshape(TAPS, TAPS, channels, hidden),
+        second_grad.reshape(TAPS, TAPS, hidden, hidden),
     )
 
 

time: 161 us -> 151 us (0.938)
  starting transfers between devices: 43.5 us -> 38.7 us
  waiting for transfers between devices: 34.4 us -> 31.4 us
  local copies, waits for them, and re-layouts: 7.75 us -> 6.12 us
    ppermute x30 -> x6, waiting for transfers between devices: 26.8 us -> 4.97 us  [swapped(): return lax.ppermute(value, 'blk', [(i, i ^ mask) for i in range(blocks)])]
    ppermute x4 -> x16, starting transfers between devices: 9.17 us -> 25.4 us  [the longest x12 17.2 us: sent(): return lax.ppermute(part, 'blk', to)]
    ppermute x30 -> x6, starting transfers between devices: 20.3 us -> 5.1 us  [swapped(): return lax.ppermute(value, 'blk', [(i, i ^ mask) for i in range(blocks)])]
    ppermute x4 -> x16, waiting for transfers between devices: 0.01 us -> 14 us  [the longest x12 14 us: sent(): return lax.ppermute(part, 'blk', to)]
    ppermute x3 -> x2, starting transfers between devices: 11.1 us -> 5.64 us  [to_next(): return lax.ppermute(value, 'blk', pairs)]
    pallas_call x2 -> x4, Pallas kernels: 35.9 us -> 38.9 us  [the longest x1 21.3 us: shards(): call(grid_kernel, [jax.ShapeDtypeStruct((grad_rows // 2, hidden), BF16),...]
    reshape x2 -> x0, other arithmetic: 2.55 us -> none  [the longest x1 1.62 us: shards(): total[:second].astype(F32).reshape(TAPS, TAPS, hidden, hidden)]
    ppermute x1, waiting for transfers between devices: 0.01 us -> 2.34 us  [shards(): passed = lax.ppermute(edge_reply, 'blk', outward)]
  transfers between devices with their start and end apart: 39 -> 26, of which waited for: 18 -> 13; matrix products, arithmetic and copies ran while one was open for 5% -> 5% of each run, Pallas kernels for 18% -> 20%
where the time goes in v1:
time: 151 us
  Pallas kernels  65.6 us (43%)
  starting transfers between devices  38.7 us (26%)
  waiting for transfers between devices  31.4 us (21%)
  other arithmetic  7.63 us (5%)
  local copies, waits for them, and re-layouts  6.12 us (4%)
    pallas_call x1, Pallas kernels, shards(): call(grid_kernel, [jax.ShapeDtypeStruct((grad_rows // 2, hidden), BF16),...  21.3 us
    ppermute x12, starting transfers between devices, sent(): return lax.ppermute(part, 'blk', to)  17.2 us
    pallas_call x2, Pallas kernels, act_grad(): call(functools.partial(act_grad_kernel, (lows, highs, starts)), jax.Shape...  15.6 us
    ppermute x12, waiting for transfers between devices, sent(): return lax.ppermute(part, 'blk', to)  14 us
    pallas_call x1, Pallas kernels, shards(): call(functools.partial(pool_kernel, rows), [jax.ShapeDtypeStruct((bins *...  11.1 us
    pallas_call x1, Pallas kernels, shards(): call(functools.partial(logit_kernel, rows), jax.ShapeDtypeStruct((bins *...  7.97 us
    ppermute x2, waiting for transfers between devices, to_next(): return lax.ppermute(value, 'blk', pairs)  7.92 us
    ppermute x1, starting transfers between devices, shards(): far_grad = lax.ppermute(ends(out_grad, False), 'blk', off_chip)  6.62 us
  transfers between devices with their start and end apart: 26, of which 13 were waited for; matrix products, arithmetic and copies ran while one was open for 5% of the time, Pallas kernels for 20%

profile of v1, /device:TPU:0, one launch (start us, length us, event | category | flops | bytes accessed | tf_op | source)
XLA Modules:
  0.0 150.6 jit_solution(589239392381324845)
XLA Ops:
  0.7 0.8 fusion.2
  2.2 0.6 pad_add_fusion.1.table
  2.8 11.1 %shard_map.111 = (f32[3584,128]{1,0:T(8,128)}, bf16[4128,128]{1,0:T(8,128)(2,1)}, bf16[4128,128]{1,0:T(8,128)(2,1)}, bf16[24,80,128]{2,1,0:T(8,128)(2,1)}, bf16[24,80,128]{2,1,0:T(8,128)(2,1)}) custom-call(s32[2,48]{1,0:T(2,128)} %pad_add_fusion.1.table, f32[3584,128]{1,0:T(8,128)} %bitcast.26, bf16[2560,128]{1,0:T(8,128)(2,1)} %bitcast.28), custom_call_target="tpu_custom_call" | custom-call | flops 150994944 | bytes 9175040 | tf_op jit(solution)/shard_map/pallas_call | solution.py:499
  14.6 6.6 %collective-permute-start.6 = (bf16[2,512,256]{2,1,0:T(8,128)(2,1)S(1)}, bf16[2,512,256]{2,1,0:T(8,128)(2,1)S(1)}, u32[]{:S(2)}, u32[]{:S(2)}) collective-permute-start(bf16[2,512,256]{2,1,0:T(8,128)(2,1)S(1)} %get-tuple-element.29), channel_id=1, source_target_pairs={{0,31},{1,2},{2,1},{3,4},{4,3},{5,6},{6,5},{7,8},{8,7},{9,10},{10,... | collective-permute-start | bytes 1572872 | tf_op jit(solution)/shard_map/ppermute | solution.py:473
  21.2 0.8 constant_dynamic-slice_fusion.9
  22.0 9.0 %shard_map.112.inner_grad = bf16[6,256,512]{2,1,0:T(8,128)(2,1)} custom-call(bf16[8,512,256]{2,1,0:T(8,128)(2,1)} %refs_2_.1, bf16[3,3,256,256]{3,2,1,0:T(8,128)(2,1)} %refs_4_.1), custom_call_target="tpu_custom_call" | custom-call | flops 3623878656 | bytes 3670016 | tf_op jit(solution)/shard_map/pallas_call | solution.py:531
  31.0 0.6 pad_add_fusion.3.place
  31.6 0.8 copy.17.ranges
  32.4 0.6 copy.19
  33.0 1.1 reshape.134.weight_t
  34.1 1.3 add_convert_fusion.1
  35.5 1.3 collective-permute-start.2
  36.8 2.7 %collective-permute-start.1 = (bf16[8,80,128]{2,1,0:T(8,128)(2,1)S(1)}, bf16[8,80,128]{2,1,0:T(8,128)(2,1)S(1)}, u32[]{:S(2)}, u32[]{:S(2)}) collective-permute-start(bf16[8,80,128]{2,1,0:T(8,128)(2,1)S(1)} %get-tuple-element.41), channel_id=1, source_target_pairs={{0,2},{1,3},{2,0},{3,1},{4,6},{5,7},{6,4},{7,5},{8,10},{9,11},{10,... | collective-permute-start | bytes 491528 | tf_op jit(solution)/shard_map/ppermute | solution.py:404
  39.5 1.0 broadcast_select_fusion
  40.5 2.2 %collective-permute-done.2 = bf16[8,80,128]{2,1,0:T(8,128)(2,1)S(1)} collective-permute-done((bf16[8,80,128]{2,1,0:T(8,128)(2,1)S(1)}, bf16[8,80,128]{2,1,0:T(8,128)(2,1)S(1)}, u32[]{:S(2)}, u32[]{:S(2)}) %collective-permute-start.2) | collective-permute-done | bytes 163872 | tf_op jit(solution)/shard_map/ppermute | solution.py:553
  42.7 1.8 %collective-permute-done.1 = bf16[8,80,128]{2,1,0:T(8,128)(2,1)S(1)} collective-permute-done((bf16[8,80,128]{2,1,0:T(8,128)(2,1)S(1)}, bf16[8,80,128]{2,1,0:T(8,128)(2,1)S(1)}, u32[]{:S(2)}, u32[]{:S(2)}) %collective-permute-start.1) | collective-permute-done | bytes 163872 | tf_op jit(solution)/shard_map/ppermute | solution.py:404
  44.7 1.4 collective-permute-start.4
  46.1 3.7 %collective-permute-start.5 = (bf16[2,80,128]{2,1,0:T(8,128)(2,1)S(1)}, bf16[2,80,128]{2,1,0:T(8,128)(2,1)S(1)}, u32[]{:S(2)}, u32[]{:S(2)}) collective-permute-start(bf16[2,80,128]{2,1,0:T(8,128)(2,1)S(1)} %slice_select_fusion), channel_id=1, source_target_pairs={{0,30},{4,2},{8,6},{12,10},{16,14},{20,18},{24,22},{28,26},{3,5},{... | collective-permute-start | bytes 122888 | tf_op jit(solution)/shard_map/ppermute | solution.py:575
  49.8 6.6 %shard_map.113.outer_grad = bf16[4,256,512]{2,1,0:T(8,128)(2,1)} custom-call(bf16[2,512,256]{2,1,0:T(8,128)(2,1)} %get-tuple-element.31.refs_0_, bf16[8,512,256]{2,1,0:T(8,128)(2,1)} %refs_2_.1, bf16[8,512,256]{2,1,0:T(8,128)(2,1)} %refs_2_.1, bf16[2,512,256]{2,1,0:T(8,128)(2,1)} %get-tuple-element.30.refs_3_, bf16[3,3,256,256]{3,2,1,0:T(8,128)(2,1)} %refs_4_.1), custom_call_target="tpu_custom_call" | custom-call | flops 2415919104 | bytes 3145728 | tf_op jit(solution)/shard_map/pallas_call | solution.py:531
  56.5 0.6 copy-done.12
  57.2 21.3 %shard_map.114 = (bf16[1536,256]{1,0:T(8,128)(2,1)}, bf16[1536,256]{1,0:T(8,128)(2,1)}, bf16[8,80,128]{2,1,0:T(8,128)(2,1)}, bf16[8,80,128]{2,1,0:T(8,128)(2,1)}) custom-call(s32[3]{0:T(128)} %pad_add_fusion.3.place, bf16[8,80,128]{2,1,0:T(8,128)(2,1)} %copy-done.7, bf16[8,80,128]{2,1,0:T(8,128)(2,1)} %copy-done.5, bf16[2,80,128]{2,1,0:T(8,128)(2,1)} %copy-done.12, ...), custom_call_target="tpu_custom_call" | custom-call | flops 12079595520 | bytes 20971520 | tf_op jit(solution)/shard_map/pallas_call | solution.py:591
  78.6 2.5 %collective-permute-done.12 = bf16[1536,256]{1,0:T(8,128)(2,1)S(1)} collective-permute-done((bf16[1536,256]{1,0:T(8,128)(2,1)}, bf16[1536,256]{1,0:T(8,128)(2,1)S(1)}, u32[]{:S(2)}, u32[]{:S(2)}) %collective-permute-start.12) | collective-permute-done | bytes 786464 | tf_op jit(solution)/shard_map/ppermute | solution.py:404
  81.0 1.3 add_convert_fusion
  82.9 3.1 %collective-permute-start.13 = (bf16[384,256]{1,0:T(8,128)(2,1)S(1)}, bf16[384,256]{1,0:T(8,128)(2,1)S(1)}, u32[]{:S(2)}, u32[]{:S(2)}) collective-permute-start(bf16[384,256]{1,0:T(8,128)(2,1)S(1)} %get-tuple-element.35), channel_id=1, source_target_pairs={{0,6},{1,25},{2,4},{3,27},{4,2},{5,29},{6,0},{7,31},{8,14},{9,17},... | collective-permute-start | bytes 589832 | tf_op jit(solution)/shard_map/ppermute | solution.py:423
  86.0 2.2 %collective-permute-done.15 = bf16[384,256]{1,0:T(8,128)(2,1)S(1)} collective-permute-done((bf16[384,256]{1,0:T(8,128)(2,1)S(1)}, bf16[384,256]{1,0:T(8,128)(2,1)S(1)}, u32[]{:S(2)}, u32[]{:S(2)}) %collective-permute-start.15) | collective-permute-done | bytes 196640 | tf_op jit(solution)/shard_map/ppermute | solution.py:423
  88.6 3.1 %collective-permute-done.13 = bf16[384,256]{1,0:T(8,128)(2,1)S(1)} collective-permute-done((bf16[384,256]{1,0:T(8,128)(2,1)S(1)}, bf16[384,256]{1,0:T(8,128)(2,1)S(1)}, u32[]{:S(2)}, u32[]{:S(2)}) %collective-permute-start.13) | collective-permute-done | bytes 196640 | tf_op jit(solution)/shard_map/ppermute | solution.py:423
  92.1 1.6 %collective-permute-start.17 = (bf16[96,256]{1,0:T(8,128)(2,1)S(1)}, bf16[96,256]{1,0:T(8,128)(2,1)S(1)}, u32[]{:S(2)}, u32[]{:S(2)}) collective-permute-start(bf16[96,256]{1,0:T(8,128)(2,1)S(1)} %get-tuple-element.48), channel_id=1, source_target_pairs={{0,8},{1,3},{2,10},{3,1},{4,12},{5,7},{6,14},{7,5},{8,0},{9,11},{1... | collective-permute-start | bytes 147464 | tf_op jit(solution)/shard_map/ppermute | solution.py:423
  93.6 2.7 %collective-permute-start.16 = (bf16[96,256]{1,0:T(8,128)(2,1)S(1)}, bf16[96,256]{1,0:T(8,128)(2,1)S(1)}, u32[]{:S(2)}, u32[]{:S(2)}) collective-permute-start(bf16[96,256]{1,0:T(8,128)(2,1)S(1)} %get-tuple-element.46), channel_id=1, source_target_pairs={{0,24},{1,7},{2,26},{3,5},{4,28},{5,3},{6,30},{7,1},{8,16},{9,15},... | collective-permute-start | bytes 147464 | tf_op jit(solution)/shard_map/ppermute | solution.py:423
  96.3 0.6 collective-permute-done.18
  97.0 2.6 %collective-permute-done.16 = bf16[96,256]{1,0:T(8,128)(2,1)S(1)} collective-permute-done((bf16[96,256]{1,0:T(8,128)(2,1)S(1)}, bf16[96,256]{1,0:T(8,128)(2,1)S(1)}, u32[]{:S(2)}, u32[]{:S(2)}) %collective-permute-start.16) | collective-permute-done | bytes 49184 | tf_op jit(solution)/shard_map/ppermute | solution.py:423
  99.6 2.8 %collective-permute-start.19 = (bf16[96,256]{1,0:T(8,128)(2,1)S(1)}, bf16[96,256]{1,0:T(8,128)(2,1)S(1)}, u32[]{:S(2)}, u32[]{:S(2)}) collective-permute-start(bf16[96,256]{1,0:T(8,128)(2,1)S(1)} %add_convert_fusion.5), channel_id=1, source_target_pairs={{0,24},{1,7},{2,26},{3,5},{4,28},{5,3},{6,30},{7,1},{8,16},{9,15},... | collective-permute-start | bytes 147464 | tf_op jit(solution)/shard_map/ppermute | solution.py:423
  102.3 1.7 %collective-permute-start.21 = (bf16[96,256]{1,0:T(8,128)(2,1)S(1)}, bf16[96,256]{1,0:T(8,128)(2,1)S(1)}, u32[]{:S(2)}, u32[]{:S(2)}) collective-permute-start(bf16[96,256]{1,0:T(8,128)(2,1)S(1)} %add_convert_fusion.5), channel_id=1, source_target_pairs={{0,8},{1,3},{2,10},{3,1},{4,12},{5,7},{6,14},{7,5},{8,0},{9,11},{1... | collective-permute-start | bytes 147464 | tf_op jit(solution)/shard_map/ppermute | solution.py:423
  104.0 1.5 collective-permute-done.19
  105.5 3.6 %collective-permute-done.20 = bf16[96,256]{1,0:T(8,128)(2,1)S(1)} collective-permute-done((bf16[96,256]{1,0:T(8,128)(2,1)S(1)}, bf16[96,256]{1,0:T(8,128)(2,1)S(1)}, u32[]{:S(2)}, u32[]{:S(2)}) %collective-permute-start.20) | collective-permute-done | bytes 49184 | tf_op jit(solution)/shard_map/ppermute | solution.py:423
  109.2 0.6 collective-permute-start.23
  109.8 3.6 %collective-permute-start.22 = (bf16[384,256]{1,0:T(8,128)(2,1)S(1)}, bf16[384,256]{1,0:T(8,128)(2,1)S(1)}, u32[]{:S(2)}, u32[]{:S(2)}) collective-permute-start(bf16[384,256]{1,0:T(8,128)(2,1)S(1)} %pad_maximum_fusion.2), channel_id=1, source_target_pairs={{0,6},{1,25},{2,4},{3,27},{4,2},{5,29},{6,0},{7,31},{8,14},{9,17},... | collective-permute-start | bytes 589832 | tf_op jit(solution)/shard_map/ppermute | solution.py:423
  113.9 1.9 %collective-permute-start.9 = (bf16[8,80,128]{2,1,0:T(8,128)(2,1)S(1)}, bf16[8,80,128]{2,1,0:T(8,128)(2,1)S(1)}, u32[]{:S(2)}, u32[]{:S(2)}) collective-permute-start(bf16[8,80,128]{2,1,0:T(8,128)(2,1)S(1)} %copy-done.11), channel_id=1, source_target_pairs={{0,31},{4,3},{8,7},{12,11},{16,15},{20,19},{24,23},{28,27},{3,4},{... | collective-permute-start | bytes 491528 | tf_op jit(solution)/shard_map/ppermute | solution.py:575
  116.3 7.9 %collective-permute-done.9 = bf16[8,80,128]{2,1,0:T(8,128)(2,1)S(1)} collective-permute-done((bf16[8,80,128]{2,1,0:T(8,128)(2,1)S(1)}, bf16[8,80,128]{2,1,0:T(8,128)(2,1)S(1)}, u32[]{:S(2)}, u32[]{:S(2)}) %collective-permute-start.9) | collective-permute-done | bytes 163872 | tf_op jit(solution)/shard_map/ppermute | solution.py:575
  124.2 1.3 collective-permute-start.10
  126.0 2.3 %collective-permute-done.10 = bf16[8,80,128]{2,1,0:T(8,128)(2,1)S(1)} collective-permute-done((bf16[8,80,128]{2,1,0:T(8,128)(2,1)S(1)}, bf16[8,80,128]{2,1,0:T(8,128)(2,1)S(1)}, u32[]{:S(2)}, u32[]{:S(2)}) %collective-permute-start.10) | collective-permute-done | bytes 163872 | tf_op jit(solution)/shard_map/ppermute | solution.py:632
  128.5 1.3 collective-permute-start.11
  129.9 0.6 pad_add_fusion.table
  130.5 0.8 collective-permute-done.11.theirs
  131.3 0.8 copy-done.2
  132.1 6.4 %shard_map.116 = bf16[2560,128]{1,0:T(8,128)(2,1)} custom-call(s32[2,48]{1,0:T(2,128)} %pad_add_fusion.table, bf16[8,80,128]{2,1,0:T(8,128)(2,1)} %get-tuple-element.17.own, bf16[8,80,128]{2,1,0:T(8,128)(2,1)} %copy-done.4, bf16[8,80,128]{2,1,0:T(8,128)(2,1)} %copy-done.1, bf16[24,80,128]{2,1,0:T(8,128)(2,1)} %copy-done.2, ...), custom_call_target="tpu_custom_call" | custom-call | flops 150994944 | bytes 4587520 | tf_op jit(solution)/shard_map/pallas_call | solution.py:642
  138.5 8.0 %shard_map.115 = f32[3584,128]{1,0:T(8,128)} custom-call(s32[2,48]{1,0:T(2,128)} %pad_add_fusion.table, bf16[8,80,128]{2,1,0:T(8,128)(2,1)} %get-tuple-element.17.own, bf16[8,80,128]{2,1,0:T(8,128)(2,1)} %copy-done.4, bf16[8,80,128]{2,1,0:T(8,128)(2,1)} %copy-done.1, bf16[24,80,128]{2,1,0:T(8,128)(2,1)} %copy-done.2, f32[3584,128]{1,0:T(8,128)} %get-tuple-element.19.probs, ...), custom_call_target="tpu_custom_call" | custom-call | flops 150994944 | bytes 9175040 | tf_op jit(solution)/shard_map/pallas_call | solution.py:650
  146.5 0.9 copy-done.6
  147.4 3.2 %shard_map.117 = (f32[2304,256]{1,0:T(8,128)}, f32[720,256]{1,0:T(8,128)}) custom-call(s32[3]{0:T(128)} %pad_add_fusion.3.place, bf16[1536,256]{1,0:T(8,128)(2,1)} %copy-done, bf16[1536,256]{1,0:T(8,128)(2,1)} %copy-done.6), custom_call_target="tpu_custom_call" | custom-call | flops 1 | bytes 4718592 | tf_op jit(solution)/shard_map/pallas_call | solution.py:661
  (81 shorter events, 4.8 us)
Async XLA Ops:
  0.6 13.7 %copy-start.8 = (bf16[8,512,256]{2,1,0:T(8,128)(2,1)S(1)}, bf16[8,512,256]{2,1,0:T(8,128)(2,1)}, u32[]{:S(2)}) copy-start(bf16[8,512,256]{2,1,0:T(8,128)(2,1)} %refs_2_.1) | copy-start | bytes 6291460
  13.8 20.3 %collective-permute-start = (bf16[24,80,128]{2,1,0:T(8,128)(2,1)}, bf16[24,80,128]{2,1,0:T(8,128)(2,1)}, u32[]{:S(2)}, u32[]{:S(2)}) collective-permute-start(bf16[24,80,128]{2,1,0:T(8,128)(2,1)} %get-tuple-element.16), channel_id=1, source_target_pairs={{0,1},{1,0},{2,3},{3,2},{4,5},{5,4},{6,7},{7,6},{8,9},{9,8},{10,11... | collective-permute-start | bytes 1474568 | tf_op jit(solution)/shard_map/ppermute | solution.py:404
  14.5 25.0 %collective-permute-start.7 = (bf16[2,512,256]{2,1,0:T(8,128)(2,1)S(1)}, bf16[2,512,256]{2,1,0:T(8,128)(2,1)S(1)}, u32[]{:S(2)}, u32[]{:S(2)}) collective-permute-start(bf16[2,512,256]{2,1,0:T(8,128)(2,1)S(1)} %get-tuple-element.28), channel_id=1, source_target_pairs={{0,1},{1,0},{2,3},{3,2},{4,5},{5,4},{6,7},{7,6},{8,9},{9,8},{10,11... | collective-permute-start | bytes 1572872 | tf_op jit(solution)/shard_map/ppermute | solution.py:472
  14.6 24.9 %collective-permute-start.6 = (bf16[2,512,256]{2,1,0:T(8,128)(2,1)S(1)}, bf16[2,512,256]{2,1,0:T(8,128)(2,1)S(1)}, u32[]{:S(2)}, u32[]{:S(2)}) collective-permute-start(bf16[2,512,256]{2,1,0:T(8,128)(2,1)S(1)} %get-tuple-element.29), channel_id=1, source_target_pairs={{0,31},{1,2},{2,1},{3,4},{4,3},{5,6},{6,5},{7,8},{8,7},{9,10},{10,... | collective-permute-start | bytes 1572872 | tf_op jit(solution)/shard_map/ppermute | solution.py:473
  22.0 10.4 %copy-start.9 = (bf16[3,3,80,256]{3,2,1,0:T(8,128)(2,1)S(1)}, bf16[3,3,80,256]{3,2,1,0:T(8,128)(2,1)}, u32[]{:S(2)}) copy-start(bf16[3,3,80,256]{3,2,1,0:T(8,128)(2,1)} %param.13) | copy-start | bytes 1105924
  35.5 7.2 %collective-permute-start.2 = (bf16[8,80,128]{2,1,0:T(8,128)(2,1)S(1)}, bf16[8,80,128]{2,1,0:T(8,128)(2,1)S(1)}, u32[]{:S(2)}, u32[]{:S(2)}) collective-permute-start(bf16[8,80,128]{2,1,0:T(8,128)(2,1)S(1)} %get-tuple-element.40), channel_id=1, source_target_pairs={{1,3},{2,0},{5,7},{6,4},{9,11},{10,8},{13,15},{14,12},{17,19},{18,... | collective-permute-start | bytes 491528 | tf_op jit(solution)/shard_map/ppermute | solution.py:553
  36.8 7.7 %collective-permute-start.1 = (bf16[8,80,128]{2,1,0:T(8,128)(2,1)S(1)}, bf16[8,80,128]{2,1,0:T(8,128)(2,1)S(1)}, u32[]{:S(2)}, u32[]{:S(2)}) collective-permute-start(bf16[8,80,128]{2,1,0:T(8,128)(2,1)S(1)} %get-tuple-element.41), channel_id=1, source_target_pairs={{0,2},{1,3},{2,0},{3,1},{4,6},{5,7},{6,4},{7,5},{8,10},{9,11},{10,... | collective-permute-start | bytes 491528 | tf_op jit(solution)/shard_map/ppermute | solution.py:404
  44.5 11.9 %copy-start.5 = (bf16[8,80,128]{2,1,0:T(8,128)(2,1)}, bf16[8,80,128]{2,1,0:T(8,128)(2,1)S(1)}, u32[]{:S(2)}) copy-start(bf16[8,80,128]{2,1,0:T(8,128)(2,1)S(1)} %get-tuple-element.38.edge) | copy-start | bytes 491524
  44.5 11.9 %copy-start.7 = (bf16[8,80,128]{2,1,0:T(8,128)(2,1)}, bf16[8,80,128]{2,1,0:T(8,128)(2,1)S(1)}, u32[]{:S(2)}) copy-start(bf16[8,80,128]{2,1,0:T(8,128)(2,1)S(1)} %get-tuple-element.39.own) | copy-start | bytes 491524
  44.6 11.9 %collective-permute-start.3 = (bf16[2,80,128]{2,1,0:T(8,128)(2,1)S(1)}, bf16[2,80,128]{2,1,0:T(8,128)(2,1)S(1)}, u32[]{:S(2)}, u32[]{:S(2)}) collective-permute-start(bf16[2,80,128]{2,1,0:T(8,128)(2,1)S(1)} %get-tuple-element.52), channel_id=1, source_target_pairs={{0,1},{1,0},{2,3},{3,2},{4,5},{5,4},{6,7},{7,6},{8,9},{9,8},{10,11... | collective-permute-start | bytes 122888 | tf_op jit(solution)/shard_map/ppermute | solution.py:579
  44.7 11.8 %collective-permute-start.4 = (bf16[10,80,128]{2,1,0:T(8,128)(2,1)S(1)}, bf16[10,80,128]{2,1,0:T(8,128)(2,1)S(1)}, u32[]{:S(2)}, u32[]{:S(2)}) collective-permute-start(bf16[10,80,128]{2,1,0:T(8,128)(2,1)S(1)} %maximum_select_fusion), channel_id=1, source_target_pairs={{0,31},{1,2},{2,1},{3,4},{4,3},{5,6},{6,5},{7,8},{8,7},{9,10},{10,... | collective-permute-start | bytes 614408 | tf_op jit(solution)/shard_map/ppermute | solution.py:577
  46.1 10.4 %collective-permute-start.5 = (bf16[2,80,128]{2,1,0:T(8,128)(2,1)S(1)}, bf16[2,80,128]{2,1,0:T(8,128)(2,1)S(1)}, u32[]{:S(2)}, u32[]{:S(2)}) collective-permute-start(bf16[2,80,128]{2,1,0:T(8,128)(2,1)S(1)} %slice_select_fusion), channel_id=1, source_target_pairs={{0,30},{4,2},{8,6},{12,10},{16,14},{20,18},{24,22},{28,26},{3,5},{... | collective-permute-start | bytes 122888 | tf_op jit(solution)/shard_map/ppermute | solution.py:575
  56.5 0.6 copy-start.12
  56.5 0.6 copy-start.13
  56.5 0.7 copy-start.10
  78.5 2.6 %collective-permute-start.12 = (bf16[1536,256]{1,0:T(8,128)(2,1)}, bf16[1536,256]{1,0:T(8,128)(2,1)S(1)}, u32[]{:S(2)}, u32[]{:S(2)}) collective-permute-start(bf16[1536,256]{1,0:T(8,128)(2,1)} %get-tuple-element.23), channel_id=1, source_target_pairs={{0,1},{1,0},{2,3},{3,2},{4,5},{5,4},{6,7},{7,6},{8,9},{9,8},{10,11... | collective-permute-start | bytes 2359304 | tf_op jit(solution)/shard_map/ppermute | solution.py:404
  82.4 31.5 %copy-start.11 = (bf16[8,80,128]{2,1,0:T(8,128)(2,1)S(1)}, bf16[8,80,128]{2,1,0:T(8,128)(2,1)}, u32[]{:S(2)}) copy-start(bf16[8,80,128]{2,1,0:T(8,128)(2,1)} %get-tuple-element.18) | copy-start | bytes 491524
  82.4 33.6 %copy-start.3 = (bf16[8,80,128]{2,1,0:T(8,128)(2,1)S(1)}, bf16[8,80,128]{2,1,0:T(8,128)(2,1)}, u32[]{:S(2)}) copy-start(bf16[8,80,128]{2,1,0:T(8,128)(2,1)} %get-tuple-element.17.own) | copy-start | bytes 491524
  82.5 5.7 %collective-permute-start.15 = (bf16[384,256]{1,0:T(8,128)(2,1)S(1)}, bf16[384,256]{1,0:T(8,128)(2,1)S(1)}, u32[]{:S(2)}, u32[]{:S(2)}) collective-permute-start(bf16[384,256]{1,0:T(8,128)(2,1)S(1)} %get-tuple-element.36), channel_id=1, source_target_pairs={{0,4},{1,17},{2,6},{3,19},{4,0},{5,21},{6,2},{7,23},{8,12},{9,25},... | collective-permute-start | bytes 589832 | tf_op jit(solution)/shard_map/ppermute | solution.py:423
  82.9 5.7 %collective-permute-start.14 = (bf16[384,256]{1,0:T(8,128)(2,1)S(1)}, bf16[384,256]{1,0:T(8,128)(2,1)S(1)}, u32[]{:S(2)}, u32[]{:S(2)}) collective-permute-start(bf16[384,256]{1,0:T(8,128)(2,1)S(1)} %get-tuple-element.37), channel_id=1, source_target_pairs={{0,2},{1,9},{2,0},{3,11},{4,6},{5,13},{6,4},{7,15},{8,10},{9,1},{1... | collective-permute-start | bytes 589832 | tf_op jit(solution)/shard_map/ppermute | solution.py:423
  82.9 8.8 %collective-permute-start.13 = (bf16[384,256]{1,0:T(8,128)(2,1)S(1)}, bf16[384,256]{1,0:T(8,128)(2,1)S(1)}, u32[]{:S(2)}, u32[]{:S(2)}) collective-permute-start(bf16[384,256]{1,0:T(8,128)(2,1)S(1)} %get-tuple-element.35), channel_id=1, source_target_pairs={{0,6},{1,25},{2,4},{3,27},{4,2},{5,29},{6,0},{7,31},{8,14},{9,17},... | collective-permute-start | bytes 589832 | tf_op jit(solution)/shard_map/ppermute | solution.py:423
  91.9 5.1 %collective-permute-start.18 = (bf16[96,256]{1,0:T(8,128)(2,1)S(1)}, bf16[96,256]{1,0:T(8,128)(2,1)S(1)}, u32[]{:S(2)}, u32[]{:S(2)}) collective-permute-start(bf16[96,256]{1,0:T(8,128)(2,1)S(1)} %get-tuple-element.47), channel_id=1, source_target_pairs={{0,16},{1,5},{2,18},{3,7},{4,20},{5,1},{6,22},{7,3},{8,24},{9,13},... | collective-permute-start | bytes 147464 | tf_op jit(solution)/shard_map/ppermute | solution.py:423
  92.1 4.9 %collective-permute-start.17 = (bf16[96,256]{1,0:T(8,128)(2,1)S(1)}, bf16[96,256]{1,0:T(8,128)(2,1)S(1)}, u32[]{:S(2)}, u32[]{:S(2)}) collective-permute-start(bf16[96,256]{1,0:T(8,128)(2,1)S(1)} %get-tuple-element.48), channel_id=1, source_target_pairs={{0,8},{1,3},{2,10},{3,1},{4,12},{5,7},{6,14},{7,5},{8,0},{9,11},{1... | collective-permute-start | bytes 147464 | tf_op jit(solution)/shard_map/ppermute | solution.py:423
  93.6 5.9 %collective-permute-start.16 = (bf16[96,256]{1,0:T(8,128)(2,1)S(1)}, bf16[96,256]{1,0:T(8,128)(2,1)S(1)}, u32[]{:S(2)}, u32[]{:S(2)}) collective-permute-start(bf16[96,256]{1,0:T(8,128)(2,1)S(1)} %get-tuple-element.46), channel_id=1, source_target_pairs={{0,24},{1,7},{2,26},{3,5},{4,28},{5,3},{6,30},{7,1},{8,16},{9,15},... | collective-permute-start | bytes 147464 | tf_op jit(solution)/shard_map/ppermute | solution.py:423
  99.6 6.0 %collective-permute-start.19 = (bf16[96,256]{1,0:T(8,128)(2,1)S(1)}, bf16[96,256]{1,0:T(8,128)(2,1)S(1)}, u32[]{:S(2)}, u32[]{:S(2)}) collective-permute-start(bf16[96,256]{1,0:T(8,128)(2,1)S(1)} %add_convert_fusion.5), channel_id=1, source_target_pairs={{0,24},{1,7},{2,26},{3,5},{4,28},{5,3},{6,30},{7,1},{8,16},{9,15},... | collective-permute-start | bytes 147464 | tf_op jit(solution)/shard_map/ppermute | solution.py:423
  102.3 6.8 %collective-permute-start.20 = (bf16[96,256]{1,0:T(8,128)(2,1)S(1)}, bf16[96,256]{1,0:T(8,128)(2,1)S(1)}, u32[]{:S(2)}, u32[]{:S(2)}) collective-permute-start(bf16[96,256]{1,0:T(8,128)(2,1)S(1)} %add_convert_fusion.5), channel_id=1, source_target_pairs={{0,16},{1,5},{2,18},{3,7},{4,20},{5,1},{6,22},{7,3},{8,24},{9,13},... | collective-permute-start | bytes 147464 | tf_op jit(solution)/shard_map/ppermute | solution.py:423
  102.3 6.8 %collective-permute-start.21 = (bf16[96,256]{1,0:T(8,128)(2,1)S(1)}, bf16[96,256]{1,0:T(8,128)(2,1)S(1)}, u32[]{:S(2)}, u32[]{:S(2)}) collective-permute-start(bf16[96,256]{1,0:T(8,128)(2,1)S(1)} %add_convert_fusion.5), channel_id=1, source_target_pairs={{0,8},{1,3},{2,10},{3,1},{4,12},{5,7},{6,14},{7,5},{8,0},{9,11},{1... | collective-permute-start | bytes 147464 | tf_op jit(solution)/shard_map/ppermute | solution.py:423
  109.2 16.4 %collective-permute-start.23 = (bf16[384,256]{1,0:T(8,128)(2,1)S(1)}, bf16[384,256]{1,0:T(8,128)(2,1)S(1)}, u32[]{:S(2)}, u32[]{:S(2)}) collective-permute-start(bf16[384,256]{1,0:T(8,128)(2,1)S(1)} %pad_maximum_fusion.2), channel_id=1, source_target_pairs={{0,4},{1,17},{2,6},{3,19},{4,0},{5,21},{6,2},{7,23},{8,12},{9,25},... | collective-permute-start | bytes 589832 | tf_op jit(solution)/shard_map/ppermute | solution.py:423
  109.8 15.7 %collective-permute-start.22 = (bf16[384,256]{1,0:T(8,128)(2,1)S(1)}, bf16[384,256]{1,0:T(8,128)(2,1)S(1)}, u32[]{:S(2)}, u32[]{:S(2)}) collective-permute-start(bf16[384,256]{1,0:T(8,128)(2,1)S(1)} %pad_maximum_fusion.2), channel_id=1, source_target_pairs={{0,6},{1,25},{2,4},{3,27},{4,2},{5,29},{6,0},{7,31},{8,14},{9,17},... | collective-permute-start | bytes 589832 | tf_op jit(solution)/shard_map/ppermute | solution.py:423
  113.4 12.1 %collective-permute-start.24 = (bf16[384,256]{1,0:T(8,128)(2,1)S(1)}, bf16[384,256]{1,0:T(8,128)(2,1)S(1)}, u32[]{:S(2)}, u32[]{:S(2)}) collective-permute-start(bf16[384,256]{1,0:T(8,128)(2,1)S(1)} %pad_maximum_fusion.2), channel_id=1, source_target_pairs={{0,2},{1,9},{2,0},{3,11},{4,6},{5,13},{6,4},{7,15},{8,10},{9,1},{1... | collective-permute-start | bytes 589832 | tf_op jit(solution)/shard_map/ppermute | solution.py:423
  113.9 10.3 %collective-permute-start.9 = (bf16[8,80,128]{2,1,0:T(8,128)(2,1)S(1)}, bf16[8,80,128]{2,1,0:T(8,128)(2,1)S(1)}, u32[]{:S(2)}, u32[]{:S(2)}) collective-permute-start(bf16[8,80,128]{2,1,0:T(8,128)(2,1)S(1)} %copy-done.11), channel_id=1, source_target_pairs={{0,31},{4,3},{8,7},{12,11},{16,15},{20,19},{24,23},{28,27},{3,4},{... | collective-permute-start | bytes 491528 | tf_op jit(solution)/shard_map/ppermute | solution.py:575
  116.0 12.4 %collective-permute-start.8 = (bf16[8,80,128]{2,1,0:T(8,128)(2,1)S(1)}, bf16[8,80,128]{2,1,0:T(8,128)(2,1)S(1)}, u32[]{:S(2)}, u32[]{:S(2)}) collective-permute-start(bf16[8,80,128]{2,1,0:T(8,128)(2,1)S(1)} %copy-done.3), channel_id=1, source_target_pairs={{0,2},{1,3},{2,0},{3,1},{4,6},{5,7},{6,4},{7,5},{8,10},{9,11},{10,... | collective-permute-start | bytes 491528 | tf_op jit(solution)/shard_map/ppermute | solution.py:404
  124.2 4.1 %collective-permute-start.10 = (bf16[8,80,128]{2,1,0:T(8,128)(2,1)S(1)}, bf16[8,80,128]{2,1,0:T(8,128)(2,1)S(1)}, u32[]{:S(2)}, u32[]{:S(2)}) collective-permute-start(bf16[8,80,128]{2,1,0:T(8,128)(2,1)S(1)} %collective-permute-done.9), channel_id=1, source_target_pairs={{3,1},{0,2},{7,5},{4,6},{11,9},{8,10},{15,13},{12,14},{19,17},{16,... | collective-permute-start | bytes 491528 | tf_op jit(solution)/shard_map/ppermute | solution.py:632
  125.9 12.6 %copy-start = (bf16[1536,256]{1,0:T(8,128)(2,1)}, bf16[1536,256]{1,0:T(8,128)(2,1)S(1)}, u32[]{:S(2)}) copy-start(bf16[1536,256]{1,0:T(8,128)(2,1)S(1)} %pad_maximum_fusion.value) | copy-start | bytes 2359300
  125.9 20.5 %collective-permute-start.25 = (bf16[1536,256]{1,0:T(8,128)(2,1)S(1)}, bf16[1536,256]{1,0:T(8,128)(2,1)S(1)}, u32[]{:S(2)}, u32[]{:S(2)}) collective-permute-start(bf16[1536,256]{1,0:T(8,128)(2,1)S(1)} %pad_maximum_fusion.value), channel_id=1, source_target_pairs={{0,1},{1,0},{2,3},{3,2},{4,5},{5,4},{6,7},{7,6},{8,9},{9,8},{10,11... | collective-permute-start | bytes 2359304 | tf_op jit(solution)/shard_map/ppermute | solution.py:404
  128.4 2.9 %copy-start.1 = (bf16[8,80,128]{2,1,0:T(8,128)(2,1)}, bf16[8,80,128]{2,1,0:T(8,128)(2,1)S(1)}, u32[]{:S(2)}) copy-start(bf16[8,80,128]{2,1,0:T(8,128)(2,1)S(1)} %broadcast_select_fusion.10.edge) | copy-start | bytes 491524
  128.4 2.9 %copy-start.4 = (bf16[8,80,128]{2,1,0:T(8,128)(2,1)}, bf16[8,80,128]{2,1,0:T(8,128)(2,1)S(1)}, u32[]{:S(2)}) copy-start(bf16[8,80,128]{2,1,0:T(8,128)(2,1)S(1)} %collective-permute-done.8.partner) | copy-start | bytes 491524
  128.5 2.8 %collective-permute-start.11 = (bf16[24,80,128]{2,1,0:T(8,128)(2,1)S(1)}, bf16[24,80,128]{2,1,0:T(8,128)(2,1)S(1)}, u32[]{:S(2)}, u32[]{:S(2)}) collective-permute-start(bf16[24,80,128]{2,1,0:T(8,128)(2,1)S(1)} %pad_maximum_fusion.1), channel_id=1, source_target_pairs={{0,1},{1,0},{2,3},{3,2},{4,5},{5,4},{6,7},{7,6},{8,9},{9,8},{10,11... | collective-permute-start | bytes 1474568 | tf_op jit(solution)/shard_map/ppermute | solution.py:404
  131.3 0.8 copy-start.2
  146.5 0.9 copy-start.6

commit v2 on v1

--- a/solution.py
+++ b/solution.py
@@ -10,7 +10,6 @@
 DEPTH_WEIGHT = 3.0
 TAPS = 3
 LANES = 128
-LIMIT = 60 * 1024 * 1024
 F32 = jnp.float32
 BF16 = jnp.bfloat16
 
@@ -28,9 +27,17 @@
     return jnp.concatenate([value, jnp.zeros((missing, value.shape[1]), value.dtype)], axis=0)
 
 
+def sectors_of(band, bands):
+    partner = (band + 2) % bands
+    return 1 + band, 1 + partner, (bands + 1) * (band % 2)
+
+
 def pool_kernel(
     rows,
-    table,
+    sight,
+    around,
+    place,
+    az_map,
     logits,
     context,
     probs_out,
@@ -38,6 +45,7 @@
     context_t_out,
     kept,
     sent,
+    begins,
     probs,
     probs_t,
     context_t,
@@ -50,6 +58,21 @@
     bins = logits.shape[0] // rows
     channels = context.shape[0] // rows
     half = kept.shape[0]
+    sector = half // 3
+    bands = 4
+    position = place[0]
+    band, camera = position % bands, position // bands
+    seen = 2 * half
+    begins[seen] = columns
+
+    def mark(step, _):
+        column = columns - 1 - step
+        cell = az_map[camera, column] - camera * sight + sight // 4
+        cell = jnp.where(cell < 0, cell + around, cell)
+        begins[jnp.where(cell >= around, cell - around, cell)] = column
+        return 0
+
+    lax.fori_loop(0, columns, mark, 0, unroll=8)
     scores = logits[...].reshape(bins, rows, columns)
     powers = jnp.exp(scores - jnp.max(scores, axis=0, keepdims=True))
     shares = powers / jnp.sum(powers, axis=0, keepdims=True)
@@ -76,56 +99,78 @@
         copies[-1].start()
     line = lax.broadcasted_iota(jnp.int32, (TAPS * rows, LANES), 0)
 
-    def cell_sum(slot):
-        span = pl.ds(pl.multiple_of(table[0, slot] * rows, rows), TAPS * rows)
+    def cell_sum(cell):
+        start = begins[cell]
+        span = pl.ds(pl.multiple_of(start * rows, rows), TAPS * rows)
         features = context_t[span, :]
-        features = jnp.where(line < table[1, slot] * rows, features, jnp.zeros_like(features))
+        width = (begins[cell + 1] - start) * rows
+        features = jnp.where(line < width, features, jnp.zeros_like(features))
         return product(features, probs_t[span, :], 0, 0)[:channels].astype(BF16)
 
-    def one_cell(slot, _):
-        sent[slot] = cell_sum(half + slot)
-        kept[slot] = cell_sum(slot)
-        return 0
-
-    lax.fori_loop(0, half, one_cell, 0, unroll=4)
+    near = band + 1 - 2 * (band % 2)
+    for group, (mine, theirs) in enumerate(
+        zip(sectors_of(band, bands), sectors_of(near, bands))
+    ):
+
+        def one_cell(step, _, group=group, mine=mine, theirs=theirs):
+            sent[group * sector + step] = cell_sum(theirs * sector + step)
+            kept[group * sector + step] = cell_sum(mine * sector + step)
+            return 0
+
+        lax.fori_loop(0, sector, one_cell, 0, unroll=4)
     for copy in copies:
         copy.wait()
 
 
-def act_grad_kernel(first, *refs):
-    *sources, weight, out, grid = refs
-    base = 0
-    for source, low, high in zip(sources, first[0], first[1]):
-        grid[base : base + high - low] = source[low:high]
-        base += high - low
+def act_row(taps, source, start, out, row):
+    hidden, length = out.shape[1:]
+    stacked = jnp.concatenate([source[start + i] for i in range(TAPS)], axis=1)
+    sums = product(taps, stacked, 1, 1)
+    place = lax.broadcasted_iota(jnp.int32, (hidden, length), 1)
+    ahead = pltpu.roll(sums[:hidden], length - 1, 1)
+    behind = pltpu.roll(sums[2 * hidden :], 1, 1)
+    total = sums[hidden : 2 * hidden]
+    total = total + jnp.where(place < length - 1, ahead, 0.0)
+    total = total + jnp.where(place > 0, behind, 0.0)
+    out[row] = total.astype(BF16)
+
+
+def act_taps_of(weight):
     hidden = weight.shape[3]
-    taps = jnp.concatenate(
+    return jnp.concatenate(
         [weight[TAPS - 1 - i].reshape(TAPS * hidden, hidden) for i in range(TAPS)], axis=1
     )
-    length = grid.shape[1]
-    place = lax.broadcasted_iota(jnp.int32, (hidden, length), 1)
-
-    def one_row(row, start):
-        stacked = jnp.concatenate([grid[start + i] for i in range(TAPS)], axis=1)
-        sums = product(taps, stacked, 1, 1)
-        ahead = pltpu.roll(sums[:hidden], length - 1, 1)
-        behind = pltpu.roll(sums[2 * hidden :], 1, 1)
-        total = sums[hidden : 2 * hidden]
-        total = total + jnp.where(place < length - 1, ahead, 0.0)
-        total = total + jnp.where(place > 0, behind, 0.0)
-        out[row] = total.astype(BF16)
-
-    starts = first[2]
-    if len(starts) > 4 or tuple(starts) == tuple(range(len(starts))):
-
-        def step(row, _):
-            one_row(row, row)
-            return 0
-
-        lax.fori_loop(0, len(starts), step, 0)
-    else:
-        for row, start in enumerate(starts):
-            one_row(row, start)
+
+
+def inner_acts_kernel(upstream, weight, out):
+    def step(row, _):
+        act_row(act_taps_of(weight), upstream, row, out, row)
+        return 0
+
+    lax.fori_loop(0, out.shape[0], step, 0)
+
+
+def outer_acts_kernel(place, near, far, upstream, weight, out, low, high):
+    sector = upstream.shape[0]
+    low[2:4] = upstream[0:2]
+    high[0:2] = upstream[sector - 2 :]
+
+    @pl.when(place[0] % 2 == 0)
+    def _():
+        low[0:2] = far[...]
+        high[2:4] = near[...]
+
+    @pl.when(place[0] % 2 == 1)
+    def _():
+        low[0:2] = near[...]
+        high[2:4] = far[...]
+
+    def step(row, _):
+        act_row(act_taps_of(weight), low, row, out, row)
+        act_row(act_taps_of(weight), high, row, out, row + 2)
+        return 0
+
+    lax.fori_loop(0, 2, step, 0)
 
 
 def grid_kernel(
@@ -136,11 +181,10 @@
     far_halo,
     two,
     ranges,
-    weight_t,
     weight,
     inner_grad,
     outer_grad,
-    upstream_in,
+    upstream,
     keep,
     send,
     own_reply,
@@ -152,29 +196,20 @@
     slope_rows,
     slope_lanes,
     grid_grad,
-    act_grads,
-    upstream,
+    weight_t,
+    range_hot,
+    picks,
     grads,
-    done,
 ):
     sector, channels, lanes = own.shape
     hidden, length = outer_grad.shape[1:]
-    mine, bands, core = place[0], place[1], place[2]
+    bands = 4
+    cameras, bins = ranges.shape
+    position = place[0]
+    mine, core = position % bands, position % 2
+    camera = position // bands
+    other = jnp.where(mine < bands // 2, camera + cameras - 1, camera + 1) % cameras
     wide = sector + 4
-    rows = sector + 2
-    copies = [
-        pltpu.make_async_copy(source, target, done.at[k])
-        for k, (source, target) in enumerate(
-            (
-                (inner_grad, act_grads.at[2:sector]),
-                (outer_grad.at[0:2], act_grads.at[0:2]),
-                (outer_grad.at[2:4], act_grads.at[sector:]),
-                (upstream_in, upstream),
-            )
-        )
-    ]
-    for copy in copies:
-        copy.start()
     cells[2 : 2 + sector, :, :lanes] = own[...]
     cells[:, :, lanes:] = jnp.zeros((wide, channels, lanes), BF16)
 
@@ -202,8 +237,18 @@
         cells[2 + sector :, :, :lanes] = edge[0:2]
         cells[2:, :, lanes:] = far_halo[...]
 
-    spots = lax.broadcasted_iota(jnp.int32, (2 * lanes, length), 1)
-    range_hot = (spots == ranges[...]).astype(F32).astype(BF16)
+    picks[...] = jnp.full(picks.shape, -1, jnp.int32)
+    picks[0:1, 0:bins] = ranges[pl.ds(camera, 1), :]
+    picks[0:1, lanes : lanes + bins] = ranges[pl.ds(other, 1), :]
+    spots = lax.broadcasted_iota(jnp.int32, (length, 2 * lanes), 0)
+    range_hot[...] = (spots == picks[0:1, :]).astype(F32).astype(BF16)
+    for column in range(TAPS):
+        for row in range(TAPS):
+            weight_t[column * hidden : (column + 1) * hidden, row * channels : (row + 1) * channels] = (
+                jnp.transpose(
+                    weight[row, column * channels : (column + 1) * channels, :].astype(F32)
+                ).astype(BF16)
+            )
 
     def behind(value):
         turned = pltpu.roll(value, 1, 1)
@@ -219,7 +264,7 @@
 
     for chunk in range(0, wide, 4):
         block = cells[chunk : chunk + 4].reshape(4 * channels, 2 * lanes)
-        summed = product(block, range_hot, 1, 0)
+        summed = product(block, range_hot[...], 1, 1)
         for row in range(chunk, chunk + 4):
             value = summed[(row - chunk) * channels : (row - chunk + 1) * channels]
             grid_low[row * channels : (row + 1) * channels, :] = value.astype(BF16)
@@ -228,10 +273,8 @@
                 grid_taps[0:channels, spread] = behind(value).astype(BF16)
                 grid_taps[channels : 2 * channels, spread] = value.astype(BF16)
                 grid_taps[2 * channels :, spread] = ahead(value).astype(BF16)
-    for copy in copies[:3]:
-        copy.wait()
-
-    def one_row(row, _):
+
+    def one_row(row, act_grad):
         source = pl.ds(pl.multiple_of(row * channels, channels), TAPS * channels)
         sums = product(weight_t[...], grid_low[source, :], 1, 0)
         value = behind(sums[:hidden]) + sums[hidden : 2 * hidden] + ahead(sums[2 * hidden :])
@@ -242,13 +285,21 @@
         act_taps[hidden : 2 * hidden, spread] = active.astype(BF16)
         act_taps[2 * hidden :, spread] = ahead(active).astype(BF16)
         slope = logistic * (1.0 + value * (1.0 - logistic))
-        result = (act_grads[row].astype(F32) * slope).astype(BF16)
+        result = (act_grad.astype(F32) * slope).astype(BF16)
         slope_rows[pl.ds(pl.multiple_of(row * hidden, hidden), hidden), :] = result
         slope_lanes[:, spread] = result
-        return 0
-
-    lax.fori_loop(0, rows, one_row, 0, unroll=2)
-    copies[3].wait()
+
+    def outside(pair, _):
+        one_row(pair, outer_grad[pair])
+        one_row(pair + sector, outer_grad[pair + 2])
+        return 0
+
+    def inside(row, _):
+        one_row(row + 2, inner_grad[row])
+        return 0
+
+    lax.fori_loop(0, 2, outside, 0)
+    lax.fori_loop(0, sector - 2, inside, 0, unroll=2)
     count = sector * length
     tall = TAPS * hidden
     short = TAPS * channels
@@ -285,44 +336,61 @@
         return 0
 
     lax.fori_loop(0, sector, back, 0, unroll=2)
-    picked = product(grid_grad[...], range_hot, 1, 1).astype(BF16)
+    picked = product(grid_grad[...], range_hot[...], 1, 0).astype(BF16)
     own_reply[...] = picked[:, :lanes].reshape(sector, channels, lanes)
     other_reply[...] = picked[:, lanes:].reshape(sector, channels, lanes)
 
 
-def finish_kernel(place, value, other, second, first):
+def finish_kernel(shifts, place, value, other, second, first, total):
     half = value.shape[0]
-    cut = second.shape[0] - half
-
-    def write(low, high):
-        second[0:half, :] = low[...].astype(F32)
-        second[half:, :] = high[0:cut, :].astype(F32)
-        first[...] = high[cut : cut + first.shape[0], :].astype(F32)
-
-    @pl.when(place[2] == 0)
-    def _():
-        write(value, other)
-
-    @pl.when(place[2] == 1)
-    def _():
-        write(other, value)
+    size = half // 4
+    position = place[0]
+    core = position % 2
+    for source, side in ((value, core), (other, 1 - core)):
+        digit = jnp.where(side == 0, position >> shifts[0], position >> shifts[1]) & 3
+        for mask in range(4):
+            spot = side * half + (digit ^ mask) * size
+            total[pl.ds(pl.multiple_of(spot, size), size), :] = source[
+                mask * size : (mask + 1) * size, :
+            ]
+    count = second.shape[0]
+    second[...] = total[0:count, :].astype(F32)
+    first[...] = total[count : count + first.shape[0], :].astype(F32)
+
+
+def lay_out(place, sector, mine, theirs, wedges):
+    bands = 4
+    band = place[0] % bands
+    near = band + 1 - 2 * (band % 2)
+    for group, spot in enumerate(sectors_of(band, bands)):
+        wedges[pl.ds(spot * sector, sector)] = mine[group][...]
+    for group, spot in enumerate(sectors_of(near, bands)):
+        wedges[pl.ds(spot * sector, sector)] = theirs[group * sector : (group + 1) * sector]
 
 
 def logit_kernel(
-    rows, table, own, partner, edge, theirs, probs, context_t, lidar, logit_grad, wedges, wide
+    rows,
+    place,
+    begins,
+    own,
+    partner,
+    edge,
+    theirs,
+    probs,
+    context_t,
+    lidar,
+    logit_grad,
+    wedges,
+    wide,
 ):
     columns = probs.shape[1]
     bins = probs.shape[0] // rows
     sector, channels, _ = own.shape
-    wedges[0:sector] = own[...]
-    wedges[sector : 2 * sector] = partner[...]
-    wedges[2 * sector : 3 * sector] = edge[...]
-    wedges[3 * sector :] = theirs[...]
+    lay_out(place, sector, (own, partner, edge), theirs, wedges)
 
     def one_cell(cell, _):
-        span = pl.ds(pl.multiple_of(table[0, cell] * rows, rows), TAPS * rows)
-        slope = wedges[table[1, cell]]
-        wide[span, :] = product(context_t[span, :][:, :channels], slope, 1, 0)
+        span = pl.ds(pl.multiple_of(begins[cell] * rows, rows), TAPS * rows)
+        wide[span, :] = product(context_t[span, :][:, :channels], wedges[cell], 1, 0)
         return 0
 
     lax.fori_loop(0, wedges.shape[0], one_cell, 0, unroll=8)
@@ -345,19 +413,27 @@
 
 
 def context_kernel(
-    rows, table, own, partner, edge, theirs, probs_t, context_grad, wedges, wide, plain
+    rows,
+    place,
+    begins,
+    own,
+    partner,
+    edge,
+    theirs,
+    probs_t,
+    context_grad,
+    wedges,
+    wide,
+    plain,
 ):
     columns = context_grad.shape[1]
     sector, channels, _ = own.shape
-    wedges[0:sector] = own[...]
-    wedges[sector : 2 * sector] = partner[...]
-    wedges[2 * sector : 3 * sector] = edge[...]
-    wedges[3 * sector :] = theirs[...]
+    lay_out(place, sector, (own, partner, edge), theirs, wedges)
     wide[...] = jnp.zeros_like(wide)
 
     def one_cell(cell, _):
-        span = pl.ds(pl.multiple_of(table[0, cell] * rows, rows), TAPS * rows)
-        wide[span, 0:channels] = product(probs_t[span, :], wedges[table[1, cell]], 1, 1)
+        span = pl.ds(pl.multiple_of(begins[cell] * rows, rows), TAPS * rows)
+        wide[span, 0:channels] = product(probs_t[span, :], wedges[cell], 1, 1)
         return 0
 
     lax.fori_loop(0, wedges.shape[0], one_cell, 0, unroll=8)
@@ -380,10 +456,10 @@
 
 
 def anywhere():
-    return pl.BlockSpec(memory_space=pl.ANY)
-
-
-def call(kernel, out_shape, scratch, spaces, flops, moved, outs=None):
+    return pl.BlockSpec(memory_space=pltpu.HBM)
+
+
+def call(kernel, out_shape, scratch, spaces, flops, moved, outs=None, limit=16):
     many = isinstance(out_shape, (list, tuple))
     return pl.pallas_call(
         kernel,
@@ -391,7 +467,7 @@
         in_specs=spaces,
         out_specs=outs or ([vmem() for _ in out_shape] if many else vmem()),
         scratch_shapes=scratch,
-        compiler_params=pltpu.CompilerParams(vmem_limit_bytes=LIMIT),
+        compiler_params=pltpu.CompilerParams(vmem_limit_bytes=limit * 1024 * 1024),
         cost_estimate=pl.CostEstimate(flops=flops, bytes_accessed=moved, transcendentals=0),
     )
 
@@ -409,10 +485,14 @@
     return lax.dynamic_slice_in_dim(value, index * size, size, 0)
 
 
+def axis_orders(count):
+    pairs = list(range(1, count, 2))
+    return pairs, pairs[1:] + pairs[:1]
+
+
 def total_over_blocks(keep, send, position, blocks):
     count = blocks.bit_length() - 1
-    pairs = list(range(1, count, 2))
-    orders = (pairs, pairs[1:] + pairs[:1])
+    orders = axis_orders(count)
     core = position & 1
     digits = [
         jnp.where(core == 0, position >> one, position >> two) & 3 for one, two in zip(*orders)
@@ -424,13 +504,17 @@
 
     value = rounded_sum(keep, swapped(send, blocks, 1))
     for step, digit in enumerate(digits):
-        arrived = [sent(piece(value, digit ^ mask, 4), step, mask) for mask in (3, 1, 2)]
+        leaving = [piece(value, digit ^ mask, 4) for mask in (3, 1, 2)]
+        arrived = [sent(part, step, mask) for part, mask in zip(leaving, (3, 1, 2))]
         total = piece(value, digit, 4).astype(F32)
         for part in arrived:
             total = total + part.astype(F32)
         value = total.astype(BF16)
     for step, digit in reversed(list(enumerate(digits))):
         held = [value] + [sent(value, step, mask) for mask in (1, 2, 3)]
+        if step == 0:
+            value = jnp.concatenate(held, axis=0)
+            break
         high, low = digit >> 1 == 1, digit & 1 == 1
 
         def at(k):
@@ -454,13 +538,12 @@
     channels = context.shape[1]
     if bands != 4 or blocks != 1 << (blocks.bit_length() - 1) or blocks.bit_length() % 2 or bins > LANES or channels > LANES or sector < 6:
         raise ValueError("unsupported sizes")
-    camera = position // bands
     band = position % bands
     sight = bands * sector
     seen = sight + sight // 2
 
     core = position & 1
-    place = jnp.stack([band, jnp.full_like(band, bands), core])
+    place = position.reshape(1)
     on_chip = [(i, i ^ 1) for i in range(blocks)]
     off_chip = [(i, (i + 1 if i & 1 else i - 1) % blocks) for i in range(blocks)]
 
@@ -469,41 +552,20 @@
         start = jnp.where((core == 0) == near, count - 2, 0)
         return lax.dynamic_slice_in_dim(value, start, 2, 0)
 
+    far_grad = lax.ppermute(ends(out_grad, False), "blk", off_chip)
     near_grad = lax.ppermute(ends(out_grad, True), "blk", on_chip)
-    far_grad = lax.ppermute(ends(out_grad, False), "blk", off_chip)
-    low_grad = jnp.where(core == 0, far_grad, near_grad)
-    high_grad = jnp.where(core == 0, near_grad, far_grad)
-
-    az_row = lax.dynamic_slice_in_dim(az_map, camera, 1, 0)[0]
-    local = (az_row - (camera * sight - sight // 4)) % (blocks * sector)
-    marks = jnp.arange(seen + 1, dtype=jnp.int32)
-    begins = jnp.sum((local[None, :] < marks[:, None]).astype(jnp.int32), axis=1)
-    near = band ^ 1
-    order = jnp.stack(
-        [1 + band, 1 + (band ^ 2), 5 * (band % 2), 1 + near, 1 + (near ^ 2), 5 * (near % 2)]
-    )
-    sixth = jnp.arange(6, dtype=jnp.int32)
-    inverse = jnp.sum(jnp.where(order[None, :] == sixth[:, None], sixth[None, :], 0), axis=1)
-    steps = jnp.arange(sector, dtype=jnp.int32)
-    cells = (order[:, None] * sector + steps[None, :]).reshape(-1)
-    slots = (inverse[:, None] * sector + steps[None, :]).reshape(-1)
-    hot = (cells[:, None] == marks[None, :seen]).astype(jnp.int32)
-    widths = begins[1:] - begins[:-1]
-    pool_table = jnp.stack(
-        [jnp.sum(hot * begins[None, :seen], axis=1), jnp.sum(hot * widths[None, :], axis=1)]
-    )
-    pixel_table = jnp.stack([begins[:seen], slots])
 
     turned = (columns + 1) * rows
     half = 3 * sector
-    probs, probs_t, context_t, kept, sent = call(
-        functools.partial(pool_kernel, rows),
+    probs, probs_t, context_t, kept, sent, begins = call(
+        functools.partial(pool_kernel, rows, sight, blocks * sector),
         [
             jax.ShapeDtypeStruct((bins * rows, columns), F32),
             jax.ShapeDtypeStruct((turned, LANES), BF16),
             jax.ShapeDtypeStruct((turned, LANES), BF16),
             jax.ShapeDtypeStruct((half, channels, LANES), BF16),
             jax.ShapeDtypeStruct((half, channels, LANES), BF16),
+            jax.ShapeDtypeStruct((seen + 1,), jnp.int32),
         ],
         [
             pltpu.VMEM((bins * rows, columns), F32),
@@ -514,36 +576,36 @@
             pltpu.VMEM((channels * rows, columns), F32),
             pltpu.SemaphoreType.DMA((3,)),
         ],
-        [smem(), vmem(), vmem()],
+        [smem(), smem(), vmem(), vmem()],
         2 * seen * 3 * rows * LANES * LANES,
         20 * bins * rows * columns,
-        [anywhere()] * 3 + [vmem()] * 2,
+        [anywhere()] * 3 + [vmem()] * 2 + [smem()],
+        limit=56,
     )(
-        pool_table,
+        place,
+        az_map,
         depth_logits[0].reshape(bins * rows, columns),
         context[0].reshape(channels * rows, columns),
     )
 
     row_flops = 2 * TAPS * TAPS * hidden * hidden * length
 
-    def act_grad(sources, lows, highs, starts):
-        total = sum(h - l for l, h in zip(lows, highs))
-        return call(
-            functools.partial(act_grad_kernel, (lows, highs, starts)),
-            jax.ShapeDtypeStruct((len(starts), hidden, length), BF16),
-            [pltpu.VMEM((total, length, hidden), BF16)],
-            [vmem() for _ in sources] + [vmem()],
-            row_flops * len(starts),
-            2 * (total + len(starts)) * length * hidden,
-        )(*sources, conv2_weight)
-
-    inner_grad = act_grad([out_grad], (0,), (sector,), tuple(range(sector - 2)))
-    outer_grad = act_grad(
-        [low_grad, out_grad, out_grad, high_grad],
-        (0, 0, sector - 2, 0),
-        (2, 2, sector, 2),
-        (0, 1, 4, 5),
-    )
+    inner_grad = call(
+        inner_acts_kernel,
+        jax.ShapeDtypeStruct((sector - 2, hidden, length), BF16),
+        [],
+        [vmem()] * 2,
+        row_flops * (sector - 2),
+        4 * sector * length * hidden,
+    )(out_grad, conv2_weight)
+    outer_grad = call(
+        outer_acts_kernel,
+        jax.ShapeDtypeStruct((4, hidden, length), BF16),
+        [pltpu.VMEM((4, length, hidden), BF16)] * 2,
+        [smem()] + [vmem()] * 4,
+        row_flops * 4,
+        16 * length * hidden,
+    )(place, near_grad, far_grad, out_grad, conv2_weight)
 
     summed = rounded_sum(kept, swapped(sent, blocks, 1))
     own = rounded_sum(summed[:sector], swapped(summed[sector : 2 * sector], blocks, 2))
@@ -577,12 +639,6 @@
     far_halo = lax.ppermute(far, "blk", off_chip)
     two = to_next(two, 1)
     near_halo = lax.ppermute(ends(own, True), "blk", on_chip)
-    other = jnp.where(band < bands // 2, camera - 1, camera + 1) % cameras
-    ranges = jnp.concatenate(
-        [lax.dynamic_slice_in_dim(rng_map, k, 1, 0) for k in (camera, other)], axis=0
-    )
-    ranges = jnp.pad(ranges, ((0, 0), (0, LANES - bins)), constant_values=-1).reshape(-1, 1)
-    weight_t = conv1_weight.transpose(1, 3, 0, 2).reshape(TAPS * hidden, TAPS * channels)
     weight = conv1_weight.reshape(TAPS, TAPS * channels, hidden)
     grad_rows = TAPS * TAPS * (hidden + channels)
     unit = blocks * 16
@@ -604,14 +660,15 @@
             pltpu.VMEM((wide * hidden, length), BF16),
             pltpu.VMEM((hidden, wide * length), BF16),
             pltpu.VMEM((sector * channels, length), BF16),
-            pltpu.VMEM((wide, hidden, length), BF16),
-            pltpu.VMEM((sector * length, hidden), BF16),
+            pltpu.VMEM((TAPS * hidden, TAPS * channels), BF16),
+            pltpu.VMEM((length, 2 * LANES), BF16),
+            pltpu.VMEM((8, 2 * LANES), jnp.int32),
             pltpu.VMEM((grad_rows, hidden), BF16),
-            pltpu.SemaphoreType.DMA((4,)),
         ],
-        [smem()] + [vmem()] * 8 + [anywhere()] * 3,
+        [smem()] + [vmem()] * 10,
         row_flops * (sector + 3 * sector // 2),
         20 * sector * length * hidden,
+        limit=32,
     )(
         place,
         own,
@@ -619,8 +676,7 @@
         near_halo,
         far_halo,
         two,
-        ranges,
-        weight_t,
+        rng_map,
         weight,
         inner_grad,
         outer_grad,
@@ -643,28 +699,30 @@
         functools.partial(context_kernel, rows),
         jax.ShapeDtypeStruct((channels * rows, columns), BF16),
         scratch + [pltpu.VMEM((channels * rows, columns), F32)],
-        [smem()] + [vmem()] * 5,
+        [smem()] * 2 + [vmem()] * 5,
         cell_flops,
         10 * bins * rows * columns,
-    )(pixel_table, *replies, probs_t)
+    )(place, begins, *replies, probs_t)
     logit_grad = call(
         functools.partial(logit_kernel, rows),
         jax.ShapeDtypeStruct((bins * rows, columns), F32),
         scratch,
-        [smem()] + [vmem()] * 7,
+        [smem()] * 2 + [vmem()] * 7,
         cell_flops,
         20 * bins * rows * columns,
-    )(pixel_table, *replies, probs, context_t, lidar_bins[0])
+    )(place, begins, *replies, probs, context_t, lidar_bins[0])
 
     second = TAPS * TAPS * hidden
     first_rows = TAPS * TAPS * channels
     second_grad, first_grad = call(
-        finish_kernel,
+        functools.partial(
+            finish_kernel, [order[0] for order in axis_orders(blocks.bit_length() - 1)]
+        ),
         [
             jax.ShapeDtypeStruct((second, hidden), F32),
             jax.ShapeDtypeStruct((first_rows, hidden), F32),
         ],
-        [],
+        [pltpu.VMEM((grad_rows, hidden), BF16)],
         [smem(), vmem(), vmem()],
         1,
         6 * grad_rows * hidden,

time: 151 us -> 133 us (0.88)
  Pallas kernels: 65.6 us -> 54.5 us
  other arithmetic: 7.63 us -> 2.83 us
  local copies, waits for them, and re-layouts: 6.12 us -> 4.42 us
    pallas_call x4, Pallas kernels: 29.9 us -> 23.9 us  [the longest x1 11.9 us: shards(): call(functools.partial(pool_kernel, rows, sight, blocks * sector), [jax.S...]
    ppermute x12, waiting for transfers between devices: 14 us -> 19.4 us  [sent(): return lax.ppermute(part, 'blk', to)]
    ppermute x12, starting transfers between devices: 17.2 us -> 13.3 us  [sent(): return lax.ppermute(part, 'blk', to)]
    ppermute x1, starting transfers between devices: 1.39 us -> 4.94 us  [shards(): far_halo = lax.ppermute(far, 'blk', off_chip)]
    reshape x3 -> x0, local copies, waits for them, and re-layouts: 2.52 us -> none  [the longest x2 1.72 us: shards(): conv1_weight.transpose(1, 3, 0, 2).reshape(TAPS * hidden, TAPS * channels)]
    pallas_call x1, Pallas kernels: 21.3 us -> 18.8 us  [shards(): call(grid_kernel, [jax.ShapeDtypeStruct((grad_rows // 2, hidden), BF16),...]
    ppermute x1, waiting for transfers between devices: 2.34 us -> 0.01 us  [shards(): passed = lax.ppermute(edge_reply, 'blk', outward)]
    ppermute x1, waiting for transfers between devices: 2.15 us -> 0.01 us  [shards(): lax.ppermute(summed[2 * sector:], 'blk', inward)]
  transfers between devices with their start and end apart: 26 -> 26, of which waited for: 13 -> 13; matrix products, arithmetic and copies ran while one was open for 5% -> 3% of each run, Pallas kernels for 20% -> 16%
where the time goes in v2:
time: 133 us
  Pallas kernels  54.5 us (41%)
  starting transfers between devices  37.5 us (28%)
  waiting for transfers between devices  32.6 us (25%)
  local copies, waits for them, and re-layouts  4.42 us (3%)
  other arithmetic  2.83 us (2%)
    ppermute x12, waiting for transfers between devices, sent(): return lax.ppermute(part, 'blk', to)  19.4 us
    pallas_call x1, Pallas kernels, shards(): call(grid_kernel, [jax.ShapeDtypeStruct((grad_rows // 2, hidden), BF16),...  18.8 us
    ppermute x12, starting transfers between devices, sent(): return lax.ppermute(part, 'blk', to)  13.3 us
    pallas_call x1, Pallas kernels, shards(): call(functools.partial(pool_kernel, rows, sight, blocks * sector), [jax.S...  11.9 us
    ppermute x2, waiting for transfers between devices, to_next(): return lax.ppermute(value, 'blk', pairs)  7.11 us
    ppermute x1, starting transfers between devices, shards(): far_grad = lax.ppermute(ends(out_grad, False), 'blk', off_chip)  6.58 us
    pallas_call x1, Pallas kernels, shards(): call(functools.partial(logit_kernel, rows), jax.ShapeDtypeStruct((bins *...  6.47 us
    ppermute x6, waiting for transfers between devices, swapped(): return lax.ppermute(value, 'blk', [(i, i ^ mask) for i in range(blocks)])  6.04 us
  transfers between devices with their start and end apart: 26, of which 13 were waited for; matrix products, arithmetic and copies ran while one was open for 3% of the time, Pallas kernels for 16%

profile of v2, /device:TPU:0, one launch (start us, length us, event | category | flops | bytes accessed | tf_op | source)
XLA Modules:
  0.0 133.0 jit_solution(6979951918281607788)
XLA Ops:
  0.6 11.9 %shard_map.111 = (f32[3584,128]{1,0:T(8,128)}, bf16[4128,128]{1,0:T(8,128)(2,1)}, bf16[4128,128]{1,0:T(8,128)(2,1)}, bf16[24,80,128]{2,1,0:T(8,128)(2,1)}, bf16[24,80,128]{2,1,0:T(8,128)(2,1)}, /*index=5*/s32[49]{0:T(128)}) custom-call(s32[1]{0:T(128)} %bitcast.place, s32[8,128]{1,0:T(8,128)} %az_map.1, f32[3584,128]{1,0:T(8,128)} %bitcast.13, ...), custom_call_target="tpu_custom_call" | custom-call | flops 150994944 | bytes 9175040 | tf_op jit(solution)/shard_map/pallas_call | solution.py:560
  12.5 0.6 collective-permute-start
  13.1 1.0 constant_dynamic-slice_fusion.6
  14.2 6.6 %collective-permute-start.7 = (bf16[2,512,256]{2,1,0:T(8,128)(2,1)}, bf16[2,512,256]{2,1,0:T(8,128)(2,1)}, u32[]{:S(2)}, u32[]{:S(2)}) collective-permute-start(bf16[2,512,256]{2,1,0:T(8,128)(2,1)} %get-tuple-element.36), channel_id=1, source_target_pairs={{0,31},{1,2},{2,1},{3,4},{4,3},{5,6},{6,5},{7,8},{8,7},{9,10},{10,... | collective-permute-start | bytes 1572872 | tf_op jit(solution)/shard_map/ppermute | solution.py:555
  20.8 0.8 copy-done.13
  21.6 1.2 add_convert_fusion.1
  22.8 1.3 collective-permute-start.2
  24.1 3.3 %collective-permute-start.1 = (bf16[8,80,128]{2,1,0:T(8,128)(2,1)S(1)}, bf16[8,80,128]{2,1,0:T(8,128)(2,1)}, u32[]{:S(2)}, u32[]{:S(2)}) collective-permute-start(bf16[8,80,128]{2,1,0:T(8,128)(2,1)S(1)} %get-tuple-element.44), channel_id=1, source_target_pairs={{0,2},{1,3},{2,0},{3,1},{4,6},{5,7},{6,4},{7,5},{8,10},{9,11},{10,... | collective-permute-start | bytes 491528 | tf_op jit(solution)/shard_map/ppermute | solution.py:480
  27.4 5.7 %shard_map.112.inner_grad = bf16[6,256,512]{2,1,0:T(8,128)(2,1)S(1)} custom-call(bf16[8,512,256]{2,1,0:T(8,128)(2,1)S(1)} %copy-done.3, bf16[3,3,256,256]{3,2,1,0:T(8,128)(2,1)S(1)} %copy-done.6), custom_call_target="tpu_custom_call" | custom-call | flops 3623878656 | bytes 4194304 | tf_op jit(solution)/shard_map/pallas_call | solution.py:593
  33.0 1.1 copy-done.10
  34.2 1.3 collective-permute-done.1
  35.5 1.1 add_convert_fusion.3
  36.6 0.1 collective-permute-start.3
  36.7 4.9 %collective-permute-start.4 = (bf16[10,80,128]{2,1,0:T(8,128)(2,1)S(1)}, bf16[10,80,128]{2,1,0:T(8,128)(2,1)S(1)}, u32[]{:S(2)}, u32[]{:S(2)}) collective-permute-start(bf16[10,80,128]{2,1,0:T(8,128)(2,1)S(1)} %maximum_select_fusion), channel_id=1, source_target_pairs={{0,31},{1,2},{2,1},{3,4},{4,3},{5,6},{6,5},{7,8},{8,7},{9,10},{10,... | collective-permute-start | bytes 614408 | tf_op jit(solution)/shard_map/ppermute | solution.py:639
  41.7 3.3 %collective-permute-start.5 = (bf16[2,80,128]{2,1,0:T(8,128)(2,1)S(1)}, bf16[2,80,128]{2,1,0:T(8,128)(2,1)S(1)}, u32[]{:S(2)}, u32[]{:S(2)}) collective-permute-start(bf16[2,80,128]{2,1,0:T(8,128)(2,1)S(1)} %slice_select_fusion), channel_id=1, source_target_pairs={{0,30},{4,2},{8,6},{12,10},{16,14},{20,18},{24,22},{28,26},{3,5},{... | collective-permute-start | bytes 122888 | tf_op jit(solution)/shard_map/ppermute | solution.py:637
  45.0 1.3 copy-done.7
  46.3 4.4 %shard_map.113.outer_grad = bf16[4,256,512]{2,1,0:T(8,128)(2,1)S(1)} custom-call(s32[1]{0:T(128)} %bitcast.place, bf16[2,512,256]{2,1,0:T(8,128)(2,1)S(1)} %collective-permute-done.6.near, bf16[2,512,256]{2,1,0:T(8,128)(2,1)} %collective-permute-done.7.far, bf16[8,512,256]{2,1,0:T(8,128)(2,1)S(1)} %copy-done.3, bf16[3,3,256,256]{3,2,1,0:T(8,128)(2,1)S(1)} %copy-done.7), custom_call_target="tpu_custom_call" | custom-call | flops 2415919104 | bytes 2097152 | tf_op jit(solution)/shard_map/pallas_call | solution.py:601
  50.8 18.8 %shard_map.114 = (bf16[1536,256]{1,0:T(8,128)(2,1)S(1)}, bf16[1536,256]{1,0:T(8,128)(2,1)}, bf16[8,80,128]{2,1,0:T(8,128)(2,1)S(1)}, bf16[8,80,128]{2,1,0:T(8,128)(2,1)S(1)}) custom-call(s32[1]{0:T(128)} %bitcast.place, bf16[8,80,128]{2,1,0:T(8,128)(2,1)S(1)} %get-tuple-element.42.own, bf16[8,80,128]{2,1,0:T(8,128)(2,1)S(1)} %get-tuple-element.41.edge, ...), custom_call_target="tpu_custom_call" | custom-call | flops 12079595520 | bytes 20971520 | tf_op jit(solution)/shard_map/pallas_call | solution.py:647
  69.7 2.5 %collective-permute-done.12 = bf16[1536,256]{1,0:T(8,128)(2,1)S(1)} collective-permute-done((bf16[1536,256]{1,0:T(8,128)(2,1)}, bf16[1536,256]{1,0:T(8,128)(2,1)S(1)}, u32[]{:S(2)}, u32[]{:S(2)}) %collective-permute-start.12) | collective-permute-done | bytes 786464 | tf_op jit(solution)/shard_map/ppermute | solution.py:480
  72.2 0.2 add_convert_fusion
  72.5 0.1 collective-permute-start.15
  72.5 0.1 collective-permute-start.14
  72.6 3.4 %collective-permute-start.13 = (bf16[384,256]{1,0:T(8,128)(2,1)S(1)}, bf16[384,256]{1,0:T(8,128)(2,1)S(1)}, u32[]{:S(2)}, u32[]{:S(2)}) collective-permute-start(bf16[384,256]{1,0:T(8,128)(2,1)S(1)} %get-tuple-element.38), channel_id=1, source_target_pairs={{0,6},{1,25},{2,4},{3,27},{4,2},{5,29},{6,0},{7,31},{8,14},{9,17},... | collective-permute-start | bytes 589832 | tf_op jit(solution)/shard_map/ppermute | solution.py:503
  76.0 2.2 %collective-permute-done.15 = bf16[384,256]{1,0:T(8,128)(2,1)S(1)} collective-permute-done((bf16[384,256]{1,0:T(8,128)(2,1)S(1)}, bf16[384,256]{1,0:T(8,128)(2,1)S(1)}, u32[]{:S(2)}, u32[]{:S(2)}) %collective-permute-start.15) | collective-permute-done | bytes 196640 | tf_op jit(solution)/shard_map/ppermute | solution.py:503
  78.2 0.1 collective-permute-done.14
  78.3 3.5 %collective-permute-done.13 = bf16[384,256]{1,0:T(8,128)(2,1)S(1)} collective-permute-done((bf16[384,256]{1,0:T(8,128)(2,1)S(1)}, bf16[384,256]{1,0:T(8,128)(2,1)S(1)}, u32[]{:S(2)}, u32[]{:S(2)}) %collective-permute-start.13) | collective-permute-done | bytes 196640 | tf_op jit(solution)/shard_map/ppermute | solution.py:503
  81.8 0.1 add_convert_fusion.2
  82.0 1.0 collective-permute-start.17
  83.0 3.4 %collective-permute-start.16 = (bf16[96,256]{1,0:T(8,128)(2,1)S(1)}, bf16[96,256]{1,0:T(8,128)(2,1)S(1)}, u32[]{:S(2)}, u32[]{:S(2)}) collective-permute-start(bf16[96,256]{1,0:T(8,128)(2,1)S(1)} %get-tuple-element.45), channel_id=1, source_target_pairs={{0,24},{1,7},{2,26},{3,5},{4,28},{5,3},{6,30},{7,1},{8,16},{9,15},... | collective-permute-start | bytes 147464 | tf_op jit(solution)/shard_map/ppermute | solution.py:503
  86.4 0.6 collective-permute-done.18
  87.0 2.0 %collective-permute-done.16 = bf16[96,256]{1,0:T(8,128)(2,1)S(1)} collective-permute-done((bf16[96,256]{1,0:T(8,128)(2,1)S(1)}, bf16[96,256]{1,0:T(8,128)(2,1)S(1)}, u32[]{:S(2)}, u32[]{:S(2)}) %collective-permute-start.16) | collective-permute-done | bytes 49184 | tf_op jit(solution)/shard_map/ppermute | solution.py:503
  89.0 0.1 collective-permute-start.21
  89.1 3.4 %collective-permute-start.19 = (bf16[96,256]{1,0:T(8,128)(2,1)S(1)}, bf16[96,256]{1,0:T(8,128)(2,1)S(1)}, u32[]{:S(2)}, u32[]{:S(2)}) collective-permute-start(bf16[96,256]{1,0:T(8,128)(2,1)S(1)} %add_convert_fusion.5), channel_id=1, source_target_pairs={{0,24},{1,7},{2,26},{3,5},{4,28},{5,3},{6,30},{7,1},{8,16},{9,15},... | collective-permute-start | bytes 147464 | tf_op jit(solution)/shard_map/ppermute | solution.py:503
  92.4 0.5 collective-permute-start.20
  92.9 0.2 collective-permute-done.21
  93.1 2.0 %collective-permute-done.19 = bf16[96,256]{1,0:T(8,128)(2,1)S(1)} collective-permute-done((bf16[96,256]{1,0:T(8,128)(2,1)S(1)}, bf16[96,256]{1,0:T(8,128)(2,1)S(1)}, u32[]{:S(2)}, u32[]{:S(2)}) %collective-permute-start.19) | collective-permute-done | bytes 49184 | tf_op jit(solution)/shard_map/ppermute | solution.py:503
  95.1 2.4 %collective-permute-done.20 = bf16[96,256]{1,0:T(8,128)(2,1)S(1)} collective-permute-done((bf16[96,256]{1,0:T(8,128)(2,1)S(1)}, bf16[96,256]{1,0:T(8,128)(2,1)S(1)}, u32[]{:S(2)}, u32[]{:S(2)}) %collective-permute-start.20) | collective-permute-done | bytes 49184 | tf_op jit(solution)/shard_map/ppermute | solution.py:503
  97.7 0.1 collective-permute-start.22
  97.8 2.1 %collective-permute-start.9 = (bf16[8,80,128]{2,1,0:T(8,128)(2,1)S(1)}, bf16[8,80,128]{2,1,0:T(8,128)(2,1)S(1)}, u32[]{:S(2)}, u32[]{:S(2)}) collective-permute-start(bf16[8,80,128]{2,1,0:T(8,128)(2,1)S(1)} %get-tuple-element.20), channel_id=1, source_target_pairs={{0,31},{4,3},{8,7},{12,11},{16,15},{20,19},{24,23},{28,27},{3,4},{... | collective-permute-start | bytes 491528 | tf_op jit(solution)/shard_map/ppermute | solution.py:637
  99.8 1.3 collective-permute-start.23
  101.1 7.1 %collective-permute-done.9 = bf16[8,80,128]{2,1,0:T(8,128)(2,1)S(1)} collective-permute-done((bf16[8,80,128]{2,1,0:T(8,128)(2,1)S(1)}, bf16[8,80,128]{2,1,0:T(8,128)(2,1)S(1)}, u32[]{:S(2)}, u32[]{:S(2)}) %collective-permute-start.9) | collective-permute-done | bytes 163872 | tf_op jit(solution)/shard_map/ppermute | solution.py:637
  108.2 1.3 collective-permute-start.10
  109.7 6.5 %collective-permute-done.24 = bf16[384,256]{1,0:T(8,128)(2,1)S(1)} collective-permute-done((bf16[384,256]{1,0:T(8,128)(2,1)S(1)}, bf16[384,256]{1,0:T(8,128)(2,1)S(1)}, u32[]{:S(2)}, u32[]{:S(2)}) %collective-permute-start.24) | collective-permute-done | bytes 196640 | tf_op jit(solution)/shard_map/ppermute | solution.py:503
  116.4 0.5 collective-permute-start.11
  117.0 2.3 %collective-permute-done.11.theirs = bf16[24,80,128]{2,1,0:T(8,128)(2,1)S(1)} collective-permute-done((bf16[24,80,128]{2,1,0:T(8,128)(2,1)S(1)}, bf16[24,80,128]{2,1,0:T(8,128)(2,1)S(1)}, u32[]{:S(2)}, u32[]{:S(2)}) %collective-permute-start.11) | collective-permute-done | bytes 491552 | tf_op jit(solution)/shard_map/ppermute | solution.py:480
  119.3 5.4 %shard_map.116 = bf16[2560,128]{1,0:T(8,128)(2,1)} custom-call(s32[1]{0:T(128)} %bitcast.place, s32[49]{0:T(128)S(1)} %copy-done.5, bf16[8,80,128]{2,1,0:T(8,128)(2,1)S(1)} %get-tuple-element.19.own, bf16[8,80,128]{2,1,0:T(8,128)(2,1)S(1)} %collective-permute-done.8.partner, bf16[8,80,128]{2,1,0:T(8,128)(2,1)S(1)} %broadcast_select_fusion.edge, ...), custom_call_target="tpu_custom_call" | custom-call | flops 150994944 | bytes 4587520 | tf_op jit(solution)/shard_map/pallas_call | solution.py:698
  124.6 6.5 %shard_map.115 = f32[3584,128]{1,0:T(8,128)} custom-call(s32[1]{0:T(128)} %bitcast.place, s32[49]{0:T(128)S(1)} %copy-done.5, bf16[8,80,128]{2,1,0:T(8,128)(2,1)S(1)} %get-tuple-element.19.own, bf16[8,80,128]{2,1,0:T(8,128)(2,1)S(1)} %collective-permute-done.8.partner, bf16[8,80,128]{2,1,0:T(8,128)(2,1)S(1)} %broadcast_select_fusion.edge, ...), custom_call_target="tpu_custom_call" | custom-call | flops 150994944 | bytes 9175040 | tf_op jit(solution)/shard_map/pallas_call | solution.py:706
  131.1 1.9 %shard_map.117 = (f32[2304,256]{1,0:T(8,128)}, f32[720,256]{1,0:T(8,128)}) custom-call(s32[1]{0:T(128)} %bitcast.place, bf16[1536,256]{1,0:T(8,128)(2,1)S(1)} %constant_dynamic-update-slice_fusion.value, bf16[1536,256]{1,0:T(8,128)(2,1)S(1)} %collective-permute-done.25.other), custom_call_target="tpu_custom_call" | custom-call | flops 1 | bytes 4718592 | tf_op jit(solution)/shard_map/pallas_call | solution.py:717
  (61 shorter events, 0.9 us)
Async XLA Ops:
  0.6 12.5 %copy-start.3 = (bf16[8,512,256]{2,1,0:T(8,128)(2,1)S(1)}, bf16[8,512,256]{2,1,0:T(8,128)(2,1)}, u32[]{:S(2)}) copy-start(bf16[8,512,256]{2,1,0:T(8,128)(2,1)} %upstream.3) | copy-start | bytes 6291460
  12.5 8.2 %collective-permute-start = (bf16[24,80,128]{2,1,0:T(8,128)(2,1)}, bf16[24,80,128]{2,1,0:T(8,128)(2,1)S(1)}, u32[]{:S(2)}, u32[]{:S(2)}) collective-permute-start(bf16[24,80,128]{2,1,0:T(8,128)(2,1)} %get-tuple-element.18), channel_id=1, source_target_pairs={{0,1},{1,0},{2,3},{3,2},{4,5},{5,4},{6,7},{7,6},{8,9},{9,8},{10,11... | collective-permute-start | bytes 1474568 | tf_op jit(solution)/shard_map/ppermute | solution.py:480
  13.1 8.5 %copy-start.12 = (bf16[24,80,128]{2,1,0:T(8,128)(2,1)S(1)}, bf16[24,80,128]{2,1,0:T(8,128)(2,1)}, u32[]{:S(2)}) copy-start(bf16[24,80,128]{2,1,0:T(8,128)(2,1)} %get-tuple-element.17) | copy-start | bytes 1474564
  14.1 13.2 %copy-start.6 = (bf16[3,3,256,256]{3,2,1,0:T(8,128)(2,1)S(1)}, bf16[3,3,256,256]{3,2,1,0:T(8,128)(2,1)}, u32[]{:S(2)}) copy-start(bf16[3,3,256,256]{3,2,1,0:T(8,128)(2,1)} %weight.3) | copy-start | bytes 3538948
  14.1 30.9 %collective-permute-start.6 = (bf16[2,512,256]{2,1,0:T(8,128)(2,1)}, bf16[2,512,256]{2,1,0:T(8,128)(2,1)S(1)}, u32[]{:S(2)}, u32[]{:S(2)}) collective-permute-start(bf16[2,512,256]{2,1,0:T(8,128)(2,1)} %get-tuple-element.37), channel_id=1, source_target_pairs={{0,1},{1,0},{2,3},{3,2},{4,5},{5,4},{6,7},{7,6},{8,9},{9,8},{10,11... | collective-permute-start | bytes 1572872 | tf_op jit(solution)/shard_map/ppermute | solution.py:556
  14.2 30.8 %collective-permute-start.7 = (bf16[2,512,256]{2,1,0:T(8,128)(2,1)}, bf16[2,512,256]{2,1,0:T(8,128)(2,1)}, u32[]{:S(2)}, u32[]{:S(2)}) collective-permute-start(bf16[2,512,256]{2,1,0:T(8,128)(2,1)} %get-tuple-element.36), channel_id=1, source_target_pairs={{0,31},{1,2},{2,1},{3,4},{4,3},{5,6},{6,5},{7,8},{8,7},{9,10},{10,... | collective-permute-start | bytes 1572872 | tf_op jit(solution)/shard_map/ppermute | solution.py:555
  20.8 0.8 copy-start.13
  22.8 11.4 %collective-permute-start.2 = (bf16[8,80,128]{2,1,0:T(8,128)(2,1)S(1)}, bf16[8,80,128]{2,1,0:T(8,128)(2,1)}, u32[]{:S(2)}, u32[]{:S(2)}) collective-permute-start(bf16[8,80,128]{2,1,0:T(8,128)(2,1)S(1)} %get-tuple-element.43), channel_id=1, source_target_pairs={{1,3},{2,0},{5,7},{6,4},{9,11},{10,8},{13,15},{14,12},{17,19},{18,... | collective-permute-start | bytes 491528 | tf_op jit(solution)/shard_map/ppermute | solution.py:615
  24.1 11.4 %collective-permute-start.1 = (bf16[8,80,128]{2,1,0:T(8,128)(2,1)S(1)}, bf16[8,80,128]{2,1,0:T(8,128)(2,1)}, u32[]{:S(2)}, u32[]{:S(2)}) collective-permute-start(bf16[8,80,128]{2,1,0:T(8,128)(2,1)S(1)} %get-tuple-element.44), channel_id=1, source_target_pairs={{0,2},{1,3},{2,0},{3,1},{4,6},{5,7},{6,4},{7,5},{8,10},{9,11},{10,... | collective-permute-start | bytes 491528 | tf_op jit(solution)/shard_map/ppermute | solution.py:480
  33.0 1.1 copy-start.10
  36.6 14.2 %collective-permute-start.3 = (bf16[2,80,128]{2,1,0:T(8,128)(2,1)S(1)}, bf16[2,80,128]{2,1,0:T(8,128)(2,1)S(1)}, u32[]{:S(2)}, u32[]{:S(2)}) collective-permute-start(bf16[2,80,128]{2,1,0:T(8,128)(2,1)S(1)} %get-tuple-element.51), channel_id=1, source_target_pairs={{0,1},{1,0},{2,3},{3,2},{4,5},{5,4},{6,7},{7,6},{8,9},{9,8},{10,11... | collective-permute-start | bytes 122888 | tf_op jit(solution)/shard_map/ppermute | solution.py:641
  36.7 14.1 %collective-permute-start.4 = (bf16[10,80,128]{2,1,0:T(8,128)(2,1)S(1)}, bf16[10,80,128]{2,1,0:T(8,128)(2,1)S(1)}, u32[]{:S(2)}, u32[]{:S(2)}) collective-permute-start(bf16[10,80,128]{2,1,0:T(8,128)(2,1)S(1)} %maximum_select_fusion), channel_id=1, source_target_pairs={{0,31},{1,2},{2,1},{3,4},{4,3},{5,6},{6,5},{7,8},{8,7},{9,10},{10,... | collective-permute-start | bytes 614408 | tf_op jit(solution)/shard_map/ppermute | solution.py:639
  41.6 9.1 %copy-start.9 = (s32[8,112]{1,0:T(8,128)S(1)}, s32[8,112]{1,0:T(8,128)}, u32[]{:S(2)}) copy-start(s32[8,112]{1,0:T(8,128)} %ranges.1) | copy-start | bytes 10756
  41.7 9.1 %collective-permute-start.5 = (bf16[2,80,128]{2,1,0:T(8,128)(2,1)S(1)}, bf16[2,80,128]{2,1,0:T(8,128)(2,1)S(1)}, u32[]{:S(2)}, u32[]{:S(2)}) collective-permute-start(bf16[2,80,128]{2,1,0:T(8,128)(2,1)S(1)} %slice_select_fusion), channel_id=1, source_target_pairs={{0,30},{4,2},{8,6},{12,10},{16,14},{20,18},{24,22},{28,26},{3,5},{... | collective-permute-start | bytes 122888 | tf_op jit(solution)/shard_map/ppermute | solution.py:637
  45.0 1.3 copy-start.7
  46.3 4.5 %copy-start.8 = (bf16[3,3,80,256]{3,2,1,0:T(8,128)(2,1)S(1)}, bf16[3,3,80,256]{3,2,1,0:T(8,128)(2,1)}, u32[]{:S(2)}) copy-start(bf16[3,3,80,256]{3,2,1,0:T(8,128)(2,1)} %param.13) | copy-start | bytes 1105924
  46.3 4.5 %copy-start.11 = (bf16[6,256,512]{2,1,0:T(8,128)(2,1)S(1)}, bf16[6,256,512]{2,1,0:T(8,128)(2,1)}, u32[]{:S(2)}) copy-start(bf16[6,256,512]{2,1,0:T(8,128)(2,1)} %copy-done.10) | copy-start | bytes 4718596
  69.6 2.6 %collective-permute-start.12 = (bf16[1536,256]{1,0:T(8,128)(2,1)}, bf16[1536,256]{1,0:T(8,128)(2,1)S(1)}, u32[]{:S(2)}, u32[]{:S(2)}) collective-permute-start(bf16[1536,256]{1,0:T(8,128)(2,1)} %get-tuple-element.25), channel_id=1, source_target_pairs={{0,1},{1,0},{2,3},{3,2},{4,5},{5,4},{6,7},{7,6},{8,9},{9,8},{10,11... | collective-permute-start | bytes 2359304 | tf_op jit(solution)/shard_map/ppermute | solution.py:480
  72.5 5.7 %collective-permute-start.15 = (bf16[384,256]{1,0:T(8,128)(2,1)S(1)}, bf16[384,256]{1,0:T(8,128)(2,1)S(1)}, u32[]{:S(2)}, u32[]{:S(2)}) collective-permute-start(bf16[384,256]{1,0:T(8,128)(2,1)S(1)} %get-tuple-element.39), channel_id=1, source_target_pairs={{0,4},{1,17},{2,6},{3,19},{4,0},{5,21},{6,2},{7,23},{8,12},{9,25},... | collective-permute-start | bytes 589832 | tf_op jit(solution)/shard_map/ppermute | solution.py:503
  72.5 5.7 %collective-permute-start.14 = (bf16[384,256]{1,0:T(8,128)(2,1)S(1)}, bf16[384,256]{1,0:T(8,128)(2,1)S(1)}, u32[]{:S(2)}, u32[]{:S(2)}) collective-permute-start(bf16[384,256]{1,0:T(8,128)(2,1)S(1)} %get-tuple-element.40), channel_id=1, source_target_pairs={{0,2},{1,9},{2,0},{3,11},{4,6},{5,13},{6,4},{7,15},{8,10},{9,1},{1... | collective-permute-start | bytes 589832 | tf_op jit(solution)/shard_map/ppermute | solution.py:503
  72.6 9.1 %collective-permute-start.13 = (bf16[384,256]{1,0:T(8,128)(2,1)S(1)}, bf16[384,256]{1,0:T(8,128)(2,1)S(1)}, u32[]{:S(2)}, u32[]{:S(2)}) collective-permute-start(bf16[384,256]{1,0:T(8,128)(2,1)S(1)} %get-tuple-element.38), channel_id=1, source_target_pairs={{0,6},{1,25},{2,4},{3,27},{4,2},{5,29},{6,0},{7,31},{8,14},{9,17},... | collective-permute-start | bytes 589832 | tf_op jit(solution)/shard_map/ppermute | solution.py:503
  81.9 5.1 %collective-permute-start.18 = (bf16[96,256]{1,0:T(8,128)(2,1)S(1)}, bf16[96,256]{1,0:T(8,128)(2,1)S(1)}, u32[]{:S(2)}, u32[]{:S(2)}) collective-permute-start(bf16[96,256]{1,0:T(8,128)(2,1)S(1)} %get-tuple-element.46), channel_id=1, source_target_pairs={{0,16},{1,5},{2,18},{3,7},{4,20},{5,1},{6,22},{7,3},{8,24},{9,13},... | collective-permute-start | bytes 147464 | tf_op jit(solution)/shard_map/ppermute | solution.py:503
  82.0 5.0 %collective-permute-start.17 = (bf16[96,256]{1,0:T(8,128)(2,1)S(1)}, bf16[96,256]{1,0:T(8,128)(2,1)S(1)}, u32[]{:S(2)}, u32[]{:S(2)}) collective-permute-start(bf16[96,256]{1,0:T(8,128)(2,1)S(1)} %get-tuple-element.47), channel_id=1, source_target_pairs={{0,8},{1,3},{2,10},{3,1},{4,12},{5,7},{6,14},{7,5},{8,0},{9,11},{1... | collective-permute-start | bytes 147464 | tf_op jit(solution)/shard_map/ppermute | solution.py:503
  83.0 6.0 %collective-permute-start.16 = (bf16[96,256]{1,0:T(8,128)(2,1)S(1)}, bf16[96,256]{1,0:T(8,128)(2,1)S(1)}, u32[]{:S(2)}, u32[]{:S(2)}) collective-permute-start(bf16[96,256]{1,0:T(8,128)(2,1)S(1)} %get-tuple-element.45), channel_id=1, source_target_pairs={{0,24},{1,7},{2,26},{3,5},{4,28},{5,3},{6,30},{7,1},{8,16},{9,15},... | collective-permute-start | bytes 147464 | tf_op jit(solution)/shard_map/ppermute | solution.py:503
  89.0 4.2 %collective-permute-start.21 = (bf16[96,256]{1,0:T(8,128)(2,1)S(1)}, bf16[96,256]{1,0:T(8,128)(2,1)S(1)}, u32[]{:S(2)}, u32[]{:S(2)}) collective-permute-start(bf16[96,256]{1,0:T(8,128)(2,1)S(1)} %add_convert_fusion.5), channel_id=1, source_target_pairs={{0,8},{1,3},{2,10},{3,1},{4,12},{5,7},{6,14},{7,5},{8,0},{9,11},{1... | collective-permute-start | bytes 147464 | tf_op jit(solution)/shard_map/ppermute | solution.py:503
  89.1 6.1 %collective-permute-start.19 = (bf16[96,256]{1,0:T(8,128)(2,1)S(1)}, bf16[96,256]{1,0:T(8,128)(2,1)S(1)}, u32[]{:S(2)}, u32[]{:S(2)}) collective-permute-start(bf16[96,256]{1,0:T(8,128)(2,1)S(1)} %add_convert_fusion.5), channel_id=1, source_target_pairs={{0,24},{1,7},{2,26},{3,5},{4,28},{5,3},{6,30},{7,1},{8,16},{9,15},... | collective-permute-start | bytes 147464 | tf_op jit(solution)/shard_map/ppermute | solution.py:503
  92.4 5.1 %collective-permute-start.20 = (bf16[96,256]{1,0:T(8,128)(2,1)S(1)}, bf16[96,256]{1,0:T(8,128)(2,1)S(1)}, u32[]{:S(2)}, u32[]{:S(2)}) collective-permute-start(bf16[96,256]{1,0:T(8,128)(2,1)S(1)} %add_convert_fusion.5), channel_id=1, source_target_pairs={{0,16},{1,5},{2,18},{3,7},{4,20},{5,1},{6,22},{7,3},{8,24},{9,13},... | collective-permute-start | bytes 147464 | tf_op jit(solution)/shard_map/ppermute | solution.py:503
  97.7 21.6 %copy-start.1 = (bf16[4128,128]{1,0:T(8,128)(2,1)S(1)}, bf16[4128,128]{1,0:T(8,128)(2,1)}, u32[]{:S(2)}) copy-start(bf16[4128,128]{1,0:T(8,128)(2,1)} %get-tuple-element.23.probs_t) | copy-start | bytes 3170308
  97.7 21.6 %copy-start.5 = (s32[49]{0:T(128)S(1)}, s32[49]{0:T(128)}, u32[]{:S(2)}) copy-start(s32[49]{0:T(128)} %get-tuple-element.16.begins) | copy-start | bytes 592
  97.7 11.9 %collective-permute-start.22 = (bf16[384,256]{1,0:T(8,128)(2,1)S(1)}, bf16[384,256]{1,0:T(8,128)(2,1)S(1)}, u32[]{:S(2)}, u32[]{:S(2)}) collective-permute-start(bf16[384,256]{1,0:T(8,128)(2,1)S(1)} %pad_maximum_fusion.1), channel_id=1, source_target_pairs={{0,2},{1,9},{2,0},{3,11},{4,6},{5,13},{6,4},{7,15},{8,10},{9,1},{1... | collective-permute-start | bytes 589832 | tf_op jit(solution)/shard_map/ppermute | solution.py:503
  97.8 10.5 %collective-permute-start.9 = (bf16[8,80,128]{2,1,0:T(8,128)(2,1)S(1)}, bf16[8,80,128]{2,1,0:T(8,128)(2,1)S(1)}, u32[]{:S(2)}, u32[]{:S(2)}) collective-permute-start(bf16[8,80,128]{2,1,0:T(8,128)(2,1)S(1)} %get-tuple-element.20), channel_id=1, source_target_pairs={{0,31},{4,3},{8,7},{12,11},{16,15},{20,19},{24,23},{28,27},{3,4},{... | collective-permute-start | bytes 491528 | tf_op jit(solution)/shard_map/ppermute | solution.py:637
  99.8 9.8 %collective-permute-start.23 = (bf16[384,256]{1,0:T(8,128)(2,1)S(1)}, bf16[384,256]{1,0:T(8,128)(2,1)S(1)}, u32[]{:S(2)}, u32[]{:S(2)}) collective-permute-start(bf16[384,256]{1,0:T(8,128)(2,1)S(1)} %pad_maximum_fusion.1), channel_id=1, source_target_pairs={{0,4},{1,17},{2,6},{3,19},{4,0},{5,21},{6,2},{7,23},{8,12},{9,25},... | collective-permute-start | bytes 589832 | tf_op jit(solution)/shard_map/ppermute | solution.py:503
  101.1 15.2 %collective-permute-start.8 = (bf16[8,80,128]{2,1,0:T(8,128)(2,1)S(1)}, bf16[8,80,128]{2,1,0:T(8,128)(2,1)S(1)}, u32[]{:S(2)}, u32[]{:S(2)}) collective-permute-start(bf16[8,80,128]{2,1,0:T(8,128)(2,1)S(1)} %get-tuple-element.19.own), channel_id=1, source_target_pairs={{0,2},{1,3},{2,0},{3,1},{4,6},{5,7},{6,4},{7,5},{8,10},{9,11},{10,... | collective-permute-start | bytes 491528 | tf_op jit(solution)/shard_map/ppermute | solution.py:480
  108.2 8.0 %collective-permute-start.10 = (bf16[8,80,128]{2,1,0:T(8,128)(2,1)S(1)}, bf16[8,80,128]{2,1,0:T(8,128)(2,1)S(1)}, u32[]{:S(2)}, u32[]{:S(2)}) collective-permute-start(bf16[8,80,128]{2,1,0:T(8,128)(2,1)S(1)} %collective-permute-done.9), channel_id=1, source_target_pairs={{3,1},{0,2},{7,5},{4,6},{11,9},{8,10},{15,13},{12,14},{19,17},{16,... | collective-permute-start | bytes 491528 | tf_op jit(solution)/shard_map/ppermute | solution.py:688
  109.5 6.6 %collective-permute-start.24 = (bf16[384,256]{1,0:T(8,128)(2,1)S(1)}, bf16[384,256]{1,0:T(8,128)(2,1)S(1)}, u32[]{:S(2)}, u32[]{:S(2)}) collective-permute-start(bf16[384,256]{1,0:T(8,128)(2,1)S(1)} %pad_maximum_fusion.1), channel_id=1, source_target_pairs={{0,6},{1,25},{2,4},{3,27},{4,2},{5,29},{6,0},{7,31},{8,14},{9,17},... | collective-permute-start | bytes 589832 | tf_op jit(solution)/shard_map/ppermute | solution.py:503
  116.2 14.9 %collective-permute-start.25 = (bf16[1536,256]{1,0:T(8,128)(2,1)S(1)}, bf16[1536,256]{1,0:T(8,128)(2,1)S(1)}, u32[]{:S(2)}, u32[]{:S(2)}) collective-permute-start(bf16[1536,256]{1,0:T(8,128)(2,1)S(1)} %constant_dynamic-update-slice_fusion.value), channel_id=1, source_target_pairs={{0,1},{1,0},{2,3},{3,2},{4,5},{5,4},{6,7},{7,6},{8,9},{9,8},{10,11... | collective-permute-start | bytes 2359304 | tf_op jit(solution)/shard_map/ppermute | solution.py:480
  116.3 8.3 %copy-start.2 = (bf16[4128,128]{1,0:T(8,128)(2,1)S(1)}, bf16[4128,128]{1,0:T(8,128)(2,1)}, u32[]{:S(2)}) copy-start(bf16[4128,128]{1,0:T(8,128)(2,1)} %get-tuple-element.22.context_t) | copy-start | bytes 3170308
  116.4 8.2 %copy-start = (f32[3584,128]{1,0:T(8,128)S(1)}, f32[3584,128]{1,0:T(8,128)}, u32[]{:S(2)}) copy-start(f32[3584,128]{1,0:T(8,128)} %get-tuple-element.21.probs) | copy-start | bytes 5505028
  116.4 8.2 %copy-start.4 = (s32[1,32,128]{2,1,0:T(8,128)S(1)}, s32[1,32,128]{2,1,0:T(8,128)}, u32[]{:S(2)}) copy-start(s32[1,32,128]{2,1,0:T(8,128)} %param.10) | copy-start | bytes 49156
  116.4 2.8 %collective-permute-start.11 = (bf16[24,80,128]{2,1,0:T(8,128)(2,1)S(1)}, bf16[24,80,128]{2,1,0:T(8,128)(2,1)S(1)}, u32[]{:S(2)}, u32[]{:S(2)}) collective-permute-start(bf16[24,80,128]{2,1,0:T(8,128)(2,1)S(1)} %pad_maximum_fusion), channel_id=1, source_target_pairs={{0,1},{1,0},{2,3},{3,2},{4,5},{5,4},{6,7},{7,6},{8,9},{9,8},{10,11... | collective-permute-start | bytes 1474568 | tf_op jit(solution)/shard_map/ppermute | solution.py:480

commit v3 on v2

--- a/solution.py
+++ b/solution.py
@@ -47,8 +47,6 @@
     sent,
     begins,
     probs,
-    probs_t,
-    context_t,
     wide_p,
     wide_c,
     plain_c,
@@ -64,15 +62,6 @@
     band, camera = position % bands, position // bands
     seen = 2 * half
     begins[seen] = columns
-
-    def mark(step, _):
-        column = columns - 1 - step
-        cell = az_map[camera, column] - camera * sight + sight // 4
-        cell = jnp.where(cell < 0, cell + around, cell)
-        begins[jnp.where(cell >= around, cell - around, cell)] = column
-        return 0
-
-    lax.fori_loop(0, columns, mark, 0, unroll=8)
     scores = logits[...].reshape(bins, rows, columns)
     powers = jnp.exp(scores - jnp.max(scores, axis=0, keepdims=True))
     shares = powers / jnp.sum(powers, axis=0, keepdims=True)
@@ -80,32 +69,35 @@
     copies = [pltpu.make_async_copy(probs, probs_out, done.at[0])]
     copies[0].start()
     plain_c[...] = context[...].astype(F32)
+    one = lax.broadcasted_iota(jnp.int32, (columns, columns), 0)
+    same = (one == lax.broadcasted_iota(jnp.int32, (columns, columns), 1)).astype(F32)
+    same = same.astype(BF16)
 
     def turn(row, _):
+        for k in range(columns // rows):
+            column = columns - 1 - row * (columns // rows) - k
+            cell = az_map[camera, column] - camera * sight + sight // 4
+            cell = jnp.where(cell < 0, cell + around, cell)
+            begins[jnp.where(cell >= around, cell - around, cell)] = column
         block = padded_rows(probs[pl.ds(row, bins, stride=rows), :], LANES)
         wide_p[pl.ds(row, columns, stride=rows), :] = jnp.transpose(block)
-        block = padded_rows(plain_c[pl.ds(row, channels, stride=rows), :], LANES)
-        wide_c[pl.ds(row, columns, stride=rows), :] = jnp.transpose(block)
-        return 0
-
-    lax.fori_loop(0, rows, turn, 0, unroll=4)
-    for wide, narrow, out in (
-        (wide_p, probs_t, probs_t_out),
-        (wide_c, context_t, context_t_out),
-    ):
-        narrow[0 : columns * rows, :] = wide[...].astype(BF16)
-        narrow[columns * rows :, :] = jnp.zeros((rows, LANES), BF16)
-        copies.append(pltpu.make_async_copy(narrow, out, done.at[len(copies)]))
+        block = padded_rows(plain_c[pl.ds(row, channels, stride=rows), :].astype(BF16), LANES)
+        wide_c[pl.ds(row, columns, stride=rows), :] = product(same, block, 1, 1)
+        return 0
+
+    lax.fori_loop(0, rows, turn, 0, unroll=8)
+    for wide, out in ((wide_p, probs_t_out), (wide_c, context_t_out)):
+        wide[columns * rows :, :] = jnp.zeros((rows, LANES), F32)
+        copies.append(pltpu.make_async_copy(wide, out, done.at[len(copies)]))
         copies[-1].start()
     line = lax.broadcasted_iota(jnp.int32, (TAPS * rows, LANES), 0)
 
     def cell_sum(cell):
         start = begins[cell]
         span = pl.ds(pl.multiple_of(start * rows, rows), TAPS * rows)
-        features = context_t[span, :]
         width = (begins[cell + 1] - start) * rows
-        features = jnp.where(line < width, features, jnp.zeros_like(features))
-        return product(features, probs_t[span, :], 0, 0)[:channels].astype(BF16)
+        features = jnp.where(line < width, wide_c[span, :], 0.0).astype(BF16)
+        return product(features, wide_p[span, :].astype(BF16), 0, 0)[:channels].astype(BF16)
 
     near = band + 1 - 2 * (band % 2)
     for group, (mine, theirs) in enumerate(
@@ -179,7 +171,6 @@
     edge,
     near_halo,
     far_halo,
-    two,
     ranges,
     weight,
     inner_grad,
@@ -200,6 +191,9 @@
     range_hot,
     picks,
     grads,
+    act_grads,
+    sums_a,
+    sums_b,
 ):
     sector, channels, lanes = own.shape
     hidden, length = outer_grad.shape[1:]
@@ -216,24 +210,24 @@
     @pl.when(mine == 0)
     def _():
         cells[0:2, :, :lanes] = edge[sector - 2 : sector]
-        cells[2 + sector :, :, :lanes] = near_halo[...]
+        cells[2 + sector :, :, :lanes] = near_halo[0:2]
         cells[0 : sector + 2, :, lanes:] = far_halo[...]
 
     @pl.when(mine == 1)
     def _():
-        cells[0:2, :, :lanes] = near_halo[...]
+        cells[0:2, :, :lanes] = near_halo[0:2]
         cells[2 + sector :, :, :lanes] = far_halo[0:2]
-        cells[0:2, :, lanes:] = two[...]
+        cells[0:2, :, lanes:] = near_halo[2:4]
 
     @pl.when(mine == bands - 2)
     def _():
         cells[0:2, :, :lanes] = far_halo[0:2]
-        cells[2 + sector :, :, :lanes] = near_halo[...]
-        cells[2 + sector :, :, lanes:] = two[...]
+        cells[2 + sector :, :, :lanes] = near_halo[0:2]
+        cells[2 + sector :, :, lanes:] = near_halo[2:4]
 
     @pl.when(mine == bands - 1)
     def _():
-        cells[0:2, :, :lanes] = near_halo[...]
+        cells[0:2, :, :lanes] = near_halo[0:2]
         cells[2 + sector :, :, :lanes] = edge[0:2]
         cells[2:, :, lanes:] = far_halo[...]
 
@@ -274,32 +268,62 @@
                 grid_taps[channels : 2 * channels, spread] = value.astype(BF16)
                 grid_taps[2 * channels :, spread] = ahead(value).astype(BF16)
 
-    def one_row(row, act_grad):
+    flipped = jnp.concatenate([weight[TAPS - 1 - i] for i in range(TAPS)], axis=1)
+
+    def convolved(row, into):
         source = pl.ds(pl.multiple_of(row * channels, channels), TAPS * channels)
-        sums = product(weight_t[...], grid_low[source, :], 1, 0)
-        value = behind(sums[:hidden]) + sums[hidden : 2 * hidden] + ahead(sums[2 * hidden :])
+        into[...] = product(weight_t[...], grid_low[source, :], 1, 0)
+
+    def back(row):
+        source = pl.ds(pl.multiple_of(row * hidden, hidden), TAPS * hidden)
+        sums = product(flipped, slope_rows[source, :], 1, 0)
+        value = ahead(sums[:channels]) + sums[channels : 2 * channels]
+        value = value + behind(sums[2 * channels :])
+        grid_grad[pl.ds(pl.multiple_of(row * channels, channels), channels), :] = value.astype(BF16)
+
+    def activated(row, sums):
+        value = behind(sums[:hidden, :]) + sums[hidden : 2 * hidden, :]
+        value = value + ahead(sums[2 * hidden :, :])
         logistic = 0.5 + 0.5 * jnp.tanh(0.5 * value)
         active = value * logistic
-        spread = pl.ds(pl.multiple_of(row * length, length), length)
-        act_taps[0:hidden, spread] = behind(active).astype(BF16)
-        act_taps[hidden : 2 * hidden, spread] = active.astype(BF16)
-        act_taps[2 * hidden :, spread] = ahead(active).astype(BF16)
+        start = pl.multiple_of(row * length, length)
+        spread = pl.ds(start, length)
+        low = active.astype(BF16)
+        act_taps[0:hidden, spread] = pltpu.roll(low, 1, 1)
+        act_taps[hidden : 2 * hidden, spread] = low
+        act_taps[2 * hidden :, spread] = pltpu.roll(low, length - 1, 1)
+        nothing = jnp.zeros((hidden, LANES), BF16)
+        lane = lax.broadcasted_iota(jnp.int32, (hidden, LANES), 1)
+        first = pl.ds(start, LANES)
+        act_taps[0:hidden, first] = jnp.where(lane > 0, act_taps[0:hidden, first], nothing)
+        last = pl.ds(pl.multiple_of(start + length - LANES, LANES), LANES)
+        act_taps[2 * hidden :, last] = jnp.where(
+            lane < LANES - 1, act_taps[2 * hidden :, last], nothing
+        )
         slope = logistic * (1.0 + value * (1.0 - logistic))
-        result = (act_grad.astype(F32) * slope).astype(BF16)
+        result = (act_grads[row].astype(F32) * slope).astype(BF16)
         slope_rows[pl.ds(pl.multiple_of(row * hidden, hidden), hidden), :] = result
         slope_lanes[:, spread] = result
 
-    def outside(pair, _):
-        one_row(pair, outer_grad[pair])
-        one_row(pair + sector, outer_grad[pair + 2])
-        return 0
-
-    def inside(row, _):
-        one_row(row + 2, inner_grad[row])
-        return 0
-
-    lax.fori_loop(0, 2, outside, 0)
-    lax.fori_loop(0, sector - 2, inside, 0, unroll=2)
+    act_grads[0:2] = outer_grad[0:2]
+    act_grads[2:sector] = inner_grad[...]
+    act_grads[sector:] = outer_grad[2:4]
+    rows = sector + 2
+    slope_rows[0 : 3 * hidden, :] = jnp.zeros((3 * hidden, length), BF16)
+
+    def two_rows(pair, _):
+        row = 2 * pair
+        back(jnp.maximum(row - 3, 0))
+        convolved(row + 1, sums_b)
+        activated(row, sums_a)
+        back(jnp.maximum(row - 2, 0))
+        convolved(jnp.minimum(row + 2, rows - 1), sums_a)
+        activated(row + 1, sums_b)
+        return 0
+
+    convolved(0, sums_a)
+    lax.fori_loop(0, rows // 2, two_rows, 0)
+    back(sector - 1)
     count = sector * length
     tall = TAPS * hidden
     short = TAPS * channels
@@ -311,31 +335,16 @@
         return 0
 
     lax.fori_loop(0, TAPS, second, 0)
-    for tap in range(TAPS):
-        result = product(
-            grid_taps[:, tap * length : tap * length + count],
-            slope_lanes[:, length : length + count],
-            1,
-            1,
-        )
-        base = TAPS * tall + tap * short
-        grads[base : base + short, :] = result.astype(BF16)
+    windows = [grid_taps[:, tap * length : tap * length + count] for tap in range(TAPS)]
+    result = product(
+        jnp.concatenate(windows, axis=0), slope_lanes[:, length : length + count], 1, 1
+    )
+    grads[TAPS * tall : TAPS * (tall + short), :] = result.astype(BF16)
     base = TAPS * (tall + short)
     grads[base:, :] = jnp.zeros((grads.shape[0] - base, hidden), BF16)
     half = keep.shape[0]
     keep[...] = grads[pl.ds(pl.multiple_of(core * half, half), half), :]
     send[...] = grads[pl.ds(pl.multiple_of((1 - core) * half, half), half), :]
-    flipped = jnp.concatenate([weight[TAPS - 1 - i] for i in range(TAPS)], axis=1)
-
-    def back(row, _):
-        source = pl.ds(pl.multiple_of(row * hidden, hidden), TAPS * hidden)
-        sums = product(flipped, slope_rows[source, :], 1, 0)
-        value = ahead(sums[:channels]) + sums[channels : 2 * channels]
-        value = value + behind(sums[2 * channels :])
-        grid_grad[pl.ds(pl.multiple_of(row * channels, channels), channels), :] = value.astype(BF16)
-        return 0
-
-    lax.fori_loop(0, sector, back, 0, unroll=2)
     picked = product(grid_grad[...], range_hot[...], 1, 0).astype(BF16)
     own_reply[...] = picked[:, :lanes].reshape(sector, channels, lanes)
     other_reply[...] = picked[:, lanes:].reshape(sector, channels, lanes)
@@ -390,7 +399,8 @@
 
     def one_cell(cell, _):
         span = pl.ds(pl.multiple_of(begins[cell] * rows, rows), TAPS * rows)
-        wide[span, :] = product(context_t[span, :][:, :channels], wedges[cell], 1, 0)
+        features = context_t[span, :][:, :channels].astype(BF16)
+        wide[span, :] = product(features, wedges[cell], 1, 0)
         return 0
 
     lax.fori_loop(0, wedges.shape[0], one_cell, 0, unroll=8)
@@ -433,7 +443,8 @@
 
     def one_cell(cell, _):
         span = pl.ds(pl.multiple_of(begins[cell] * rows, rows), TAPS * rows)
-        wide[span, 0:channels] = product(probs_t[span, :], wedges[cell], 1, 1)
+        shares = probs_t[span, :].astype(BF16)
+        wide[span, 0:channels] = product(shares, wedges[cell], 1, 1)
         return 0
 
     lax.fori_loop(0, wedges.shape[0], one_cell, 0, unroll=8)
@@ -536,7 +547,7 @@
     sector, length, hidden = out_grad.shape
     bins, rows = depth_logits.shape[1:3]
     channels = context.shape[1]
-    if bands != 4 or blocks != 1 << (blocks.bit_length() - 1) or blocks.bit_length() % 2 or bins > LANES or channels > LANES or sector < 6:
+    if bands != 4 or blocks != 1 << (blocks.bit_length() - 1) or blocks.bit_length() % 2 or bins > LANES or channels > LANES or sector < 6 or sector % 2:
         raise ValueError("unsupported sizes")
     band = position % bands
     sight = bands * sector
@@ -548,9 +559,7 @@
     off_chip = [(i, (i + 1 if i & 1 else i - 1) % blocks) for i in range(blocks)]
 
     def ends(value, near):
-        count = value.shape[0]
-        start = jnp.where((core == 0) == near, count - 2, 0)
-        return lax.dynamic_slice_in_dim(value, start, 2, 0)
+        return jnp.where((core == 0) == near, value[-2:], value[:2])
 
     far_grad = lax.ppermute(ends(out_grad, False), "blk", off_chip)
     near_grad = lax.ppermute(ends(out_grad, True), "blk", on_chip)
@@ -561,18 +570,16 @@
         functools.partial(pool_kernel, rows, sight, blocks * sector),
         [
             jax.ShapeDtypeStruct((bins * rows, columns), F32),
-            jax.ShapeDtypeStruct((turned, LANES), BF16),
-            jax.ShapeDtypeStruct((turned, LANES), BF16),
+            jax.ShapeDtypeStruct((turned, LANES), F32),
+            jax.ShapeDtypeStruct((turned, LANES), F32),
             jax.ShapeDtypeStruct((half, channels, LANES), BF16),
             jax.ShapeDtypeStruct((half, channels, LANES), BF16),
             jax.ShapeDtypeStruct((seen + 1,), jnp.int32),
         ],
         [
             pltpu.VMEM((bins * rows, columns), F32),
-            pltpu.VMEM((turned, LANES), BF16),
-            pltpu.VMEM((turned, LANES), BF16),
-            pltpu.VMEM((columns * rows, LANES), F32),
-            pltpu.VMEM((columns * rows, LANES), F32),
+            pltpu.VMEM((turned, LANES), F32),
+            pltpu.VMEM((turned, LANES), F32),
             pltpu.VMEM((channels * rows, columns), F32),
             pltpu.SemaphoreType.DMA((3,)),
         ],
@@ -629,16 +636,17 @@
             jnp.pad(ends(own, False), more),
         ),
     )
-    two = jnp.where(first, edge[:2], edge[sector - 2 :])
-
-    def to_next(value, more):
-        pairs = [(i, (i - 1 - more) % blocks) for i in firsts]
-        pairs = pairs + [(i, (i + 1 + more) % blocks) for i in lasts]
+
+    def to_next(value):
+        pairs = [(i, (i - 1) % blocks) for i in firsts]
+        pairs = pairs + [(i, (i + 1) % blocks) for i in lasts]
         return lax.ppermute(value, "blk", pairs)
 
     far_halo = lax.ppermute(far, "blk", off_chip)
-    two = to_next(two, 1)
-    near_halo = lax.ppermute(ends(own, True), "blk", on_chip)
+    passed = jnp.where(first, far_halo[sector:], far_halo[:2])
+    near_halo = lax.ppermute(
+        jnp.concatenate([ends(own, True), passed], axis=0), "blk", on_chip
+    )
     weight = conv1_weight.reshape(TAPS, TAPS * channels, hidden)
     grad_rows = TAPS * TAPS * (hidden + channels)
     unit = blocks * 16
@@ -664,18 +672,20 @@
             pltpu.VMEM((length, 2 * LANES), BF16),
             pltpu.VMEM((8, 2 * LANES), jnp.int32),
             pltpu.VMEM((grad_rows, hidden), BF16),
+            pltpu.VMEM((wide, hidden, length), BF16),
+            pltpu.VMEM((TAPS * hidden, length), F32),
+            pltpu.VMEM((TAPS * hidden, length), F32),
         ],
-        [smem()] + [vmem()] * 10,
+        [smem()] + [vmem()] * 9,
         row_flops * (sector + 3 * sector // 2),
         20 * sector * length * hidden,
-        limit=32,
+        limit=34,
     )(
         place,
         own,
         edge,
         near_halo,
         far_halo,
-        two,
         rng_map,
         weight,
         inner_grad,
@@ -684,7 +694,7 @@
     )
 
     partner = swapped(own_reply, blocks, 2)
-    edge_reply = to_next(other_reply, 0)
+    edge_reply = to_next(other_reply)
     passed = lax.ppermute(edge_reply, "blk", outward)
     edge_reply = jnp.where(outer, edge_reply, passed)
     theirs = swapped(

time: 133 us -> 132 us (level)
  other arithmetic: 2.83 us -> 6.12 us
  Pallas kernels: 54.5 us -> 52.2 us
  local copies, waits for them, and re-layouts: 4.42 us -> 2.79 us
    ppermute x2 -> x1, starting transfers between devices: 5.4 us -> 1.91 us  [to_next(): return lax.ppermute(value, 'blk', pairs)]
    ppermute x1, starting transfers between devices: 4.94 us -> 1.92 us  [shards(): far_halo = lax.ppermute(far, 'blk', off_chip)]
    ppermute x12, starting transfers between devices: 13.3 us -> 16.1 us  [sent(): return lax.ppermute(part, 'blk', to)]
    ppermute x1, starting transfers between devices: 0.07 us -> 2.41 us  [shards(): lax.ppermute(jnp.concatenate([ends(own, True), passed], axis=0), 'blk', o...]
    ppermute x12, waiting for transfers between devices: 19.4 us -> 17.5 us  [sent(): return lax.ppermute(part, 'blk', to)]
    pallas_call x1, Pallas kernels: 11.9 us -> 10.3 us  [shards(): call(functools.partial(pool_kernel, rows, sight, blocks * sector), [jax.S...]
    ppermute x1, waiting for transfers between devices: 0.01 us -> 1.36 us  [shards(): far_halo = lax.ppermute(far, 'blk', off_chip)]
    unnamed x30 -> x24, local copies, waits for them, and re-layouts: 3.26 us -> 1.94 us
  transfers between devices with their start and end apart: 26 -> 25, of which waited for: 13 -> 14; matrix products, arithmetic and copies ran while one was open for 3% -> 4% of each run, Pallas kernels for 16% -> 17%
where the time goes in v3:
time: 132 us; the launch traced here: 131 us
  Pallas kernels  52.2 us (40%)
  starting transfers between devices  36.4 us (28%)
  waiting for transfers between devices  32.6 us (25%)
  other arithmetic  6.12 us (5%)
  local copies, waits for them, and re-layouts  2.79 us (2%)
    pallas_call x1, Pallas kernels, shards(): call(grid_kernel, [jax.ShapeDtypeStruct((grad_rows // 2, hidden), BF16),...  18.1 us
    ppermute x12, waiting for transfers between devices, sent(): return lax.ppermute(part, 'blk', to)  17.5 us
    ppermute x12, starting transfers between devices, sent(): return lax.ppermute(part, 'blk', to)  16.1 us
    pallas_call x1, Pallas kernels, shards(): call(functools.partial(pool_kernel, rows, sight, blocks * sector), [jax.S...  10.3 us
    ppermute x1, waiting for transfers between devices, to_next(): return lax.ppermute(value, 'blk', pairs)  7.94 us
    pallas_call x1, Pallas kernels, shards(): call(functools.partial(logit_kernel, rows), jax.ShapeDtypeStruct((bins *...  6.5 us
    ppermute x1, starting transfers between devices, shards(): far_grad = lax.ppermute(ends(out_grad, False), 'blk', off_chip)  6.21 us
    ppermute x6, waiting for transfers between devices, swapped(): return lax.ppermute(value, 'blk', [(i, i ^ mask) for i in range(blocks)])  5.83 us
  transfers between devices with their start and end apart: 25, of which 14 were waited for; matrix products, arithmetic and copies ran while one was open for 4% of the time, Pallas kernels for 17%

profile of v3, /device:TPU:0, one launch (start us, length us, event | category | flops | bytes accessed | tf_op | source)
XLA Modules:
  0.0 131.2 jit_solution(14843095878887298879)
XLA Ops:
  0.6 10.3 %shard_map.111 = (f32[3584,128]{1,0:T(8,128)}, f32[4128,128]{1,0:T(8,128)}, f32[4128,128]{1,0:T(8,128)}, bf16[24,80,128]{2,1,0:T(8,128)(2,1)}, bf16[24,80,128]{2,1,0:T(8,128)(2,1)}, /*index=5*/s32[49]{0:T(128)}) custom-call(s32[1]{0:T(128)} %bitcast.place, s32[8,128]{1,0:T(8,128)} %az_map.1, f32[3584,128]{1,0:T(8,128)} %bitcast.13, bf16[2560,128]{1,0:T(8,128)(2,1)} %bitcast.15), custom_call_target="tpu_custom_call" | custom-call | flops 150994944 | bytes 9175040 | tf_op jit(solution)/shard_map/pallas_call | solution.py:569
  11.0 0.6 collective-permute-start
  11.5 1.7 %collective-permute-done = bf16[24,80,128]{2,1,0:T(8,128)(2,1)S(1)} collective-permute-done((bf16[24,80,128]{2,1,0:T(8,128)(2,1)}, bf16[24,80,128]{2,1,0:T(8,128)(2,1)S(1)}, u32[]{:S(2)}, u32[]{:S(2)}) %collective-permute-start) | collective-permute-done | bytes 491552 | tf_op jit(solution)/shard_map/ppermute | solution.py:491
  13.2 1.2 add_convert_fusion.1
  14.4 0.8 fusion
  15.2 2.8 %collective-permute-start.1 = (bf16[8,80,128]{2,1,0:T(8,128)(2,1)}, bf16[8,80,128]{2,1,0:T(8,128)(2,1)}, u32[]{:S(2)}, u32[]{:S(2)}) collective-permute-start(bf16[8,80,128]{2,1,0:T(8,128)(2,1)} %get-tuple-element.44), channel_id=1, source_target_pairs={{0,2},{1,3},{2,0},{3,1},{4,6},{5,7},{6,4},{7,5},{8,10},{9,11},{10,... | collective-permute-start | bytes 491528 | tf_op jit(solution)/shard_map/ppermute | solution.py:491
  18.0 1.4 %collective-permute-start.2 = (bf16[8,80,128]{2,1,0:T(8,128)(2,1)S(1)}, bf16[8,80,128]{2,1,0:T(8,128)(2,1)}, u32[]{:S(2)}, u32[]{:S(2)}) collective-permute-start(bf16[8,80,128]{2,1,0:T(8,128)(2,1)S(1)} %get-tuple-element.43), channel_id=1, source_target_pairs={{1,3},{2,0},{5,7},{6,4},{9,11},{10,8},{13,15},{14,12},{17,19},{18,... | collective-permute-start | bytes 491528 | tf_op jit(solution)/shard_map/ppermute | solution.py:622
  19.4 1.0 broadcast_select_fusion
  20.5 1.2 collective-permute-start.5
  21.7 6.2 %collective-permute-start.6 = (bf16[2,512,256]{2,1,0:T(8,128)(2,1)}, bf16[2,512,256]{2,1,0:T(8,128)(2,1)}, u32[]{:S(2)}, u32[]{:S(2)}) collective-permute-start(bf16[2,512,256]{2,1,0:T(8,128)(2,1)} %get-tuple-element.36), channel_id=1, source_target_pairs={{0,31},{1,2},{2,1},{3,4},{4,3},{5,6},{6,5},{7,8},{8,7},{9,10},{10,... | collective-permute-start | bytes 1572872 | tf_op jit(solution)/shard_map/ppermute | solution.py:564
  27.9 1.2 add_convert_fusion.3
  29.2 1.9 %collective-permute-start.3 = (bf16[10,80,128]{2,1,0:T(8,128)(2,1)S(1)}, bf16[10,80,128]{2,1,0:T(8,128)(2,1)S(1)}, u32[]{:S(2)}, u32[]{:S(2)}) collective-permute-start(bf16[10,80,128]{2,1,0:T(8,128)(2,1)S(1)} %maximum_select_fusion), channel_id=1, source_target_pairs={{0,31},{1,2},{2,1},{3,4},{4,3},{5,6},{6,5},{7,8},{8,7},{9,10},{10,... | collective-permute-start | bytes 614408 | tf_op jit(solution)/shard_map/ppermute | solution.py:645
  31.1 5.7 %shard_map.112.inner_grad = bf16[6,256,512]{2,1,0:T(8,128)(2,1)S(1)} custom-call(bf16[8,512,256]{2,1,0:T(8,128)(2,1)S(1)} %copy-done.3, bf16[3,3,256,256]{3,2,1,0:T(8,128)(2,1)S(1)} %copy-done.7), custom_call_target="tpu_custom_call" | custom-call | flops 3623878656 | bytes 4194304 | tf_op jit(solution)/shard_map/pallas_call | solution.py:600
  36.8 1.4 %collective-permute-done.3.far_halo = bf16[10,80,128]{2,1,0:T(8,128)(2,1)S(1)} collective-permute-done((bf16[10,80,128]{2,1,0:T(8,128)(2,1)S(1)}, bf16[10,80,128]{2,1,0:T(8,128)(2,1)S(1)}, u32[]{:S(2)}, u32[]{:S(2)}) %collective-permute-start.3) | collective-permute-done | bytes 204832 | tf_op jit(solution)/shard_map/ppermute | solution.py:645
  38.2 2.4 %collective-permute-start.4 = (bf16[4,80,128]{2,1,0:T(8,128)(2,1)S(1)}, bf16[4,80,128]{2,1,0:T(8,128)(2,1)S(1)}, u32[]{:S(2)}, u32[]{:S(2)}) collective-permute-start(bf16[4,80,128]{2,1,0:T(8,128)(2,1)S(1)} %pad_maximum_fusion.2), channel_id=1, source_target_pairs={{0,1},{1,0},{2,3},{3,2},{4,5},{5,4},{6,7},{7,6},{8,9},{9,8},{10,11... | collective-permute-start | bytes 245768 | tf_op jit(solution)/shard_map/ppermute | solution.py:647
  40.6 4.5 %shard_map.113.outer_grad = bf16[4,256,512]{2,1,0:T(8,128)(2,1)S(1)} custom-call(s32[1]{0:T(128)} %bitcast.place, bf16[2,512,256]{2,1,0:T(8,128)(2,1)} %collective-permute-done.5.near, bf16[2,512,256]{2,1,0:T(8,128)(2,1)} %collective-permute-done.6.far, bf16[8,512,256]{2,1,0:T(8,128)(2,1)S(1)} %copy-done.3, bf16[3,3,256,256]{3,2,1,0:T(8,128)(2,1)S(1)} %copy-done.7), custom_call_target="tpu_custom_call" | custom-call | flops 2415919104 | bytes 2097152 | tf_op jit(solution)/shard_map/pallas_call | solution.py:608
  45.1 18.1 %shard_map.114 = (bf16[1536,256]{1,0:T(8,128)(2,1)S(1)}, bf16[1536,256]{1,0:T(8,128)(2,1)S(1)}, bf16[8,80,128]{2,1,0:T(8,128)(2,1)S(1)}, bf16[8,80,128]{2,1,0:T(8,128)(2,1)S(1)}) custom-call(s32[1]{0:T(128)} %bitcast.place, bf16[8,80,128]{2,1,0:T(8,128)(2,1)S(1)} %get-tuple-element.42.own, bf16[8,80,128]{2,1,0:T(8,128)(2,1)S(1)} %get-tuple-element.41.edge, ...), custom_call_target="tpu_custom_call" | custom-call | flops 12079595520 | bytes 20971520 | tf_op jit(solution)/shard_map/pallas_call | solution.py:655
  63.4 2.3 %collective-permute-done.11 = bf16[1536,256]{1,0:T(8,128)(2,1)} collective-permute-done((bf16[1536,256]{1,0:T(8,128)(2,1)S(1)}, bf16[1536,256]{1,0:T(8,128)(2,1)}, u32[]{:S(2)}, u32[]{:S(2)}) %collective-permute-start.11) | collective-permute-done | bytes 786464 | tf_op jit(solution)/shard_map/ppermute | solution.py:491
  65.7 1.3 %add_convert_fusion = bf16[1536,256]{1,0:T(8,128)(2,1)S(1)} fusion(bf16[1536,256]{1,0:T(8,128)(2,1)} %collective-permute-done.11, bf16[1536,256]{1,0:T(8,128)(2,1)S(1)} %get-tuple-element.24), kind=kLoop, calls=%fused_computation | loop fusion | flops 1572864 | bytes 2359296 | tf_op jit(solution)/shard_map/convert_element_type | solution.py:487
  67.1 2.7 %collective-permute-start.12 = (bf16[384,256]{1,0:T(8,128)(2,1)S(1)}, bf16[384,256]{1,0:T(8,128)(2,1)S(1)}, u32[]{:S(2)}, u32[]{:S(2)}) collective-permute-start(bf16[384,256]{1,0:T(8,128)(2,1)S(1)} %get-tuple-element.38), channel_id=1, source_target_pairs={{0,6},{1,25},{2,4},{3,27},{4,2},{5,29},{6,0},{7,31},{8,14},{9,17},... | collective-permute-start | bytes 589832 | tf_op jit(solution)/shard_map/ppermute | solution.py:514
  69.7 1.4 %collective-permute-start.13 = (bf16[384,256]{1,0:T(8,128)(2,1)S(1)}, bf16[384,256]{1,0:T(8,128)(2,1)S(1)}, u32[]{:S(2)}, u32[]{:S(2)}) collective-permute-start(bf16[384,256]{1,0:T(8,128)(2,1)S(1)} %get-tuple-element.40), channel_id=1, source_target_pairs={{0,2},{1,9},{2,0},{3,11},{4,6},{5,13},{6,4},{7,15},{8,10},{9,1},{1... | collective-permute-start | bytes 589832 | tf_op jit(solution)/shard_map/ppermute | solution.py:514
  71.1 0.4 collective-permute-start.14
  71.5 2.2 %collective-permute-done.12 = bf16[384,256]{1,0:T(8,128)(2,1)S(1)} collective-permute-done((bf16[384,256]{1,0:T(8,128)(2,1)S(1)}, bf16[384,256]{1,0:T(8,128)(2,1)S(1)}, u32[]{:S(2)}, u32[]{:S(2)}) %collective-permute-start.12) | collective-permute-done | bytes 196640 | tf_op jit(solution)/shard_map/ppermute | solution.py:514
  73.7 3.1 %collective-permute-done.13 = bf16[384,256]{1,0:T(8,128)(2,1)S(1)} collective-permute-done((bf16[384,256]{1,0:T(8,128)(2,1)S(1)}, bf16[384,256]{1,0:T(8,128)(2,1)S(1)}, u32[]{:S(2)}, u32[]{:S(2)}) %collective-permute-start.13) | collective-permute-done | bytes 196640 | tf_op jit(solution)/shard_map/ppermute | solution.py:514
  77.0 3.7 %collective-permute-start.15 = (bf16[96,256]{1,0:T(8,128)(2,1)S(1)}, bf16[96,256]{1,0:T(8,128)(2,1)S(1)}, u32[]{:S(2)}, u32[]{:S(2)}) collective-permute-start(bf16[96,256]{1,0:T(8,128)(2,1)S(1)} %get-tuple-element.45), channel_id=1, source_target_pairs={{0,24},{1,7},{2,26},{3,5},{4,28},{5,3},{6,30},{7,1},{8,16},{9,15},... | collective-permute-start | bytes 147464 | tf_op jit(solution)/shard_map/ppermute | solution.py:514
  80.6 0.8 collective-permute-start.17
  81.4 1.5 %collective-permute-done.15 = bf16[96,256]{1,0:T(8,128)(2,1)S(1)} collective-permute-done((bf16[96,256]{1,0:T(8,128)(2,1)S(1)}, bf16[96,256]{1,0:T(8,128)(2,1)S(1)}, u32[]{:S(2)}, u32[]{:S(2)}) %collective-permute-start.15) | collective-permute-done | bytes 49184 | tf_op jit(solution)/shard_map/ppermute | solution.py:514
  82.9 1.8 %collective-permute-done.16 = bf16[96,256]{1,0:T(8,128)(2,1)S(1)} collective-permute-done((bf16[96,256]{1,0:T(8,128)(2,1)S(1)}, bf16[96,256]{1,0:T(8,128)(2,1)S(1)}, u32[]{:S(2)}, u32[]{:S(2)}) %collective-permute-start.16) | collective-permute-done | bytes 49184 | tf_op jit(solution)/shard_map/ppermute | solution.py:514
  84.7 0.9 collective-permute-done.17
  85.7 1.5 %collective-permute-start.18 = (bf16[96,256]{1,0:T(8,128)(2,1)S(1)}, bf16[96,256]{1,0:T(8,128)(2,1)S(1)}, u32[]{:S(2)}, u32[]{:S(2)}) collective-permute-start(bf16[96,256]{1,0:T(8,128)(2,1)S(1)} %add_convert_fusion.5), channel_id=1, source_target_pairs={{0,24},{1,7},{2,26},{3,5},{4,28},{5,3},{6,30},{7,1},{8,16},{9,15},... | collective-permute-start | bytes 147464 | tf_op jit(solution)/shard_map/ppermute | solution.py:514
  87.2 2.0 %collective-permute-start.19 = (bf16[96,256]{1,0:T(8,128)(2,1)S(1)}, bf16[96,256]{1,0:T(8,128)(2,1)S(1)}, u32[]{:S(2)}, u32[]{:S(2)}) collective-permute-start(bf16[96,256]{1,0:T(8,128)(2,1)S(1)} %add_convert_fusion.5), channel_id=1, source_target_pairs={{0,16},{1,5},{2,18},{3,7},{4,20},{5,1},{6,22},{7,3},{8,24},{9,13},... | collective-permute-start | bytes 147464 | tf_op jit(solution)/shard_map/ppermute | solution.py:514
  89.2 0.9 collective-permute-start.20
  90.1 1.6 %collective-permute-done.18 = bf16[96,256]{1,0:T(8,128)(2,1)S(1)} collective-permute-done((bf16[96,256]{1,0:T(8,128)(2,1)S(1)}, bf16[96,256]{1,0:T(8,128)(2,1)S(1)}, u32[]{:S(2)}, u32[]{:S(2)}) %collective-permute-start.18) | collective-permute-done | bytes 49184 | tf_op jit(solution)/shard_map/ppermute | solution.py:514
  91.7 1.1 collective-permute-done.19
  92.9 0.5 collective-permute-done.20
  93.6 2.4 %collective-permute-start.21 = (bf16[384,256]{1,0:T(8,128)(2,1)S(1)}, bf16[384,256]{1,0:T(8,128)(2,1)}, u32[]{:S(2)}, u32[]{:S(2)}) collective-permute-start(bf16[384,256]{1,0:T(8,128)(2,1)S(1)} %pad_maximum_fusion.1), channel_id=1, source_target_pairs={{0,2},{1,9},{2,0},{3,11},{4,6},{5,13},{6,4},{7,15},{8,10},{9,1},{1... | collective-permute-start | bytes 589832 | tf_op jit(solution)/shard_map/ppermute | solution.py:514
  96.0 1.9 %collective-permute-start.8 = (bf16[8,80,128]{2,1,0:T(8,128)(2,1)S(1)}, bf16[8,80,128]{2,1,0:T(8,128)(2,1)}, u32[]{:S(2)}, u32[]{:S(2)}) collective-permute-start(bf16[8,80,128]{2,1,0:T(8,128)(2,1)S(1)} %get-tuple-element.20), channel_id=1, source_target_pairs={{0,31},{4,3},{8,7},{12,11},{16,15},{20,19},{24,23},{28,27},{3,4},{... | collective-permute-start | bytes 491528 | tf_op jit(solution)/shard_map/ppermute | solution.py:643
  97.9 0.4 collective-permute-start.22
  98.5 7.9 %collective-permute-done.8 = bf16[8,80,128]{2,1,0:T(8,128)(2,1)} collective-permute-done((bf16[8,80,128]{2,1,0:T(8,128)(2,1)S(1)}, bf16[8,80,128]{2,1,0:T(8,128)(2,1)}, u32[]{:S(2)}, u32[]{:S(2)}) %collective-permute-start.8) | collective-permute-done | bytes 163872 | tf_op jit(solution)/shard_map/ppermute | solution.py:643
  106.4 1.3 collective-permute-start.9
  107.8 0.9 constant_dynamic-update-slice_fusion.2
  108.7 0.9 constant_dynamic-update-slice_fusion.1
  109.7 4.6 %collective-permute-done.23 = bf16[384,256]{1,0:T(8,128)(2,1)S(1)} collective-permute-done((bf16[384,256]{1,0:T(8,128)(2,1)S(1)}, bf16[384,256]{1,0:T(8,128)(2,1)S(1)}, u32[]{:S(2)}, u32[]{:S(2)}) %collective-permute-start.23) | collective-permute-done | bytes 196640 | tf_op jit(solution)/shard_map/ppermute | solution.py:514
  114.4 1.0 broadcast_select_fusion.2.edge
  115.6 1.9 %collective-permute-done.10.theirs = bf16[24,80,128]{2,1,0:T(8,128)(2,1)S(1)} collective-permute-done((bf16[24,80,128]{2,1,0:T(8,128)(2,1)S(1)}, bf16[24,80,128]{2,1,0:T(8,128)(2,1)S(1)}, u32[]{:S(2)}, u32[]{:S(2)}) %collective-permute-start.10) | collective-permute-done | bytes 491552 | tf_op jit(solution)/shard_map/ppermute | solution.py:491
  117.4 5.3 %shard_map.116 = bf16[2560,128]{1,0:T(8,128)(2,1)} custom-call(s32[1]{0:T(128)} %bitcast.place, s32[49]{0:T(128)S(1)} %copy-done.6, bf16[8,80,128]{2,1,0:T(8,128)(2,1)S(1)} %get-tuple-element.19.own, bf16[8,80,128]{2,1,0:T(8,128)(2,1)S(1)} %collective-permute-done.7.partner, bf16[8,80,128]{2,1,0:T(8,128)(2,1)S(1)} %broadcast_select_fusion.2.edge, ...), custom_call_target="tpu_custom_call" | custom-call | flops 150994944 | bytes 4587520 | tf_op jit(solution)/shard_map/pallas_call | solution.py:708
  122.8 6.5 %shard_map.115 = f32[3584,128]{1,0:T(8,128)} custom-call(s32[1]{0:T(128)} %bitcast.place, s32[49]{0:T(128)S(1)} %copy-done.6, bf16[8,80,128]{2,1,0:T(8,128)(2,1)S(1)} %get-tuple-element.19.own, bf16[8,80,128]{2,1,0:T(8,128)(2,1)S(1)} %collective-permute-done.7.partner, bf16[8,80,128]{2,1,0:T(8,128)(2,1)S(1)} %broadcast_select_fusion.2.edge, ...), custom_call_target="tpu_custom_call" | custom-call | flops 150994944 | bytes 9175040 | tf_op jit(solution)/shard_map/pallas_call | solution.py:716
  129.3 1.9 %shard_map.117 = (f32[2304,256]{1,0:T(8,128)}, f32[720,256]{1,0:T(8,128)}) custom-call(s32[1]{0:T(128)} %bitcast.place, bf16[1536,256]{1,0:T(8,128)(2,1)S(1)} %constant_dynamic-update-slice_fusion.value, bf16[1536,256]{1,0:T(8,128)(2,1)S(1)} %collective-permute-done.24.other), custom_call_target="tpu_custom_call" | custom-call | flops 1 | bytes 4718592 | tf_op jit(solution)/shard_map/pallas_call | solution.py:727
  (54 shorter events, 1.2 us)
Async XLA Ops:
  0.6 18.8 %copy-start.3 = (bf16[8,512,256]{2,1,0:T(8,128)(2,1)S(1)}, bf16[8,512,256]{2,1,0:T(8,128)(2,1)}, u32[]{:S(2)}) copy-start(bf16[8,512,256]{2,1,0:T(8,128)(2,1)} %upstream.3) | copy-start | bytes 6291460
  11.0 2.3 %collective-permute-start = (bf16[24,80,128]{2,1,0:T(8,128)(2,1)}, bf16[24,80,128]{2,1,0:T(8,128)(2,1)S(1)}, u32[]{:S(2)}, u32[]{:S(2)}) collective-permute-start(bf16[24,80,128]{2,1,0:T(8,128)(2,1)} %get-tuple-element.18), channel_id=1, source_target_pairs={{0,1},{1,0},{2,3},{3,2},{4,5},{5,4},{6,7},{7,6},{8,9},{9,8},{10,11... | collective-permute-start | bytes 1474568 | tf_op jit(solution)/shard_map/ppermute | solution.py:491
  14.4 3.6 %copy-start.10 = (bf16[24,80,128]{2,1,0:T(8,128)(2,1)}, bf16[24,80,128]{2,1,0:T(8,128)(2,1)S(1)}, u32[]{:S(2)}) copy-start(bf16[24,80,128]{2,1,0:T(8,128)(2,1)S(1)} %add_convert_fusion.1) | copy-start | bytes 1474564
  15.2 12.7 %collective-permute-start.1 = (bf16[8,80,128]{2,1,0:T(8,128)(2,1)}, bf16[8,80,128]{2,1,0:T(8,128)(2,1)}, u32[]{:S(2)}, u32[]{:S(2)}) collective-permute-start(bf16[8,80,128]{2,1,0:T(8,128)(2,1)} %get-tuple-element.44), channel_id=1, source_target_pairs={{0,2},{1,3},{2,0},{3,1},{4,6},{5,7},{6,4},{7,5},{8,10},{9,11},{10,... | collective-permute-start | bytes 491528 | tf_op jit(solution)/shard_map/ppermute | solution.py:491
  18.0 13.1 %copy-start.7 = (bf16[3,3,256,256]{3,2,1,0:T(8,128)(2,1)S(1)}, bf16[3,3,256,256]{3,2,1,0:T(8,128)(2,1)}, u32[]{:S(2)}) copy-start(bf16[3,3,256,256]{3,2,1,0:T(8,128)(2,1)} %weight.3) | copy-start | bytes 3538948
  18.0 9.9 %collective-permute-start.2 = (bf16[8,80,128]{2,1,0:T(8,128)(2,1)S(1)}, bf16[8,80,128]{2,1,0:T(8,128)(2,1)}, u32[]{:S(2)}, u32[]{:S(2)}) collective-permute-start(bf16[8,80,128]{2,1,0:T(8,128)(2,1)S(1)} %get-tuple-element.43), channel_id=1, source_target_pairs={{1,3},{2,0},{5,7},{6,4},{9,11},{10,8},{13,15},{14,12},{17,19},{18,... | collective-permute-start | bytes 491528 | tf_op jit(solution)/shard_map/ppermute | solution.py:622
  20.5 20.1 %collective-permute-start.5 = (bf16[2,512,256]{2,1,0:T(8,128)(2,1)}, bf16[2,512,256]{2,1,0:T(8,128)(2,1)}, u32[]{:S(2)}, u32[]{:S(2)}) collective-permute-start(bf16[2,512,256]{2,1,0:T(8,128)(2,1)} %get-tuple-element.37), channel_id=1, source_target_pairs={{0,1},{1,0},{2,3},{3,2},{4,5},{5,4},{6,7},{7,6},{8,9},{9,8},{10,11... | collective-permute-start | bytes 1572872 | tf_op jit(solution)/shard_map/ppermute | solution.py:565
  21.7 19.0 %collective-permute-start.6 = (bf16[2,512,256]{2,1,0:T(8,128)(2,1)}, bf16[2,512,256]{2,1,0:T(8,128)(2,1)}, u32[]{:S(2)}, u32[]{:S(2)}) collective-permute-start(bf16[2,512,256]{2,1,0:T(8,128)(2,1)} %get-tuple-element.36), channel_id=1, source_target_pairs={{0,31},{1,2},{2,1},{3,4},{4,3},{5,6},{6,5},{7,8},{8,7},{9,10},{10,... | collective-permute-start | bytes 1572872 | tf_op jit(solution)/shard_map/ppermute | solution.py:564
  29.2 8.9 %collective-permute-start.3 = (bf16[10,80,128]{2,1,0:T(8,128)(2,1)S(1)}, bf16[10,80,128]{2,1,0:T(8,128)(2,1)S(1)}, u32[]{:S(2)}, u32[]{:S(2)}) collective-permute-start(bf16[10,80,128]{2,1,0:T(8,128)(2,1)S(1)} %maximum_select_fusion), channel_id=1, source_target_pairs={{0,31},{1,2},{2,1},{3,4},{4,3},{5,6},{6,5},{7,8},{8,7},{9,10},{10,... | collective-permute-start | bytes 614408 | tf_op jit(solution)/shard_map/ppermute | solution.py:645
  38.2 6.9 %copy-start.4 = (bf16[8,512,256]{2,1,0:T(8,128)(2,1)S(1)}, bf16[8,512,256]{2,1,0:T(8,128)(2,1)}, u32[]{:S(2)}) copy-start(bf16[8,512,256]{2,1,0:T(8,128)(2,1)} %upstream.3) | copy-start | bytes 6291460
  38.2 6.9 %copy-start.8 = (bf16[3,3,80,256]{3,2,1,0:T(8,128)(2,1)S(1)}, bf16[3,3,80,256]{3,2,1,0:T(8,128)(2,1)}, u32[]{:S(2)}) copy-start(bf16[3,3,80,256]{3,2,1,0:T(8,128)(2,1)} %param.13) | copy-start | bytes 1105924
  38.2 6.9 %copy-start.9 = (s32[8,112]{1,0:T(8,128)S(1)}, s32[8,112]{1,0:T(8,128)}, u32[]{:S(2)}) copy-start(s32[8,112]{1,0:T(8,128)} %ranges.1) | copy-start | bytes 10756
  38.2 6.9 %collective-permute-start.4 = (bf16[4,80,128]{2,1,0:T(8,128)(2,1)S(1)}, bf16[4,80,128]{2,1,0:T(8,128)(2,1)S(1)}, u32[]{:S(2)}, u32[]{:S(2)}) collective-permute-start(bf16[4,80,128]{2,1,0:T(8,128)(2,1)S(1)} %pad_maximum_fusion.2), channel_id=1, source_target_pairs={{0,1},{1,0},{2,3},{3,2},{4,5},{5,4},{6,7},{7,6},{8,9},{9,8},{10,11... | collective-permute-start | bytes 245768 | tf_op jit(solution)/shard_map/ppermute | solution.py:647
  63.2 2.5 %collective-permute-start.11 = (bf16[1536,256]{1,0:T(8,128)(2,1)S(1)}, bf16[1536,256]{1,0:T(8,128)(2,1)}, u32[]{:S(2)}, u32[]{:S(2)}) collective-permute-start(bf16[1536,256]{1,0:T(8,128)(2,1)S(1)} %get-tuple-element.25), channel_id=1, source_target_pairs={{0,1},{1,0},{2,3},{3,2},{4,5},{5,4},{6,7},{7,6},{8,9},{9,8},{10,11... | collective-permute-start | bytes 2359304 | tf_op jit(solution)/shard_map/ppermute | solution.py:491
  67.1 6.6 %collective-permute-start.12 = (bf16[384,256]{1,0:T(8,128)(2,1)S(1)}, bf16[384,256]{1,0:T(8,128)(2,1)S(1)}, u32[]{:S(2)}, u32[]{:S(2)}) collective-permute-start(bf16[384,256]{1,0:T(8,128)(2,1)S(1)} %get-tuple-element.38), channel_id=1, source_target_pairs={{0,6},{1,25},{2,4},{3,27},{4,2},{5,29},{6,0},{7,31},{8,14},{9,17},... | collective-permute-start | bytes 589832 | tf_op jit(solution)/shard_map/ppermute | solution.py:514
  69.7 7.1 %collective-permute-start.13 = (bf16[384,256]{1,0:T(8,128)(2,1)S(1)}, bf16[384,256]{1,0:T(8,128)(2,1)S(1)}, u32[]{:S(2)}, u32[]{:S(2)}) collective-permute-start(bf16[384,256]{1,0:T(8,128)(2,1)S(1)} %get-tuple-element.40), channel_id=1, source_target_pairs={{0,2},{1,9},{2,0},{3,11},{4,6},{5,13},{6,4},{7,15},{8,10},{9,1},{1... | collective-permute-start | bytes 589832 | tf_op jit(solution)/shard_map/ppermute | solution.py:514
  71.1 5.8 %collective-permute-start.14 = (bf16[384,256]{1,0:T(8,128)(2,1)S(1)}, bf16[384,256]{1,0:T(8,128)(2,1)S(1)}, u32[]{:S(2)}, u32[]{:S(2)}) collective-permute-start(bf16[384,256]{1,0:T(8,128)(2,1)S(1)} %get-tuple-element.39), channel_id=1, source_target_pairs={{0,4},{1,17},{2,6},{3,19},{4,0},{5,21},{6,2},{7,23},{8,12},{9,25},... | collective-permute-start | bytes 589832 | tf_op jit(solution)/shard_map/ppermute | solution.py:514
  77.0 6.0 %collective-permute-start.15 = (bf16[96,256]{1,0:T(8,128)(2,1)S(1)}, bf16[96,256]{1,0:T(8,128)(2,1)S(1)}, u32[]{:S(2)}, u32[]{:S(2)}) collective-permute-start(bf16[96,256]{1,0:T(8,128)(2,1)S(1)} %get-tuple-element.45), channel_id=1, source_target_pairs={{0,24},{1,7},{2,26},{3,5},{4,28},{5,3},{6,30},{7,1},{8,16},{9,15},... | collective-permute-start | bytes 147464 | tf_op jit(solution)/shard_map/ppermute | solution.py:514
  80.6 4.1 %collective-permute-start.16 = (bf16[96,256]{1,0:T(8,128)(2,1)S(1)}, bf16[96,256]{1,0:T(8,128)(2,1)S(1)}, u32[]{:S(2)}, u32[]{:S(2)}) collective-permute-start(bf16[96,256]{1,0:T(8,128)(2,1)S(1)} %get-tuple-element.47), channel_id=1, source_target_pairs={{0,8},{1,3},{2,10},{3,1},{4,12},{5,7},{6,14},{7,5},{8,0},{9,11},{1... | collective-permute-start | bytes 147464 | tf_op jit(solution)/shard_map/ppermute | solution.py:514
  80.6 5.0 %collective-permute-start.17 = (bf16[96,256]{1,0:T(8,128)(2,1)S(1)}, bf16[96,256]{1,0:T(8,128)(2,1)S(1)}, u32[]{:S(2)}, u32[]{:S(2)}) collective-permute-start(bf16[96,256]{1,0:T(8,128)(2,1)S(1)} %get-tuple-element.46), channel_id=1, source_target_pairs={{0,16},{1,5},{2,18},{3,7},{4,20},{5,1},{6,22},{7,3},{8,24},{9,13},... | collective-permute-start | bytes 147464 | tf_op jit(solution)/shard_map/ppermute | solution.py:514
  85.7 6.1 %collective-permute-start.18 = (bf16[96,256]{1,0:T(8,128)(2,1)S(1)}, bf16[96,256]{1,0:T(8,128)(2,1)S(1)}, u32[]{:S(2)}, u32[]{:S(2)}) collective-permute-start(bf16[96,256]{1,0:T(8,128)(2,1)S(1)} %add_convert_fusion.5), channel_id=1, source_target_pairs={{0,24},{1,7},{2,26},{3,5},{4,28},{5,3},{6,30},{7,1},{8,16},{9,15},... | collective-permute-start | bytes 147464 | tf_op jit(solution)/shard_map/ppermute | solution.py:514
  87.2 5.7 %collective-permute-start.19 = (bf16[96,256]{1,0:T(8,128)(2,1)S(1)}, bf16[96,256]{1,0:T(8,128)(2,1)S(1)}, u32[]{:S(2)}, u32[]{:S(2)}) collective-permute-start(bf16[96,256]{1,0:T(8,128)(2,1)S(1)} %add_convert_fusion.5), channel_id=1, source_target_pairs={{0,16},{1,5},{2,18},{3,7},{4,20},{5,1},{6,22},{7,3},{8,24},{9,13},... | collective-permute-start | bytes 147464 | tf_op jit(solution)/shard_map/ppermute | solution.py:514
  89.2 4.2 %collective-permute-start.20 = (bf16[96,256]{1,0:T(8,128)(2,1)S(1)}, bf16[96,256]{1,0:T(8,128)(2,1)S(1)}, u32[]{:S(2)}, u32[]{:S(2)}) collective-permute-start(bf16[96,256]{1,0:T(8,128)(2,1)S(1)} %add_convert_fusion.5), channel_id=1, source_target_pairs={{0,8},{1,3},{2,10},{3,1},{4,12},{5,7},{6,14},{7,5},{8,0},{9,11},{1... | collective-permute-start | bytes 147464 | tf_op jit(solution)/shard_map/ppermute | solution.py:514
  93.5 23.9 %copy-start = (f32[4128,128]{1,0:T(8,128)S(1)}, f32[4128,128]{1,0:T(8,128)}, u32[]{:S(2)}) copy-start(f32[4128,128]{1,0:T(8,128)} %get-tuple-element.23.probs_t) | copy-start | bytes 6340612
  93.5 23.9 %copy-start.6 = (s32[49]{0:T(128)S(1)}, s32[49]{0:T(128)}, u32[]{:S(2)}) copy-start(s32[49]{0:T(128)} %get-tuple-element.16.begins) | copy-start | bytes 592
  93.6 14.2 %collective-permute-start.21 = (bf16[384,256]{1,0:T(8,128)(2,1)S(1)}, bf16[384,256]{1,0:T(8,128)(2,1)}, u32[]{:S(2)}, u32[]{:S(2)}) collective-permute-start(bf16[384,256]{1,0:T(8,128)(2,1)S(1)} %pad_maximum_fusion.1), channel_id=1, source_target_pairs={{0,2},{1,9},{2,0},{3,11},{4,6},{5,13},{6,4},{7,15},{8,10},{9,1},{1... | collective-permute-start | bytes 589832 | tf_op jit(solution)/shard_map/ppermute | solution.py:514
  96.0 10.4 %collective-permute-start.8 = (bf16[8,80,128]{2,1,0:T(8,128)(2,1)S(1)}, bf16[8,80,128]{2,1,0:T(8,128)(2,1)}, u32[]{:S(2)}, u32[]{:S(2)}) collective-permute-start(bf16[8,80,128]{2,1,0:T(8,128)(2,1)S(1)} %get-tuple-element.20), channel_id=1, source_target_pairs={{0,31},{4,3},{8,7},{12,11},{16,15},{20,19},{24,23},{28,27},{3,4},{... | collective-permute-start | bytes 491528 | tf_op jit(solution)/shard_map/ppermute | solution.py:643
  97.9 10.8 %collective-permute-start.22 = (bf16[384,256]{1,0:T(8,128)(2,1)S(1)}, bf16[384,256]{1,0:T(8,128)(2,1)}, u32[]{:S(2)}, u32[]{:S(2)}) collective-permute-start(bf16[384,256]{1,0:T(8,128)(2,1)S(1)} %pad_maximum_fusion.1), channel_id=1, source_target_pairs={{0,4},{1,17},{2,6},{3,19},{4,0},{5,21},{6,2},{7,23},{8,12},{9,25},... | collective-permute-start | bytes 589832 | tf_op jit(solution)/shard_map/ppermute | solution.py:514
  98.3 17.1 %collective-permute-start.7 = (bf16[8,80,128]{2,1,0:T(8,128)(2,1)S(1)}, bf16[8,80,128]{2,1,0:T(8,128)(2,1)S(1)}, u32[]{:S(2)}, u32[]{:S(2)}) collective-permute-start(bf16[8,80,128]{2,1,0:T(8,128)(2,1)S(1)} %get-tuple-element.19.own), channel_id=1, source_target_pairs={{0,2},{1,3},{2,0},{3,1},{4,6},{5,7},{6,4},{7,5},{8,10},{9,11},{10,... | collective-permute-start | bytes 491528 | tf_op jit(solution)/shard_map/ppermute | solution.py:491
  106.4 8.0 %collective-permute-start.9 = (bf16[8,80,128]{2,1,0:T(8,128)(2,1)}, bf16[8,80,128]{2,1,0:T(8,128)(2,1)S(1)}, u32[]{:S(2)}, u32[]{:S(2)}) collective-permute-start(bf16[8,80,128]{2,1,0:T(8,128)(2,1)} %collective-permute-done.8), channel_id=1, source_target_pairs={{3,1},{0,2},{7,5},{4,6},{11,9},{8,10},{15,13},{12,14},{19,17},{16,... | collective-permute-start | bytes 491528 | tf_op jit(solution)/shard_map/ppermute | solution.py:698
  107.7 6.6 %collective-permute-start.23 = (bf16[384,256]{1,0:T(8,128)(2,1)S(1)}, bf16[384,256]{1,0:T(8,128)(2,1)S(1)}, u32[]{:S(2)}, u32[]{:S(2)}) collective-permute-start(bf16[384,256]{1,0:T(8,128)(2,1)S(1)} %pad_maximum_fusion.1), channel_id=1, source_target_pairs={{0,6},{1,25},{2,4},{3,27},{4,2},{5,29},{6,0},{7,31},{8,14},{9,17},... | collective-permute-start | bytes 589832 | tf_op jit(solution)/shard_map/ppermute | solution.py:514
  114.3 14.9 %collective-permute-start.24 = (bf16[1536,256]{1,0:T(8,128)(2,1)S(1)}, bf16[1536,256]{1,0:T(8,128)(2,1)S(1)}, u32[]{:S(2)}, u32[]{:S(2)}) collective-permute-start(bf16[1536,256]{1,0:T(8,128)(2,1)S(1)} %constant_dynamic-update-slice_fusion.value), channel_id=1, source_target_pairs={{0,1},{1,0},{2,3},{3,2},{4,5},{5,4},{6,7},{7,6},{8,9},{9,8},{10,11... | collective-permute-start | bytes 2359304 | tf_op jit(solution)/shard_map/ppermute | solution.py:491
  115.4 7.4 %copy-start.2 = (f32[3584,128]{1,0:T(8,128)S(1)}, f32[3584,128]{1,0:T(8,128)}, u32[]{:S(2)}) copy-start(f32[3584,128]{1,0:T(8,128)} %get-tuple-element.21.probs) | copy-start | bytes 5505028
  115.5 1.9 %collective-permute-start.10 = (bf16[24,80,128]{2,1,0:T(8,128)(2,1)S(1)}, bf16[24,80,128]{2,1,0:T(8,128)(2,1)S(1)}, u32[]{:S(2)}, u32[]{:S(2)}) collective-permute-start(bf16[24,80,128]{2,1,0:T(8,128)(2,1)S(1)} %pad_maximum_fusion), channel_id=1, source_target_pairs={{0,1},{1,0},{2,3},{3,2},{4,5},{5,4},{6,7},{7,6},{8,9},{9,8},{10,11... | collective-permute-start | bytes 1474568 | tf_op jit(solution)/shard_map/ppermute | solution.py:491
  117.4 5.4 %copy-start.1 = (f32[4128,128]{1,0:T(8,128)S(1)}, f32[4128,128]{1,0:T(8,128)}, u32[]{:S(2)}) copy-start(f32[4128,128]{1,0:T(8,128)} %get-tuple-element.22.context_t) | copy-start | bytes 6340612
  117.4 5.4 %copy-start.5 = (s32[1,32,128]{2,1,0:T(8,128)S(1)}, s32[1,32,128]{2,1,0:T(8,128)}, u32[]{:S(2)}) copy-start(s32[1,32,128]{2,1,0:T(8,128)} %param.10) | copy-start | bytes 49156

commit v4 on v3

--- a/solution.py
+++ b/solution.py
@@ -10,6 +10,7 @@
 DEPTH_WEIGHT = 3.0
 TAPS = 3
 LANES = 128
+SLACK = 8
 F32 = jnp.float32
 BF16 = jnp.bfloat16
 
@@ -47,9 +48,10 @@
     sent,
     begins,
     probs,
+    apart_p,
+    apart_c,
     wide_p,
     wide_c,
-    plain_c,
     done,
 ):
     columns = logits.shape[1]
@@ -68,7 +70,12 @@
     probs[...] = shares.reshape(bins * rows, columns)
     copies = [pltpu.make_async_copy(probs, probs_out, done.at[0])]
     copies[0].start()
-    plain_c[...] = context[...].astype(F32)
+    pitch = rows + SLACK
+    for level in range(bins):
+        apart_p[level * pitch : level * pitch + rows, :] = shares[level]
+    for level in range(channels):
+        features = context[level * rows : (level + 1) * rows, :]
+        apart_c[level * pitch : level * pitch + rows, :] = features.astype(F32)
     one = lax.broadcasted_iota(jnp.int32, (columns, columns), 0)
     same = (one == lax.broadcasted_iota(jnp.int32, (columns, columns), 1)).astype(F32)
     same = same.astype(BF16)
@@ -79,25 +86,28 @@
             cell = az_map[camera, column] - camera * sight + sight // 4
             cell = jnp.where(cell < 0, cell + around, cell)
             begins[jnp.where(cell >= around, cell - around, cell)] = column
-        block = padded_rows(probs[pl.ds(row, bins, stride=rows), :], LANES)
-        wide_p[pl.ds(row, columns, stride=rows), :] = jnp.transpose(block)
-        block = padded_rows(plain_c[pl.ds(row, channels, stride=rows), :].astype(BF16), LANES)
-        wide_c[pl.ds(row, columns, stride=rows), :] = product(same, block, 1, 1)
+        block = padded_rows(apart_p[pl.ds(row, bins, stride=pitch), :], LANES)
+        wide_p[pl.ds(row, columns, stride=pitch), :] = jnp.transpose(block)
+        block = padded_rows(apart_c[pl.ds(row, channels, stride=pitch), :].astype(BF16), LANES)
+        wide_c[pl.ds(row, columns, stride=pitch), :] = product(same, block, 1, 1)
         return 0
 
     lax.fori_loop(0, rows, turn, 0, unroll=8)
     for wide, out in ((wide_p, probs_t_out), (wide_c, context_t_out)):
-        wide[columns * rows :, :] = jnp.zeros((rows, LANES), F32)
-        copies.append(pltpu.make_async_copy(wide, out, done.at[len(copies)]))
+        wide[columns * pitch :, :] = jnp.zeros((pitch, LANES), F32)
+        source = wide.reshape(columns + 1, pitch, LANES).at[:, 0:rows, :]
+        copies.append(pltpu.make_async_copy(source, out, done.at[len(copies)]))
         copies[-1].start()
     line = lax.broadcasted_iota(jnp.int32, (TAPS * rows, LANES), 0)
 
     def cell_sum(cell):
         start = begins[cell]
-        span = pl.ds(pl.multiple_of(start * rows, rows), TAPS * rows)
+        spans = [pl.ds(pl.multiple_of((start + k) * pitch, 8), rows) for k in range(TAPS)]
+        features = jnp.concatenate([wide_c[span, :] for span in spans], axis=0)
+        shares = jnp.concatenate([wide_p[span, :] for span in spans], axis=0)
         width = (begins[cell + 1] - start) * rows
-        features = jnp.where(line < width, wide_c[span, :], 0.0).astype(BF16)
-        return product(features, wide_p[span, :].astype(BF16), 0, 0)[:channels].astype(BF16)
+        features = jnp.where(line < width, features, 0.0).astype(BF16)
+        return product(features, shares.astype(BF16), 0, 0)[:channels].astype(BF16)
 
     near = band + 1 - 2 * (band % 2)
     for group, (mine, theirs) in enumerate(
@@ -142,8 +152,42 @@
     lax.fori_loop(0, out.shape[0], step, 0)
 
 
-def outer_acts_kernel(place, near, far, upstream, weight, out, low, high):
-    sector = upstream.shape[0]
+def outer_acts_kernel(
+    place,
+    near,
+    far,
+    upstream,
+    weight,
+    inner,
+    first_weight,
+    ranges,
+    out,
+    weight_t,
+    range_hot,
+    low,
+    high,
+    picks,
+):
+    sector, length, hidden = upstream.shape
+    bands = 4
+    cameras, bins = ranges.shape
+    channels = first_weight.shape[1] // TAPS
+    lanes = range_hot.shape[1] // 2
+    mine, camera = place[0] % bands, place[0] // bands
+    other = jnp.where(mine < bands // 2, camera + cameras - 1, camera + 1) % cameras
+    picks[...] = jnp.full(picks.shape, -1, jnp.int32)
+    picks[0:1, 0:bins] = ranges[pl.ds(camera, 1), :]
+    picks[0:1, lanes : lanes + bins] = ranges[pl.ds(other, 1), :]
+    spots = lax.broadcasted_iota(jnp.int32, (length, 2 * lanes), 0)
+    range_hot[...] = (spots == picks[0:1, :]).astype(F32).astype(BF16)
+    for column in range(TAPS):
+        for row in range(TAPS):
+            weight_t[column * hidden : (column + 1) * hidden, row * channels : (row + 1) * channels] = (
+                jnp.transpose(
+                    first_weight[row, column * channels : (column + 1) * channels, :].astype(F32)
+                ).astype(BF16)
+            )
+    out[2:sector] = inner[...]
     low[2:4] = upstream[0:2]
     high[0:2] = upstream[sector - 2 :]
 
@@ -159,7 +203,7 @@
 
     def step(row, _):
         act_row(act_taps_of(weight), low, row, out, row)
-        act_row(act_taps_of(weight), high, row, out, row + 2)
+        act_row(act_taps_of(weight), high, row, out, row + sector)
         return 0
 
     lax.fori_loop(0, 2, step, 0)
@@ -171,10 +215,10 @@
     edge,
     near_halo,
     far_halo,
-    ranges,
     weight,
-    inner_grad,
-    outer_grad,
+    weight_t,
+    range_hot,
+    act_grads,
     upstream,
     keep,
     send,
@@ -187,22 +231,15 @@
     slope_rows,
     slope_lanes,
     grid_grad,
-    weight_t,
-    range_hot,
-    picks,
     grads,
-    act_grads,
     sums_a,
     sums_b,
 ):
     sector, channels, lanes = own.shape
-    hidden, length = outer_grad.shape[1:]
+    hidden, length = act_grads.shape[1:]
     bands = 4
-    cameras, bins = ranges.shape
     position = place[0]
     mine, core = position % bands, position % 2
-    camera = position // bands
-    other = jnp.where(mine < bands // 2, camera + cameras - 1, camera + 1) % cameras
     wide = sector + 4
     cells[2 : 2 + sector, :, :lanes] = own[...]
     cells[:, :, lanes:] = jnp.zeros((wide, channels, lanes), BF16)
@@ -230,19 +267,6 @@
         cells[0:2, :, :lanes] = near_halo[0:2]
         cells[2 + sector :, :, :lanes] = edge[0:2]
         cells[2:, :, lanes:] = far_halo[...]
-
-    picks[...] = jnp.full(picks.shape, -1, jnp.int32)
-    picks[0:1, 0:bins] = ranges[pl.ds(camera, 1), :]
-    picks[0:1, lanes : lanes + bins] = ranges[pl.ds(other, 1), :]
-    spots = lax.broadcasted_iota(jnp.int32, (length, 2 * lanes), 0)
-    range_hot[...] = (spots == picks[0:1, :]).astype(F32).astype(BF16)
-    for column in range(TAPS):
-        for row in range(TAPS):
-            weight_t[column * hidden : (column + 1) * hidden, row * channels : (row + 1) * channels] = (
-                jnp.transpose(
-                    weight[row, column * channels : (column + 1) * channels, :].astype(F32)
-                ).astype(BF16)
-            )
 
     def behind(value):
         turned = pltpu.roll(value, 1, 1)
@@ -305,9 +329,6 @@
         slope_rows[pl.ds(pl.multiple_of(row * hidden, hidden), hidden), :] = result
         slope_lanes[:, spread] = result
 
-    act_grads[0:2] = outer_grad[0:2]
-    act_grads[2:sector] = inner_grad[...]
-    act_grads[sector:] = outer_grad[2:4]
     rows = sector + 2
     slope_rows[0 : 3 * hidden, :] = jnp.zeros((3 * hidden, length), BF16)
 
@@ -391,35 +412,45 @@
     logit_grad,
     wedges,
     wide,
+    apart,
 ):
     columns = probs.shape[1]
     bins = probs.shape[0] // rows
     sector, channels, _ = own.shape
     lay_out(place, sector, (own, partner, edge), theirs, wedges)
 
+    pitch = rows + SLACK
+
     def one_cell(cell, _):
-        span = pl.ds(pl.multiple_of(begins[cell] * rows, rows), TAPS * rows)
-        features = context_t[span, :][:, :channels].astype(BF16)
-        wide[span, :] = product(features, wedges[cell], 1, 0)
+        start = begins[cell]
+        features = context_t[pl.ds(start, TAPS)].reshape(TAPS * rows, LANES)
+        result = product(features[:, :channels].astype(BF16), wedges[cell], 1, 0)
+        for k in range(TAPS):
+            span = pl.ds(pl.multiple_of((start + k) * pitch, 8), rows)
+            wide[span, :] = result[k * rows : (k + 1) * rows]
         return 0
 
     lax.fori_loop(0, wedges.shape[0], one_cell, 0, unroll=8)
 
     def turn(row, _):
-        block = jnp.transpose(wide[pl.ds(row, columns, stride=rows), :])
-        logit_grad[pl.ds(row, bins, stride=rows), :] = block[:bins]
+        block = jnp.transpose(wide[pl.ds(row, columns, stride=pitch), :])
+        apart[pl.ds(row, bins, stride=pitch), :] = block[:bins]
         return 0
 
-    lax.fori_loop(0, rows, turn, 0, unroll=4)
-    share = probs[...].reshape(bins, rows, columns)
-    slope = logit_grad[...].reshape(bins, rows, columns)
-    expected = jnp.sum(share * slope, axis=0, keepdims=True)
-    target = lidar[...][None]
+    lax.fori_loop(0, rows, turn, 0, unroll=8)
+    sums = [jnp.zeros((rows, columns), F32) for _ in range(4)]
+    for level in range(bins):
+        share = probs[level * rows : (level + 1) * rows, :]
+        sums[level % 4] += share * apart[level * pitch : level * pitch + rows, :]
+    expected = (sums[0] + sums[1]) + (sums[2] + sums[3])
+    target = lidar[...]
     seen = jnp.where(target >= 0, DEPTH_WEIGHT, 0.0)
-    level = lax.broadcasted_iota(jnp.int32, share.shape, 0)
-    hit = jnp.where(level == target, DEPTH_WEIGHT, 0.0)
-    result = share * (slope - expected) + (seen * share - hit)
-    logit_grad[...] = result.reshape(bins * rows, columns)
+    for level in range(bins):
+        share = probs[level * rows : (level + 1) * rows, :]
+        slope = apart[level * pitch : level * pitch + rows, :]
+        hit = jnp.where(target == level, DEPTH_WEIGHT, 0.0)
+        result = share * (slope - expected) + (seen * share - hit)
+        logit_grad[level * rows : (level + 1) * rows, :] = result
 
 
 def context_kernel(
@@ -434,28 +465,37 @@
     context_grad,
     wedges,
     wide,
-    plain,
+    apart,
 ):
     columns = context_grad.shape[1]
     sector, channels, _ = own.shape
     lay_out(place, sector, (own, partner, edge), theirs, wedges)
-    wide[...] = jnp.zeros_like(wide)
+
+    pitch = rows + SLACK
 
     def one_cell(cell, _):
-        span = pl.ds(pl.multiple_of(begins[cell] * rows, rows), TAPS * rows)
-        shares = probs_t[span, :].astype(BF16)
-        wide[span, 0:channels] = product(shares, wedges[cell], 1, 1)
+        start = begins[cell]
+        shares = probs_t[pl.ds(start, TAPS)].reshape(TAPS * rows, LANES)
+        result = product(shares.astype(BF16), wedges[cell], 1, 1)
+        for k in range(TAPS):
+            span = pl.ds(pl.multiple_of((start + k) * pitch, 8), rows)
+            wide[span, 0:channels] = result[k * rows : (k + 1) * rows]
         return 0
 
     lax.fori_loop(0, wedges.shape[0], one_cell, 0, unroll=8)
+    one = lax.broadcasted_iota(jnp.int32, (channels, channels), 0)
+    same = (one == lax.broadcasted_iota(jnp.int32, (channels, channels), 1)).astype(F32)
+    same = same.astype(BF16)
 
     def turn(row, _):
-        block = jnp.transpose(wide[pl.ds(row, columns, stride=rows), :])
-        plain[pl.ds(row, channels, stride=rows), :] = block[:channels]
+        block = wide[pl.ds(row, columns, stride=pitch), :][:, :channels].astype(BF16)
+        apart[pl.ds(row, channels, stride=pitch), :] = product(same, block, 1, 1)
         return 0
 
-    lax.fori_loop(0, rows, turn, 0, unroll=4)
-    context_grad[...] = plain[...].astype(BF16)
+    lax.fori_loop(0, rows, turn, 0, unroll=8)
+    for level in range(channels):
+        block = apart[level * pitch : level * pitch + rows, :]
+        context_grad[level * rows : (level + 1) * rows, :] = block.astype(BF16)
 
 
 def vmem():
@@ -564,23 +604,24 @@
     far_grad = lax.ppermute(ends(out_grad, False), "blk", off_chip)
     near_grad = lax.ppermute(ends(out_grad, True), "blk", on_chip)
 
-    turned = (columns + 1) * rows
+    turned = (columns + 1) * (rows + SLACK)
     half = 3 * sector
     probs, probs_t, context_t, kept, sent, begins = call(
         functools.partial(pool_kernel, rows, sight, blocks * sector),
         [
             jax.ShapeDtypeStruct((bins * rows, columns), F32),
-            jax.ShapeDtypeStruct((turned, LANES), F32),
-            jax.ShapeDtypeStruct((turned, LANES), F32),
+            jax.ShapeDtypeStruct((columns + 1, rows, LANES), F32),
+            jax.ShapeDtypeStruct((columns + 1, rows, LANES), F32),
             jax.ShapeDtypeStruct((half, channels, LANES), BF16),
             jax.ShapeDtypeStruct((half, channels, LANES), BF16),
             jax.ShapeDtypeStruct((seen + 1,), jnp.int32),
         ],
         [
             pltpu.VMEM((bins * rows, columns), F32),
+            pltpu.VMEM((bins * (rows + SLACK), columns), F32),
+            pltpu.VMEM((channels * (rows + SLACK), columns), F32),
             pltpu.VMEM((turned, LANES), F32),
             pltpu.VMEM((turned, LANES), F32),
-            pltpu.VMEM((channels * rows, columns), F32),
             pltpu.SemaphoreType.DMA((3,)),
         ],
         [smem(), smem(), vmem(), vmem()],
@@ -605,14 +646,19 @@
         row_flops * (sector - 2),
         4 * sector * length * hidden,
     )(out_grad, conv2_weight)
-    outer_grad = call(
+    weight = conv1_weight.reshape(TAPS, TAPS * channels, hidden)
+    act_grads, weight_t, range_hot = call(
         outer_acts_kernel,
-        jax.ShapeDtypeStruct((4, hidden, length), BF16),
-        [pltpu.VMEM((4, length, hidden), BF16)] * 2,
-        [smem()] + [vmem()] * 4,
+        [
+            jax.ShapeDtypeStruct((sector + 2, hidden, length), BF16),
+            jax.ShapeDtypeStruct((TAPS * hidden, TAPS * channels), BF16),
+            jax.ShapeDtypeStruct((length, 2 * LANES), BF16),
+        ],
+        [pltpu.VMEM((4, length, hidden), BF16)] * 2 + [pltpu.VMEM((8, 2 * LANES), jnp.int32)],
+        [smem()] + [vmem()] * 7,
         row_flops * 4,
         16 * length * hidden,
-    )(place, near_grad, far_grad, out_grad, conv2_weight)
+    )(place, near_grad, far_grad, out_grad, conv2_weight, inner_grad, weight, rng_map)
 
     summed = rounded_sum(kept, swapped(sent, blocks, 1))
     own = rounded_sum(summed[:sector], swapped(summed[sector : 2 * sector], blocks, 2))
@@ -647,7 +693,6 @@
     near_halo = lax.ppermute(
         jnp.concatenate([ends(own, True), passed], axis=0), "blk", on_chip
     )
-    weight = conv1_weight.reshape(TAPS, TAPS * channels, hidden)
     grad_rows = TAPS * TAPS * (hidden + channels)
     unit = blocks * 16
     grad_rows = -(-grad_rows // unit) * unit
@@ -668,28 +713,24 @@
             pltpu.VMEM((wide * hidden, length), BF16),
             pltpu.VMEM((hidden, wide * length), BF16),
             pltpu.VMEM((sector * channels, length), BF16),
-            pltpu.VMEM((TAPS * hidden, TAPS * channels), BF16),
-            pltpu.VMEM((length, 2 * LANES), BF16),
-            pltpu.VMEM((8, 2 * LANES), jnp.int32),
             pltpu.VMEM((grad_rows, hidden), BF16),
-            pltpu.VMEM((wide, hidden, length), BF16),
             pltpu.VMEM((TAPS * hidden, length), F32),
             pltpu.VMEM((TAPS * hidden, length), F32),
         ],
         [smem()] + [vmem()] * 9,
         row_flops * (sector + 3 * sector // 2),
         20 * sector * length * hidden,
-        limit=34,
+        limit=32,
     )(
         place,
         own,
         edge,
         near_halo,
         far_halo,
-        rng_map,
         weight,
-        inner_grad,
-        outer_grad,
+        weight_t,
+        range_hot,
+        act_grads,
         out_grad.reshape(sector * length, hidden),
     )
 
@@ -708,7 +749,7 @@
     context_grad = call(
         functools.partial(context_kernel, rows),
         jax.ShapeDtypeStruct((channels * rows, columns), BF16),
-        scratch + [pltpu.VMEM((channels * rows, columns), F32)],
+        scratch + [pltpu.VMEM((channels * (rows + SLACK), columns), F32)],
         [smem()] * 2 + [vmem()] * 5,
         cell_flops,
         10 * bins * rows * columns,
@@ -716,7 +757,7 @@
     logit_grad = call(
         functools.partial(logit_kernel, rows),
         jax.ShapeDtypeStruct((bins * rows, columns), F32),
-        scratch,
+        scratch + [pltpu.VMEM((bins * (rows + SLACK), columns), F32)],
         [smem()] * 2 + [vmem()] * 7,
         cell_flops,
         20 * bins * rows * columns,

time: 132 us -> 125 us (0.947)
  Pallas kernels: 52.2 us -> 45.9 us
  starting transfers between devices: 36.4 us -> 38.8 us
  waiting for transfers between devices: 32.6 us -> 31.2 us
    pallas_call x1, Pallas kernels: 10.3 us -> 7.03 us  [shards(): call(functools.partial(pool_kernel, rows, sight, blocks * sector), [jax.S...]
    ppermute x1, starting transfers between devices: 1.92 us -> 5.04 us  [shards(): far_halo = lax.ppermute(far, 'blk', off_chip)]
    pallas_call x1, Pallas kernels: 6.5 us -> 4.47 us  [shards(): call(functools.partial(logit_kernel, rows), jax.ShapeDtypeStruct((bins *...]
    ppermute x1, waiting for transfers between devices: 1.36 us -> 0.01 us  [shards(): far_halo = lax.ppermute(far, 'blk', off_chip)]
  transfers between devices with their start and end apart: 25 -> 25, of which waited for: 14 -> 12; matrix products, arithmetic and copies ran while one was open for 4% -> 4% of each run, Pallas kernels for 17% -> 16%
where the time goes in v4:
time: 125 us
  Pallas kernels  45.9 us (37%)
  starting transfers between devices  38.8 us (31%)
  waiting for transfers between devices  31.2 us (25%)
  other arithmetic  4.99 us (4%)
  local copies, waits for them, and re-layouts  2.79 us (2%)
    ppermute x12, waiting for transfers between devices, sent(): return lax.ppermute(part, 'blk', to)  18.3 us
    pallas_call x1, Pallas kernels, shards(): call(grid_kernel, [jax.ShapeDtypeStruct((grad_rows // 2, hidden), BF16),...  17.5 us
    ppermute x12, starting transfers between devices, sent(): return lax.ppermute(part, 'blk', to)  16 us
    pallas_call x1, Pallas kernels, shards(): call(functools.partial(pool_kernel, rows, sight, blocks * sector), [jax.S...  7.03 us
    ppermute x1, waiting for transfers between devices, to_next(): return lax.ppermute(value, 'blk', pairs)  7 us
    ppermute x1, starting transfers between devices, shards(): far_grad = lax.ppermute(ends(out_grad, False), 'blk', off_chip)  5.82 us
    ppermute x6, waiting for transfers between devices, swapped(): return lax.ppermute(value, 'blk', [(i, i ^ mask) for i in range(blocks)])  5.8 us
    pallas_call x1, Pallas kernels, shards(): call(inner_acts_kernel, jax.ShapeDtypeStruct((sector - 2, hidden, length)...  5.66 us
  transfers between devices with their start and end apart: 25, of which 12 were waited for; matrix products, arithmetic and copies ran while one was open for 4% of the time, Pallas kernels for 16%

profile of v4, /device:TPU:0, one launch (start us, length us, event | category | flops | bytes accessed | tf_op | source)
XLA Modules:
  0.0 124.7 jit_solution(15633960252151184041)
XLA Ops:
  0.6 7.0 %shard_map.111 = (f32[3584,128]{1,0:T(8,128)}, f32[129,32,128]{2,1,0:T(8,128)}, f32[129,32,128]{2,1,0:T(8,128)}, bf16[24,80,128]{2,1,0:T(8,128)(2,1)}, bf16[24,80,128]{2,1,0:T(8,128)(2,1)}, /*index=5*/s32[49]{0:T(128)}) custom-call(s32[1]{0:T(128)} %bitcast.place, s32[8,128]{1,0:T(8,128)} %az_map.1, f32[3584,128]{1,0:T(8,128)} %bitcast.14, ...), custom_call_target="tpu_custom_call" | custom-call | flops 150994944 | bytes 9175040 | tf_op jit(solution)/shard_map/pallas_call | solution.py:609
  7.7 0.6 collective-permute-start
  8.2 1.7 %collective-permute-done = bf16[24,80,128]{2,1,0:T(8,128)(2,1)S(1)} collective-permute-done((bf16[24,80,128]{2,1,0:T(8,128)(2,1)}, bf16[24,80,128]{2,1,0:T(8,128)(2,1)S(1)}, u32[]{:S(2)}, u32[]{:S(2)}) %collective-permute-start) | collective-permute-done | bytes 491552 | tf_op jit(solution)/shard_map/ppermute | solution.py:531
  9.9 1.2 add_convert_fusion.1
  11.1 0.8 fusion
  11.9 1.3 %collective-permute-start.2 = (bf16[8,80,128]{2,1,0:T(8,128)(2,1)}, bf16[8,80,128]{2,1,0:T(8,128)(2,1)}, u32[]{:S(2)}, u32[]{:S(2)}) collective-permute-start(bf16[8,80,128]{2,1,0:T(8,128)(2,1)} %get-tuple-element.49), channel_id=1, source_target_pairs={{1,3},{2,0},{5,7},{6,4},{9,11},{10,8},{13,15},{14,12},{17,19},{18,... | collective-permute-start | bytes 491528 | tf_op jit(solution)/shard_map/ppermute | solution.py:668
  13.2 3.5 %collective-permute-start.1 = (bf16[8,80,128]{2,1,0:T(8,128)(2,1)S(1)}, bf16[8,80,128]{2,1,0:T(8,128)(2,1)}, u32[]{:S(2)}, u32[]{:S(2)}) collective-permute-start(bf16[8,80,128]{2,1,0:T(8,128)(2,1)S(1)} %get-tuple-element.50), channel_id=1, source_target_pairs={{0,2},{1,3},{2,0},{3,1},{4,6},{5,7},{6,4},{7,5},{8,10},{9,11},{10,... | collective-permute-start | bytes 491528 | tf_op jit(solution)/shard_map/ppermute | solution.py:531
  16.7 1.0 broadcast_select_fusion
  17.7 5.8 %collective-permute-start.6 = (bf16[2,512,256]{2,1,0:T(8,128)(2,1)}, bf16[2,512,256]{2,1,0:T(8,128)(2,1)}, u32[]{:S(2)}, u32[]{:S(2)}) collective-permute-start(bf16[2,512,256]{2,1,0:T(8,128)(2,1)} %get-tuple-element.42), channel_id=1, source_target_pairs={{0,31},{1,2},{2,1},{3,4},{4,3},{5,6},{6,5},{7,8},{8,7},{9,10},{10,... | collective-permute-start | bytes 1572872 | tf_op jit(solution)/shard_map/ppermute | solution.py:604
  23.6 1.2 add_convert_fusion.3
  24.9 5.0 %collective-permute-start.3 = (bf16[10,80,128]{2,1,0:T(8,128)(2,1)S(1)}, bf16[10,80,128]{2,1,0:T(8,128)(2,1)S(1)}, u32[]{:S(2)}, u32[]{:S(2)}) collective-permute-start(bf16[10,80,128]{2,1,0:T(8,128)(2,1)S(1)} %maximum_select_fusion), channel_id=1, source_target_pairs={{0,31},{1,2},{2,1},{3,4},{4,3},{5,6},{6,5},{7,8},{8,7},{9,10},{10,... | collective-permute-start | bytes 614408 | tf_op jit(solution)/shard_map/ppermute | solution.py:691
  29.9 5.7 %shard_map.112.inner = bf16[6,256,512]{2,1,0:T(8,128)(2,1)S(1)} custom-call(bf16[8,512,256]{2,1,0:T(8,128)(2,1)S(1)} %copy-done.3, bf16[3,3,256,256]{3,2,1,0:T(8,128)(2,1)S(1)} %copy-done.7), custom_call_target="tpu_custom_call" | custom-call | flops 3623878656 | bytes 4194304 | tf_op jit(solution)/shard_map/pallas_call | solution.py:641
  35.6 2.5 %collective-permute-start.4 = (bf16[4,80,128]{2,1,0:T(8,128)(2,1)S(1)}, bf16[4,80,128]{2,1,0:T(8,128)(2,1)S(1)}, u32[]{:S(2)}, u32[]{:S(2)}) collective-permute-start(bf16[4,80,128]{2,1,0:T(8,128)(2,1)S(1)} %pad_maximum_fusion.2), channel_id=1, source_target_pairs={{0,1},{1,0},{2,3},{3,2},{4,5},{5,4},{6,7},{7,6},{8,9},{9,8},{10,11... | collective-permute-start | bytes 245768 | tf_op jit(solution)/shard_map/ppermute | solution.py:693
  38.2 5.2 %shard_map.113 = (bf16[10,256,512]{2,1,0:T(8,128)(2,1)S(1)}, bf16[768,240]{1,0:T(8,128)(2,1)S(1)}, bf16[512,256]{1,0:T(8,128)(2,1)S(1)}) custom-call(s32[1]{0:T(128)} %bitcast.place, bf16[2,512,256]{2,1,0:T(8,128)(2,1)} %collective-permute-done.5.near, bf16[2,512,256]{2,1,0:T(8,128)(2,1)} %collective-permute-done.6.far, bf16[8,512,256]{2,1,0:T(8,128)(2,1)S(1)} %copy-done.3, ...), custom_call_target="tpu_custom_call" | custom-call | flops 2415919104 | bytes 2097152 | tf_op jit(solution)/shard_map/pallas_call | solution.py:650
  43.4 17.5 %shard_map.114 = (bf16[1536,256]{1,0:T(8,128)(2,1)S(1)}, bf16[1536,256]{1,0:T(8,128)(2,1)S(1)}, bf16[8,80,128]{2,1,0:T(8,128)(2,1)S(1)}, bf16[8,80,128]{2,1,0:T(8,128)(2,1)S(1)}) custom-call(s32[1]{0:T(128)} %bitcast.place, bf16[8,80,128]{2,1,0:T(8,128)(2,1)S(1)} %get-tuple-element.48.own, bf16[8,80,128]{2,1,0:T(8,128)(2,1)S(1)} %get-tuple-element.47.edge, ...), custom_call_target="tpu_custom_call" | custom-call | flops 12079595520 | bytes 20971520 | tf_op jit(solution)/shard_map/pallas_call | solution.py:700
  60.9 0.1 collective-permute-start.11
  61.0 2.2 %collective-permute-done.11 = bf16[1536,256]{1,0:T(8,128)(2,1)S(1)} collective-permute-done((bf16[1536,256]{1,0:T(8,128)(2,1)S(1)}, bf16[1536,256]{1,0:T(8,128)(2,1)S(1)}, u32[]{:S(2)}, u32[]{:S(2)}) %collective-permute-start.11) | collective-permute-done | bytes 786464 | tf_op jit(solution)/shard_map/ppermute | solution.py:531
  63.3 0.2 add_convert_fusion
  63.5 3.5 %collective-permute-start.12 = (bf16[384,256]{1,0:T(8,128)(2,1)S(1)}, bf16[384,256]{1,0:T(8,128)(2,1)S(1)}, u32[]{:S(2)}, u32[]{:S(2)}) collective-permute-start(bf16[384,256]{1,0:T(8,128)(2,1)S(1)} %get-tuple-element.44), channel_id=1, source_target_pairs={{0,6},{1,25},{2,4},{3,27},{4,2},{5,29},{6,0},{7,31},{8,14},{9,17},... | collective-permute-start | bytes 589832 | tf_op jit(solution)/shard_map/ppermute | solution.py:554
  67.0 1.2 collective-permute-start.14
  68.2 2.5 %collective-permute-done.12 = bf16[384,256]{1,0:T(8,128)(2,1)S(1)} collective-permute-done((bf16[384,256]{1,0:T(8,128)(2,1)S(1)}, bf16[384,256]{1,0:T(8,128)(2,1)S(1)}, u32[]{:S(2)}, u32[]{:S(2)}) %collective-permute-start.12) | collective-permute-done | bytes 196640 | tf_op jit(solution)/shard_map/ppermute | solution.py:554
  70.7 2.2 %collective-permute-done.14 = bf16[384,256]{1,0:T(8,128)(2,1)S(1)} collective-permute-done((bf16[384,256]{1,0:T(8,128)(2,1)S(1)}, bf16[384,256]{1,0:T(8,128)(2,1)S(1)}, u32[]{:S(2)}, u32[]{:S(2)}) %collective-permute-start.14) | collective-permute-done | bytes 196640 | tf_op jit(solution)/shard_map/ppermute | solution.py:554
  72.8 1.0 collective-permute-done.13
  73.9 0.1 add_convert_fusion.2
  74.0 3.8 %collective-permute-start.15 = (bf16[96,256]{1,0:T(8,128)(2,1)S(1)}, bf16[96,256]{1,0:T(8,128)(2,1)S(1)}, u32[]{:S(2)}, u32[]{:S(2)}) collective-permute-start(bf16[96,256]{1,0:T(8,128)(2,1)S(1)} %get-tuple-element.51), channel_id=1, source_target_pairs={{0,24},{1,7},{2,26},{3,5},{4,28},{5,3},{6,30},{7,1},{8,16},{9,15},... | collective-permute-start | bytes 147464 | tf_op jit(solution)/shard_map/ppermute | solution.py:554
  77.8 0.7 collective-permute-start.16
  78.5 1.5 %collective-permute-done.15 = bf16[96,256]{1,0:T(8,128)(2,1)S(1)} collective-permute-done((bf16[96,256]{1,0:T(8,128)(2,1)S(1)}, bf16[96,256]{1,0:T(8,128)(2,1)S(1)}, u32[]{:S(2)}, u32[]{:S(2)}) %collective-permute-start.15) | collective-permute-done | bytes 49184 | tf_op jit(solution)/shard_map/ppermute | solution.py:554
  80.0 2.8 %collective-permute-done.17 = bf16[96,256]{1,0:T(8,128)(2,1)S(1)} collective-permute-done((bf16[96,256]{1,0:T(8,128)(2,1)S(1)}, bf16[96,256]{1,0:T(8,128)(2,1)S(1)}, u32[]{:S(2)}, u32[]{:S(2)}) %collective-permute-start.17) | collective-permute-done | bytes 49184 | tf_op jit(solution)/shard_map/ppermute | solution.py:554
  82.8 0.2 collective-permute-start.20
  83.0 2.0 %collective-permute-start.19 = (bf16[96,256]{1,0:T(8,128)(2,1)S(1)}, bf16[96,256]{1,0:T(8,128)(2,1)S(1)}, u32[]{:S(2)}, u32[]{:S(2)}) collective-permute-start(bf16[96,256]{1,0:T(8,128)(2,1)S(1)} %add_convert_fusion.5), channel_id=1, source_target_pairs={{0,16},{1,5},{2,18},{3,7},{4,20},{5,1},{6,22},{7,3},{8,24},{9,13},... | collective-permute-start | bytes 147464 | tf_op jit(solution)/shard_map/ppermute | solution.py:554
  85.0 2.3 %collective-permute-start.18 = (bf16[96,256]{1,0:T(8,128)(2,1)S(1)}, bf16[96,256]{1,0:T(8,128)(2,1)S(1)}, u32[]{:S(2)}, u32[]{:S(2)}) collective-permute-start(bf16[96,256]{1,0:T(8,128)(2,1)S(1)} %add_convert_fusion.5), channel_id=1, source_target_pairs={{0,24},{1,7},{2,26},{3,5},{4,28},{5,3},{6,30},{7,1},{8,16},{9,15},... | collective-permute-start | bytes 147464 | tf_op jit(solution)/shard_map/ppermute | solution.py:554
  87.3 0.7 collective-permute-done.19
  88.0 3.0 %collective-permute-done.18 = bf16[96,256]{1,0:T(8,128)(2,1)S(1)} collective-permute-done((bf16[96,256]{1,0:T(8,128)(2,1)S(1)}, bf16[96,256]{1,0:T(8,128)(2,1)S(1)}, u32[]{:S(2)}, u32[]{:S(2)}) %collective-permute-start.18) | collective-permute-done | bytes 49184 | tf_op jit(solution)/shard_map/ppermute | solution.py:554
  91.1 1.5 %collective-permute-start.21 = (bf16[384,256]{1,0:T(8,128)(2,1)S(1)}, bf16[384,256]{1,0:T(8,128)(2,1)}, u32[]{:S(2)}, u32[]{:S(2)}) collective-permute-start(bf16[384,256]{1,0:T(8,128)(2,1)S(1)} %pad_maximum_fusion.1), channel_id=1, source_target_pairs={{0,2},{1,9},{2,0},{3,11},{4,6},{5,13},{6,4},{7,15},{8,10},{9,1},{1... | collective-permute-start | bytes 589832 | tf_op jit(solution)/shard_map/ppermute | solution.py:554
  92.6 1.9 %collective-permute-start.8 = (bf16[8,80,128]{2,1,0:T(8,128)(2,1)S(1)}, bf16[8,80,128]{2,1,0:T(8,128)(2,1)}, u32[]{:S(2)}, u32[]{:S(2)}) collective-permute-start(bf16[8,80,128]{2,1,0:T(8,128)(2,1)S(1)} %get-tuple-element.26), channel_id=1, source_target_pairs={{0,31},{4,3},{8,7},{12,11},{16,15},{20,19},{24,23},{28,27},{3,4},{... | collective-permute-start | bytes 491528 | tf_op jit(solution)/shard_map/ppermute | solution.py:689
  94.6 0.9 collective-permute-start.22
  95.5 0.6 collective-permute-start.7
  96.1 7.0 %collective-permute-done.8 = bf16[8,80,128]{2,1,0:T(8,128)(2,1)} collective-permute-done((bf16[8,80,128]{2,1,0:T(8,128)(2,1)S(1)}, bf16[8,80,128]{2,1,0:T(8,128)(2,1)}, u32[]{:S(2)}, u32[]{:S(2)}) %collective-permute-start.8) | collective-permute-done | bytes 163872 | tf_op jit(solution)/shard_map/ppermute | solution.py:689
  103.1 1.3 %collective-permute-start.9 = (bf16[8,80,128]{2,1,0:T(8,128)(2,1)}, bf16[8,80,128]{2,1,0:T(8,128)(2,1)S(1)}, u32[]{:S(2)}, u32[]{:S(2)}) collective-permute-start(bf16[8,80,128]{2,1,0:T(8,128)(2,1)} %collective-permute-done.8), channel_id=1, source_target_pairs={{3,1},{0,2},{7,5},{4,6},{11,9},{8,10},{15,13},{12,14},{19,17},{16,... | collective-permute-start | bytes 491528 | tf_op jit(solution)/shard_map/ppermute | solution.py:739
  104.5 0.9 constant_dynamic-update-slice_fusion.2
  105.4 0.9 constant_dynamic-update-slice_fusion.1
  106.4 4.6 %collective-permute-done.23 = bf16[384,256]{1,0:T(8,128)(2,1)S(1)} collective-permute-done((bf16[384,256]{1,0:T(8,128)(2,1)S(1)}, bf16[384,256]{1,0:T(8,128)(2,1)S(1)}, u32[]{:S(2)}, u32[]{:S(2)}) %collective-permute-start.23) | collective-permute-done | bytes 196640 | tf_op jit(solution)/shard_map/ppermute | solution.py:554
  111.0 0.1 collective-permute-start.24
  111.1 1.0 broadcast_select_fusion.2.edge
  112.2 1.9 %collective-permute-done.10.theirs = bf16[24,80,128]{2,1,0:T(8,128)(2,1)S(1)} collective-permute-done((bf16[24,80,128]{2,1,0:T(8,128)(2,1)S(1)}, bf16[24,80,128]{2,1,0:T(8,128)(2,1)S(1)}, u32[]{:S(2)}, u32[]{:S(2)}) %collective-permute-start.10) | collective-permute-done | bytes 491552 | tf_op jit(solution)/shard_map/ppermute | solution.py:531
  114.1 4.2 %shard_map.116 = bf16[2560,128]{1,0:T(8,128)(2,1)} custom-call(s32[1]{0:T(128)} %bitcast.place, s32[49]{0:T(128)S(1)} %copy-done.6, bf16[8,80,128]{2,1,0:T(8,128)(2,1)S(1)} %get-tuple-element.25.own, bf16[8,80,128]{2,1,0:T(8,128)(2,1)S(1)} %collective-permute-done.7.partner, bf16[8,80,128]{2,1,0:T(8,128)(2,1)S(1)} %broadcast_select_fusion.2.edge, ...), custom_call_target="tpu_custom_call" | custom-call | flops 150994944 | bytes 4587520 | tf_op jit(solution)/shard_map/pallas_call | solution.py:749
  118.3 4.5 %shard_map.115 = f32[3584,128]{1,0:T(8,128)} custom-call(s32[1]{0:T(128)} %bitcast.place, s32[49]{0:T(128)S(1)} %copy-done.6, bf16[8,80,128]{2,1,0:T(8,128)(2,1)S(1)} %get-tuple-element.25.own, bf16[8,80,128]{2,1,0:T(8,128)(2,1)S(1)} %collective-permute-done.7.partner, bf16[8,80,128]{2,1,0:T(8,128)(2,1)S(1)} %broadcast_select_fusion.2.edge, ...), custom_call_target="tpu_custom_call" | custom-call | flops 150994944 | bytes 9175040 | tf_op jit(solution)/shard_map/pallas_call | solution.py:757
  122.7 1.9 %shard_map.117 = (f32[2304,256]{1,0:T(8,128)}, f32[720,256]{1,0:T(8,128)}) custom-call(s32[1]{0:T(128)} %bitcast.place, bf16[1536,256]{1,0:T(8,128)(2,1)S(1)} %constant_dynamic-update-slice_fusion.value, bf16[1536,256]{1,0:T(8,128)(2,1)S(1)} %collective-permute-done.24.other), custom_call_target="tpu_custom_call" | custom-call | flops 1 | bytes 4718592 | tf_op jit(solution)/shard_map/pallas_call | solution.py:768
  (54 shorter events, 0.6 us)
Async XLA Ops:
  0.6 16.0 %copy-start.3 = (bf16[8,512,256]{2,1,0:T(8,128)(2,1)S(1)}, bf16[8,512,256]{2,1,0:T(8,128)(2,1)}, u32[]{:S(2)}) copy-start(bf16[8,512,256]{2,1,0:T(8,128)(2,1)} %upstream.3) | copy-start | bytes 6291460
  7.7 2.3 %collective-permute-start = (bf16[24,80,128]{2,1,0:T(8,128)(2,1)}, bf16[24,80,128]{2,1,0:T(8,128)(2,1)S(1)}, u32[]{:S(2)}, u32[]{:S(2)}) collective-permute-start(bf16[24,80,128]{2,1,0:T(8,128)(2,1)} %get-tuple-element.21), channel_id=1, source_target_pairs={{0,1},{1,0},{2,3},{3,2},{4,5},{5,4},{6,7},{7,6},{8,9},{9,8},{10,11... | collective-permute-start | bytes 1474568 | tf_op jit(solution)/shard_map/ppermute | solution.py:531
  11.1 2.1 %copy-start.10 = (bf16[24,80,128]{2,1,0:T(8,128)(2,1)}, bf16[24,80,128]{2,1,0:T(8,128)(2,1)S(1)}, u32[]{:S(2)}) copy-start(bf16[24,80,128]{2,1,0:T(8,128)(2,1)S(1)} %add_convert_fusion.1) | copy-start | bytes 1474564
  11.9 11.7 %collective-permute-start.2 = (bf16[8,80,128]{2,1,0:T(8,128)(2,1)}, bf16[8,80,128]{2,1,0:T(8,128)(2,1)}, u32[]{:S(2)}, u32[]{:S(2)}) collective-permute-start(bf16[8,80,128]{2,1,0:T(8,128)(2,1)} %get-tuple-element.49), channel_id=1, source_target_pairs={{1,3},{2,0},{5,7},{6,4},{9,11},{10,8},{13,15},{14,12},{17,19},{18,... | collective-permute-start | bytes 491528 | tf_op jit(solution)/shard_map/ppermute | solution.py:668
  13.2 16.8 %copy-start.7 = (bf16[3,3,256,256]{3,2,1,0:T(8,128)(2,1)S(1)}, bf16[3,3,256,256]{3,2,1,0:T(8,128)(2,1)}, u32[]{:S(2)}) copy-start(bf16[3,3,256,256]{3,2,1,0:T(8,128)(2,1)} %weight.3) | copy-start | bytes 3538948
  13.2 10.4 %collective-permute-start.1 = (bf16[8,80,128]{2,1,0:T(8,128)(2,1)S(1)}, bf16[8,80,128]{2,1,0:T(8,128)(2,1)}, u32[]{:S(2)}, u32[]{:S(2)}) collective-permute-start(bf16[8,80,128]{2,1,0:T(8,128)(2,1)S(1)} %get-tuple-element.50), channel_id=1, source_target_pairs={{0,2},{1,3},{2,0},{3,1},{4,6},{5,7},{6,4},{7,5},{8,10},{9,11},{10,... | collective-permute-start | bytes 491528 | tf_op jit(solution)/shard_map/ppermute | solution.py:531
  17.7 20.4 %collective-permute-start.6 = (bf16[2,512,256]{2,1,0:T(8,128)(2,1)}, bf16[2,512,256]{2,1,0:T(8,128)(2,1)}, u32[]{:S(2)}, u32[]{:S(2)}) collective-permute-start(bf16[2,512,256]{2,1,0:T(8,128)(2,1)} %get-tuple-element.42), channel_id=1, source_target_pairs={{0,31},{1,2},{2,1},{3,4},{4,3},{5,6},{6,5},{7,8},{8,7},{9,10},{10,... | collective-permute-start | bytes 1572872 | tf_op jit(solution)/shard_map/ppermute | solution.py:604
  23.5 14.6 %collective-permute-start.5 = (bf16[2,512,256]{2,1,0:T(8,128)(2,1)}, bf16[2,512,256]{2,1,0:T(8,128)(2,1)}, u32[]{:S(2)}, u32[]{:S(2)}) collective-permute-start(bf16[2,512,256]{2,1,0:T(8,128)(2,1)} %get-tuple-element.43), channel_id=1, source_target_pairs={{0,1},{1,0},{2,3},{3,2},{4,5},{5,4},{6,7},{7,6},{8,9},{9,8},{10,11... | collective-permute-start | bytes 1572872 | tf_op jit(solution)/shard_map/ppermute | solution.py:605
  24.9 13.3 %copy-start.8 = (bf16[3,3,80,256]{3,2,1,0:T(8,128)(2,1)S(1)}, bf16[3,3,80,256]{3,2,1,0:T(8,128)(2,1)}, u32[]{:S(2)}) copy-start(bf16[3,3,80,256]{3,2,1,0:T(8,128)(2,1)} %param.13) | copy-start | bytes 1105924
  24.9 13.3 %copy-start.9 = (s32[8,112]{1,0:T(8,128)S(1)}, s32[8,112]{1,0:T(8,128)}, u32[]{:S(2)}) copy-start(s32[8,112]{1,0:T(8,128)} %ranges.1) | copy-start | bytes 10756
  24.9 10.7 %collective-permute-start.3 = (bf16[10,80,128]{2,1,0:T(8,128)(2,1)S(1)}, bf16[10,80,128]{2,1,0:T(8,128)(2,1)S(1)}, u32[]{:S(2)}, u32[]{:S(2)}) collective-permute-start(bf16[10,80,128]{2,1,0:T(8,128)(2,1)S(1)} %maximum_select_fusion), channel_id=1, source_target_pairs={{0,31},{1,2},{2,1},{3,4},{4,3},{5,6},{6,5},{7,8},{8,7},{9,10},{10,... | collective-permute-start | bytes 614408 | tf_op jit(solution)/shard_map/ppermute | solution.py:691
  35.6 7.8 %collective-permute-start.4 = (bf16[4,80,128]{2,1,0:T(8,128)(2,1)S(1)}, bf16[4,80,128]{2,1,0:T(8,128)(2,1)S(1)}, u32[]{:S(2)}, u32[]{:S(2)}) collective-permute-start(bf16[4,80,128]{2,1,0:T(8,128)(2,1)S(1)} %pad_maximum_fusion.2), channel_id=1, source_target_pairs={{0,1},{1,0},{2,3},{3,2},{4,5},{5,4},{6,7},{7,6},{8,9},{9,8},{10,11... | collective-permute-start | bytes 245768 | tf_op jit(solution)/shard_map/ppermute | solution.py:693
  38.2 5.2 %copy-start.4 = (bf16[8,512,256]{2,1,0:T(8,128)(2,1)S(1)}, bf16[8,512,256]{2,1,0:T(8,128)(2,1)}, u32[]{:S(2)}) copy-start(bf16[8,512,256]{2,1,0:T(8,128)(2,1)} %upstream.3) | copy-start | bytes 6291460
  60.9 2.3 %collective-permute-start.11 = (bf16[1536,256]{1,0:T(8,128)(2,1)S(1)}, bf16[1536,256]{1,0:T(8,128)(2,1)S(1)}, u32[]{:S(2)}, u32[]{:S(2)}) collective-permute-start(bf16[1536,256]{1,0:T(8,128)(2,1)S(1)} %get-tuple-element.31), channel_id=1, source_target_pairs={{0,1},{1,0},{2,3},{3,2},{4,5},{5,4},{6,7},{7,6},{8,9},{9,8},{10,11... | collective-permute-start | bytes 2359304 | tf_op jit(solution)/shard_map/ppermute | solution.py:531
  63.5 7.1 %collective-permute-start.12 = (bf16[384,256]{1,0:T(8,128)(2,1)S(1)}, bf16[384,256]{1,0:T(8,128)(2,1)S(1)}, u32[]{:S(2)}, u32[]{:S(2)}) collective-permute-start(bf16[384,256]{1,0:T(8,128)(2,1)S(1)} %get-tuple-element.44), channel_id=1, source_target_pairs={{0,6},{1,25},{2,4},{3,27},{4,2},{5,29},{6,0},{7,31},{8,14},{9,17},... | collective-permute-start | bytes 589832 | tf_op jit(solution)/shard_map/ppermute | solution.py:554
  67.0 5.8 %collective-permute-start.14 = (bf16[384,256]{1,0:T(8,128)(2,1)S(1)}, bf16[384,256]{1,0:T(8,128)(2,1)S(1)}, u32[]{:S(2)}, u32[]{:S(2)}) collective-permute-start(bf16[384,256]{1,0:T(8,128)(2,1)S(1)} %get-tuple-element.45), channel_id=1, source_target_pairs={{0,4},{1,17},{2,6},{3,19},{4,0},{5,21},{6,2},{7,23},{8,12},{9,25},... | collective-permute-start | bytes 589832 | tf_op jit(solution)/shard_map/ppermute | solution.py:554
  68.2 5.7 %collective-permute-start.13 = (bf16[384,256]{1,0:T(8,128)(2,1)S(1)}, bf16[384,256]{1,0:T(8,128)(2,1)S(1)}, u32[]{:S(2)}, u32[]{:S(2)}) collective-permute-start(bf16[384,256]{1,0:T(8,128)(2,1)S(1)} %get-tuple-element.46), channel_id=1, source_target_pairs={{0,2},{1,9},{2,0},{3,11},{4,6},{5,13},{6,4},{7,15},{8,10},{9,1},{1... | collective-permute-start | bytes 589832 | tf_op jit(solution)/shard_map/ppermute | solution.py:554
  74.0 6.0 %collective-permute-start.15 = (bf16[96,256]{1,0:T(8,128)(2,1)S(1)}, bf16[96,256]{1,0:T(8,128)(2,1)S(1)}, u32[]{:S(2)}, u32[]{:S(2)}) collective-permute-start(bf16[96,256]{1,0:T(8,128)(2,1)S(1)} %get-tuple-element.51), channel_id=1, source_target_pairs={{0,24},{1,7},{2,26},{3,5},{4,28},{5,3},{6,30},{7,1},{8,16},{9,15},... | collective-permute-start | bytes 147464 | tf_op jit(solution)/shard_map/ppermute | solution.py:554
  77.8 5.0 %collective-permute-start.17 = (bf16[96,256]{1,0:T(8,128)(2,1)S(1)}, bf16[96,256]{1,0:T(8,128)(2,1)S(1)}, u32[]{:S(2)}, u32[]{:S(2)}) collective-permute-start(bf16[96,256]{1,0:T(8,128)(2,1)S(1)} %get-tuple-element.52), channel_id=1, source_target_pairs={{0,16},{1,5},{2,18},{3,7},{4,20},{5,1},{6,22},{7,3},{8,24},{9,13},... | collective-permute-start | bytes 147464 | tf_op jit(solution)/shard_map/ppermute | solution.py:554
  77.8 5.0 %collective-permute-start.16 = (bf16[96,256]{1,0:T(8,128)(2,1)S(1)}, bf16[96,256]{1,0:T(8,128)(2,1)S(1)}, u32[]{:S(2)}, u32[]{:S(2)}) collective-permute-start(bf16[96,256]{1,0:T(8,128)(2,1)S(1)} %get-tuple-element.53), channel_id=1, source_target_pairs={{0,8},{1,3},{2,10},{3,1},{4,12},{5,7},{6,14},{7,5},{8,0},{9,11},{1... | collective-permute-start | bytes 147464 | tf_op jit(solution)/shard_map/ppermute | solution.py:554
  82.8 4.5 %collective-permute-start.20 = (bf16[96,256]{1,0:T(8,128)(2,1)S(1)}, bf16[96,256]{1,0:T(8,128)(2,1)S(1)}, u32[]{:S(2)}, u32[]{:S(2)}) collective-permute-start(bf16[96,256]{1,0:T(8,128)(2,1)S(1)} %add_convert_fusion.5), channel_id=1, source_target_pairs={{0,8},{1,3},{2,10},{3,1},{4,12},{5,7},{6,14},{7,5},{8,0},{9,11},{1... | collective-permute-start | bytes 147464 | tf_op jit(solution)/shard_map/ppermute | solution.py:554
  83.0 5.0 %collective-permute-start.19 = (bf16[96,256]{1,0:T(8,128)(2,1)S(1)}, bf16[96,256]{1,0:T(8,128)(2,1)S(1)}, u32[]{:S(2)}, u32[]{:S(2)}) collective-permute-start(bf16[96,256]{1,0:T(8,128)(2,1)S(1)} %add_convert_fusion.5), channel_id=1, source_target_pairs={{0,16},{1,5},{2,18},{3,7},{4,20},{5,1},{6,22},{7,3},{8,24},{9,13},... | collective-permute-start | bytes 147464 | tf_op jit(solution)/shard_map/ppermute | solution.py:554
  85.0 6.0 %collective-permute-start.18 = (bf16[96,256]{1,0:T(8,128)(2,1)S(1)}, bf16[96,256]{1,0:T(8,128)(2,1)S(1)}, u32[]{:S(2)}, u32[]{:S(2)}) collective-permute-start(bf16[96,256]{1,0:T(8,128)(2,1)S(1)} %add_convert_fusion.5), channel_id=1, source_target_pairs={{0,24},{1,7},{2,26},{3,5},{4,28},{5,3},{6,30},{7,1},{8,16},{9,15},... | collective-permute-start | bytes 147464 | tf_op jit(solution)/shard_map/ppermute | solution.py:554
  91.0 23.1 %copy-start = (f32[129,32,128]{2,1,0:T(8,128)S(1)}, f32[129,32,128]{2,1,0:T(8,128)}, u32[]{:S(2)}) copy-start(f32[129,32,128]{2,1,0:T(8,128)} %get-tuple-element.29.probs_t) | copy-start | bytes 6340612
  91.0 23.1 %copy-start.6 = (s32[49]{0:T(128)S(1)}, s32[49]{0:T(128)}, u32[]{:S(2)}) copy-start(s32[49]{0:T(128)} %get-tuple-element.19.begins) | copy-start | bytes 592
  91.1 13.3 %collective-permute-start.21 = (bf16[384,256]{1,0:T(8,128)(2,1)S(1)}, bf16[384,256]{1,0:T(8,128)(2,1)}, u32[]{:S(2)}, u32[]{:S(2)}) collective-permute-start(bf16[384,256]{1,0:T(8,128)(2,1)S(1)} %pad_maximum_fusion.1), channel_id=1, source_target_pairs={{0,2},{1,9},{2,0},{3,11},{4,6},{5,13},{6,4},{7,15},{8,10},{9,1},{1... | collective-permute-start | bytes 589832 | tf_op jit(solution)/shard_map/ppermute | solution.py:554
  92.6 10.4 %collective-permute-start.8 = (bf16[8,80,128]{2,1,0:T(8,128)(2,1)S(1)}, bf16[8,80,128]{2,1,0:T(8,128)(2,1)}, u32[]{:S(2)}, u32[]{:S(2)}) collective-permute-start(bf16[8,80,128]{2,1,0:T(8,128)(2,1)S(1)} %get-tuple-element.26), channel_id=1, source_target_pairs={{0,31},{4,3},{8,7},{12,11},{16,15},{20,19},{24,23},{28,27},{3,4},{... | collective-permute-start | bytes 491528 | tf_op jit(solution)/shard_map/ppermute | solution.py:689
  94.6 10.8 %collective-permute-start.22 = (bf16[384,256]{1,0:T(8,128)(2,1)S(1)}, bf16[384,256]{1,0:T(8,128)(2,1)}, u32[]{:S(2)}, u32[]{:S(2)}) collective-permute-start(bf16[384,256]{1,0:T(8,128)(2,1)S(1)} %pad_maximum_fusion.1), channel_id=1, source_target_pairs={{0,4},{1,17},{2,6},{3,19},{4,0},{5,21},{6,2},{7,23},{8,12},{9,25},... | collective-permute-start | bytes 589832 | tf_op jit(solution)/shard_map/ppermute | solution.py:554
  95.5 16.6 %collective-permute-start.7 = (bf16[8,80,128]{2,1,0:T(8,128)(2,1)S(1)}, bf16[8,80,128]{2,1,0:T(8,128)(2,1)S(1)}, u32[]{:S(2)}, u32[]{:S(2)}) collective-permute-start(bf16[8,80,128]{2,1,0:T(8,128)(2,1)S(1)} %get-tuple-element.25.own), channel_id=1, source_target_pairs={{0,2},{1,3},{2,0},{3,1},{4,6},{5,7},{6,4},{7,5},{8,10},{9,11},{10,... | collective-permute-start | bytes 491528 | tf_op jit(solution)/shard_map/ppermute | solution.py:531
  103.1 8.0 %collective-permute-start.9 = (bf16[8,80,128]{2,1,0:T(8,128)(2,1)}, bf16[8,80,128]{2,1,0:T(8,128)(2,1)S(1)}, u32[]{:S(2)}, u32[]{:S(2)}) collective-permute-start(bf16[8,80,128]{2,1,0:T(8,128)(2,1)} %collective-permute-done.8), channel_id=1, source_target_pairs={{3,1},{0,2},{7,5},{4,6},{11,9},{8,10},{15,13},{12,14},{19,17},{16,... | collective-permute-start | bytes 491528 | tf_op jit(solution)/shard_map/ppermute | solution.py:739
  104.4 6.6 %collective-permute-start.23 = (bf16[384,256]{1,0:T(8,128)(2,1)S(1)}, bf16[384,256]{1,0:T(8,128)(2,1)S(1)}, u32[]{:S(2)}, u32[]{:S(2)}) collective-permute-start(bf16[384,256]{1,0:T(8,128)(2,1)S(1)} %pad_maximum_fusion.1), channel_id=1, source_target_pairs={{0,6},{1,25},{2,4},{3,27},{4,2},{5,29},{6,0},{7,31},{8,14},{9,17},... | collective-permute-start | bytes 589832 | tf_op jit(solution)/shard_map/ppermute | solution.py:554
  111.0 11.7 %collective-permute-start.24 = (bf16[1536,256]{1,0:T(8,128)(2,1)S(1)}, bf16[1536,256]{1,0:T(8,128)(2,1)S(1)}, u32[]{:S(2)}, u32[]{:S(2)}) collective-permute-start(bf16[1536,256]{1,0:T(8,128)(2,1)S(1)} %constant_dynamic-update-slice_fusion.value), channel_id=1, source_target_pairs={{0,1},{1,0},{2,3},{3,2},{4,5},{5,4},{6,7},{7,6},{8,9},{9,8},{10,11... | collective-permute-start | bytes 2359304 | tf_op jit(solution)/shard_map/ppermute | solution.py:531
  112.1 6.2 %copy-start.2 = (f32[3584,128]{1,0:T(8,128)S(1)}, f32[3584,128]{1,0:T(8,128)}, u32[]{:S(2)}) copy-start(f32[3584,128]{1,0:T(8,128)} %get-tuple-element.27.probs) | copy-start | bytes 5505028
  112.2 1.9 %collective-permute-start.10 = (bf16[24,80,128]{2,1,0:T(8,128)(2,1)S(1)}, bf16[24,80,128]{2,1,0:T(8,128)(2,1)S(1)}, u32[]{:S(2)}, u32[]{:S(2)}) collective-permute-start(bf16[24,80,128]{2,1,0:T(8,128)(2,1)S(1)} %pad_maximum_fusion), channel_id=1, source_target_pairs={{0,1},{1,0},{2,3},{3,2},{4,5},{5,4},{6,7},{7,6},{8,9},{9,8},{10,11... | collective-permute-start | bytes 1474568 | tf_op jit(solution)/shard_map/ppermute | solution.py:531
  114.1 4.2 %copy-start.1 = (f32[129,32,128]{2,1,0:T(8,128)S(1)}, f32[129,32,128]{2,1,0:T(8,128)}, u32[]{:S(2)}) copy-start(f32[129,32,128]{2,1,0:T(8,128)} %get-tuple-element.28.context_t) | copy-start | bytes 6340612
  114.1 4.2 %copy-start.5 = (s32[1,32,128]{2,1,0:T(8,128)S(1)}, s32[1,32,128]{2,1,0:T(8,128)}, u32[]{:S(2)}) copy-start(s32[1,32,128]{2,1,0:T(8,128)} %param.10) | copy-start | bytes 49156

commit v5 on v4

--- a/solution.py
+++ b/solution.py
@@ -187,7 +187,8 @@
                     first_weight[row, column * channels : (column + 1) * channels, :].astype(F32)
                 ).astype(BF16)
             )
-    out[2:sector] = inner[...]
+    ready = inner.shape[0]
+    out[2 : 2 + ready] = inner[...]
     low[2:4] = upstream[0:2]
     high[0:2] = upstream[sector - 2 :]
 
@@ -206,7 +207,12 @@
         act_row(act_taps_of(weight), high, row, out, row + sector)
         return 0
 
+    def more(row, _):
+        act_row(act_taps_of(weight), upstream, row, out, row + 2)
+        return 0
+
     lax.fori_loop(0, 2, step, 0)
+    lax.fori_loop(ready, sector - 2, more, 0)
 
 
 def grid_kernel(
@@ -640,10 +646,10 @@
 
     inner_grad = call(
         inner_acts_kernel,
-        jax.ShapeDtypeStruct((sector - 2, hidden, length), BF16),
+        jax.ShapeDtypeStruct((sector - 3, hidden, length), BF16),
         [],
         [vmem()] * 2,
-        row_flops * (sector - 2),
+        row_flops * (sector - 3),
         4 * sector * length * hidden,
     )(out_grad, conv2_weight)
     weight = conv1_weight.reshape(TAPS, TAPS * channels, hidden)
@@ -656,7 +662,7 @@
         ],
         [pltpu.VMEM((4, length, hidden), BF16)] * 2 + [pltpu.VMEM((8, 2 * LANES), jnp.int32)],
         [smem()] + [vmem()] * 7,
-        row_flops * 4,
+        row_flops * 5,
         16 * length * hidden,
     )(place, near_grad, far_grad, out_grad, conv2_weight, inner_grad, weight, rng_map)
 

time: 125 us -> 126 us (level)
  no operation moved by 1% of the time
where the time goes in v5:
time: 126 us
  Pallas kernels  45.9 us (36%)
  starting transfers between devices  39.7 us (32%)
  waiting for transfers between devices  31.2 us (25%)
  other arithmetic  4.99 us (4%)
  local copies, waits for them, and re-layouts  2.79 us (2%)
    ppermute x12, waiting for transfers between devices, sent(): return lax.ppermute(part, 'blk', to)  18.3 us
    pallas_call x1, Pallas kernels, shards(): call(grid_kernel, [jax.ShapeDtypeStruct((grad_rows // 2, hidden), BF16),...  17.5 us
    ppermute x12, starting transfers between devices, sent(): return lax.ppermute(part, 'blk', to)  16 us
    pallas_call x1, Pallas kernels, shards(): call(functools.partial(pool_kernel, rows, sight, blocks * sector), [jax.S...  7.03 us
    ppermute x1, waiting for transfers between devices, to_next(): return lax.ppermute(value, 'blk', pairs)  7.01 us
    pallas_call x1, Pallas kernels, shards(): call(outer_acts_kernel, [jax.ShapeDtypeStruct((sector + 2, hidden, length...  6.13 us
    ppermute x1, starting transfers between devices, shards(): far_grad = lax.ppermute(ends(out_grad, False), 'blk', off_chip)  5.82 us
    ppermute x6, waiting for transfers between devices, swapped(): return lax.ppermute(value, 'blk', [(i, i ^ mask) for i in range(blocks)])  5.8 us
  transfers between devices with their start and end apart: 25, of which 12 were waited for; matrix products, arithmetic and copies ran while one was open for 4% of the time, Pallas kernels for 16%

profile of v5, /device:TPU:0, one launch (start us, length us, event | category | flops | bytes accessed | tf_op | source)
XLA Modules:
  0.0 125.6 jit_solution(17950363595372520018)
XLA Ops:
  0.6 7.0 %shard_map.111 = (f32[3584,128]{1,0:T(8,128)}, f32[129,32,128]{2,1,0:T(8,128)}, f32[129,32,128]{2,1,0:T(8,128)}, bf16[24,80,128]{2,1,0:T(8,128)(2,1)}, bf16[24,80,128]{2,1,0:T(8,128)(2,1)}, /*index=5*/s32[49]{0:T(128)}) custom-call(s32[1]{0:T(128)} %bitcast.place, s32[8,128]{1,0:T(8,128)} %az_map.1, f32[3584,128]{1,0:T(8,128)} %bitcast.14, ...), custom_call_target="tpu_custom_call" | custom-call | flops 150994944 | bytes 9175040 | tf_op jit(solution)/shard_map/pallas_call | solution.py:615
  7.7 0.6 collective-permute-start
  8.2 1.7 %collective-permute-done = bf16[24,80,128]{2,1,0:T(8,128)(2,1)S(1)} collective-permute-done((bf16[24,80,128]{2,1,0:T(8,128)(2,1)}, bf16[24,80,128]{2,1,0:T(8,128)(2,1)S(1)}, u32[]{:S(2)}, u32[]{:S(2)}) %collective-permute-start) | collective-permute-done | bytes 491552 | tf_op jit(solution)/shard_map/ppermute | solution.py:537
  9.9 1.2 add_convert_fusion.1
  11.1 0.8 fusion
  11.9 1.3 %collective-permute-start.2 = (bf16[8,80,128]{2,1,0:T(8,128)(2,1)}, bf16[8,80,128]{2,1,0:T(8,128)(2,1)}, u32[]{:S(2)}, u32[]{:S(2)}) collective-permute-start(bf16[8,80,128]{2,1,0:T(8,128)(2,1)} %get-tuple-element.49), channel_id=1, source_target_pairs={{1,3},{2,0},{5,7},{6,4},{9,11},{10,8},{13,15},{14,12},{17,19},{18,... | collective-permute-start | bytes 491528 | tf_op jit(solution)/shard_map/ppermute | solution.py:674
  13.2 3.5 %collective-permute-start.1 = (bf16[8,80,128]{2,1,0:T(8,128)(2,1)S(1)}, bf16[8,80,128]{2,1,0:T(8,128)(2,1)}, u32[]{:S(2)}, u32[]{:S(2)}) collective-permute-start(bf16[8,80,128]{2,1,0:T(8,128)(2,1)S(1)} %get-tuple-element.50), channel_id=1, source_target_pairs={{0,2},{1,3},{2,0},{3,1},{4,6},{5,7},{6,4},{7,5},{8,10},{9,11},{10,... | collective-permute-start | bytes 491528 | tf_op jit(solution)/shard_map/ppermute | solution.py:537
  16.7 1.0 broadcast_select_fusion
  17.7 5.8 %collective-permute-start.6 = (bf16[2,512,256]{2,1,0:T(8,128)(2,1)}, bf16[2,512,256]{2,1,0:T(8,128)(2,1)}, u32[]{:S(2)}, u32[]{:S(2)}) collective-permute-start(bf16[2,512,256]{2,1,0:T(8,128)(2,1)} %get-tuple-element.42), channel_id=1, source_target_pairs={{0,31},{1,2},{2,1},{3,4},{4,3},{5,6},{6,5},{7,8},{8,7},{9,10},{10,... | collective-permute-start | bytes 1572872 | tf_op jit(solution)/shard_map/ppermute | solution.py:610
  23.6 1.2 add_convert_fusion.3
  24.9 5.0 %collective-permute-start.3 = (bf16[10,80,128]{2,1,0:T(8,128)(2,1)S(1)}, bf16[10,80,128]{2,1,0:T(8,128)(2,1)S(1)}, u32[]{:S(2)}, u32[]{:S(2)}) collective-permute-start(bf16[10,80,128]{2,1,0:T(8,128)(2,1)S(1)} %maximum_select_fusion), channel_id=1, source_target_pairs={{0,31},{1,2},{2,1},{3,4},{4,3},{5,6},{6,5},{7,8},{8,7},{9,10},{10,... | collective-permute-start | bytes 614408 | tf_op jit(solution)/shard_map/ppermute | solution.py:697
  29.9 4.7 %shard_map.112.inner = bf16[5,256,512]{2,1,0:T(8,128)(2,1)S(1)} custom-call(bf16[8,512,256]{2,1,0:T(8,128)(2,1)S(1)} %copy-done.3, bf16[3,3,256,256]{3,2,1,0:T(8,128)(2,1)S(1)} %copy-done.7), custom_call_target="tpu_custom_call" | custom-call | flops 3019898880 | bytes 4194304 | tf_op jit(solution)/shard_map/pallas_call | solution.py:647
  34.7 3.5 %collective-permute-start.4 = (bf16[4,80,128]{2,1,0:T(8,128)(2,1)S(1)}, bf16[4,80,128]{2,1,0:T(8,128)(2,1)S(1)}, u32[]{:S(2)}, u32[]{:S(2)}) collective-permute-start(bf16[4,80,128]{2,1,0:T(8,128)(2,1)S(1)} %pad_maximum_fusion.2), channel_id=1, source_target_pairs={{0,1},{1,0},{2,3},{3,2},{4,5},{5,4},{6,7},{7,6},{8,9},{9,8},{10,11... | collective-permute-start | bytes 245768 | tf_op jit(solution)/shard_map/ppermute | solution.py:699
  38.2 6.1 %shard_map.113 = (bf16[10,256,512]{2,1,0:T(8,128)(2,1)S(1)}, bf16[768,240]{1,0:T(8,128)(2,1)S(1)}, bf16[512,256]{1,0:T(8,128)(2,1)S(1)}) custom-call(s32[1]{0:T(128)} %bitcast.place, bf16[2,512,256]{2,1,0:T(8,128)(2,1)} %collective-permute-done.5.near, bf16[2,512,256]{2,1,0:T(8,128)(2,1)} %collective-permute-done.6.far, bf16[8,512,256]{2,1,0:T(8,128)(2,1)S(1)} %copy-done.3, ...), custom_call_target="tpu_custom_call" | custom-call | flops 3019898880 | bytes 2097152 | tf_op jit(solution)/shard_map/pallas_call | solution.py:656
  44.3 17.5 %shard_map.114 = (bf16[1536,256]{1,0:T(8,128)(2,1)S(1)}, bf16[1536,256]{1,0:T(8,128)(2,1)S(1)}, bf16[8,80,128]{2,1,0:T(8,128)(2,1)S(1)}, bf16[8,80,128]{2,1,0:T(8,128)(2,1)S(1)}) custom-call(s32[1]{0:T(128)} %bitcast.place, bf16[8,80,128]{2,1,0:T(8,128)(2,1)S(1)} %get-tuple-element.48.own, bf16[8,80,128]{2,1,0:T(8,128)(2,1)S(1)} %get-tuple-element.47.edge, ...), custom_call_target="tpu_custom_call" | custom-call | flops 12079595520 | bytes 20971520 | tf_op jit(solution)/shard_map/pallas_call | solution.py:706
  61.8 0.1 collective-permute-start.11
  62.0 2.2 %collective-permute-done.11 = bf16[1536,256]{1,0:T(8,128)(2,1)S(1)} collective-permute-done((bf16[1536,256]{1,0:T(8,128)(2,1)S(1)}, bf16[1536,256]{1,0:T(8,128)(2,1)S(1)}, u32[]{:S(2)}, u32[]{:S(2)}) %collective-permute-start.11) | collective-permute-done | bytes 786464 | tf_op jit(solution)/shard_map/ppermute | solution.py:537
  64.2 0.2 add_convert_fusion
  64.5 3.5 %collective-permute-start.12 = (bf16[384,256]{1,0:T(8,128)(2,1)S(1)}, bf16[384,256]{1,0:T(8,128)(2,1)S(1)}, u32[]{:S(2)}, u32[]{:S(2)}) collective-permute-start(bf16[384,256]{1,0:T(8,128)(2,1)S(1)} %get-tuple-element.44), channel_id=1, source_target_pairs={{0,6},{1,25},{2,4},{3,27},{4,2},{5,29},{6,0},{7,31},{8,14},{9,17},... | collective-permute-start | bytes 589832 | tf_op jit(solution)/shard_map/ppermute | solution.py:560
  67.9 1.2 collective-permute-start.14
  69.1 2.5 %collective-permute-done.12 = bf16[384,256]{1,0:T(8,128)(2,1)S(1)} collective-permute-done((bf16[384,256]{1,0:T(8,128)(2,1)S(1)}, bf16[384,256]{1,0:T(8,128)(2,1)S(1)}, u32[]{:S(2)}, u32[]{:S(2)}) %collective-permute-start.12) | collective-permute-done | bytes 196640 | tf_op jit(solution)/shard_map/ppermute | solution.py:560
  71.6 2.2 %collective-permute-done.14 = bf16[384,256]{1,0:T(8,128)(2,1)S(1)} collective-permute-done((bf16[384,256]{1,0:T(8,128)(2,1)S(1)}, bf16[384,256]{1,0:T(8,128)(2,1)S(1)}, u32[]{:S(2)}, u32[]{:S(2)}) %collective-permute-start.14) | collective-permute-done | bytes 196640 | tf_op jit(solution)/shard_map/ppermute | solution.py:560
  73.8 1.0 collective-permute-done.13
  74.8 0.1 add_convert_fusion.2
  74.9 3.8 %collective-permute-start.15 = (bf16[96,256]{1,0:T(8,128)(2,1)S(1)}, bf16[96,256]{1,0:T(8,128)(2,1)S(1)}, u32[]{:S(2)}, u32[]{:S(2)}) collective-permute-start(bf16[96,256]{1,0:T(8,128)(2,1)S(1)} %get-tuple-element.51), channel_id=1, source_target_pairs={{0,24},{1,7},{2,26},{3,5},{4,28},{5,3},{6,30},{7,1},{8,16},{9,15},... | collective-permute-start | bytes 147464 | tf_op jit(solution)/shard_map/ppermute | solution.py:560
  78.7 0.7 collective-permute-start.16
  79.4 1.5 %collective-permute-done.15 = bf16[96,256]{1,0:T(8,128)(2,1)S(1)} collective-permute-done((bf16[96,256]{1,0:T(8,128)(2,1)S(1)}, bf16[96,256]{1,0:T(8,128)(2,1)S(1)}, u32[]{:S(2)}, u32[]{:S(2)}) %collective-permute-start.15) | collective-permute-done | bytes 49184 | tf_op jit(solution)/shard_map/ppermute | solution.py:560
  80.9 2.8 %collective-permute-done.17 = bf16[96,256]{1,0:T(8,128)(2,1)S(1)} collective-permute-done((bf16[96,256]{1,0:T(8,128)(2,1)S(1)}, bf16[96,256]{1,0:T(8,128)(2,1)S(1)}, u32[]{:S(2)}, u32[]{:S(2)}) %collective-permute-start.17) | collective-permute-done | bytes 49184 | tf_op jit(solution)/shard_map/ppermute | solution.py:560
  83.7 0.2 collective-permute-start.20
  83.9 2.0 %collective-permute-start.19 = (bf16[96,256]{1,0:T(8,128)(2,1)S(1)}, bf16[96,256]{1,0:T(8,128)(2,1)S(1)}, u32[]{:S(2)}, u32[]{:S(2)}) collective-permute-start(bf16[96,256]{1,0:T(8,128)(2,1)S(1)} %add_convert_fusion.5), channel_id=1, source_target_pairs={{0,16},{1,5},{2,18},{3,7},{4,20},{5,1},{6,22},{7,3},{8,24},{9,13},... | collective-permute-start | bytes 147464 | tf_op jit(solution)/shard_map/ppermute | solution.py:560
  85.9 2.3 %collective-permute-start.18 = (bf16[96,256]{1,0:T(8,128)(2,1)S(1)}, bf16[96,256]{1,0:T(8,128)(2,1)S(1)}, u32[]{:S(2)}, u32[]{:S(2)}) collective-permute-start(bf16[96,256]{1,0:T(8,128)(2,1)S(1)} %add_convert_fusion.5), channel_id=1, source_target_pairs={{0,24},{1,7},{2,26},{3,5},{4,28},{5,3},{6,30},{7,1},{8,16},{9,15},... | collective-permute-start | bytes 147464 | tf_op jit(solution)/shard_map/ppermute | solution.py:560
  88.2 0.7 collective-permute-done.19
  88.9 3.0 %collective-permute-done.18 = bf16[96,256]{1,0:T(8,128)(2,1)S(1)} collective-permute-done((bf16[96,256]{1,0:T(8,128)(2,1)S(1)}, bf16[96,256]{1,0:T(8,128)(2,1)S(1)}, u32[]{:S(2)}, u32[]{:S(2)}) %collective-permute-start.18) | collective-permute-done | bytes 49184 | tf_op jit(solution)/shard_map/ppermute | solution.py:560
  92.1 1.5 %collective-permute-start.21 = (bf16[384,256]{1,0:T(8,128)(2,1)S(1)}, bf16[384,256]{1,0:T(8,128)(2,1)}, u32[]{:S(2)}, u32[]{:S(2)}) collective-permute-start(bf16[384,256]{1,0:T(8,128)(2,1)S(1)} %pad_maximum_fusion.1), channel_id=1, source_target_pairs={{0,2},{1,9},{2,0},{3,11},{4,6},{5,13},{6,4},{7,15},{8,10},{9,1},{1... | collective-permute-start | bytes 589832 | tf_op jit(solution)/shard_map/ppermute | solution.py:560
  93.6 1.9 %collective-permute-start.8 = (bf16[8,80,128]{2,1,0:T(8,128)(2,1)S(1)}, bf16[8,80,128]{2,1,0:T(8,128)(2,1)}, u32[]{:S(2)}, u32[]{:S(2)}) collective-permute-start(bf16[8,80,128]{2,1,0:T(8,128)(2,1)S(1)} %get-tuple-element.26), channel_id=1, source_target_pairs={{0,31},{4,3},{8,7},{12,11},{16,15},{20,19},{24,23},{28,27},{3,4},{... | collective-permute-start | bytes 491528 | tf_op jit(solution)/shard_map/ppermute | solution.py:695
  95.5 0.9 collective-permute-start.22
  96.4 0.6 collective-permute-start.7
  97.0 7.0 %collective-permute-done.8 = bf16[8,80,128]{2,1,0:T(8,128)(2,1)} collective-permute-done((bf16[8,80,128]{2,1,0:T(8,128)(2,1)S(1)}, bf16[8,80,128]{2,1,0:T(8,128)(2,1)}, u32[]{:S(2)}, u32[]{:S(2)}) %collective-permute-start.8) | collective-permute-done | bytes 163872 | tf_op jit(solution)/shard_map/ppermute | solution.py:695
  104.0 1.3 %collective-permute-start.9 = (bf16[8,80,128]{2,1,0:T(8,128)(2,1)}, bf16[8,80,128]{2,1,0:T(8,128)(2,1)S(1)}, u32[]{:S(2)}, u32[]{:S(2)}) collective-permute-start(bf16[8,80,128]{2,1,0:T(8,128)(2,1)} %collective-permute-done.8), channel_id=1, source_target_pairs={{3,1},{0,2},{7,5},{4,6},{11,9},{8,10},{15,13},{12,14},{19,17},{16,... | collective-permute-start | bytes 491528 | tf_op jit(solution)/shard_map/ppermute | solution.py:745
  105.4 0.9 constant_dynamic-update-slice_fusion.2
  106.3 0.9 constant_dynamic-update-slice_fusion.1
  107.3 4.6 %collective-permute-done.23 = bf16[384,256]{1,0:T(8,128)(2,1)S(1)} collective-permute-done((bf16[384,256]{1,0:T(8,128)(2,1)S(1)}, bf16[384,256]{1,0:T(8,128)(2,1)S(1)}, u32[]{:S(2)}, u32[]{:S(2)}) %collective-permute-start.23) | collective-permute-done | bytes 196640 | tf_op jit(solution)/shard_map/ppermute | solution.py:560
  112.0 0.1 collective-permute-start.24
  112.0 1.0 broadcast_select_fusion.2.edge
  113.2 1.9 %collective-permute-done.10.theirs = bf16[24,80,128]{2,1,0:T(8,128)(2,1)S(1)} collective-permute-done((bf16[24,80,128]{2,1,0:T(8,128)(2,1)S(1)}, bf16[24,80,128]{2,1,0:T(8,128)(2,1)S(1)}, u32[]{:S(2)}, u32[]{:S(2)}) %collective-permute-start.10) | collective-permute-done | bytes 491552 | tf_op jit(solution)/shard_map/ppermute | solution.py:537
  115.0 4.2 %shard_map.116 = bf16[2560,128]{1,0:T(8,128)(2,1)} custom-call(s32[1]{0:T(128)} %bitcast.place, s32[49]{0:T(128)S(1)} %copy-done.6, bf16[8,80,128]{2,1,0:T(8,128)(2,1)S(1)} %get-tuple-element.25.own, bf16[8,80,128]{2,1,0:T(8,128)(2,1)S(1)} %collective-permute-done.7.partner, bf16[8,80,128]{2,1,0:T(8,128)(2,1)S(1)} %broadcast_select_fusion.2.edge, ...), custom_call_target="tpu_custom_call" | custom-call | flops 150994944 | bytes 4587520 | tf_op jit(solution)/shard_map/pallas_call | solution.py:755
  119.2 4.5 %shard_map.115 = f32[3584,128]{1,0:T(8,128)} custom-call(s32[1]{0:T(128)} %bitcast.place, s32[49]{0:T(128)S(1)} %copy-done.6, bf16[8,80,128]{2,1,0:T(8,128)(2,1)S(1)} %get-tuple-element.25.own, bf16[8,80,128]{2,1,0:T(8,128)(2,1)S(1)} %collective-permute-done.7.partner, bf16[8,80,128]{2,1,0:T(8,128)(2,1)S(1)} %broadcast_select_fusion.2.edge, ...), custom_call_target="tpu_custom_call" | custom-call | flops 150994944 | bytes 9175040 | tf_op jit(solution)/shard_map/pallas_call | solution.py:763
  123.7 1.9 %shard_map.117 = (f32[2304,256]{1,0:T(8,128)}, f32[720,256]{1,0:T(8,128)}) custom-call(s32[1]{0:T(128)} %bitcast.place, bf16[1536,256]{1,0:T(8,128)(2,1)S(1)} %constant_dynamic-update-slice_fusion.value, bf16[1536,256]{1,0:T(8,128)(2,1)S(1)} %collective-permute-done.24.other), custom_call_target="tpu_custom_call" | custom-call | flops 1 | bytes 4718592 | tf_op jit(solution)/shard_map/pallas_call | solution.py:774
  (54 shorter events, 0.6 us)
Async XLA Ops:
  0.6 16.0 %copy-start.3 = (bf16[8,512,256]{2,1,0:T(8,128)(2,1)S(1)}, bf16[8,512,256]{2,1,0:T(8,128)(2,1)}, u32[]{:S(2)}) copy-start(bf16[8,512,256]{2,1,0:T(8,128)(2,1)} %upstream.3) | copy-start | bytes 6291460
  7.7 2.3 %collective-permute-start = (bf16[24,80,128]{2,1,0:T(8,128)(2,1)}, bf16[24,80,128]{2,1,0:T(8,128)(2,1)S(1)}, u32[]{:S(2)}, u32[]{:S(2)}) collective-permute-start(bf16[24,80,128]{2,1,0:T(8,128)(2,1)} %get-tuple-element.21), channel_id=1, source_target_pairs={{0,1},{1,0},{2,3},{3,2},{4,5},{5,4},{6,7},{7,6},{8,9},{9,8},{10,11... | collective-permute-start | bytes 1474568 | tf_op jit(solution)/shard_map/ppermute | solution.py:537
  11.1 2.1 %copy-start.10 = (bf16[24,80,128]{2,1,0:T(8,128)(2,1)}, bf16[24,80,128]{2,1,0:T(8,128)(2,1)S(1)}, u32[]{:S(2)}) copy-start(bf16[24,80,128]{2,1,0:T(8,128)(2,1)S(1)} %add_convert_fusion.1) | copy-start | bytes 1474564
  11.9 11.7 %collective-permute-start.2 = (bf16[8,80,128]{2,1,0:T(8,128)(2,1)}, bf16[8,80,128]{2,1,0:T(8,128)(2,1)}, u32[]{:S(2)}, u32[]{:S(2)}) collective-permute-start(bf16[8,80,128]{2,1,0:T(8,128)(2,1)} %get-tuple-element.49), channel_id=1, source_target_pairs={{1,3},{2,0},{5,7},{6,4},{9,11},{10,8},{13,15},{14,12},{17,19},{18,... | collective-permute-start | bytes 491528 | tf_op jit(solution)/shard_map/ppermute | solution.py:674
  13.2 16.8 %copy-start.7 = (bf16[3,3,256,256]{3,2,1,0:T(8,128)(2,1)S(1)}, bf16[3,3,256,256]{3,2,1,0:T(8,128)(2,1)}, u32[]{:S(2)}) copy-start(bf16[3,3,256,256]{3,2,1,0:T(8,128)(2,1)} %weight.3) | copy-start | bytes 3538948
  13.2 10.4 %collective-permute-start.1 = (bf16[8,80,128]{2,1,0:T(8,128)(2,1)S(1)}, bf16[8,80,128]{2,1,0:T(8,128)(2,1)}, u32[]{:S(2)}, u32[]{:S(2)}) collective-permute-start(bf16[8,80,128]{2,1,0:T(8,128)(2,1)S(1)} %get-tuple-element.50), channel_id=1, source_target_pairs={{0,2},{1,3},{2,0},{3,1},{4,6},{5,7},{6,4},{7,5},{8,10},{9,11},{10,... | collective-permute-start | bytes 491528 | tf_op jit(solution)/shard_map/ppermute | solution.py:537
  17.7 20.4 %collective-permute-start.6 = (bf16[2,512,256]{2,1,0:T(8,128)(2,1)}, bf16[2,512,256]{2,1,0:T(8,128)(2,1)}, u32[]{:S(2)}, u32[]{:S(2)}) collective-permute-start(bf16[2,512,256]{2,1,0:T(8,128)(2,1)} %get-tuple-element.42), channel_id=1, source_target_pairs={{0,31},{1,2},{2,1},{3,4},{4,3},{5,6},{6,5},{7,8},{8,7},{9,10},{10,... | collective-permute-start | bytes 1572872 | tf_op jit(solution)/shard_map/ppermute | solution.py:610
  23.5 14.6 %collective-permute-start.5 = (bf16[2,512,256]{2,1,0:T(8,128)(2,1)}, bf16[2,512,256]{2,1,0:T(8,128)(2,1)}, u32[]{:S(2)}, u32[]{:S(2)}) collective-permute-start(bf16[2,512,256]{2,1,0:T(8,128)(2,1)} %get-tuple-element.43), channel_id=1, source_target_pairs={{0,1},{1,0},{2,3},{3,2},{4,5},{5,4},{6,7},{7,6},{8,9},{9,8},{10,11... | collective-permute-start | bytes 1572872 | tf_op jit(solution)/shard_map/ppermute | solution.py:611
  24.9 13.3 %copy-start.8 = (bf16[3,3,80,256]{3,2,1,0:T(8,128)(2,1)S(1)}, bf16[3,3,80,256]{3,2,1,0:T(8,128)(2,1)}, u32[]{:S(2)}) copy-start(bf16[3,3,80,256]{3,2,1,0:T(8,128)(2,1)} %param.13) | copy-start | bytes 1105924
  24.9 13.3 %copy-start.9 = (s32[8,112]{1,0:T(8,128)S(1)}, s32[8,112]{1,0:T(8,128)}, u32[]{:S(2)}) copy-start(s32[8,112]{1,0:T(8,128)} %ranges.1) | copy-start | bytes 10756
  24.9 9.8 %collective-permute-start.3 = (bf16[10,80,128]{2,1,0:T(8,128)(2,1)S(1)}, bf16[10,80,128]{2,1,0:T(8,128)(2,1)S(1)}, u32[]{:S(2)}, u32[]{:S(2)}) collective-permute-start(bf16[10,80,128]{2,1,0:T(8,128)(2,1)S(1)} %maximum_select_fusion), channel_id=1, source_target_pairs={{0,31},{1,2},{2,1},{3,4},{4,3},{5,6},{6,5},{7,8},{8,7},{9,10},{10,... | collective-permute-start | bytes 614408 | tf_op jit(solution)/shard_map/ppermute | solution.py:697
  34.7 9.6 %collective-permute-start.4 = (bf16[4,80,128]{2,1,0:T(8,128)(2,1)S(1)}, bf16[4,80,128]{2,1,0:T(8,128)(2,1)S(1)}, u32[]{:S(2)}, u32[]{:S(2)}) collective-permute-start(bf16[4,80,128]{2,1,0:T(8,128)(2,1)S(1)} %pad_maximum_fusion.2), channel_id=1, source_target_pairs={{0,1},{1,0},{2,3},{3,2},{4,5},{5,4},{6,7},{7,6},{8,9},{9,8},{10,11... | collective-permute-start | bytes 245768 | tf_op jit(solution)/shard_map/ppermute | solution.py:699
  38.2 6.2 %copy-start.4 = (bf16[8,512,256]{2,1,0:T(8,128)(2,1)S(1)}, bf16[8,512,256]{2,1,0:T(8,128)(2,1)}, u32[]{:S(2)}) copy-start(bf16[8,512,256]{2,1,0:T(8,128)(2,1)} %upstream.3) | copy-start | bytes 6291460
  61.8 2.3 %collective-permute-start.11 = (bf16[1536,256]{1,0:T(8,128)(2,1)S(1)}, bf16[1536,256]{1,0:T(8,128)(2,1)S(1)}, u32[]{:S(2)}, u32[]{:S(2)}) collective-permute-start(bf16[1536,256]{1,0:T(8,128)(2,1)S(1)} %get-tuple-element.31), channel_id=1, source_target_pairs={{0,1},{1,0},{2,3},{3,2},{4,5},{5,4},{6,7},{7,6},{8,9},{9,8},{10,11... | collective-permute-start | bytes 2359304 | tf_op jit(solution)/shard_map/ppermute | solution.py:537
  64.5 7.1 %collective-permute-start.12 = (bf16[384,256]{1,0:T(8,128)(2,1)S(1)}, bf16[384,256]{1,0:T(8,128)(2,1)S(1)}, u32[]{:S(2)}, u32[]{:S(2)}) collective-permute-start(bf16[384,256]{1,0:T(8,128)(2,1)S(1)} %get-tuple-element.44), channel_id=1, source_target_pairs={{0,6},{1,25},{2,4},{3,27},{4,2},{5,29},{6,0},{7,31},{8,14},{9,17},... | collective-permute-start | bytes 589832 | tf_op jit(solution)/shard_map/ppermute | solution.py:560
  67.9 5.9 %collective-permute-start.14 = (bf16[384,256]{1,0:T(8,128)(2,1)S(1)}, bf16[384,256]{1,0:T(8,128)(2,1)S(1)}, u32[]{:S(2)}, u32[]{:S(2)}) collective-permute-start(bf16[384,256]{1,0:T(8,128)(2,1)S(1)} %get-tuple-element.45), channel_id=1, source_target_pairs={{0,4},{1,17},{2,6},{3,19},{4,0},{5,21},{6,2},{7,23},{8,12},{9,25},... | collective-permute-start | bytes 589832 | tf_op jit(solution)/shard_map/ppermute | solution.py:560
  69.1 5.7 %collective-permute-start.13 = (bf16[384,256]{1,0:T(8,128)(2,1)S(1)}, bf16[384,256]{1,0:T(8,128)(2,1)S(1)}, u32[]{:S(2)}, u32[]{:S(2)}) collective-permute-start(bf16[384,256]{1,0:T(8,128)(2,1)S(1)} %get-tuple-element.46), channel_id=1, source_target_pairs={{0,2},{1,9},{2,0},{3,11},{4,6},{5,13},{6,4},{7,15},{8,10},{9,1},{1... | collective-permute-start | bytes 589832 | tf_op jit(solution)/shard_map/ppermute | solution.py:560
  74.9 6.0 %collective-permute-start.15 = (bf16[96,256]{1,0:T(8,128)(2,1)S(1)}, bf16[96,256]{1,0:T(8,128)(2,1)S(1)}, u32[]{:S(2)}, u32[]{:S(2)}) collective-permute-start(bf16[96,256]{1,0:T(8,128)(2,1)S(1)} %get-tuple-element.51), channel_id=1, source_target_pairs={{0,24},{1,7},{2,26},{3,5},{4,28},{5,3},{6,30},{7,1},{8,16},{9,15},... | collective-permute-start | bytes 147464 | tf_op jit(solution)/shard_map/ppermute | solution.py:560
  78.7 5.0 %collective-permute-start.17 = (bf16[96,256]{1,0:T(8,128)(2,1)S(1)}, bf16[96,256]{1,0:T(8,128)(2,1)S(1)}, u32[]{:S(2)}, u32[]{:S(2)}) collective-permute-start(bf16[96,256]{1,0:T(8,128)(2,1)S(1)} %get-tuple-element.52), channel_id=1, source_target_pairs={{0,16},{1,5},{2,18},{3,7},{4,20},{5,1},{6,22},{7,3},{8,24},{9,13},... | collective-permute-start | bytes 147464 | tf_op jit(solution)/shard_map/ppermute | solution.py:560
  78.7 5.0 %collective-permute-start.16 = (bf16[96,256]{1,0:T(8,128)(2,1)S(1)}, bf16[96,256]{1,0:T(8,128)(2,1)S(1)}, u32[]{:S(2)}, u32[]{:S(2)}) collective-permute-start(bf16[96,256]{1,0:T(8,128)(2,1)S(1)} %get-tuple-element.53), channel_id=1, source_target_pairs={{0,8},{1,3},{2,10},{3,1},{4,12},{5,7},{6,14},{7,5},{8,0},{9,11},{1... | collective-permute-start | bytes 147464 | tf_op jit(solution)/shard_map/ppermute | solution.py:560
  83.7 4.5 %collective-permute-start.20 = (bf16[96,256]{1,0:T(8,128)(2,1)S(1)}, bf16[96,256]{1,0:T(8,128)(2,1)S(1)}, u32[]{:S(2)}, u32[]{:S(2)}) collective-permute-start(bf16[96,256]{1,0:T(8,128)(2,1)S(1)} %add_convert_fusion.5), channel_id=1, source_target_pairs={{0,8},{1,3},{2,10},{3,1},{4,12},{5,7},{6,14},{7,5},{8,0},{9,11},{1... | collective-permute-start | bytes 147464 | tf_op jit(solution)/shard_map/ppermute | solution.py:560
  83.9 5.0 %collective-permute-start.19 = (bf16[96,256]{1,0:T(8,128)(2,1)S(1)}, bf16[96,256]{1,0:T(8,128)(2,1)S(1)}, u32[]{:S(2)}, u32[]{:S(2)}) collective-permute-start(bf16[96,256]{1,0:T(8,128)(2,1)S(1)} %add_convert_fusion.5), channel_id=1, source_target_pairs={{0,16},{1,5},{2,18},{3,7},{4,20},{5,1},{6,22},{7,3},{8,24},{9,13},... | collective-permute-start | bytes 147464 | tf_op jit(solution)/shard_map/ppermute | solution.py:560
  85.9 6.0 %collective-permute-start.18 = (bf16[96,256]{1,0:T(8,128)(2,1)S(1)}, bf16[96,256]{1,0:T(8,128)(2,1)S(1)}, u32[]{:S(2)}, u32[]{:S(2)}) collective-permute-start(bf16[96,256]{1,0:T(8,128)(2,1)S(1)} %add_convert_fusion.5), channel_id=1, source_target_pairs={{0,24},{1,7},{2,26},{3,5},{4,28},{5,3},{6,30},{7,1},{8,16},{9,15},... | collective-permute-start | bytes 147464 | tf_op jit(solution)/shard_map/ppermute | solution.py:560
  91.9 23.1 %copy-start = (f32[129,32,128]{2,1,0:T(8,128)S(1)}, f32[129,32,128]{2,1,0:T(8,128)}, u32[]{:S(2)}) copy-start(f32[129,32,128]{2,1,0:T(8,128)} %get-tuple-element.29.probs_t) | copy-start | bytes 6340612
  92.0 23.1 %copy-start.6 = (s32[49]{0:T(128)S(1)}, s32[49]{0:T(128)}, u32[]{:S(2)}) copy-start(s32[49]{0:T(128)} %get-tuple-element.19.begins) | copy-start | bytes 592
  92.1 13.3 %collective-permute-start.21 = (bf16[384,256]{1,0:T(8,128)(2,1)S(1)}, bf16[384,256]{1,0:T(8,128)(2,1)}, u32[]{:S(2)}, u32[]{:S(2)}) collective-permute-start(bf16[384,256]{1,0:T(8,128)(2,1)S(1)} %pad_maximum_fusion.1), channel_id=1, source_target_pairs={{0,2},{1,9},{2,0},{3,11},{4,6},{5,13},{6,4},{7,15},{8,10},{9,1},{1... | collective-permute-start | bytes 589832 | tf_op jit(solution)/shard_map/ppermute | solution.py:560
  93.6 10.4 %collective-permute-start.8 = (bf16[8,80,128]{2,1,0:T(8,128)(2,1)S(1)}, bf16[8,80,128]{2,1,0:T(8,128)(2,1)}, u32[]{:S(2)}, u32[]{:S(2)}) collective-permute-start(bf16[8,80,128]{2,1,0:T(8,128)(2,1)S(1)} %get-tuple-element.26), channel_id=1, source_target_pairs={{0,31},{4,3},{8,7},{12,11},{16,15},{20,19},{24,23},{28,27},{3,4},{... | collective-permute-start | bytes 491528 | tf_op jit(solution)/shard_map/ppermute | solution.py:695
  95.5 10.8 %collective-permute-start.22 = (bf16[384,256]{1,0:T(8,128)(2,1)S(1)}, bf16[384,256]{1,0:T(8,128)(2,1)}, u32[]{:S(2)}, u32[]{:S(2)}) collective-permute-start(bf16[384,256]{1,0:T(8,128)(2,1)S(1)} %pad_maximum_fusion.1), channel_id=1, source_target_pairs={{0,4},{1,17},{2,6},{3,19},{4,0},{5,21},{6,2},{7,23},{8,12},{9,25},... | collective-permute-start | bytes 589832 | tf_op jit(solution)/shard_map/ppermute | solution.py:560
  96.4 16.6 %collective-permute-start.7 = (bf16[8,80,128]{2,1,0:T(8,128)(2,1)S(1)}, bf16[8,80,128]{2,1,0:T(8,128)(2,1)S(1)}, u32[]{:S(2)}, u32[]{:S(2)}) collective-permute-start(bf16[8,80,128]{2,1,0:T(8,128)(2,1)S(1)} %get-tuple-element.25.own), channel_id=1, source_target_pairs={{0,2},{1,3},{2,0},{3,1},{4,6},{5,7},{6,4},{7,5},{8,10},{9,11},{10,... | collective-permute-start | bytes 491528 | tf_op jit(solution)/shard_map/ppermute | solution.py:537
  104.0 8.0 %collective-permute-start.9 = (bf16[8,80,128]{2,1,0:T(8,128)(2,1)}, bf16[8,80,128]{2,1,0:T(8,128)(2,1)S(1)}, u32[]{:S(2)}, u32[]{:S(2)}) collective-permute-start(bf16[8,80,128]{2,1,0:T(8,128)(2,1)} %collective-permute-done.8), channel_id=1, source_target_pairs={{3,1},{0,2},{7,5},{4,6},{11,9},{8,10},{15,13},{12,14},{19,17},{16,... | collective-permute-start | bytes 491528 | tf_op jit(solution)/shard_map/ppermute | solution.py:745
  105.3 6.6 %collective-permute-start.23 = (bf16[384,256]{1,0:T(8,128)(2,1)S(1)}, bf16[384,256]{1,0:T(8,128)(2,1)S(1)}, u32[]{:S(2)}, u32[]{:S(2)}) collective-permute-start(bf16[384,256]{1,0:T(8,128)(2,1)S(1)} %pad_maximum_fusion.1), channel_id=1, source_target_pairs={{0,6},{1,25},{2,4},{3,27},{4,2},{5,29},{6,0},{7,31},{8,14},{9,17},... | collective-permute-start | bytes 589832 | tf_op jit(solution)/shard_map/ppermute | solution.py:560
  112.0 11.7 %collective-permute-start.24 = (bf16[1536,256]{1,0:T(8,128)(2,1)S(1)}, bf16[1536,256]{1,0:T(8,128)(2,1)S(1)}, u32[]{:S(2)}, u32[]{:S(2)}) collective-permute-start(bf16[1536,256]{1,0:T(8,128)(2,1)S(1)} %constant_dynamic-update-slice_fusion.value), channel_id=1, source_target_pairs={{0,1},{1,0},{2,3},{3,2},{4,5},{5,4},{6,7},{7,6},{8,9},{9,8},{10,11... | collective-permute-start | bytes 2359304 | tf_op jit(solution)/shard_map/ppermute | solution.py:537
  113.0 6.2 %copy-start.2 = (f32[3584,128]{1,0:T(8,128)S(1)}, f32[3584,128]{1,0:T(8,128)}, u32[]{:S(2)}) copy-start(f32[3584,128]{1,0:T(8,128)} %get-tuple-element.27.probs) | copy-start | bytes 5505028
  113.1 1.9 %collective-permute-start.10 = (bf16[24,80,128]{2,1,0:T(8,128)(2,1)S(1)}, bf16[24,80,128]{2,1,0:T(8,128)(2,1)S(1)}, u32[]{:S(2)}, u32[]{:S(2)}) collective-permute-start(bf16[24,80,128]{2,1,0:T(8,128)(2,1)S(1)} %pad_maximum_fusion), channel_id=1, source_target_pairs={{0,1},{1,0},{2,3},{3,2},{4,5},{5,4},{6,7},{7,6},{8,9},{9,8},{10,11... | collective-permute-start | bytes 1474568 | tf_op jit(solution)/shard_map/ppermute | solution.py:537
  115.0 4.2 %copy-start.1 = (f32[129,32,128]{2,1,0:T(8,128)S(1)}, f32[129,32,128]{2,1,0:T(8,128)}, u32[]{:S(2)}) copy-start(f32[129,32,128]{2,1,0:T(8,128)} %get-tuple-element.28.context_t) | copy-start | bytes 6340612
  115.0 4.2 %copy-start.5 = (s32[1,32,128]{2,1,0:T(8,128)S(1)}, s32[1,32,128]{2,1,0:T(8,128)}, u32[]{:S(2)}) copy-start(s32[1,32,128]{2,1,0:T(8,128)} %param.10) | copy-start | bytes 49156

commit v6 on v5

--- a/solution.py
+++ b/solution.py
@@ -624,8 +624,8 @@
         ],
         [
             pltpu.VMEM((bins * rows, columns), F32),
-            pltpu.VMEM((bins * (rows + SLACK), columns), F32),
-            pltpu.VMEM((channels * (rows + SLACK), columns), F32),
+            pltpu.VMEM(((bins + 1) * (rows + SLACK), columns), F32),
+            pltpu.VMEM(((channels + 1) * (rows + SLACK), columns), F32),
             pltpu.VMEM((turned, LANES), F32),
             pltpu.VMEM((turned, LANES), F32),
             pltpu.SemaphoreType.DMA((3,)),
@@ -755,7 +755,7 @@
     context_grad = call(
         functools.partial(context_kernel, rows),
         jax.ShapeDtypeStruct((channels * rows, columns), BF16),
-        scratch + [pltpu.VMEM((channels * (rows + SLACK), columns), F32)],
+        scratch + [pltpu.VMEM(((channels + 1) * (rows + SLACK), columns), F32)],
         [smem()] * 2 + [vmem()] * 5,
         cell_flops,
         10 * bins * rows * columns,
@@ -763,7 +763,7 @@
     logit_grad = call(
         functools.partial(logit_kernel, rows),
         jax.ShapeDtypeStruct((bins * rows, columns), F32),
-        scratch + [pltpu.VMEM((bins * (rows + SLACK), columns), F32)],
+        scratch + [pltpu.VMEM(((bins + 1) * (rows + SLACK), columns), F32)],
         [smem()] * 2 + [vmem()] * 7,
         cell_flops,
         20 * bins * rows * columns,

time: 126 us -> 126 us (level)
  no operation moved by 1% of the time
where the time goes in v6:
time: 126 us
  Pallas kernels  45.9 us (36%)
  starting transfers between devices  39.7 us (32%)
  waiting for transfers between devices  31.2 us (25%)
  other arithmetic  4.99 us (4%)
  local copies, waits for them, and re-layouts  2.79 us (2%)
    ppermute x12, waiting for transfers between devices, sent(): return lax.ppermute(part, 'blk', to)  18.3 us
    pallas_call x1, Pallas kernels, shards(): call(grid_kernel, [jax.ShapeDtypeStruct((grad_rows // 2, hidden), BF16),...  17.5 us
    ppermute x12, starting transfers between devices, sent(): return lax.ppermute(part, 'blk', to)  16 us
    pallas_call x1, Pallas kernels, shards(): call(functools.partial(pool_kernel, rows, sight, blocks * sector), [jax.S...  7.03 us
    ppermute x1, waiting for transfers between devices, to_next(): return lax.ppermute(value, 'blk', pairs)  7.01 us
    pallas_call x1, Pallas kernels, shards(): call(outer_acts_kernel, [jax.ShapeDtypeStruct((sector + 2, hidden, length...  6.13 us
    ppermute x1, starting transfers between devices, shards(): far_grad = lax.ppermute(ends(out_grad, False), 'blk', off_chip)  5.82 us
    ppermute x6, waiting for transfers between devices, swapped(): return lax.ppermute(value, 'blk', [(i, i ^ mask) for i in range(blocks)])  5.8 us
  transfers between devices with their start and end apart: 25, of which 12 were waited for; matrix products, arithmetic and copies ran while one was open for 4% of the time, Pallas kernels for 16%

profile of v6, /device:TPU:0, one launch (start us, length us, event | category | flops | bytes accessed | tf_op | source)
XLA Modules:
  0.0 125.6 jit_solution(2558908826514527139)
XLA Ops:
  0.6 7.0 %shard_map.111 = (f32[3584,128]{1,0:T(8,128)}, f32[129,32,128]{2,1,0:T(8,128)}, f32[129,32,128]{2,1,0:T(8,128)}, bf16[24,80,128]{2,1,0:T(8,128)(2,1)}, bf16[24,80,128]{2,1,0:T(8,128)(2,1)}, /*index=5*/s32[49]{0:T(128)}) custom-call(s32[1]{0:T(128)} %bitcast.place, s32[8,128]{1,0:T(8,128)} %az_map.1, f32[3584,128]{1,0:T(8,128)} %bitcast.14, ...), custom_call_target="tpu_custom_call" | custom-call | flops 150994944 | bytes 9175040 | tf_op jit(solution)/shard_map/pallas_call | solution.py:615
  7.7 0.6 collective-permute-start
  8.2 1.7 %collective-permute-done = bf16[24,80,128]{2,1,0:T(8,128)(2,1)S(1)} collective-permute-done((bf16[24,80,128]{2,1,0:T(8,128)(2,1)}, bf16[24,80,128]{2,1,0:T(8,128)(2,1)S(1)}, u32[]{:S(2)}, u32[]{:S(2)}) %collective-permute-start) | collective-permute-done | bytes 491552 | tf_op jit(solution)/shard_map/ppermute | solution.py:537
  9.9 1.2 add_convert_fusion.1
  11.1 0.8 fusion
  11.9 1.3 %collective-permute-start.2 = (bf16[8,80,128]{2,1,0:T(8,128)(2,1)}, bf16[8,80,128]{2,1,0:T(8,128)(2,1)}, u32[]{:S(2)}, u32[]{:S(2)}) collective-permute-start(bf16[8,80,128]{2,1,0:T(8,128)(2,1)} %get-tuple-element.49), channel_id=1, source_target_pairs={{1,3},{2,0},{5,7},{6,4},{9,11},{10,8},{13,15},{14,12},{17,19},{18,... | collective-permute-start | bytes 491528 | tf_op jit(solution)/shard_map/ppermute | solution.py:674
  13.2 3.5 %collective-permute-start.1 = (bf16[8,80,128]{2,1,0:T(8,128)(2,1)S(1)}, bf16[8,80,128]{2,1,0:T(8,128)(2,1)}, u32[]{:S(2)}, u32[]{:S(2)}) collective-permute-start(bf16[8,80,128]{2,1,0:T(8,128)(2,1)S(1)} %get-tuple-element.50), channel_id=1, source_target_pairs={{0,2},{1,3},{2,0},{3,1},{4,6},{5,7},{6,4},{7,5},{8,10},{9,11},{10,... | collective-permute-start | bytes 491528 | tf_op jit(solution)/shard_map/ppermute | solution.py:537
  16.7 1.0 broadcast_select_fusion
  17.7 5.8 %collective-permute-start.6 = (bf16[2,512,256]{2,1,0:T(8,128)(2,1)}, bf16[2,512,256]{2,1,0:T(8,128)(2,1)}, u32[]{:S(2)}, u32[]{:S(2)}) collective-permute-start(bf16[2,512,256]{2,1,0:T(8,128)(2,1)} %get-tuple-element.42), channel_id=1, source_target_pairs={{0,31},{1,2},{2,1},{3,4},{4,3},{5,6},{6,5},{7,8},{8,7},{9,10},{10,... | collective-permute-start | bytes 1572872 | tf_op jit(solution)/shard_map/ppermute | solution.py:610
  23.6 1.2 add_convert_fusion.3
  24.9 5.0 %collective-permute-start.3 = (bf16[10,80,128]{2,1,0:T(8,128)(2,1)S(1)}, bf16[10,80,128]{2,1,0:T(8,128)(2,1)S(1)}, u32[]{:S(2)}, u32[]{:S(2)}) collective-permute-start(bf16[10,80,128]{2,1,0:T(8,128)(2,1)S(1)} %maximum_select_fusion), channel_id=1, source_target_pairs={{0,31},{1,2},{2,1},{3,4},{4,3},{5,6},{6,5},{7,8},{8,7},{9,10},{10,... | collective-permute-start | bytes 614408 | tf_op jit(solution)/shard_map/ppermute | solution.py:697
  29.9 4.7 %shard_map.112.inner = bf16[5,256,512]{2,1,0:T(8,128)(2,1)S(1)} custom-call(bf16[8,512,256]{2,1,0:T(8,128)(2,1)S(1)} %copy-done.3, bf16[3,3,256,256]{3,2,1,0:T(8,128)(2,1)S(1)} %copy-done.7), custom_call_target="tpu_custom_call" | custom-call | flops 3019898880 | bytes 4194304 | tf_op jit(solution)/shard_map/pallas_call | solution.py:647
  34.7 3.5 %collective-permute-start.4 = (bf16[4,80,128]{2,1,0:T(8,128)(2,1)S(1)}, bf16[4,80,128]{2,1,0:T(8,128)(2,1)S(1)}, u32[]{:S(2)}, u32[]{:S(2)}) collective-permute-start(bf16[4,80,128]{2,1,0:T(8,128)(2,1)S(1)} %pad_maximum_fusion.2), channel_id=1, source_target_pairs={{0,1},{1,0},{2,3},{3,2},{4,5},{5,4},{6,7},{7,6},{8,9},{9,8},{10,11... | collective-permute-start | bytes 245768 | tf_op jit(solution)/shard_map/ppermute | solution.py:699
  38.2 6.1 %shard_map.113 = (bf16[10,256,512]{2,1,0:T(8,128)(2,1)S(1)}, bf16[768,240]{1,0:T(8,128)(2,1)S(1)}, bf16[512,256]{1,0:T(8,128)(2,1)S(1)}) custom-call(s32[1]{0:T(128)} %bitcast.place, bf16[2,512,256]{2,1,0:T(8,128)(2,1)} %collective-permute-done.5.near, bf16[2,512,256]{2,1,0:T(8,128)(2,1)} %collective-permute-done.6.far, bf16[8,512,256]{2,1,0:T(8,128)(2,1)S(1)} %copy-done.3, ...), custom_call_target="tpu_custom_call" | custom-call | flops 3019898880 | bytes 2097152 | tf_op jit(solution)/shard_map/pallas_call | solution.py:656
  44.3 17.5 %shard_map.114 = (bf16[1536,256]{1,0:T(8,128)(2,1)S(1)}, bf16[1536,256]{1,0:T(8,128)(2,1)S(1)}, bf16[8,80,128]{2,1,0:T(8,128)(2,1)S(1)}, bf16[8,80,128]{2,1,0:T(8,128)(2,1)S(1)}) custom-call(s32[1]{0:T(128)} %bitcast.place, bf16[8,80,128]{2,1,0:T(8,128)(2,1)S(1)} %get-tuple-element.48.own, bf16[8,80,128]{2,1,0:T(8,128)(2,1)S(1)} %get-tuple-element.47.edge, ...), custom_call_target="tpu_custom_call" | custom-call | flops 12079595520 | bytes 20971520 | tf_op jit(solution)/shard_map/pallas_call | solution.py:706
  61.8 0.1 collective-permute-start.11
  62.0 2.2 %collective-permute-done.11 = bf16[1536,256]{1,0:T(8,128)(2,1)S(1)} collective-permute-done((bf16[1536,256]{1,0:T(8,128)(2,1)S(1)}, bf16[1536,256]{1,0:T(8,128)(2,1)S(1)}, u32[]{:S(2)}, u32[]{:S(2)}) %collective-permute-start.11) | collective-permute-done | bytes 786464 | tf_op jit(solution)/shard_map/ppermute | solution.py:537
  64.2 0.2 add_convert_fusion
  64.5 3.5 %collective-permute-start.12 = (bf16[384,256]{1,0:T(8,128)(2,1)S(1)}, bf16[384,256]{1,0:T(8,128)(2,1)S(1)}, u32[]{:S(2)}, u32[]{:S(2)}) collective-permute-start(bf16[384,256]{1,0:T(8,128)(2,1)S(1)} %get-tuple-element.44), channel_id=1, source_target_pairs={{0,6},{1,25},{2,4},{3,27},{4,2},{5,29},{6,0},{7,31},{8,14},{9,17},... | collective-permute-start | bytes 589832 | tf_op jit(solution)/shard_map/ppermute | solution.py:560
  67.9 1.2 collective-permute-start.14
  69.1 2.5 %collective-permute-done.12 = bf16[384,256]{1,0:T(8,128)(2,1)S(1)} collective-permute-done((bf16[384,256]{1,0:T(8,128)(2,1)S(1)}, bf16[384,256]{1,0:T(8,128)(2,1)S(1)}, u32[]{:S(2)}, u32[]{:S(2)}) %collective-permute-start.12) | collective-permute-done | bytes 196640 | tf_op jit(solution)/shard_map/ppermute | solution.py:560
  71.6 2.2 %collective-permute-done.14 = bf16[384,256]{1,0:T(8,128)(2,1)S(1)} collective-permute-done((bf16[384,256]{1,0:T(8,128)(2,1)S(1)}, bf16[384,256]{1,0:T(8,128)(2,1)S(1)}, u32[]{:S(2)}, u32[]{:S(2)}) %collective-permute-start.14) | collective-permute-done | bytes 196640 | tf_op jit(solution)/shard_map/ppermute | solution.py:560
  73.8 1.0 collective-permute-done.13
  74.8 0.1 add_convert_fusion.2
  74.9 3.8 %collective-permute-start.15 = (bf16[96,256]{1,0:T(8,128)(2,1)S(1)}, bf16[96,256]{1,0:T(8,128)(2,1)S(1)}, u32[]{:S(2)}, u32[]{:S(2)}) collective-permute-start(bf16[96,256]{1,0:T(8,128)(2,1)S(1)} %get-tuple-element.51), channel_id=1, source_target_pairs={{0,24},{1,7},{2,26},{3,5},{4,28},{5,3},{6,30},{7,1},{8,16},{9,15},... | collective-permute-start | bytes 147464 | tf_op jit(solution)/shard_map/ppermute | solution.py:560
  78.7 0.7 collective-permute-start.16
  79.4 1.5 %collective-permute-done.15 = bf16[96,256]{1,0:T(8,128)(2,1)S(1)} collective-permute-done((bf16[96,256]{1,0:T(8,128)(2,1)S(1)}, bf16[96,256]{1,0:T(8,128)(2,1)S(1)}, u32[]{:S(2)}, u32[]{:S(2)}) %collective-permute-start.15) | collective-permute-done | bytes 49184 | tf_op jit(solution)/shard_map/ppermute | solution.py:560
  80.9 2.8 %collective-permute-done.17 = bf16[96,256]{1,0:T(8,128)(2,1)S(1)} collective-permute-done((bf16[96,256]{1,0:T(8,128)(2,1)S(1)}, bf16[96,256]{1,0:T(8,128)(2,1)S(1)}, u32[]{:S(2)}, u32[]{:S(2)}) %collective-permute-start.17) | collective-permute-done | bytes 49184 | tf_op jit(solution)/shard_map/ppermute | solution.py:560
  83.7 0.2 collective-permute-start.20
  83.9 2.0 %collective-permute-start.19 = (bf16[96,256]{1,0:T(8,128)(2,1)S(1)}, bf16[96,256]{1,0:T(8,128)(2,1)S(1)}, u32[]{:S(2)}, u32[]{:S(2)}) collective-permute-start(bf16[96,256]{1,0:T(8,128)(2,1)S(1)} %add_convert_fusion.5), channel_id=1, source_target_pairs={{0,16},{1,5},{2,18},{3,7},{4,20},{5,1},{6,22},{7,3},{8,24},{9,13},... | collective-permute-start | bytes 147464 | tf_op jit(solution)/shard_map/ppermute | solution.py:560
  85.9 2.3 %collective-permute-start.18 = (bf16[96,256]{1,0:T(8,128)(2,1)S(1)}, bf16[96,256]{1,0:T(8,128)(2,1)S(1)}, u32[]{:S(2)}, u32[]{:S(2)}) collective-permute-start(bf16[96,256]{1,0:T(8,128)(2,1)S(1)} %add_convert_fusion.5), channel_id=1, source_target_pairs={{0,24},{1,7},{2,26},{3,5},{4,28},{5,3},{6,30},{7,1},{8,16},{9,15},... | collective-permute-start | bytes 147464 | tf_op jit(solution)/shard_map/ppermute | solution.py:560
  88.2 0.7 collective-permute-done.19
  88.9 3.0 %collective-permute-done.18 = bf16[96,256]{1,0:T(8,128)(2,1)S(1)} collective-permute-done((bf16[96,256]{1,0:T(8,128)(2,1)S(1)}, bf16[96,256]{1,0:T(8,128)(2,1)S(1)}, u32[]{:S(2)}, u32[]{:S(2)}) %collective-permute-start.18) | collective-permute-done | bytes 49184 | tf_op jit(solution)/shard_map/ppermute | solution.py:560
  92.1 1.5 %collective-permute-start.21 = (bf16[384,256]{1,0:T(8,128)(2,1)S(1)}, bf16[384,256]{1,0:T(8,128)(2,1)}, u32[]{:S(2)}, u32[]{:S(2)}) collective-permute-start(bf16[384,256]{1,0:T(8,128)(2,1)S(1)} %pad_maximum_fusion.1), channel_id=1, source_target_pairs={{0,2},{1,9},{2,0},{3,11},{4,6},{5,13},{6,4},{7,15},{8,10},{9,1},{1... | collective-permute-start | bytes 589832 | tf_op jit(solution)/shard_map/ppermute | solution.py:560
  93.6 1.9 %collective-permute-start.8 = (bf16[8,80,128]{2,1,0:T(8,128)(2,1)S(1)}, bf16[8,80,128]{2,1,0:T(8,128)(2,1)}, u32[]{:S(2)}, u32[]{:S(2)}) collective-permute-start(bf16[8,80,128]{2,1,0:T(8,128)(2,1)S(1)} %get-tuple-element.26), channel_id=1, source_target_pairs={{0,31},{4,3},{8,7},{12,11},{16,15},{20,19},{24,23},{28,27},{3,4},{... | collective-permute-start | bytes 491528 | tf_op jit(solution)/shard_map/ppermute | solution.py:695
  95.5 0.9 collective-permute-start.22
  96.4 0.6 collective-permute-start.7
  97.0 7.0 %collective-permute-done.8 = bf16[8,80,128]{2,1,0:T(8,128)(2,1)} collective-permute-done((bf16[8,80,128]{2,1,0:T(8,128)(2,1)S(1)}, bf16[8,80,128]{2,1,0:T(8,128)(2,1)}, u32[]{:S(2)}, u32[]{:S(2)}) %collective-permute-start.8) | collective-permute-done | bytes 163872 | tf_op jit(solution)/shard_map/ppermute | solution.py:695
  104.0 1.3 %collective-permute-start.9 = (bf16[8,80,128]{2,1,0:T(8,128)(2,1)}, bf16[8,80,128]{2,1,0:T(8,128)(2,1)S(1)}, u32[]{:S(2)}, u32[]{:S(2)}) collective-permute-start(bf16[8,80,128]{2,1,0:T(8,128)(2,1)} %collective-permute-done.8), channel_id=1, source_target_pairs={{3,1},{0,2},{7,5},{4,6},{11,9},{8,10},{15,13},{12,14},{19,17},{16,... | collective-permute-start | bytes 491528 | tf_op jit(solution)/shard_map/ppermute | solution.py:745
  105.4 0.9 constant_dynamic-update-slice_fusion.2
  106.3 0.9 constant_dynamic-update-slice_fusion.1
  107.3 4.6 %collective-permute-done.23 = bf16[384,256]{1,0:T(8,128)(2,1)S(1)} collective-permute-done((bf16[384,256]{1,0:T(8,128)(2,1)S(1)}, bf16[384,256]{1,0:T(8,128)(2,1)S(1)}, u32[]{:S(2)}, u32[]{:S(2)}) %collective-permute-start.23) | collective-permute-done | bytes 196640 | tf_op jit(solution)/shard_map/ppermute | solution.py:560
  112.0 0.1 collective-permute-start.24
  112.0 1.0 broadcast_select_fusion.2.edge
  113.2 1.9 %collective-permute-done.10.theirs = bf16[24,80,128]{2,1,0:T(8,128)(2,1)S(1)} collective-permute-done((bf16[24,80,128]{2,1,0:T(8,128)(2,1)S(1)}, bf16[24,80,128]{2,1,0:T(8,128)(2,1)S(1)}, u32[]{:S(2)}, u32[]{:S(2)}) %collective-permute-start.10) | collective-permute-done | bytes 491552 | tf_op jit(solution)/shard_map/ppermute | solution.py:537
  115.0 4.2 %shard_map.116 = bf16[2560,128]{1,0:T(8,128)(2,1)} custom-call(s32[1]{0:T(128)} %bitcast.place, s32[49]{0:T(128)S(1)} %copy-done.6, bf16[8,80,128]{2,1,0:T(8,128)(2,1)S(1)} %get-tuple-element.25.own, bf16[8,80,128]{2,1,0:T(8,128)(2,1)S(1)} %collective-permute-done.7.partner, bf16[8,80,128]{2,1,0:T(8,128)(2,1)S(1)} %broadcast_select_fusion.2.edge, ...), custom_call_target="tpu_custom_call" | custom-call | flops 150994944 | bytes 4587520 | tf_op jit(solution)/shard_map/pallas_call | solution.py:755
  119.2 4.5 %shard_map.115 = f32[3584,128]{1,0:T(8,128)} custom-call(s32[1]{0:T(128)} %bitcast.place, s32[49]{0:T(128)S(1)} %copy-done.6, bf16[8,80,128]{2,1,0:T(8,128)(2,1)S(1)} %get-tuple-element.25.own, bf16[8,80,128]{2,1,0:T(8,128)(2,1)S(1)} %collective-permute-done.7.partner, bf16[8,80,128]{2,1,0:T(8,128)(2,1)S(1)} %broadcast_select_fusion.2.edge, ...), custom_call_target="tpu_custom_call" | custom-call | flops 150994944 | bytes 9175040 | tf_op jit(solution)/shard_map/pallas_call | solution.py:763
  123.7 1.9 %shard_map.117 = (f32[2304,256]{1,0:T(8,128)}, f32[720,256]{1,0:T(8,128)}) custom-call(s32[1]{0:T(128)} %bitcast.place, bf16[1536,256]{1,0:T(8,128)(2,1)S(1)} %constant_dynamic-update-slice_fusion.value, bf16[1536,256]{1,0:T(8,128)(2,1)S(1)} %collective-permute-done.24.other), custom_call_target="tpu_custom_call" | custom-call | flops 1 | bytes 4718592 | tf_op jit(solution)/shard_map/pallas_call | solution.py:774
  (54 shorter events, 0.6 us)
Async XLA Ops:
  0.6 16.0 %copy-start.3 = (bf16[8,512,256]{2,1,0:T(8,128)(2,1)S(1)}, bf16[8,512,256]{2,1,0:T(8,128)(2,1)}, u32[]{:S(2)}) copy-start(bf16[8,512,256]{2,1,0:T(8,128)(2,1)} %upstream.3) | copy-start | bytes 6291460
  7.7 2.3 %collective-permute-start = (bf16[24,80,128]{2,1,0:T(8,128)(2,1)}, bf16[24,80,128]{2,1,0:T(8,128)(2,1)S(1)}, u32[]{:S(2)}, u32[]{:S(2)}) collective-permute-start(bf16[24,80,128]{2,1,0:T(8,128)(2,1)} %get-tuple-element.21), channel_id=1, source_target_pairs={{0,1},{1,0},{2,3},{3,2},{4,5},{5,4},{6,7},{7,6},{8,9},{9,8},{10,11... | collective-permute-start | bytes 1474568 | tf_op jit(solution)/shard_map/ppermute | solution.py:537
  11.1 2.1 %copy-start.10 = (bf16[24,80,128]{2,1,0:T(8,128)(2,1)}, bf16[24,80,128]{2,1,0:T(8,128)(2,1)S(1)}, u32[]{:S(2)}) copy-start(bf16[24,80,128]{2,1,0:T(8,128)(2,1)S(1)} %add_convert_fusion.1) | copy-start | bytes 1474564
  11.9 11.7 %collective-permute-start.2 = (bf16[8,80,128]{2,1,0:T(8,128)(2,1)}, bf16[8,80,128]{2,1,0:T(8,128)(2,1)}, u32[]{:S(2)}, u32[]{:S(2)}) collective-permute-start(bf16[8,80,128]{2,1,0:T(8,128)(2,1)} %get-tuple-element.49), channel_id=1, source_target_pairs={{1,3},{2,0},{5,7},{6,4},{9,11},{10,8},{13,15},{14,12},{17,19},{18,... | collective-permute-start | bytes 491528 | tf_op jit(solution)/shard_map/ppermute | solution.py:674
  13.2 16.8 %copy-start.7 = (bf16[3,3,256,256]{3,2,1,0:T(8,128)(2,1)S(1)}, bf16[3,3,256,256]{3,2,1,0:T(8,128)(2,1)}, u32[]{:S(2)}) copy-start(bf16[3,3,256,256]{3,2,1,0:T(8,128)(2,1)} %weight.3) | copy-start | bytes 3538948
  13.2 10.4 %collective-permute-start.1 = (bf16[8,80,128]{2,1,0:T(8,128)(2,1)S(1)}, bf16[8,80,128]{2,1,0:T(8,128)(2,1)}, u32[]{:S(2)}, u32[]{:S(2)}) collective-permute-start(bf16[8,80,128]{2,1,0:T(8,128)(2,1)S(1)} %get-tuple-element.50), channel_id=1, source_target_pairs={{0,2},{1,3},{2,0},{3,1},{4,6},{5,7},{6,4},{7,5},{8,10},{9,11},{10,... | collective-permute-start | bytes 491528 | tf_op jit(solution)/shard_map/ppermute | solution.py:537
  17.7 20.4 %collective-permute-start.6 = (bf16[2,512,256]{2,1,0:T(8,128)(2,1)}, bf16[2,512,256]{2,1,0:T(8,128)(2,1)}, u32[]{:S(2)}, u32[]{:S(2)}) collective-permute-start(bf16[2,512,256]{2,1,0:T(8,128)(2,1)} %get-tuple-element.42), channel_id=1, source_target_pairs={{0,31},{1,2},{2,1},{3,4},{4,3},{5,6},{6,5},{7,8},{8,7},{9,10},{10,... | collective-permute-start | bytes 1572872 | tf_op jit(solution)/shard_map/ppermute | solution.py:610
  23.5 14.6 %collective-permute-start.5 = (bf16[2,512,256]{2,1,0:T(8,128)(2,1)}, bf16[2,512,256]{2,1,0:T(8,128)(2,1)}, u32[]{:S(2)}, u32[]{:S(2)}) collective-permute-start(bf16[2,512,256]{2,1,0:T(8,128)(2,1)} %get-tuple-element.43), channel_id=1, source_target_pairs={{0,1},{1,0},{2,3},{3,2},{4,5},{5,4},{6,7},{7,6},{8,9},{9,8},{10,11... | collective-permute-start | bytes 1572872 | tf_op jit(solution)/shard_map/ppermute | solution.py:611
  24.9 13.3 %copy-start.8 = (bf16[3,3,80,256]{3,2,1,0:T(8,128)(2,1)S(1)}, bf16[3,3,80,256]{3,2,1,0:T(8,128)(2,1)}, u32[]{:S(2)}) copy-start(bf16[3,3,80,256]{3,2,1,0:T(8,128)(2,1)} %param.13) | copy-start | bytes 1105924
  24.9 13.3 %copy-start.9 = (s32[8,112]{1,0:T(8,128)S(1)}, s32[8,112]{1,0:T(8,128)}, u32[]{:S(2)}) copy-start(s32[8,112]{1,0:T(8,128)} %ranges.1) | copy-start | bytes 10756
  24.9 9.8 %collective-permute-start.3 = (bf16[10,80,128]{2,1,0:T(8,128)(2,1)S(1)}, bf16[10,80,128]{2,1,0:T(8,128)(2,1)S(1)}, u32[]{:S(2)}, u32[]{:S(2)}) collective-permute-start(bf16[10,80,128]{2,1,0:T(8,128)(2,1)S(1)} %maximum_select_fusion), channel_id=1, source_target_pairs={{0,31},{1,2},{2,1},{3,4},{4,3},{5,6},{6,5},{7,8},{8,7},{9,10},{10,... | collective-permute-start | bytes 614408 | tf_op jit(solution)/shard_map/ppermute | solution.py:697
  34.7 9.6 %collective-permute-start.4 = (bf16[4,80,128]{2,1,0:T(8,128)(2,1)S(1)}, bf16[4,80,128]{2,1,0:T(8,128)(2,1)S(1)}, u32[]{:S(2)}, u32[]{:S(2)}) collective-permute-start(bf16[4,80,128]{2,1,0:T(8,128)(2,1)S(1)} %pad_maximum_fusion.2), channel_id=1, source_target_pairs={{0,1},{1,0},{2,3},{3,2},{4,5},{5,4},{6,7},{7,6},{8,9},{9,8},{10,11... | collective-permute-start | bytes 245768 | tf_op jit(solution)/shard_map/ppermute | solution.py:699
  38.2 6.2 %copy-start.4 = (bf16[8,512,256]{2,1,0:T(8,128)(2,1)S(1)}, bf16[8,512,256]{2,1,0:T(8,128)(2,1)}, u32[]{:S(2)}) copy-start(bf16[8,512,256]{2,1,0:T(8,128)(2,1)} %upstream.3) | copy-start | bytes 6291460
  61.8 2.3 %collective-permute-start.11 = (bf16[1536,256]{1,0:T(8,128)(2,1)S(1)}, bf16[1536,256]{1,0:T(8,128)(2,1)S(1)}, u32[]{:S(2)}, u32[]{:S(2)}) collective-permute-start(bf16[1536,256]{1,0:T(8,128)(2,1)S(1)} %get-tuple-element.31), channel_id=1, source_target_pairs={{0,1},{1,0},{2,3},{3,2},{4,5},{5,4},{6,7},{7,6},{8,9},{9,8},{10,11... | collective-permute-start | bytes 2359304 | tf_op jit(solution)/shard_map/ppermute | solution.py:537
  64.5 7.1 %collective-permute-start.12 = (bf16[384,256]{1,0:T(8,128)(2,1)S(1)}, bf16[384,256]{1,0:T(8,128)(2,1)S(1)}, u32[]{:S(2)}, u32[]{:S(2)}) collective-permute-start(bf16[384,256]{1,0:T(8,128)(2,1)S(1)} %get-tuple-element.44), channel_id=1, source_target_pairs={{0,6},{1,25},{2,4},{3,27},{4,2},{5,29},{6,0},{7,31},{8,14},{9,17},... | collective-permute-start | bytes 589832 | tf_op jit(solution)/shard_map/ppermute | solution.py:560
  67.9 5.9 %collective-permute-start.14 = (bf16[384,256]{1,0:T(8,128)(2,1)S(1)}, bf16[384,256]{1,0:T(8,128)(2,1)S(1)}, u32[]{:S(2)}, u32[]{:S(2)}) collective-permute-start(bf16[384,256]{1,0:T(8,128)(2,1)S(1)} %get-tuple-element.45), channel_id=1, source_target_pairs={{0,4},{1,17},{2,6},{3,19},{4,0},{5,21},{6,2},{7,23},{8,12},{9,25},... | collective-permute-start | bytes 589832 | tf_op jit(solution)/shard_map/ppermute | solution.py:560
  69.1 5.7 %collective-permute-start.13 = (bf16[384,256]{1,0:T(8,128)(2,1)S(1)}, bf16[384,256]{1,0:T(8,128)(2,1)S(1)}, u32[]{:S(2)}, u32[]{:S(2)}) collective-permute-start(bf16[384,256]{1,0:T(8,128)(2,1)S(1)} %get-tuple-element.46), channel_id=1, source_target_pairs={{0,2},{1,9},{2,0},{3,11},{4,6},{5,13},{6,4},{7,15},{8,10},{9,1},{1... | collective-permute-start | bytes 589832 | tf_op jit(solution)/shard_map/ppermute | solution.py:560
  74.9 6.0 %collective-permute-start.15 = (bf16[96,256]{1,0:T(8,128)(2,1)S(1)}, bf16[96,256]{1,0:T(8,128)(2,1)S(1)}, u32[]{:S(2)}, u32[]{:S(2)}) collective-permute-start(bf16[96,256]{1,0:T(8,128)(2,1)S(1)} %get-tuple-element.51), channel_id=1, source_target_pairs={{0,24},{1,7},{2,26},{3,5},{4,28},{5,3},{6,30},{7,1},{8,16},{9,15},... | collective-permute-start | bytes 147464 | tf_op jit(solution)/shard_map/ppermute | solution.py:560
  78.7 5.0 %collective-permute-start.17 = (bf16[96,256]{1,0:T(8,128)(2,1)S(1)}, bf16[96,256]{1,0:T(8,128)(2,1)S(1)}, u32[]{:S(2)}, u32[]{:S(2)}) collective-permute-start(bf16[96,256]{1,0:T(8,128)(2,1)S(1)} %get-tuple-element.52), channel_id=1, source_target_pairs={{0,16},{1,5},{2,18},{3,7},{4,20},{5,1},{6,22},{7,3},{8,24},{9,13},... | collective-permute-start | bytes 147464 | tf_op jit(solution)/shard_map/ppermute | solution.py:560
  78.7 5.0 %collective-permute-start.16 = (bf16[96,256]{1,0:T(8,128)(2,1)S(1)}, bf16[96,256]{1,0:T(8,128)(2,1)S(1)}, u32[]{:S(2)}, u32[]{:S(2)}) collective-permute-start(bf16[96,256]{1,0:T(8,128)(2,1)S(1)} %get-tuple-element.53), channel_id=1, source_target_pairs={{0,8},{1,3},{2,10},{3,1},{4,12},{5,7},{6,14},{7,5},{8,0},{9,11},{1... | collective-permute-start | bytes 147464 | tf_op jit(solution)/shard_map/ppermute | solution.py:560
  83.7 4.5 %collective-permute-start.20 = (bf16[96,256]{1,0:T(8,128)(2,1)S(1)}, bf16[96,256]{1,0:T(8,128)(2,1)S(1)}, u32[]{:S(2)}, u32[]{:S(2)}) collective-permute-start(bf16[96,256]{1,0:T(8,128)(2,1)S(1)} %add_convert_fusion.5), channel_id=1, source_target_pairs={{0,8},{1,3},{2,10},{3,1},{4,12},{5,7},{6,14},{7,5},{8,0},{9,11},{1... | collective-permute-start | bytes 147464 | tf_op jit(solution)/shard_map/ppermute | solution.py:560
  83.9 5.0 %collective-permute-start.19 = (bf16[96,256]{1,0:T(8,128)(2,1)S(1)}, bf16[96,256]{1,0:T(8,128)(2,1)S(1)}, u32[]{:S(2)}, u32[]{:S(2)}) collective-permute-start(bf16[96,256]{1,0:T(8,128)(2,1)S(1)} %add_convert_fusion.5), channel_id=1, source_target_pairs={{0,16},{1,5},{2,18},{3,7},{4,20},{5,1},{6,22},{7,3},{8,24},{9,13},... | collective-permute-start | bytes 147464 | tf_op jit(solution)/shard_map/ppermute | solution.py:560
  85.9 6.0 %collective-permute-start.18 = (bf16[96,256]{1,0:T(8,128)(2,1)S(1)}, bf16[96,256]{1,0:T(8,128)(2,1)S(1)}, u32[]{:S(2)}, u32[]{:S(2)}) collective-permute-start(bf16[96,256]{1,0:T(8,128)(2,1)S(1)} %add_convert_fusion.5), channel_id=1, source_target_pairs={{0,24},{1,7},{2,26},{3,5},{4,28},{5,3},{6,30},{7,1},{8,16},{9,15},... | collective-permute-start | bytes 147464 | tf_op jit(solution)/shard_map/ppermute | solution.py:560
  91.9 23.1 %copy-start = (f32[129,32,128]{2,1,0:T(8,128)S(1)}, f32[129,32,128]{2,1,0:T(8,128)}, u32[]{:S(2)}) copy-start(f32[129,32,128]{2,1,0:T(8,128)} %get-tuple-element.29.probs_t) | copy-start | bytes 6340612
  92.0 23.1 %copy-start.6 = (s32[49]{0:T(128)S(1)}, s32[49]{0:T(128)}, u32[]{:S(2)}) copy-start(s32[49]{0:T(128)} %get-tuple-element.19.begins) | copy-start | bytes 592
  92.1 13.3 %collective-permute-start.21 = (bf16[384,256]{1,0:T(8,128)(2,1)S(1)}, bf16[384,256]{1,0:T(8,128)(2,1)}, u32[]{:S(2)}, u32[]{:S(2)}) collective-permute-start(bf16[384,256]{1,0:T(8,128)(2,1)S(1)} %pad_maximum_fusion.1), channel_id=1, source_target_pairs={{0,2},{1,9},{2,0},{3,11},{4,6},{5,13},{6,4},{7,15},{8,10},{9,1},{1... | collective-permute-start | bytes 589832 | tf_op jit(solution)/shard_map/ppermute | solution.py:560
  93.6 10.4 %collective-permute-start.8 = (bf16[8,80,128]{2,1,0:T(8,128)(2,1)S(1)}, bf16[8,80,128]{2,1,0:T(8,128)(2,1)}, u32[]{:S(2)}, u32[]{:S(2)}) collective-permute-start(bf16[8,80,128]{2,1,0:T(8,128)(2,1)S(1)} %get-tuple-element.26), channel_id=1, source_target_pairs={{0,31},{4,3},{8,7},{12,11},{16,15},{20,19},{24,23},{28,27},{3,4},{... | collective-permute-start | bytes 491528 | tf_op jit(solution)/shard_map/ppermute | solution.py:695
  95.5 10.8 %collective-permute-start.22 = (bf16[384,256]{1,0:T(8,128)(2,1)S(1)}, bf16[384,256]{1,0:T(8,128)(2,1)}, u32[]{:S(2)}, u32[]{:S(2)}) collective-permute-start(bf16[384,256]{1,0:T(8,128)(2,1)S(1)} %pad_maximum_fusion.1), channel_id=1, source_target_pairs={{0,4},{1,17},{2,6},{3,19},{4,0},{5,21},{6,2},{7,23},{8,12},{9,25},... | collective-permute-start | bytes 589832 | tf_op jit(solution)/shard_map/ppermute | solution.py:560
  96.4 16.6 %collective-permute-start.7 = (bf16[8,80,128]{2,1,0:T(8,128)(2,1)S(1)}, bf16[8,80,128]{2,1,0:T(8,128)(2,1)S(1)}, u32[]{:S(2)}, u32[]{:S(2)}) collective-permute-start(bf16[8,80,128]{2,1,0:T(8,128)(2,1)S(1)} %get-tuple-element.25.own), channel_id=1, source_target_pairs={{0,2},{1,3},{2,0},{3,1},{4,6},{5,7},{6,4},{7,5},{8,10},{9,11},{10,... | collective-permute-start | bytes 491528 | tf_op jit(solution)/shard_map/ppermute | solution.py:537
  104.0 8.0 %collective-permute-start.9 = (bf16[8,80,128]{2,1,0:T(8,128)(2,1)}, bf16[8,80,128]{2,1,0:T(8,128)(2,1)S(1)}, u32[]{:S(2)}, u32[]{:S(2)}) collective-permute-start(bf16[8,80,128]{2,1,0:T(8,128)(2,1)} %collective-permute-done.8), channel_id=1, source_target_pairs={{3,1},{0,2},{7,5},{4,6},{11,9},{8,10},{15,13},{12,14},{19,17},{16,... | collective-permute-start | bytes 491528 | tf_op jit(solution)/shard_map/ppermute | solution.py:745
  105.3 6.6 %collective-permute-start.23 = (bf16[384,256]{1,0:T(8,128)(2,1)S(1)}, bf16[384,256]{1,0:T(8,128)(2,1)S(1)}, u32[]{:S(2)}, u32[]{:S(2)}) collective-permute-start(bf16[384,256]{1,0:T(8,128)(2,1)S(1)} %pad_maximum_fusion.1), channel_id=1, source_target_pairs={{0,6},{1,25},{2,4},{3,27},{4,2},{5,29},{6,0},{7,31},{8,14},{9,17},... | collective-permute-start | bytes 589832 | tf_op jit(solution)/shard_map/ppermute | solution.py:560
  112.0 11.7 %collective-permute-start.24 = (bf16[1536,256]{1,0:T(8,128)(2,1)S(1)}, bf16[1536,256]{1,0:T(8,128)(2,1)S(1)}, u32[]{:S(2)}, u32[]{:S(2)}) collective-permute-start(bf16[1536,256]{1,0:T(8,128)(2,1)S(1)} %constant_dynamic-update-slice_fusion.value), channel_id=1, source_target_pairs={{0,1},{1,0},{2,3},{3,2},{4,5},{5,4},{6,7},{7,6},{8,9},{9,8},{10,11... | collective-permute-start | bytes 2359304 | tf_op jit(solution)/shard_map/ppermute | solution.py:537
  113.0 6.2 %copy-start.2 = (f32[3584,128]{1,0:T(8,128)S(1)}, f32[3584,128]{1,0:T(8,128)}, u32[]{:S(2)}) copy-start(f32[3584,128]{1,0:T(8,128)} %get-tuple-element.27.probs) | copy-start | bytes 5505028
  113.1 1.9 %collective-permute-start.10 = (bf16[24,80,128]{2,1,0:T(8,128)(2,1)S(1)}, bf16[24,80,128]{2,1,0:T(8,128)(2,1)S(1)}, u32[]{:S(2)}, u32[]{:S(2)}) collective-permute-start(bf16[24,80,128]{2,1,0:T(8,128)(2,1)S(1)} %pad_maximum_fusion), channel_id=1, source_target_pairs={{0,1},{1,0},{2,3},{3,2},{4,5},{5,4},{6,7},{7,6},{8,9},{9,8},{10,11... | collective-permute-start | bytes 1474568 | tf_op jit(solution)/shard_map/ppermute | solution.py:537
  115.0 4.2 %copy-start.1 = (f32[129,32,128]{2,1,0:T(8,128)S(1)}, f32[129,32,128]{2,1,0:T(8,128)}, u32[]{:S(2)}) copy-start(f32[129,32,128]{2,1,0:T(8,128)} %get-tuple-element.28.context_t) | copy-start | bytes 6340612
  115.0 4.2 %copy-start.5 = (s32[1,32,128]{2,1,0:T(8,128)S(1)}, s32[1,32,128]{2,1,0:T(8,128)}, u32[]{:S(2)}) copy-start(s32[1,32,128]{2,1,0:T(8,128)} %param.10) | copy-start | bytes 49156

commit v7 on v6

--- a/solution.py
+++ b/solution.py
@@ -666,12 +666,15 @@
         16 * length * hidden,
     )(place, near_grad, far_grad, out_grad, conv2_weight, inner_grad, weight, rng_map)
 
-    summed = rounded_sum(kept, swapped(sent, blocks, 1))
-    own = rounded_sum(summed[:sector], swapped(summed[sector : 2 * sector], blocks, 2))
+    arrived = swapped(sent, blocks, 1)
+    summed = rounded_sum(kept[sector:], arrived[sector:])
+    other_pair = swapped(summed[:sector], blocks, 2)
+    own = kept[:sector].astype(F32) + arrived[:sector].astype(F32) + other_pair.astype(F32)
+    own = own.astype(BF16)
     inward = [(i, i ^ 2) for i in range(blocks) if i % bands in (1, 2)]
     outward = [(i ^ 2, i) for i in range(blocks) if i % bands in (1, 2)]
     edge = rounded_sum(
-        summed[2 * sector :], lax.ppermute(summed[2 * sector :], "blk", inward)
+        summed[sector:], lax.ppermute(summed[sector:], "blk", inward)
     )
     first = band == 0
     firsts = [i for i in range(blocks) if i % bands == 0]

time: 126 us -> 129 us (1.024)
  waiting for transfers between devices: 31.2 us -> 38.7 us
  starting transfers between devices: 39.7 us -> 34 us
    ppermute x1, waiting for transfers between devices: 0.01 us -> 6.16 us  [shards(): lax.ppermute(summed[sector:], 'blk', inward)]
    ppermute x6, waiting for transfers between devices: 5.8 us -> 9.52 us  [swapped(): return lax.ppermute(value, 'blk', [(i, i ^ mask) for i in range(blocks)])]
    ppermute x1, starting transfers between devices: 3.46 us -> 0.07 us  [shards(): lax.ppermute(jnp.concatenate([ends(own, True), passed], axis=0), 'blk', o...]
    ppermute x12, waiting for transfers between devices: 18.3 us -> 16.4 us  [sent(): return lax.ppermute(part, 'blk', to)]
    ppermute x1, starting transfers between devices: 5.82 us -> 3.99 us  [shards(): far_grad = lax.ppermute(ends(out_grad, False), 'blk', off_chip)]
  transfers between devices with their start and end apart: 25 -> 25, of which waited for: 12 -> 13; matrix products, arithmetic and copies ran while one was open for 4% -> 5% of each run, Pallas kernels for 16% -> 15%
where the time goes in v7:
time: 129 us; the launch traced here: 128 us
  Pallas kernels  45.9 us (36%)
  waiting for transfers between devices  38.7 us (30%)
  starting transfers between devices  34 us (26%)
  other arithmetic  5.93 us (5%)
  local copies, waits for them, and re-layouts  2.83 us (2%)
    pallas_call x1, Pallas kernels, shards(): call(grid_kernel, [jax.ShapeDtypeStruct((grad_rows // 2, hidden), BF16),...  17.5 us
    ppermute x12, waiting for transfers between devices, sent(): return lax.ppermute(part, 'blk', to)  16.4 us
    ppermute x12, starting transfers between devices, sent(): return lax.ppermute(part, 'blk', to)  15.1 us
    ppermute x6, waiting for transfers between devices, swapped(): return lax.ppermute(value, 'blk', [(i, i ^ mask) for i in range(blocks)])  9.52 us
    pallas_call x1, Pallas kernels, shards(): call(functools.partial(pool_kernel, rows, sight, blocks * sector), [jax.S...  7.03 us
    ppermute x1, waiting for transfers between devices, to_next(): return lax.ppermute(value, 'blk', pairs)  6.66 us
    ppermute x1, waiting for transfers between devices, shards(): lax.ppermute(summed[sector:], 'blk', inward)  6.16 us
    pallas_call x1, Pallas kernels, shards(): call(outer_acts_kernel, [jax.ShapeDtypeStruct((sector + 2, hidden, length...  6.12 us
  transfers between devices with their start and end apart: 25, of which 13 were waited for; matrix products, arithmetic and copies ran while one was open for 5% of the time, Pallas kernels for 15%

profile of v7, /device:TPU:0, one launch (start us, length us, event | category | flops | bytes accessed | tf_op | source)
XLA Modules:
  0.0 128.4 jit_solution(10575893720353027388)
XLA Ops:
  0.6 7.0 %shard_map.111 = (f32[3584,128]{1,0:T(8,128)}, f32[129,32,128]{2,1,0:T(8,128)}, f32[129,32,128]{2,1,0:T(8,128)}, bf16[24,80,128]{2,1,0:T(8,128)(2,1)}, bf16[24,80,128]{2,1,0:T(8,128)(2,1)}, /*index=5*/s32[49]{0:T(128)}) custom-call(s32[1]{0:T(128)} %bitcast.place, s32[8,128]{1,0:T(8,128)} %az_map.1, f32[3584,128]{1,0:T(8,128)} %bitcast.14, ...), custom_call_target="tpu_custom_call" | custom-call | flops 150994944 | bytes 9175040 | tf_op jit(solution)/shard_map/pallas_call | solution.py:615
  7.7 0.6 collective-permute-start
  8.2 1.7 %collective-permute-done = bf16[24,80,128]{2,1,0:T(8,128)(2,1)S(1)} collective-permute-done((bf16[24,80,128]{2,1,0:T(8,128)(2,1)}, bf16[24,80,128]{2,1,0:T(8,128)(2,1)S(1)}, u32[]{:S(2)}, u32[]{:S(2)}) %collective-permute-start) | collective-permute-done | bytes 491552 | tf_op jit(solution)/shard_map/ppermute | solution.py:537
  9.9 1.2 add_convert_fusion.1
  11.2 0.8 fusion
  12.0 2.8 %collective-permute-start.1 = (bf16[8,80,128]{2,1,0:T(8,128)(2,1)}, bf16[8,80,128]{2,1,0:T(8,128)(2,1)}, u32[]{:S(2)}, u32[]{:S(2)}) collective-permute-start(bf16[8,80,128]{2,1,0:T(8,128)(2,1)} %get-tuple-element.48), channel_id=1, source_target_pairs={{0,2},{1,3},{2,0},{3,1},{4,6},{5,7},{6,4},{7,5},{8,10},{9,11},{10,... | collective-permute-start | bytes 491528 | tf_op jit(solution)/shard_map/ppermute | solution.py:537
  14.8 1.0 broadcast_select_fusion
  15.9 4.0 %collective-permute-start.6 = (bf16[2,512,256]{2,1,0:T(8,128)(2,1)}, bf16[2,512,256]{2,1,0:T(8,128)(2,1)}, u32[]{:S(2)}, u32[]{:S(2)}) collective-permute-start(bf16[2,512,256]{2,1,0:T(8,128)(2,1)} %get-tuple-element.42), channel_id=1, source_target_pairs={{0,31},{1,2},{2,1},{3,4},{4,3},{5,6},{6,5},{7,8},{8,7},{9,10},{10,... | collective-permute-start | bytes 1572872 | tf_op jit(solution)/shard_map/ppermute | solution.py:610
  19.9 1.3 collective-permute-start.2
  21.2 4.1 %collective-permute-done.1 = bf16[8,80,128]{2,1,0:T(8,128)(2,1)} collective-permute-done((bf16[8,80,128]{2,1,0:T(8,128)(2,1)}, bf16[8,80,128]{2,1,0:T(8,128)(2,1)}, u32[]{:S(2)}, u32[]{:S(2)}) %collective-permute-start.1) | collective-permute-done | bytes 163872 | tf_op jit(solution)/shard_map/ppermute | solution.py:537
  25.2 1.1 add_convert_fusion.4.own
  26.4 6.2 %collective-permute-done.2 = bf16[8,80,128]{2,1,0:T(8,128)(2,1)S(1)} collective-permute-done((bf16[8,80,128]{2,1,0:T(8,128)(2,1)S(1)}, bf16[8,80,128]{2,1,0:T(8,128)(2,1)S(1)}, u32[]{:S(2)}, u32[]{:S(2)}) %collective-permute-start.2) | collective-permute-done | bytes 163872 | tf_op jit(solution)/shard_map/ppermute | solution.py:677
  32.5 1.0 add_convert_fusion.3.edge
  33.6 5.2 %collective-permute-start.3 = (bf16[10,80,128]{2,1,0:T(8,128)(2,1)S(1)}, bf16[10,80,128]{2,1,0:T(8,128)(2,1)S(1)}, u32[]{:S(2)}, u32[]{:S(2)}) collective-permute-start(bf16[10,80,128]{2,1,0:T(8,128)(2,1)S(1)} %maximum_select_fusion), channel_id=1, source_target_pairs={{0,31},{1,2},{2,1},{3,4},{4,3},{5,6},{6,5},{7,8},{8,7},{9,10},{10,... | collective-permute-start | bytes 614408 | tf_op jit(solution)/shard_map/ppermute | solution.py:700
  38.8 4.7 %shard_map.112.inner = bf16[5,256,512]{2,1,0:T(8,128)(2,1)S(1)} custom-call(bf16[8,512,256]{2,1,0:T(8,128)(2,1)S(1)} %copy-done.3, bf16[3,3,256,256]{3,2,1,0:T(8,128)(2,1)S(1)} %copy-done.7), custom_call_target="tpu_custom_call" | custom-call | flops 3019898880 | bytes 4194304 | tf_op jit(solution)/shard_map/pallas_call | solution.py:647
  43.6 0.1 collective-permute-start.4
  43.7 6.1 %shard_map.113 = (bf16[10,256,512]{2,1,0:T(8,128)(2,1)S(1)}, bf16[768,240]{1,0:T(8,128)(2,1)S(1)}, bf16[512,256]{1,0:T(8,128)(2,1)S(1)}) custom-call(s32[1]{0:T(128)} %bitcast.place, bf16[2,512,256]{2,1,0:T(8,128)(2,1)} %collective-permute-done.5.near, bf16[2,512,256]{2,1,0:T(8,128)(2,1)} %collective-permute-done.6.far, bf16[8,512,256]{2,1,0:T(8,128)(2,1)S(1)} %copy-done.3, ...), custom_call_target="tpu_custom_call" | custom-call | flops 3019898880 | bytes 2097152 | tf_op jit(solution)/shard_map/pallas_call | solution.py:656
  49.9 17.5 %shard_map.114 = (bf16[1536,256]{1,0:T(8,128)(2,1)S(1)}, bf16[1536,256]{1,0:T(8,128)(2,1)S(1)}, bf16[8,80,128]{2,1,0:T(8,128)(2,1)S(1)}, bf16[8,80,128]{2,1,0:T(8,128)(2,1)S(1)}) custom-call(s32[1]{0:T(128)} %bitcast.place, bf16[8,80,128]{2,1,0:T(8,128)(2,1)S(1)} %add_convert_fusion.4.own, bf16[8,80,128]{2,1,0:T(8,128)(2,1)S(1)} %add_convert_fusion.3.edge, ...), custom_call_target="tpu_custom_call" | custom-call | flops 12079595520 | bytes 20971520 | tf_op jit(solution)/shard_map/pallas_call | solution.py:709
  67.4 0.5 collective-permute-start.11
  67.9 1.9 %collective-permute-done.11 = bf16[1536,256]{1,0:T(8,128)(2,1)S(1)} collective-permute-done((bf16[1536,256]{1,0:T(8,128)(2,1)S(1)}, bf16[1536,256]{1,0:T(8,128)(2,1)S(1)}, u32[]{:S(2)}, u32[]{:S(2)}) %collective-permute-start.11) | collective-permute-done | bytes 786464 | tf_op jit(solution)/shard_map/ppermute | solution.py:537
  69.8 0.2 add_convert_fusion
  70.2 3.4 %collective-permute-start.13 = (bf16[384,256]{1,0:T(8,128)(2,1)S(1)}, bf16[384,256]{1,0:T(8,128)(2,1)S(1)}, u32[]{:S(2)}, u32[]{:S(2)}) collective-permute-start(bf16[384,256]{1,0:T(8,128)(2,1)S(1)} %get-tuple-element.46), channel_id=1, source_target_pairs={{0,2},{1,9},{2,0},{3,11},{4,6},{5,13},{6,4},{7,15},{8,10},{9,1},{1... | collective-permute-start | bytes 589832 | tf_op jit(solution)/shard_map/ppermute | solution.py:560
  73.6 3.2 %collective-permute-done.12 = bf16[384,256]{1,0:T(8,128)(2,1)S(1)} collective-permute-done((bf16[384,256]{1,0:T(8,128)(2,1)S(1)}, bf16[384,256]{1,0:T(8,128)(2,1)S(1)}, u32[]{:S(2)}, u32[]{:S(2)}) %collective-permute-start.12) | collective-permute-done | bytes 196640 | tf_op jit(solution)/shard_map/ppermute | solution.py:560
  76.8 1.2 collective-permute-done.14
  78.0 0.1 add_convert_fusion.2
  78.2 2.8 %collective-permute-start.15 = (bf16[96,256]{1,0:T(8,128)(2,1)S(1)}, bf16[96,256]{1,0:T(8,128)(2,1)S(1)}, u32[]{:S(2)}, u32[]{:S(2)}) collective-permute-start(bf16[96,256]{1,0:T(8,128)(2,1)S(1)} %get-tuple-element.49), channel_id=1, source_target_pairs={{0,24},{1,7},{2,26},{3,5},{4,28},{5,3},{6,30},{7,1},{8,16},{9,15},... | collective-permute-start | bytes 147464 | tf_op jit(solution)/shard_map/ppermute | solution.py:560
  80.9 1.7 %collective-permute-start.16 = (bf16[96,256]{1,0:T(8,128)(2,1)S(1)}, bf16[96,256]{1,0:T(8,128)(2,1)S(1)}, u32[]{:S(2)}, u32[]{:S(2)}) collective-permute-start(bf16[96,256]{1,0:T(8,128)(2,1)S(1)} %get-tuple-element.51), channel_id=1, source_target_pairs={{0,8},{1,3},{2,10},{3,1},{4,12},{5,7},{6,14},{7,5},{8,0},{9,11},{1... | collective-permute-start | bytes 147464 | tf_op jit(solution)/shard_map/ppermute | solution.py:560
  82.6 1.5 %collective-permute-done.15 = bf16[96,256]{1,0:T(8,128)(2,1)S(1)} collective-permute-done((bf16[96,256]{1,0:T(8,128)(2,1)S(1)}, bf16[96,256]{1,0:T(8,128)(2,1)S(1)}, u32[]{:S(2)}, u32[]{:S(2)}) %collective-permute-start.15) | collective-permute-done | bytes 49184 | tf_op jit(solution)/shard_map/ppermute | solution.py:560
  84.1 1.8 %collective-permute-done.17 = bf16[96,256]{1,0:T(8,128)(2,1)S(1)} collective-permute-done((bf16[96,256]{1,0:T(8,128)(2,1)S(1)}, bf16[96,256]{1,0:T(8,128)(2,1)S(1)}, u32[]{:S(2)}, u32[]{:S(2)}) %collective-permute-start.17) | collective-permute-done | bytes 49184 | tf_op jit(solution)/shard_map/ppermute | solution.py:560
  85.9 0.8 collective-permute-start.20
  86.8 1.7 %collective-permute-start.19 = (bf16[96,256]{1,0:T(8,128)(2,1)S(1)}, bf16[96,256]{1,0:T(8,128)(2,1)S(1)}, u32[]{:S(2)}, u32[]{:S(2)}) collective-permute-start(bf16[96,256]{1,0:T(8,128)(2,1)S(1)} %add_convert_fusion.5), channel_id=1, source_target_pairs={{0,16},{1,5},{2,18},{3,7},{4,20},{5,1},{6,22},{7,3},{8,24},{9,13},... | collective-permute-start | bytes 147464 | tf_op jit(solution)/shard_map/ppermute | solution.py:560
  88.5 1.9 %collective-permute-start.18 = (bf16[96,256]{1,0:T(8,128)(2,1)S(1)}, bf16[96,256]{1,0:T(8,128)(2,1)S(1)}, u32[]{:S(2)}, u32[]{:S(2)}) collective-permute-start(bf16[96,256]{1,0:T(8,128)(2,1)S(1)} %add_convert_fusion.5), channel_id=1, source_target_pairs={{0,24},{1,7},{2,26},{3,5},{4,28},{5,3},{6,30},{7,1},{8,16},{9,15},... | collective-permute-start | bytes 147464 | tf_op jit(solution)/shard_map/ppermute | solution.py:560
  90.4 1.4 %collective-permute-done.19 = bf16[96,256]{1,0:T(8,128)(2,1)S(1)} collective-permute-done((bf16[96,256]{1,0:T(8,128)(2,1)S(1)}, bf16[96,256]{1,0:T(8,128)(2,1)S(1)}, u32[]{:S(2)}, u32[]{:S(2)}) %collective-permute-start.19) | collective-permute-done | bytes 49184 | tf_op jit(solution)/shard_map/ppermute | solution.py:560
  91.8 2.7 %collective-permute-done.18 = bf16[96,256]{1,0:T(8,128)(2,1)S(1)} collective-permute-done((bf16[96,256]{1,0:T(8,128)(2,1)S(1)}, bf16[96,256]{1,0:T(8,128)(2,1)S(1)}, u32[]{:S(2)}, u32[]{:S(2)}) %collective-permute-start.18) | collective-permute-done | bytes 49184 | tf_op jit(solution)/shard_map/ppermute | solution.py:560
  94.7 1.8 %collective-permute-start.21 = (bf16[384,256]{1,0:T(8,128)(2,1)S(1)}, bf16[384,256]{1,0:T(8,128)(2,1)}, u32[]{:S(2)}, u32[]{:S(2)}) collective-permute-start(bf16[384,256]{1,0:T(8,128)(2,1)S(1)} %pad_maximum_fusion.1), channel_id=1, source_target_pairs={{0,2},{1,9},{2,0},{3,11},{4,6},{5,13},{6,4},{7,15},{8,10},{9,1},{1... | collective-permute-start | bytes 589832 | tf_op jit(solution)/shard_map/ppermute | solution.py:560
  96.4 1.9 %collective-permute-start.8 = (bf16[8,80,128]{2,1,0:T(8,128)(2,1)S(1)}, bf16[8,80,128]{2,1,0:T(8,128)(2,1)}, u32[]{:S(2)}, u32[]{:S(2)}) collective-permute-start(bf16[8,80,128]{2,1,0:T(8,128)(2,1)S(1)} %get-tuple-element.26), channel_id=1, source_target_pairs={{0,31},{4,3},{8,7},{12,11},{16,15},{20,19},{24,23},{28,27},{3,4},{... | collective-permute-start | bytes 491528 | tf_op jit(solution)/shard_map/ppermute | solution.py:698
  98.3 0.8 collective-permute-start.22
  99.2 1.0 collective-permute-start.7
  100.2 6.7 %collective-permute-done.8 = bf16[8,80,128]{2,1,0:T(8,128)(2,1)} collective-permute-done((bf16[8,80,128]{2,1,0:T(8,128)(2,1)S(1)}, bf16[8,80,128]{2,1,0:T(8,128)(2,1)}, u32[]{:S(2)}, u32[]{:S(2)}) %collective-permute-start.8) | collective-permute-done | bytes 163872 | tf_op jit(solution)/shard_map/ppermute | solution.py:698
  106.9 1.3 %collective-permute-start.9 = (bf16[8,80,128]{2,1,0:T(8,128)(2,1)}, bf16[8,80,128]{2,1,0:T(8,128)(2,1)S(1)}, u32[]{:S(2)}, u32[]{:S(2)}) collective-permute-start(bf16[8,80,128]{2,1,0:T(8,128)(2,1)} %collective-permute-done.8), channel_id=1, source_target_pairs={{3,1},{0,2},{7,5},{4,6},{11,9},{8,10},{15,13},{12,14},{19,17},{16,... | collective-permute-start | bytes 491528 | tf_op jit(solution)/shard_map/ppermute | solution.py:748
  108.2 0.9 constant_dynamic-update-slice_fusion.2
  109.2 0.9 constant_dynamic-update-slice_fusion.1
  110.1 4.6 %collective-permute-done.23 = bf16[384,256]{1,0:T(8,128)(2,1)S(1)} collective-permute-done((bf16[384,256]{1,0:T(8,128)(2,1)S(1)}, bf16[384,256]{1,0:T(8,128)(2,1)S(1)}, u32[]{:S(2)}, u32[]{:S(2)}) %collective-permute-start.23) | collective-permute-done | bytes 196640 | tf_op jit(solution)/shard_map/ppermute | solution.py:560
  114.9 1.0 broadcast_select_fusion.2.edge
  116.0 1.9 %collective-permute-done.10.theirs = bf16[24,80,128]{2,1,0:T(8,128)(2,1)S(1)} collective-permute-done((bf16[24,80,128]{2,1,0:T(8,128)(2,1)S(1)}, bf16[24,80,128]{2,1,0:T(8,128)(2,1)S(1)}, u32[]{:S(2)}, u32[]{:S(2)}) %collective-permute-start.10) | collective-permute-done | bytes 491552 | tf_op jit(solution)/shard_map/ppermute | solution.py:537
  117.9 4.2 %shard_map.116 = bf16[2560,128]{1,0:T(8,128)(2,1)} custom-call(s32[1]{0:T(128)} %bitcast.place, s32[49]{0:T(128)S(1)} %copy-done.6, bf16[8,80,128]{2,1,0:T(8,128)(2,1)S(1)} %get-tuple-element.25.own, bf16[8,80,128]{2,1,0:T(8,128)(2,1)S(1)} %collective-permute-done.7.partner, bf16[8,80,128]{2,1,0:T(8,128)(2,1)S(1)} %broadcast_select_fusion.2.edge, ...), custom_call_target="tpu_custom_call" | custom-call | flops 150994944 | bytes 4587520 | tf_op jit(solution)/shard_map/pallas_call | solution.py:758
  122.1 4.5 %shard_map.115 = f32[3584,128]{1,0:T(8,128)} custom-call(s32[1]{0:T(128)} %bitcast.place, s32[49]{0:T(128)S(1)} %copy-done.6, bf16[8,80,128]{2,1,0:T(8,128)(2,1)S(1)} %get-tuple-element.25.own, bf16[8,80,128]{2,1,0:T(8,128)(2,1)S(1)} %collective-permute-done.7.partner, bf16[8,80,128]{2,1,0:T(8,128)(2,1)S(1)} %broadcast_select_fusion.2.edge, ...), custom_call_target="tpu_custom_call" | custom-call | flops 150994944 | bytes 9175040 | tf_op jit(solution)/shard_map/pallas_call | solution.py:766
  126.5 1.9 %shard_map.117 = (f32[2304,256]{1,0:T(8,128)}, f32[720,256]{1,0:T(8,128)}) custom-call(s32[1]{0:T(128)} %bitcast.place, bf16[1536,256]{1,0:T(8,128)(2,1)S(1)} %constant_dynamic-update-slice_fusion.value, bf16[1536,256]{1,0:T(8,128)(2,1)S(1)} %collective-permute-done.24.other), custom_call_target="tpu_custom_call" | custom-call | flops 1 | bytes 4718592 | tf_op jit(solution)/shard_map/pallas_call | solution.py:777
  (57 shorter events, 0.9 us)
Async XLA Ops:
  0.6 14.2 %copy-start.3 = (bf16[8,512,256]{2,1,0:T(8,128)(2,1)S(1)}, bf16[8,512,256]{2,1,0:T(8,128)(2,1)}, u32[]{:S(2)}) copy-start(bf16[8,512,256]{2,1,0:T(8,128)(2,1)} %upstream.3) | copy-start | bytes 6291460
  7.7 2.3 %collective-permute-start = (bf16[24,80,128]{2,1,0:T(8,128)(2,1)}, bf16[24,80,128]{2,1,0:T(8,128)(2,1)S(1)}, u32[]{:S(2)}, u32[]{:S(2)}) collective-permute-start(bf16[24,80,128]{2,1,0:T(8,128)(2,1)} %get-tuple-element.21), channel_id=1, source_target_pairs={{0,1},{1,0},{2,3},{3,2},{4,5},{5,4},{6,7},{7,6},{8,9},{9,8},{10,11... | collective-permute-start | bytes 1474568 | tf_op jit(solution)/shard_map/ppermute | solution.py:537
  9.9 2.0 %copy-start.11 = (bf16[24,80,128]{2,1,0:T(8,128)(2,1)}, bf16[24,80,128]{2,1,0:T(8,128)(2,1)S(1)}, u32[]{:S(2)}) copy-start(bf16[24,80,128]{2,1,0:T(8,128)(2,1)S(1)} %collective-permute-done) | copy-start | bytes 1474564
  11.2 0.8 copy-start.10
  12.0 26.8 %copy-start.7 = (bf16[3,3,256,256]{3,2,1,0:T(8,128)(2,1)S(1)}, bf16[3,3,256,256]{3,2,1,0:T(8,128)(2,1)}, u32[]{:S(2)}) copy-start(bf16[3,3,256,256]{3,2,1,0:T(8,128)(2,1)} %weight.3) | copy-start | bytes 3538948
  12.0 13.2 %collective-permute-start.1 = (bf16[8,80,128]{2,1,0:T(8,128)(2,1)}, bf16[8,80,128]{2,1,0:T(8,128)(2,1)}, u32[]{:S(2)}, u32[]{:S(2)}) collective-permute-start(bf16[8,80,128]{2,1,0:T(8,128)(2,1)} %get-tuple-element.48), channel_id=1, source_target_pairs={{0,2},{1,3},{2,0},{3,1},{4,6},{5,7},{6,4},{7,5},{8,10},{9,11},{10,... | collective-permute-start | bytes 491528 | tf_op jit(solution)/shard_map/ppermute | solution.py:537
  15.9 27.8 %collective-permute-start.6 = (bf16[2,512,256]{2,1,0:T(8,128)(2,1)}, bf16[2,512,256]{2,1,0:T(8,128)(2,1)}, u32[]{:S(2)}, u32[]{:S(2)}) collective-permute-start(bf16[2,512,256]{2,1,0:T(8,128)(2,1)} %get-tuple-element.42), channel_id=1, source_target_pairs={{0,31},{1,2},{2,1},{3,4},{4,3},{5,6},{6,5},{7,8},{8,7},{9,10},{10,... | collective-permute-start | bytes 1572872 | tf_op jit(solution)/shard_map/ppermute | solution.py:610
  19.9 23.8 %collective-permute-start.5 = (bf16[2,512,256]{2,1,0:T(8,128)(2,1)}, bf16[2,512,256]{2,1,0:T(8,128)(2,1)}, u32[]{:S(2)}, u32[]{:S(2)}) collective-permute-start(bf16[2,512,256]{2,1,0:T(8,128)(2,1)} %get-tuple-element.43), channel_id=1, source_target_pairs={{0,1},{1,0},{2,3},{3,2},{4,5},{5,4},{6,7},{7,6},{8,9},{9,8},{10,11... | collective-permute-start | bytes 1572872 | tf_op jit(solution)/shard_map/ppermute | solution.py:611
  19.9 12.7 %collective-permute-start.2 = (bf16[8,80,128]{2,1,0:T(8,128)(2,1)S(1)}, bf16[8,80,128]{2,1,0:T(8,128)(2,1)S(1)}, u32[]{:S(2)}, u32[]{:S(2)}) collective-permute-start(bf16[8,80,128]{2,1,0:T(8,128)(2,1)S(1)} %get-tuple-element.47), channel_id=1, source_target_pairs={{1,3},{2,0},{5,7},{6,4},{9,11},{10,8},{13,15},{14,12},{17,19},{18,... | collective-permute-start | bytes 491528 | tf_op jit(solution)/shard_map/ppermute | solution.py:677
  33.6 10.1 %copy-start.8 = (bf16[3,3,80,256]{3,2,1,0:T(8,128)(2,1)S(1)}, bf16[3,3,80,256]{3,2,1,0:T(8,128)(2,1)}, u32[]{:S(2)}) copy-start(bf16[3,3,80,256]{3,2,1,0:T(8,128)(2,1)} %param.13) | copy-start | bytes 1105924
  33.6 10.1 %copy-start.9 = (s32[8,112]{1,0:T(8,128)S(1)}, s32[8,112]{1,0:T(8,128)}, u32[]{:S(2)}) copy-start(s32[8,112]{1,0:T(8,128)} %ranges.1) | copy-start | bytes 10756
  33.6 10.0 %collective-permute-start.3 = (bf16[10,80,128]{2,1,0:T(8,128)(2,1)S(1)}, bf16[10,80,128]{2,1,0:T(8,128)(2,1)S(1)}, u32[]{:S(2)}, u32[]{:S(2)}) collective-permute-start(bf16[10,80,128]{2,1,0:T(8,128)(2,1)S(1)} %maximum_select_fusion), channel_id=1, source_target_pairs={{0,31},{1,2},{2,1},{3,4},{4,3},{5,6},{6,5},{7,8},{8,7},{9,10},{10,... | collective-permute-start | bytes 614408 | tf_op jit(solution)/shard_map/ppermute | solution.py:700
  43.6 6.3 %collective-permute-start.4 = (bf16[4,80,128]{2,1,0:T(8,128)(2,1)S(1)}, bf16[4,80,128]{2,1,0:T(8,128)(2,1)S(1)}, u32[]{:S(2)}, u32[]{:S(2)}) collective-permute-start(bf16[4,80,128]{2,1,0:T(8,128)(2,1)S(1)} %pad_maximum_fusion.2), channel_id=1, source_target_pairs={{0,1},{1,0},{2,3},{3,2},{4,5},{5,4},{6,7},{7,6},{8,9},{9,8},{10,11... | collective-permute-start | bytes 245768 | tf_op jit(solution)/shard_map/ppermute | solution.py:702
  43.7 6.2 %copy-start.4 = (bf16[8,512,256]{2,1,0:T(8,128)(2,1)S(1)}, bf16[8,512,256]{2,1,0:T(8,128)(2,1)}, u32[]{:S(2)}) copy-start(bf16[8,512,256]{2,1,0:T(8,128)(2,1)} %upstream.3) | copy-start | bytes 6291460
  67.4 2.5 %collective-permute-start.11 = (bf16[1536,256]{1,0:T(8,128)(2,1)S(1)}, bf16[1536,256]{1,0:T(8,128)(2,1)S(1)}, u32[]{:S(2)}, u32[]{:S(2)}) collective-permute-start(bf16[1536,256]{1,0:T(8,128)(2,1)S(1)} %get-tuple-element.31), channel_id=1, source_target_pairs={{0,1},{1,0},{2,3},{3,2},{4,5},{5,4},{6,7},{7,6},{8,9},{9,8},{10,11... | collective-permute-start | bytes 2359304 | tf_op jit(solution)/shard_map/ppermute | solution.py:537
  70.1 6.7 %collective-permute-start.12 = (bf16[384,256]{1,0:T(8,128)(2,1)S(1)}, bf16[384,256]{1,0:T(8,128)(2,1)S(1)}, u32[]{:S(2)}, u32[]{:S(2)}) collective-permute-start(bf16[384,256]{1,0:T(8,128)(2,1)S(1)} %get-tuple-element.44), channel_id=1, source_target_pairs={{0,6},{1,25},{2,4},{3,27},{4,2},{5,29},{6,0},{7,31},{8,14},{9,17},... | collective-permute-start | bytes 589832 | tf_op jit(solution)/shard_map/ppermute | solution.py:560
  70.2 7.8 %collective-permute-start.14 = (bf16[384,256]{1,0:T(8,128)(2,1)S(1)}, bf16[384,256]{1,0:T(8,128)(2,1)S(1)}, u32[]{:S(2)}, u32[]{:S(2)}) collective-permute-start(bf16[384,256]{1,0:T(8,128)(2,1)S(1)} %get-tuple-element.45), channel_id=1, source_target_pairs={{0,4},{1,17},{2,6},{3,19},{4,0},{5,21},{6,2},{7,23},{8,12},{9,25},... | collective-permute-start | bytes 589832 | tf_op jit(solution)/shard_map/ppermute | solution.py:560
  70.2 7.8 %collective-permute-start.13 = (bf16[384,256]{1,0:T(8,128)(2,1)S(1)}, bf16[384,256]{1,0:T(8,128)(2,1)S(1)}, u32[]{:S(2)}, u32[]{:S(2)}) collective-permute-start(bf16[384,256]{1,0:T(8,128)(2,1)S(1)} %get-tuple-element.46), channel_id=1, source_target_pairs={{0,2},{1,9},{2,0},{3,11},{4,6},{5,13},{6,4},{7,15},{8,10},{9,1},{1... | collective-permute-start | bytes 589832 | tf_op jit(solution)/shard_map/ppermute | solution.py:560
  78.2 6.0 %collective-permute-start.15 = (bf16[96,256]{1,0:T(8,128)(2,1)S(1)}, bf16[96,256]{1,0:T(8,128)(2,1)S(1)}, u32[]{:S(2)}, u32[]{:S(2)}) collective-permute-start(bf16[96,256]{1,0:T(8,128)(2,1)S(1)} %get-tuple-element.49), channel_id=1, source_target_pairs={{0,24},{1,7},{2,26},{3,5},{4,28},{5,3},{6,30},{7,1},{8,16},{9,15},... | collective-permute-start | bytes 147464 | tf_op jit(solution)/shard_map/ppermute | solution.py:560
  80.9 5.0 %collective-permute-start.17 = (bf16[96,256]{1,0:T(8,128)(2,1)S(1)}, bf16[96,256]{1,0:T(8,128)(2,1)S(1)}, u32[]{:S(2)}, u32[]{:S(2)}) collective-permute-start(bf16[96,256]{1,0:T(8,128)(2,1)S(1)} %get-tuple-element.50), channel_id=1, source_target_pairs={{0,16},{1,5},{2,18},{3,7},{4,20},{5,1},{6,22},{7,3},{8,24},{9,13},... | collective-permute-start | bytes 147464 | tf_op jit(solution)/shard_map/ppermute | solution.py:560
  80.9 5.0 %collective-permute-start.16 = (bf16[96,256]{1,0:T(8,128)(2,1)S(1)}, bf16[96,256]{1,0:T(8,128)(2,1)S(1)}, u32[]{:S(2)}, u32[]{:S(2)}) collective-permute-start(bf16[96,256]{1,0:T(8,128)(2,1)S(1)} %get-tuple-element.51), channel_id=1, source_target_pairs={{0,8},{1,3},{2,10},{3,1},{4,12},{5,7},{6,14},{7,5},{8,0},{9,11},{1... | collective-permute-start | bytes 147464 | tf_op jit(solution)/shard_map/ppermute | solution.py:560
  85.9 4.5 %collective-permute-start.20 = (bf16[96,256]{1,0:T(8,128)(2,1)S(1)}, bf16[96,256]{1,0:T(8,128)(2,1)S(1)}, u32[]{:S(2)}, u32[]{:S(2)}) collective-permute-start(bf16[96,256]{1,0:T(8,128)(2,1)S(1)} %add_convert_fusion.5), channel_id=1, source_target_pairs={{0,8},{1,3},{2,10},{3,1},{4,12},{5,7},{6,14},{7,5},{8,0},{9,11},{1... | collective-permute-start | bytes 147464 | tf_op jit(solution)/shard_map/ppermute | solution.py:560
  86.8 5.0 %collective-permute-start.19 = (bf16[96,256]{1,0:T(8,128)(2,1)S(1)}, bf16[96,256]{1,0:T(8,128)(2,1)S(1)}, u32[]{:S(2)}, u32[]{:S(2)}) collective-permute-start(bf16[96,256]{1,0:T(8,128)(2,1)S(1)} %add_convert_fusion.5), channel_id=1, source_target_pairs={{0,16},{1,5},{2,18},{3,7},{4,20},{5,1},{6,22},{7,3},{8,24},{9,13},... | collective-permute-start | bytes 147464 | tf_op jit(solution)/shard_map/ppermute | solution.py:560
  88.5 5.9 %collective-permute-start.18 = (bf16[96,256]{1,0:T(8,128)(2,1)S(1)}, bf16[96,256]{1,0:T(8,128)(2,1)S(1)}, u32[]{:S(2)}, u32[]{:S(2)}) collective-permute-start(bf16[96,256]{1,0:T(8,128)(2,1)S(1)} %add_convert_fusion.5), channel_id=1, source_target_pairs={{0,24},{1,7},{2,26},{3,5},{4,28},{5,3},{6,30},{7,1},{8,16},{9,15},... | collective-permute-start | bytes 147464 | tf_op jit(solution)/shard_map/ppermute | solution.py:560
  94.5 23.3 %copy-start = (f32[129,32,128]{2,1,0:T(8,128)S(1)}, f32[129,32,128]{2,1,0:T(8,128)}, u32[]{:S(2)}) copy-start(f32[129,32,128]{2,1,0:T(8,128)} %get-tuple-element.29.probs_t) | copy-start | bytes 6340612
  94.6 23.3 %copy-start.6 = (s32[49]{0:T(128)S(1)}, s32[49]{0:T(128)}, u32[]{:S(2)}) copy-start(s32[49]{0:T(128)} %get-tuple-element.19.begins) | copy-start | bytes 592
  94.7 13.6 %collective-permute-start.21 = (bf16[384,256]{1,0:T(8,128)(2,1)S(1)}, bf16[384,256]{1,0:T(8,128)(2,1)}, u32[]{:S(2)}, u32[]{:S(2)}) collective-permute-start(bf16[384,256]{1,0:T(8,128)(2,1)S(1)} %pad_maximum_fusion.1), channel_id=1, source_target_pairs={{0,2},{1,9},{2,0},{3,11},{4,6},{5,13},{6,4},{7,15},{8,10},{9,1},{1... | collective-permute-start | bytes 589832 | tf_op jit(solution)/shard_map/ppermute | solution.py:560
  96.4 10.4 %collective-permute-start.8 = (bf16[8,80,128]{2,1,0:T(8,128)(2,1)S(1)}, bf16[8,80,128]{2,1,0:T(8,128)(2,1)}, u32[]{:S(2)}, u32[]{:S(2)}) collective-permute-start(bf16[8,80,128]{2,1,0:T(8,128)(2,1)S(1)} %get-tuple-element.26), channel_id=1, source_target_pairs={{0,31},{4,3},{8,7},{12,11},{16,15},{20,19},{24,23},{28,27},{3,4},{... | collective-permute-start | bytes 491528 | tf_op jit(solution)/shard_map/ppermute | solution.py:698
  98.3 10.8 %collective-permute-start.22 = (bf16[384,256]{1,0:T(8,128)(2,1)S(1)}, bf16[384,256]{1,0:T(8,128)(2,1)}, u32[]{:S(2)}, u32[]{:S(2)}) collective-permute-start(bf16[384,256]{1,0:T(8,128)(2,1)S(1)} %pad_maximum_fusion.1), channel_id=1, source_target_pairs={{0,4},{1,17},{2,6},{3,19},{4,0},{5,21},{6,2},{7,23},{8,12},{9,25},... | collective-permute-start | bytes 589832 | tf_op jit(solution)/shard_map/ppermute | solution.py:560
  99.2 16.7 %collective-permute-start.7 = (bf16[8,80,128]{2,1,0:T(8,128)(2,1)S(1)}, bf16[8,80,128]{2,1,0:T(8,128)(2,1)S(1)}, u32[]{:S(2)}, u32[]{:S(2)}) collective-permute-start(bf16[8,80,128]{2,1,0:T(8,128)(2,1)S(1)} %get-tuple-element.25.own), channel_id=1, source_target_pairs={{0,2},{1,3},{2,0},{3,1},{4,6},{5,7},{6,4},{7,5},{8,10},{9,11},{10,... | collective-permute-start | bytes 491528 | tf_op jit(solution)/shard_map/ppermute | solution.py:537
  106.9 8.0 %collective-permute-start.9 = (bf16[8,80,128]{2,1,0:T(8,128)(2,1)}, bf16[8,80,128]{2,1,0:T(8,128)(2,1)S(1)}, u32[]{:S(2)}, u32[]{:S(2)}) collective-permute-start(bf16[8,80,128]{2,1,0:T(8,128)(2,1)} %collective-permute-done.8), channel_id=1, source_target_pairs={{3,1},{0,2},{7,5},{4,6},{11,9},{8,10},{15,13},{12,14},{19,17},{16,... | collective-permute-start | bytes 491528 | tf_op jit(solution)/shard_map/ppermute | solution.py:748
  108.2 6.6 %collective-permute-start.23 = (bf16[384,256]{1,0:T(8,128)(2,1)S(1)}, bf16[384,256]{1,0:T(8,128)(2,1)S(1)}, u32[]{:S(2)}, u32[]{:S(2)}) collective-permute-start(bf16[384,256]{1,0:T(8,128)(2,1)S(1)} %pad_maximum_fusion.1), channel_id=1, source_target_pairs={{0,6},{1,25},{2,4},{3,27},{4,2},{5,29},{6,0},{7,31},{8,14},{9,17},... | collective-permute-start | bytes 589832 | tf_op jit(solution)/shard_map/ppermute | solution.py:560
  114.8 11.7 %collective-permute-start.24 = (bf16[1536,256]{1,0:T(8,128)(2,1)S(1)}, bf16[1536,256]{1,0:T(8,128)(2,1)S(1)}, u32[]{:S(2)}, u32[]{:S(2)}) collective-permute-start(bf16[1536,256]{1,0:T(8,128)(2,1)S(1)} %constant_dynamic-update-slice_fusion.value), channel_id=1, source_target_pairs={{0,1},{1,0},{2,3},{3,2},{4,5},{5,4},{6,7},{7,6},{8,9},{9,8},{10,11... | collective-permute-start | bytes 2359304 | tf_op jit(solution)/shard_map/ppermute | solution.py:537
  115.9 6.2 %copy-start.2 = (f32[3584,128]{1,0:T(8,128)S(1)}, f32[3584,128]{1,0:T(8,128)}, u32[]{:S(2)}) copy-start(f32[3584,128]{1,0:T(8,128)} %get-tuple-element.27.probs) | copy-start | bytes 5505028
  115.9 1.9 %collective-permute-start.10 = (bf16[24,80,128]{2,1,0:T(8,128)(2,1)S(1)}, bf16[24,80,128]{2,1,0:T(8,128)(2,1)S(1)}, u32[]{:S(2)}, u32[]{:S(2)}) collective-permute-start(bf16[24,80,128]{2,1,0:T(8,128)(2,1)S(1)} %pad_maximum_fusion), channel_id=1, source_target_pairs={{0,1},{1,0},{2,3},{3,2},{4,5},{5,4},{6,7},{7,6},{8,9},{9,8},{10,11... | collective-permute-start | bytes 1474568 | tf_op jit(solution)/shard_map/ppermute | solution.py:537
  117.9 4.2 %copy-start.1 = (f32[129,32,128]{2,1,0:T(8,128)S(1)}, f32[129,32,128]{2,1,0:T(8,128)}, u32[]{:S(2)}) copy-start(f32[129,32,128]{2,1,0:T(8,128)} %get-tuple-element.28.context_t) | copy-start | bytes 6340612
  117.9 4.2 %copy-start.5 = (s32[1,32,128]{2,1,0:T(8,128)S(1)}, s32[1,32,128]{2,1,0:T(8,128)}, u32[]{:S(2)}) copy-start(s32[1,32,128]{2,1,0:T(8,128)} %param.10) | copy-start | bytes 49156
